TPU v7x, 32 devices: a whole 2x2x4 slice. The times are simulated.
32 devices in a mesh: wide: 8 (over y, x, core), narrow: 4 (over z).
Axes of the slice: x: 2, y: 2, z: 4, core: 2. Of those that a mesh axis runs over, the one named last changes fastest.
Arguments:
- long_tokens: bfloat16 [32, 512, 768], P(('wide', 'narrow')), may hold values from -6 to 6
- long_lengths: int32 [32], P(('wide', 'narrow')), may hold values from 129 to 512, as said below
- short_tokens: bfloat16 [64, 128, 768], P(('wide', 'narrow')), may hold values from -6 to 6
- short_lengths: int32 [64], P(('wide', 'narrow')), may hold values from 33 to 128, as said below
- w_qkv: bfloat16 [768, 1152], P('narrow'), may hold values from -0.21875 to 0.21875
- w_depth: bfloat16 [9, 768], P(None, 'narrow'), may hold values from -2 to 2
- w_point: bfloat16 [768, 384], P('narrow'), may hold values from -0.21875 to 0.21875
- w_kernel: bfloat16 [384, 54], P('narrow'), may hold values from -0.3125 to 0.3125
- w_convout: bfloat16 [768, 384], P('narrow'), may hold values from -0.21875 to 0.21875
- w_out: bfloat16 [768, 768], P('narrow'), may hold values from -0.875 to 0.875
- norm1_gain: bfloat16 [768], P('narrow'), may hold values from 0.5 to 1.5
- norm1_bias: bfloat16 [768], P('narrow'), may hold values from -1.796875 to 1.796875
- w_inner: bfloat16 [2, 384, 1536], P(None, 'narrow'), may hold values from -0.3125 to 0.3125
- w_outer: bfloat16 [2, 1536, 384], P(None, 'narrow'), may hold values from -0.15625 to 0.15625
- norm2_gain: bfloat16 [768], P('narrow'), may hold values from 0.5 to 1.5
- norm2_bias: bfloat16 [768], P('narrow'), may hold values from -1.796875 to 1.796875
- long_cotangent: bfloat16 [32, 512, 768], P(('wide', 'narrow')), may hold values from -6 to 6
- short_cotangent: bfloat16 [64, 128, 768], P(('wide', 'narrow')), may hold values from -6 to 6
Outputs:
- long_output: bfloat16 [32, 512, 768], P(('wide', 'narrow'))
- short_output: bfloat16 [64, 128, 768], P(('wide', 'narrow'))
- long_input_grad: bfloat16 [32, 512, 768], P(('wide', 'narrow'))
- short_input_grad: bfloat16 [64, 128, 768], P(('wide', 'narrow'))
- grad_qkv: float32 [768, 1152], P('narrow')
- grad_depth: float32 [9, 768], P(None, 'narrow')
- grad_point: float32 [768, 384], P('narrow')
- grad_kernel: float32 [384, 54], P('narrow')
- grad_convout: float32 [768, 384], P('narrow')
- grad_out: float32 [768, 768], P('narrow')
- grad_norm1_gain: float32 [768], P('narrow')
- grad_norm1_bias: float32 [768], P('narrow')
- grad_inner: float32 [2, 384, 1536], P(None, 'narrow')
- grad_outer: float32 [2, 1536, 384], P(None, 'narrow')
- grad_norm2_gain: float32 [768], P('narrow')
- grad_norm2_bias: float32 [768], P('narrow')
Inputs may be any that keep to these rules, and one draw needn't show every extreme that they name: `long_lengths`: each long row holds this many live tokens from its start, the rest is padding; some row is full and some row has the fewest allowed. `short_lengths`: each short row holds this many live tokens from its start, the rest is padding; some row is full and some row has the fewest allowed.
All inputs are finite; a program needn't handle non-finite values.
Results may differ from a plain program's by a relative error of at most 0.017.
Values may be sent and summed in bfloat16 or wider, within the bound.
No kernel may reach another device: no remote copies, remote signals or barrier semaphores. Data moves between devices by JAX's collectives and lax.ppermute only.
A program may use at most 192 MiB of HBM per device.

v0:
```python
import jax
import jax.numpy as jnp
from jax import lax
from jax.sharding import PartitionSpec as P

HEADS = 6


norm_eps = 1e-12


def project(left_side, right_side):
    return jnp.einsum("...d,df->...f", left_side, right_side, preferred_element_type=jnp.float32)


def layer_norm(values, norm_gain, norm_bias):
    center = values - jnp.mean(values, -1, keepdims=True)
    spread = jnp.mean(center * center, -1, keepdims=True)
    return center * lax.rsqrt(spread + norm_eps) * norm_gain + norm_bias


def exact_gelu(values):
    return jax.nn.gelu(values, approximate=False)


def depth_conv(values, taps_weight):
    kernel_taps = taps_weight.shape[0]
    half_taps = kernel_taps // 2
    length = values.shape[1]
    padded = jnp.pad(values, ((0, 0), (half_taps, half_taps), (0, 0)))
    result = jnp.zeros(values.shape, jnp.float32)
    for offset in range(kernel_taps):
        result = result + taps_weight[offset] * padded[:, offset : offset + length, :]
    return result


def dynamic_conv(logits, values):
    kernel_probs = jax.nn.softmax(logits, axis=-1)
    batches, length, head_count, kernel_taps = logits.shape
    half_taps = kernel_taps // 2
    padded = jnp.pad(values, ((0, 0), (half_taps, half_taps), (0, 0)))
    result = jnp.zeros((batches, length, head_count, values.shape[2] // head_count), jnp.float32)
    for offset in range(kernel_taps):
        window_piece = padded[:, offset : offset + length, :].reshape(
            batches, length, head_count, -1
        )
        result = result + kernel_probs[:, :, :, offset][..., None] * window_piece
    return result.reshape(batches, length, -1)


def attention_scores(query_heads, key_heads, valid_rows):
    head_size = query_heads.shape[-1]
    raw_scores = jnp.einsum(
        "blhe,bmhe->bhlm", query_heads, key_heads, preferred_element_type=jnp.float32
    ) * head_size ** (-0.5)
    return jnp.where(valid_rows[:, None, None, :], raw_scores, -1000000000.0)


def split_heads(packed, inner_width):
    batches, length = (packed.shape[0], packed.shape[1])
    head_size = inner_width // HEADS
    query_heads = packed[:, :, :inner_width].reshape(batches, length, HEADS, head_size)
    key_heads = packed[:, :, inner_width : 2 * inner_width].reshape(
        batches, length, HEADS, head_size
    )
    value_heads = packed[:, :, 2 * inner_width :].reshape(batches, length, HEADS, head_size)
    return (query_heads, key_heads, value_heads)


def forward_bucket(weights, tokens, lengths):
    (
        w_qkv,
        w_depth,
        w_point,
        w_kernel,
        w_convout,
        w_out,
        gain_one,
        bias_one,
        w_inner,
        w_outer,
        gain_two,
        bias_two,
    ) = weights
    batches, length, model_width = tokens.shape
    inner_width = w_point.shape[1]
    groups = w_inner.shape[0]
    valid_rows = jnp.arange(length)[None, :] < lengths[:, None]
    masked = jnp.where(valid_rows[:, :, None], tokens, jnp.zeros((), jnp.bfloat16))
    packed = project(masked, w_qkv).astype(jnp.bfloat16)
    query_heads, key_heads, value_heads = split_heads(packed, inner_width)
    scores = attention_scores(query_heads, key_heads, valid_rows)
    row_max = jnp.max(scores, -1, keepdims=True)
    exp_scores = jnp.exp(scores - row_max)
    row_total = jnp.sum(exp_scores, -1, keepdims=True)
    attn_probs = exp_scores / row_total
    log_total = row_max + jnp.log(row_total)
    attended = jnp.einsum(
        "bhlm,bmhe->blhe",
        attn_probs.astype(jnp.bfloat16),
        value_heads,
        preferred_element_type=jnp.float32,
    ).reshape(batches, length, inner_width)
    depthwise = depth_conv(masked.astype(jnp.float32), w_depth.astype(jnp.float32)).astype(
        jnp.bfloat16
    )
    key_conv = project(depthwise, w_point)
    conv_query = (key_conv * packed[:, :, :inner_width].astype(jnp.float32)).astype(jnp.bfloat16)
    kernel_logits = project(conv_query, w_kernel).reshape(batches, length, HEADS, -1)
    conv_values = project(masked, w_convout)
    convolved = dynamic_conv(kernel_logits, conv_values)
    context = jnp.concatenate([attended, convolved], axis=-1).astype(jnp.bfloat16)
    residual_one = project(context, w_out) + masked.astype(jnp.float32)
    first_norm = layer_norm(
        residual_one, gain_one.astype(jnp.float32), bias_one.astype(jnp.float32)
    )
    grouped = first_norm.astype(jnp.bfloat16).reshape(
        batches, length, groups, model_width // groups
    )
    hidden = jnp.einsum("blgd,gdf->blgf", grouped, w_inner, preferred_element_type=jnp.float32)
    active = exact_gelu(hidden).astype(jnp.bfloat16)
    ffn_out = jnp.einsum(
        "blgf,gfd->blgd", active, w_outer, preferred_element_type=jnp.float32
    ).reshape(batches, length, model_width)
    residual_two = ffn_out + first_norm
    output = layer_norm(
        residual_two, gain_two.astype(jnp.float32), bias_two.astype(jnp.float32)
    ).astype(jnp.bfloat16)
    saved = (
        valid_rows,
        masked,
        packed,
        log_total,
        depthwise,
        key_conv,
        conv_query,
        kernel_logits,
        conv_values,
        context,
        residual_one,
        grouped,
        hidden,
        active,
        residual_two,
    )
    return (output, saved)


def backward_top(weights, saved, cotangent):
    (
        w_qkv,
        w_depth,
        w_point,
        w_kernel,
        w_convout,
        w_out,
        gain_one,
        bias_one,
        w_inner,
        w_outer,
        gain_two,
        bias_two,
    ) = weights
    (
        valid_rows,
        masked,
        packed,
        log_total,
        depthwise,
        key_conv,
        conv_query,
        kernel_logits,
        conv_values,
        context,
        residual_one,
        grouped,
        hidden,
        active,
        residual_two,
    ) = saved
    batches, length, model_width = residual_two.shape
    groups = w_inner.shape[0]
    upstream = cotangent.astype(jnp.float32) * valid_rows[:, :, None].astype(jnp.float32)
    second_out, second_pull = jax.vjp(
        layer_norm, residual_two, gain_two.astype(jnp.float32), bias_two.astype(jnp.float32)
    )
    grad_two, grad_gain_two, grad_bias_two = second_pull(upstream)
    grad_ffn = grad_two.astype(jnp.bfloat16).reshape(batches, length, groups, model_width // groups)
    grad_outer = jnp.einsum("blgf,blgd->gfd", active, grad_ffn, preferred_element_type=jnp.float32)
    grad_active = jnp.einsum(
        "blgd,gfd->blgf", grad_ffn, w_outer, preferred_element_type=jnp.float32
    )
    gelu_out, gelu_pull = jax.vjp(exact_gelu, hidden)
    grad_hidden = gelu_pull(grad_active)[0].astype(jnp.bfloat16)
    grad_inner = jnp.einsum(
        "blgd,blgf->gdf", grouped, grad_hidden, preferred_element_type=jnp.float32
    )
    grad_first = grad_two + jnp.einsum(
        "blgf,gdf->blgd", grad_hidden, w_inner, preferred_element_type=jnp.float32
    ).reshape(batches, length, model_width)
    first_out, first_pull = jax.vjp(
        layer_norm, residual_one, gain_one.astype(jnp.float32), bias_one.astype(jnp.float32)
    )
    grad_one, grad_gain_one, grad_bias_one = first_pull(grad_first)
    return (
        grad_one,
        (grad_inner, grad_outer, grad_gain_one, grad_bias_one, grad_gain_two, grad_bias_two),
    )


def backward_mix(weights, saved, grad_one):
    (
        w_qkv,
        w_depth,
        w_point,
        w_kernel,
        w_convout,
        w_out,
        gain_one,
        bias_one,
        w_inner,
        w_outer,
        gain_two,
        bias_two,
    ) = weights
    (
        valid_rows,
        masked,
        packed,
        log_total,
        depthwise,
        key_conv,
        conv_query,
        kernel_logits,
        conv_values,
        context,
        residual_one,
        grouped,
        hidden,
        active,
        residual_two,
    ) = saved
    batches, length, model_width = masked.shape
    inner_width = w_point.shape[1]
    head_size = inner_width // HEADS
    grad_proj = grad_one.astype(jnp.bfloat16)
    grad_out = jnp.einsum("bld,blf->df", context, grad_proj, preferred_element_type=jnp.float32)
    grad_context = jnp.einsum(
        "blf,df->bld", grad_proj, w_out, preferred_element_type=jnp.float32
    ).astype(jnp.bfloat16)
    grad_attended = grad_context[:, :, :inner_width].reshape(batches, length, HEADS, head_size)
    grad_convolved = grad_context[:, :, inner_width:].astype(jnp.float32)
    conv_out, conv_pull = jax.vjp(dynamic_conv, kernel_logits, conv_values)
    grad_logits, grad_values = conv_pull(grad_convolved)
    grad_logits = grad_logits.reshape(batches, length, -1).astype(jnp.bfloat16)
    grad_values = grad_values.astype(jnp.bfloat16)
    grad_kernel = jnp.einsum(
        "bla,blk->ak", conv_query, grad_logits, preferred_element_type=jnp.float32
    )
    grad_query_in = jnp.einsum(
        "blk,ak->bla", grad_logits, w_kernel, preferred_element_type=jnp.float32
    )
    query_heads, key_heads, value_heads = split_heads(packed, inner_width)
    grad_key_conv = (grad_query_in * packed[:, :, :inner_width].astype(jnp.float32)).astype(
        jnp.bfloat16
    )
    grad_query_conv = grad_query_in * key_conv
    grad_point = jnp.einsum(
        "bld,bla->da", depthwise, grad_key_conv, preferred_element_type=jnp.float32
    )
    grad_depthwise = jnp.einsum(
        "bla,da->bld", grad_key_conv, w_point, preferred_element_type=jnp.float32
    ).astype(jnp.bfloat16)
    depth_out, depth_pull = jax.vjp(
        depth_conv, masked.astype(jnp.float32), w_depth.astype(jnp.float32)
    )
    grad_masked_depth, grad_depth = depth_pull(grad_depthwise.astype(jnp.float32))
    grad_convout = jnp.einsum(
        "bld,bla->da", masked, grad_values, preferred_element_type=jnp.float32
    )
    grad_masked = (
        grad_one
        + grad_masked_depth
        + jnp.einsum("bla,da->bld", grad_values, w_convout, preferred_element_type=jnp.float32)
    )
    scores = attention_scores(query_heads, key_heads, valid_rows)
    attn_probs = jnp.exp(scores - log_total)
    grad_value_heads = jnp.einsum(
        "bhlm,blhe->bmhe",
        attn_probs.astype(jnp.bfloat16),
        grad_attended,
        preferred_element_type=jnp.float32,
    )
    grad_probs = jnp.einsum(
        "blhe,bmhe->bhlm", grad_attended, value_heads, preferred_element_type=jnp.float32
    )
    row_inner = jnp.sum(attn_probs * grad_probs, -1, keepdims=True)
    grad_scores = (attn_probs * (grad_probs - row_inner)).astype(jnp.bfloat16)
    score_scale = head_size ** (-0.5)
    grad_query_heads = (
        jnp.einsum("bhlm,bmhe->blhe", grad_scores, key_heads, preferred_element_type=jnp.float32)
        * score_scale
    )
    grad_key_heads = (
        jnp.einsum("bhlm,blhe->bmhe", grad_scores, query_heads, preferred_element_type=jnp.float32)
        * score_scale
    )
    grad_packed = jnp.concatenate(
        [
            grad_query_heads.reshape(batches, length, inner_width) + grad_query_conv,
            grad_key_heads.reshape(batches, length, inner_width),
            grad_value_heads.reshape(batches, length, inner_width),
        ],
        axis=-1,
    ).astype(jnp.bfloat16)
    grad_qkv = jnp.einsum("bld,blf->df", masked, grad_packed, preferred_element_type=jnp.float32)
    grad_masked = grad_masked + jnp.einsum(
        "blf,df->bld", grad_packed, w_qkv, preferred_element_type=jnp.float32
    )
    input_grad = (grad_masked * valid_rows[:, :, None].astype(jnp.float32)).astype(jnp.bfloat16)
    return (input_grad, (grad_qkv, grad_depth, grad_point, grad_kernel, grad_convout, grad_out))


def add_pairs(first_set, second_set):
    return tuple(
        (first_item + second_item for first_item, second_item in zip(first_set, second_set))
    )


def body(
    long_tokens,
    long_lengths,
    short_tokens,
    short_lengths,
    w_qkv,
    w_depth,
    w_point,
    w_kernel,
    w_convout,
    w_out,
    norm1_gain,
    norm1_bias,
    w_inner,
    w_outer,
    norm2_gain,
    norm2_bias,
    long_cotangent,
    short_cotangent,
):
    gathered = (
        lax.all_gather(w_qkv, "narrow", axis=0, tiled=True),
        lax.all_gather(w_depth, "narrow", axis=1, tiled=True),
        lax.all_gather(w_point, "narrow", axis=0, tiled=True),
        lax.all_gather(w_kernel, "narrow", axis=0, tiled=True),
        lax.all_gather(w_convout, "narrow", axis=0, tiled=True),
        lax.all_gather(w_out, "narrow", axis=0, tiled=True),
        lax.all_gather(norm1_gain, "narrow", axis=0, tiled=True),
        lax.all_gather(norm1_bias, "narrow", axis=0, tiled=True),
        lax.all_gather(w_inner, "narrow", axis=1, tiled=True),
        lax.all_gather(w_outer, "narrow", axis=1, tiled=True),
        lax.all_gather(norm2_gain, "narrow", axis=0, tiled=True),
        lax.all_gather(norm2_bias, "narrow", axis=0, tiled=True),
    )
    long_output, long_saved = forward_bucket(gathered, long_tokens, long_lengths)
    short_output, short_saved = forward_bucket(gathered, short_tokens, short_lengths)
    weights_back = (
        lax.all_gather(w_qkv, "narrow", axis=0, tiled=True),
        lax.all_gather(w_depth, "narrow", axis=1, tiled=True),
        lax.all_gather(w_point, "narrow", axis=0, tiled=True),
        lax.all_gather(w_kernel, "narrow", axis=0, tiled=True),
        lax.all_gather(w_convout, "narrow", axis=0, tiled=True),
        lax.all_gather(w_out, "narrow", axis=0, tiled=True),
        lax.all_gather(norm1_gain, "narrow", axis=0, tiled=True),
        lax.all_gather(norm1_bias, "narrow", axis=0, tiled=True),
        lax.all_gather(w_inner, "narrow", axis=1, tiled=True),
        lax.all_gather(w_outer, "narrow", axis=1, tiled=True),
        lax.all_gather(norm2_gain, "narrow", axis=0, tiled=True),
        lax.all_gather(norm2_bias, "narrow", axis=0, tiled=True),
    )
    long_upper, long_top = backward_top(weights_back, long_saved, long_cotangent)
    short_upper, short_top = backward_top(weights_back, short_saved, short_cotangent)
    grad_inner, grad_outer, grad_gain_one, grad_bias_one, grad_gain_two, grad_bias_two = add_pairs(
        long_top, short_top
    )
    long_input_grad, long_mix = backward_mix(weights_back, long_saved, long_upper)
    short_input_grad, short_mix = backward_mix(weights_back, short_saved, short_upper)
    grad_qkv, grad_depth, grad_point, grad_kernel, grad_convout, grad_out = add_pairs(
        long_mix, short_mix
    )
    grad_parts = (
        lax.psum_scatter(
            grad_qkv.astype(jnp.bfloat16), "narrow", scatter_dimension=0, tiled=True
        ).astype(jnp.float32),
        lax.psum_scatter(
            grad_depth.astype(jnp.bfloat16), "narrow", scatter_dimension=1, tiled=True
        ).astype(jnp.float32),
        lax.psum_scatter(
            grad_point.astype(jnp.bfloat16), "narrow", scatter_dimension=0, tiled=True
        ).astype(jnp.float32),
        lax.psum_scatter(
            grad_kernel.astype(jnp.bfloat16), "narrow", scatter_dimension=0, tiled=True
        ).astype(jnp.float32),
        lax.psum_scatter(
            grad_convout.astype(jnp.bfloat16), "narrow", scatter_dimension=0, tiled=True
        ).astype(jnp.float32),
        lax.psum_scatter(
            grad_out.astype(jnp.bfloat16), "narrow", scatter_dimension=0, tiled=True
        ).astype(jnp.float32),
        lax.psum_scatter(
            grad_inner.astype(jnp.bfloat16), "narrow", scatter_dimension=1, tiled=True
        ).astype(jnp.float32),
        lax.psum_scatter(
            grad_outer.astype(jnp.bfloat16), "narrow", scatter_dimension=1, tiled=True
        ).astype(jnp.float32),
        lax.psum_scatter(
            grad_gain_one.astype(jnp.bfloat16), "narrow", scatter_dimension=0, tiled=True
        ).astype(jnp.float32),
        lax.psum_scatter(
            grad_bias_one.astype(jnp.bfloat16), "narrow", scatter_dimension=0, tiled=True
        ).astype(jnp.float32),
        lax.psum_scatter(
            grad_gain_two.astype(jnp.bfloat16), "narrow", scatter_dimension=0, tiled=True
        ).astype(jnp.float32),
        lax.psum_scatter(
            grad_bias_two.astype(jnp.bfloat16), "narrow", scatter_dimension=0, tiled=True
        ).astype(jnp.float32),
    )
    (
        grad_qkv,
        grad_depth,
        grad_point,
        grad_kernel,
        grad_convout,
        grad_out,
        grad_inner,
        grad_outer,
        grad_gain_one,
        grad_bias_one,
        grad_gain_two,
        grad_bias_two,
    ) = lax.psum(
        (
            grad_parts[0],
            grad_parts[1],
            grad_parts[2],
            grad_parts[3],
            grad_parts[4],
            grad_parts[5],
            grad_parts[6],
            grad_parts[7],
            grad_parts[8],
            grad_parts[9],
            grad_parts[10],
            grad_parts[11],
        ),
        "wide",
    )
    return (
        long_output,
        short_output,
        long_input_grad,
        short_input_grad,
        grad_qkv,
        grad_depth,
        grad_point,
        grad_kernel,
        grad_convout,
        grad_out,
        grad_gain_one,
        grad_bias_one,
        grad_inner,
        grad_outer,
        grad_gain_two,
        grad_bias_two,
    )


def solution(mesh):
    return jax.shard_map(
        body,
        mesh=mesh,
        in_specs=(
            P(("wide", "narrow"), None, None),
            P(("wide", "narrow")),
            P(("wide", "narrow"), None, None),
            P(("wide", "narrow")),
            P("narrow", None),
            P(None, "narrow"),
            P("narrow", None),
            P("narrow", None),
            P("narrow", None),
            P("narrow", None),
            P("narrow"),
            P("narrow"),
            P(None, "narrow", None),
            P(None, "narrow", None),
            P("narrow"),
            P("narrow"),
            P(("wide", "narrow"), None, None),
            P(("wide", "narrow"), None, None),
        ),
        out_specs=(
            P(("wide", "narrow"), None, None),
            P(("wide", "narrow"), None, None),
            P(("wide", "narrow"), None, None),
            P(("wide", "narrow"), None, None),
            P("narrow", None),
            P(None, "narrow"),
            P("narrow", None),
            P("narrow", None),
            P("narrow", None),
            P("narrow", None),
            P("narrow"),
            P("narrow"),
            P(None, "narrow", None),
            P(None, "narrow", None),
            P("narrow"),
            P("narrow"),
        ),
        check_vma=False,
    )
```

profile of v0, /device:TPU:0, one launch (start us, length us, event | category | flops | bytes accessed | tf_op | source)
XLA Modules:
  0.0 723.5 jit_solution(1136512314881286692)
XLA Ops:
  11.7 15.3 %all-gather.1 = bf16[4,96,54]{1,2,0:T(8,128)(2,1)S(1)} all-gather(bf16[1,96,54]{1,2,0:T(8,128)(2,1)} %bitcast.759), channel_id=1, replica_groups=mesh['wide'=8,'narrow'=4] {'narrow'}, dimensions={0}, use_global_device_ids=true | all-gather | bytes 51840 | tf_op jit(solution)/shard_map/all_gather | solution.py:354
  29.8 24.2 %all_gather.50 = bf16[768,384]{1,0:T(8,128)(2,1)S(1)} all-gather(bf16[192,384]{1,0:T(8,128)(2,1)S(1)} %copy-done.156), channel_id=1, replica_groups=mesh['wide'=8,'narrow'=4] {'narrow'}, dimensions={0}, use_global_device_ids=true | all-gather | bytes 737280 | tf_op jit(solution)/shard_map/all_gather | solution.py:355
  59.9 11.2 %all-reduce.86 = (bf16[768]{0:T(1024)(128)(2,1)S(1)}, bf16[768]{0:T(1024)(128)(2,1)S(1)}, bf16[768]{0:T(1024)(128)(2,1)S(1)}) all-reduce(bf16[768]{0:T(1024)(128)(2,1)S(1)} %dynamic-update-slice.1, bf16[768]{0:T(1024)(128)(2,1)S(1)} %dynamic-update-slice, ...), channel_id=1, replica_groups=mesh['wide'=8,'narrow'=4] {'narrow'}, use_global_device_ids=true, to_apply=%add.77 | all-reduce | flops 2304 | bytes 9216
  72.9 13.3 %all-gather = bf16[4,192,9]{1,2,0:T(8,128)(2,1)S(1)} all-gather(bf16[1,192,9]{1,2,0:T(8,128)(2,1)S(1)} %bitcast.760), channel_id=1, replica_groups=mesh['wide'=8,'narrow'=4] {'narrow'}, dimensions={0}, use_global_device_ids=true | all-gather | bytes 17280 | tf_op jit(solution)/shard_map/all_gather | solution.py:352
  86.4 19.6 %all_gather.48 = bf16[768,384]{1,0:T(8,128)(2,1)S(1)} all-gather(bf16[192,384]{1,0:T(8,128)(2,1)S(1)} %copy-done.157), channel_id=1, replica_groups=mesh['wide'=8,'narrow'=4] {'narrow'}, dimensions={0}, use_global_device_ids=true | all-gather | bytes 737280 | tf_op jit(solution)/shard_map/all_gather | solution.py:353
  106.0 4.9 add_convert_fusion.5
  149.5 3.5 add_convert_fusion.9
  167.9 6.0 pad_slice_fusion.8
  185.3 10.7 %fusion.38 = (bf16[2,128,2,1536]{3,1,0,2:T(8,128)(2,1)}, f32[2,128,2,1536]{3,1,0,2:T(8,128)}, f32[2,2,128,1536]{3,2,1,0:T(8,128)}) fusion(bf16[2,128,2,384]{1,3,0,2:T(8,128)(2,1)S(1)} %copy.287, bf16[2,384,1536]{2,1,0:T(8,128)(2,1)} %all-gather.11.cloned.1.call-done), kind=kOutput, calls=%fused_computation.92 | convolution fusion | flops 655097856 | bytes 10616832 | tf_op jit(solution)/shard_map/blgd,gdf->blgf/dot_general | solution.py:120
  196.0 7.8 %all-gather.13.cloned.1.call-done = bf16[2,1536,384]{1,2,0:T(8,128)(2,1)} async-done(((bf16[2,384,384]{1,2,0:T(8,128)(2,1)}), bf16[2,1536,384]{1,2,0:T(8,128)(2,1)}) %all-gather.13.cloned.1.call-update) | async-done | bytes 2359312 | tf_op jit(solution)/shard_map/all_gather | solution.py:360
  222.4 15.5 %fusion.231 = f32[2,512,384]{1,2,0:T(8,128)} fusion(bf16[2,1536,384]{1,2,0:T(8,128)(2,1)S(1)} %copy-done.84, f32[2,512,1536]{2,1,0:T(8,128)S(1)} %fusion.251), kind=kOutput, calls=%fused_computation.506 | convolution fusion | flops 1310195712 | bytes 10223616 | tf_op jit(solution)/shard_map/blgf,gfd->blgd/dot_general | solution.py:122
  247.0 17.5 %fusion.23 = bf16[512,2,1536]{2,0,1:T(8,128)(2,1)S(1)} fusion(f32[2,512,1536]{2,1,0:T(8,128)} %copy-done.26, bf16[2,1536,384]{1,2,0:T(8,128)(2,1)} %all-gather.13.cloned.1.call-done, bf16[512,2,384]{2,1,0:T(2,128)(2,1)S(1)} %reshape.1365), kind=kOutput, calls=%fused_computation.71 | convolution fusion | flops 1321205760 | bytes 12582912 | tf_op jit(solution)/shard_map/blgd,gfd->blgf/dot_general | solution.py:190
  270.1 3.3 multiply_reduce_fusion.2
  281.8 4.3 multiply_reduce_fusion
  293.1 10.0 %fusion.71 = (f32[768]{0:T(1024)S(1)}, f32[768]{0:T(1024)S(1)}, f32[768]{0:T(1024)S(1)}, f32[768]{0:T(1024)S(1)}, f32[768]{0:T(1024)S(1)}, /*index=5*/f32[768]{0...) fusion(f32[1,512,768]{2,1,0:T(8,128)} %copy-done.27, ...), kind=kOutput, calls=%fused_computation.159 | convolution fusion | flops 311223552 | bytes 4943360 | tf_op jit(solution)/shard_map/bla,da->bld/dot_general | solution.py:271
  357.6 8.5 %fusion.133 = (f32[768]{0:T(1024)S(1)}, f32[768]{0:T(1024)S(1)}, f32[768]{0:T(1024)S(1)}, f32[768]{0:T(1024)S(1)}, f32[768]{0:T(1024)S(1)}, /*index=5*/f32[768]{...) fusion(f32[2,128,768]{2,1,0:T(8,128)} %fusion.185, ...), kind=kOutput, calls=%fused_computation.283 | convolution fusion | flops 157181184 | bytes 9104896 | tf_op jit(solution)/shard_map/bla,da->bld/dot_general | solution.py:271
  405.7 4.0 fusion.112
  420.2 17.1 %fusion.20 = bf16[2,1536,384]{2,1,0:T(8,128)(2,1)} fusion(f32[2,1536,384,1]{2,1,3,0:T(8,128)S(1)} %fusion.172, bf16[512,2,384]{2,1,0:T(2,128)(2,1)S(1)} %copy-done.117, f32[2,512,1536]{2,1,0:T(8,128)} %copy-done.26), kind=kOutput, calls=%fused_computation.47 | convolution fusion | flops 1312555008 | bytes 14155776 | tf_op jit(solution)/shard_map/blgf,blgd->gfd/dot_general | solution.py:189
  445.2 17.7 %all-reduce.85 = (bf16[768]{0:T(1024)(128)(2,1)}, bf16[768]{0:T(1024)(128)(2,1)}, bf16[768]{0:T(1024)(128)(2,1)}, bf16[768]{0:T(1024)(128)(2,1)}, bf16[768]{0:T(1024)(128)(2,1)}) all-reduce(bf16[768]{0:T(1024)(128)(2,1)} %dynamic-update-slice.3, bf16[768]{0:T(1024)(128)(2,1)} %add_convert_fusion.16, ...), channel_id=1, replica_groups=mesh['wide'=8,'narrow'=4] {'narrow'}, use_global_device_ids=true, to_apply=%add.79 | all-reduce | flops 3840 | bytes 15360
  479.0 3.5 fusion.93
  484.4 38.1 %reduce-scatter.13.cloned.1.call-done = bf16[192,1152]{1,0:T(8,128)(2,1)} async-done(((bf16[768,1152]{1,0:T(8,128)(2,1)}), bf16[192,1152]{1,0:T(8,128)(2,1)}) %reduce-scatter.13.cloned.1.call-update) | async-done | bytes 442384 | tf_op jit(solution)/shard_map/reduce_scatter | solution.py:391
  522.5 49.6 %reduce-scatter.21.cloned.1.call-done = bf16[2,96,1536]{2,1,0:T(8,128)(2,1)} async-done(((bf16[2,384,1536]{2,1,0:T(8,128)(2,1)}), bf16[2,96,1536]{2,1,0:T(8,128)(2,1)}) %reduce-scatter.21.cloned.1.call-update) | async-done | bytes 589840 | tf_op jit(solution)/shard_map/reduce_scatter | solution.py:409
  572.0 49.8 %reduce-scatter.23.cloned.1.call-done = bf16[2,384,384]{2,1,0:T(8,128)(2,1)} async-done(((bf16[2,1536,384]{2,1,0:T(8,128)(2,1)}), bf16[2,384,384]{2,1,0:T(8,128)(2,1)}) %reduce-scatter.23.cloned.1.call-update) | async-done | bytes 589840 | tf_op jit(solution)/shard_map/reduce_scatter | solution.py:412
  621.9 94.6 %all-reduce.88 = (f32[192,1152]{1,0:T(8,128)}, f32[9,192]{1,0:T(8,128)}, f32[192,384]{1,0:T(8,128)}, f32[96,54]{0,1:T(8,128)}, f32[192,384]{1,0:T(8,128)}, /*ind...) all-reduce(bf16[192,1152]{1,0:T(8,128)(2,1)} %reduce-scatter.13.clo, ...), channel_id=1, replica_groups=mesh['wide'=8,'narrow'=4] {'wide'}, use_global_device_ids=true, to_apply=%region_47.48 | all-reduce | flops 1113600 | bytes 6683136 | tf_op jit(solution)/shard_map/psum | solution.py:441
  (780 shorter events, 253.5 us)
Async XLA Ops:
  7.2 46.8 %copy-start.37 = (bf16[2,128,768]{2,1,0:T(8,128)(2,1)S(1)}, bf16[2,128,768]{2,1,0:T(8,128)(2,1)}, u32[]{:S(2)}) copy-start(bf16[2,128,768]{2,1,0:T(8,128)(2,1)} %param.20) | copy-start | bytes 1179652
  7.2 107.2 %all-gather.7.cloned.1.call-start = ((), (), s32[]{:S(2)}) async-start(), calls=%async_computation.8 | async-start | bytes 2211840 | tf_op jit(solution)/shard_map/all_gather | solution.py:351
  7.9 48.4 %copy-start.12 = (bf16[1,512,768]{2,1,0:T(8,128)(2,1)S(1)}, bf16[1,512,768]{2,1,0:T(8,128)(2,1)}, u32[]{:S(2)}) copy-start(bf16[1,512,768]{2,1,0:T(8,128)(2,1)} %param.18) | copy-start | bytes 2359300
  8.0 145.1 %all-gather.9.cloned.1.call-start = ((), (), s32[]{:S(2)}) async-start(), calls=%async_computation.9 | async-start | bytes 1474560 | tf_op jit(solution)/shard_map/all_gather | solution.py:356
  8.7 176.6 %all-gather.11.cloned.1.call-start = ((), (), s32[]{:S(2)}) async-start(), calls=%async_computation.10 | async-start | bytes 2949120 | tf_op jit(solution)/shard_map/all_gather | solution.py:359
  9.4 194.3 %all-gather.13.cloned.1.call-start = ((), (), s32[]{:S(2)}) async-start(), calls=%async_computation.11 | async-start | bytes 2949120 | tf_op jit(solution)/shard_map/all_gather | solution.py:360
  11.6 470.9 %reduce-scatter.25.cloned.1.call-start = ((), (), s32[]{:S(2)}) async-start(), calls=%async_computation.18 | async-start | bytes 245760
  29.1 85.3 %copy-start.210 = (pred[512]{0:T(512)(128)(4,1)}, pred[512]{0:T(512)(128)(4,1)S(1)}, u32[]{:S(2)}) copy-start(pred[512]{0:T(512)(128)(4,1)S(1)} %iota_compare_fusion) | copy-start | bytes 1540
  29.8 90.1 %copy-start.205 = (pred[2,128]{1,0:T(4,128)(4,1)}, pred[2,128]{1,0:T(4,128)(4,1)S(1)}, u32[]{:S(2)}) copy-start(pred[2,128]{1,0:T(4,128)(4,1)S(1)} %get-tuple-element.186) | copy-start | bytes 772
  56.9 110.8 %copy-start.22 = (f32[512,384]{0,1:T(8,128)}, f32[512,384]{0,1:T(8,128)S(1)}, u32[]{:S(2)}) copy-start(f32[512,384]{0,1:T(8,128)S(1)} %fusion.150) | copy-start | bytes 2359300
  57.1 55.5 %copy-start.27 = (f32[1,512,768]{2,1,0:T(8,128)}, f32[1,512,768]{2,1,0:T(8,128)S(1)}, u32[]{:S(2)}) copy-start(f32[1,512,768]{2,1,0:T(8,128)S(1)} %fusion.233) | copy-start | bytes 4718596
  119.2 41.5 %copy-start.40 = (f32[1,512,6,9]{1,3,2,0:T(8,128)}, f32[1,512,6,9]{1,3,2,0:T(8,128)S(1)}, u32[]{:S(2)}) copy-start(f32[1,512,6,9]{1,3,2,0:T(8,128)S(1)} %reshape.1353) | copy-start | bytes 331780
  368.6 114.9 %reduce-scatter.27.cloned.1.call-start = ((), (), s32[]{:S(2)}) async-start(), calls=%async_computation.19 | async-start | bytes 122880
  378.9 105.4 %reduce-scatter.17.cloned.1.call-start = ((), (), s32[]{:S(2)}) async-start(), calls=%async_computation.14 | async-start | bytes 737280 | tf_op jit(solution)/shard_map/reduce_scatter | solution.py:403
  385.7 98.7 %reduce-scatter.15.cloned.1.call-start = ((), (), s32[]{:S(2)}) async-start(), calls=%async_computation.13 | async-start | bytes 737280 | tf_op jit(solution)/shard_map/reduce_scatter | solution.py:397
  390.2 94.2 %reduce-scatter.19.cloned.1.call-start = ((), (), s32[]{:S(2)}) async-start(), calls=%async_computation.15 | async-start | bytes 1474560 | tf_op jit(solution)/shard_map/reduce_scatter | solution.py:406
  394.3 128.2 %reduce-scatter.13.cloned.1.call-start = ((), (), s32[]{:S(2)}) async-start(), calls=%async_computation.12 | async-start | bytes 2211840 | tf_op jit(solution)/shard_map/reduce_scatter | solution.py:391
  412.5 159.5 %reduce-scatter.21.cloned.1.call-start = ((), (), s32[]{:S(2)}) async-start(), calls=%async_computation.16 | async-start | bytes 2949120 | tf_op jit(solution)/shard_map/reduce_scatter | solution.py:409
  417.7 204.2 %reduce-scatter.23.cloned.1.call-start = ((), (), s32[]{:S(2)}) async-start(), calls=%async_computation.17 | async-start | bytes 2949120 | tf_op jit(solution)/shard_map/reduce_scatter | solution.py:412
  420.2 48.6 %copy-start.160 = (f32[768]{0:T(1024)S(1)}, f32[768]{0:T(1024)}, u32[]{:S(2)}) copy-start(f32[768]{0:T(1024)} %copy-done.159) | copy-start | bytes 9220
  479.0 142.9 %copy-start.227 = (f32[192]{0:T(256)S(1)}, f32[192]{0:T(256)}, u32[]{:S(2)}) copy-start(f32[192]{0:T(256)} %dynamic-slice_convert_fusion.3) | copy-start | bytes 2308
  479.0 142.9 %copy-start.228 = (f32[192]{0:T(256)S(1)}, f32[192]{0:T(256)}, u32[]{:S(2)}) copy-start(f32[192]{0:T(256)} %dynamic-slice_convert_fusion.2) | copy-start | bytes 2308
  479.0 142.8 %copy-start.229 = (f32[192]{0:T(256)S(1)}, f32[192]{0:T(256)}, u32[]{:S(2)}) copy-start(f32[192]{0:T(256)} %dynamic-slice_convert_fusion.1) | copy-start | bytes 2308
  479.0 142.8 %copy-start.230 = (f32[192]{0:T(256)S(1)}, f32[192]{0:T(256)}, u32[]{:S(2)}) copy-start(f32[192]{0:T(256)} %dynamic-slice_convert_fusion) | copy-start | bytes 2308
  (229 other events, 1498.1 us)
Sparse Core Ops, SparseCore 0:
  9.6 53.1 all-gather.6
  64.4 37.1 all-gather.8
  103.1 49.4 all-gather.10
  154.6 49.1 all-gather.12
  368.7 18.0 reduce-scatter.24
  389.0 17.2 reduce-scatter.26
  409.2 20.1 reduce-scatter.16
  432.2 20.3 reduce-scatter.14
  455.5 27.5 reduce-scatter.18
  485.3 37.0 reduce-scatter.12
  524.9 47.1 reduce-scatter.20
  574.3 47.5 reduce-scatter.22
where the time goes:
time: 730 us; the launch traced here: 724 us
  blocking collectives  196 us (27%)
  matrix products  161 us (22%)
  waiting for transfers between devices  148 us (20%)
  local copies, waits for them, and re-layouts  105 us (14%)
  other arithmetic  92.5 us (13%)
  between operations  20 us (3%)
    psum x1, blocking collectives, body(): lax.psum((grad_parts[0], grad_parts[1], grad_parts[2], grad_parts[3], gra...  94.6 us
    reduce_scatter x1, waiting for transfers between devices, body(): lax.psum_scatter(grad_outer.astype(jnp.bfloat16), 'narrow', scatter_dimen...  49.8 us
    reduce_scatter x1, waiting for transfers between devices, body(): lax.psum_scatter(grad_inner.astype(jnp.bfloat16), 'narrow', scatter_dimen...  49.6 us
    reduce_scatter x1, waiting for transfers between devices, body(): lax.psum_scatter(grad_qkv.astype(jnp.bfloat16), 'narrow', scatter_dimensi...  38.1 us
    mul x37, local copies, waits for them, and re-layouts, dynamic_conv(): result = result + kernel_probs[:, :, :, offset][..., None] * window_piece  34.2 us
    unnamed x2, blocking collectives  28.9 us
    unnamed x501, local copies, waits for them, and re-layouts  28.9 us
    all_gather x1, blocking collectives, body(): lax.all_gather(w_convout, 'narrow', axis=0, tiled=True)  24.2 us
  transfers between devices with their start and end apart: 12, of which 4 were waited for; matrix products, arithmetic and copies ran while one was open for 26% of the time, Pallas kernels for 0%

commit v1 on v0

v1 whole, which is shorter than its diff:
```python
import jax
import jax.numpy as jnp
from jax import lax
from jax.experimental import pallas as pl
from jax.experimental.pallas import tpu as pltpu
from jax.sharding import Mesh
from jax.sharding import PartitionSpec as P

BF = jnp.bfloat16
F32 = jnp.float32
EPS = 1e-12
D = 768
AH = 384
HEADS = 6
TAPS = 9
LONG = 512
SHORT = 128
ROWS = 768
PAD = 800
SLOTS = 8
NEG = -1000000000.0
PSTART = tuple(8 + 128 * i + 8 * max(i - 3, 0) for i in range(6))
SEGS = ((0, 512, 8), (512, 128, 528), (640, 128, 664))


def nn(a, b):
    return lax.dot_general(a, b, (((1,), (0,)), ((), ())), preferred_element_type=F32)


def nt(a, b):
    return lax.dot_general(a, b, (((1,), (1,)), ((), ())), preferred_element_type=F32)


def tn(a, b):
    return lax.dot_general(a, b, (((0,), (0,)), ((), ())), preferred_element_type=F32)


def iota(shape, axis):
    return lax.broadcasted_iota(jnp.int32, shape, axis)


def loop(count, body):
    def step(i, carry):
        body(i)
        return carry

    lax.fori_loop(0, count, step, 0)


def at(i, size):
    if isinstance(i, int):
        return pl.ds(i * size, size)
    return pl.ds(pl.multiple_of(i * size, size), size)


def padded_start(i):
    return pl.multiple_of(8 + 128 * i + 8 * jnp.maximum(i - 3, 0), 8)


def zero_gaps(ref):
    for start in (0, 520, 656, 792):
        ref[start : start + 8, :] = jnp.zeros((8, ref.shape[1]), ref.dtype)


def eye(n, dtype):
    return jnp.where(iota((n, n), 0) == iota((n, n), 1), 1.0, 0.0).astype(dtype)


def tap_permutation():
    row, col = iota((128, 128), 0), iota((128, 128), 1)
    head, tap = col & 7, col >> 3
    keep = (head < HEADS) & (tap < TAPS) & (row == 64 + head * TAPS + tap)
    return jnp.where(keep, 1.0, 0.0).astype(BF)


def head_spread():
    row, col = iota((256, AH), 0), iota((256, AH), 1)
    return jnp.where((row & 127) == (col >> 6), 1.0, 0.0).astype(BF)


def head_gather():
    row, col = iota((AH, 128), 0), iota((AH, 128), 1)
    return jnp.where((row >> 6) == col, 1.0, 0.0).astype(BF)


def split_two(values):
    high = values.astype(BF)
    low = (values - high.astype(F32)).astype(BF)
    return jnp.concatenate([high, low], axis=1)


def tap_kernel(wm):
    stored = jnp.concatenate([wm[7, 192 * n : 192 * n + 96, 128:256] for n in range(4)], axis=0)
    return nn(stored, tap_permutation()).astype(BF)


def mixer_forward(
    lens, xl, xs, wm, xm, packed, plong, pshort, dw, kc, cq, kp, cv, ctx, vec, xpad, spread, wk
):
    zero_gaps(xpad)
    zero_gaps(cv)
    zero_gaps(kp)
    for i in range(6):
        seg = max(i - 3, 0)
        base = 128 * i if i < 4 else 0
        tokens = xl[128 * i : 128 * i + 128, :] if i < 4 else xs[128 * (i - 4) : 128 * (i - 3), :]
        live = base + iota((128, D), 0) < lens[seg]
        values = jnp.where(live, tokens.astype(F32), 0.0)
        xpad[PSTART[i] : PSTART[i] + 128, :] = values
        xm[128 * i : 128 * i + 128, :] = values.astype(BF)
    vec[...] = nt(eye(128, BF), wm[7, :, 128:256])[0:24, :]
    spread[...] = head_spread()
    wk[...] = tap_kernel(wm)

    def project(b):
        packed[:, at(b, 256)] = nn(xm[...], wm[b]).astype(BF)

    loop(4, project)
    part = nn(xm[...], wm[4])
    packed[:, 1024:1152] = part[:, 0:128].astype(BF)
    for start, rows, pstart in SEGS:
        cv[pstart : pstart + rows, 0:128] = part[start : start + rows, 128:256]
    part = nn(xm[...], wm[5])
    for start, rows, pstart in SEGS:
        cv[pstart : pstart + rows, 128:384] = part[start : start + rows, :]

    def depth(i):
        ps = padded_start(i)
        for c in range(3):
            lanes = slice(256 * c, 256 * c + 256)
            window = xpad[pl.ds(pl.multiple_of(ps - 8, 8), 144), lanes]
            total = jnp.zeros((128, 256), F32)
            for j in range(TAPS):
                total = total + vec[j : j + 1, lanes] * window[4 + j : 132 + j, :]
            dw[at(i, 128), lanes] = total.astype(BF)

    loop(6, depth)
    kc[:, 0:256] = nn(dw[...], wm[6])
    kc[:, 256:384] = nn(dw[...], wm[7, :, 0:128])

    def dynamic(i):
        rows = at(i, 128)
        ps = padded_start(i)
        query = (kc[rows, :] * packed[rows, 0:AH].astype(F32)).astype(BF)
        cq[rows, :] = query
        logits = nn(query, wk[...])
        lane = iota((128, 128), 1)
        real = lane < 8 * TAPS
        top = jnp.where(real, logits, NEG * 1e20)
        for shift in (64, 32, 16, 8):
            top = jnp.maximum(top, pltpu.roll(top, shift, 1))
        ex = jnp.where(real, jnp.exp(logits - top), 0.0)
        total = ex
        for shift in (64, 32, 16, 8):
            total = total + pltpu.roll(total, shift, 1)
        probs = ex / total
        kp[pl.ds(ps, 128), :] = probs
        window = cv[pl.ds(pl.multiple_of(ps - 8, 8), 144), :]
        out = jnp.zeros((128, AH), F32)
        for j in range(TAPS):
            moved = probs if j == 0 else pltpu.roll(probs, 128 - 8 * j, 1)
            out = out + nn(split_two(moved), spread[...]) * window[4 + j : 132 + j, :]
        ctx[rows, AH:D] = out.astype(BF)

    loop(6, dynamic)

    def attend(row0, nq, key0, nk, limit, pair, store):
        queries = packed[pl.ds(row0, nq), at(pair, 128)].astype(F32)
        keys = packed[pl.ds(key0, nk), pl.ds(pl.multiple_of(AH + pair * 128, 128), 128)]
        vals = packed[pl.ds(key0, nk), pl.ds(pl.multiple_of(2 * AH + pair * 128, 128), 128)]
        lane = iota((nq, 128), 1)
        outs = []
        for hh in range(2):
            mine = (lane >> 6) == hh
            scores = nt(jnp.where(mine, queries, 0.0).astype(BF), keys) * 0.125
            scores = jnp.where(iota((nq, nk), 1) < limit, scores, NEG)
            ex = jnp.exp(scores - jnp.max(scores, axis=1, keepdims=True))
            probs = (ex / jnp.sum(ex, axis=1, keepdims=True)).astype(BF)
            store(hh, probs)
            outs.append(nn(probs, vals))
        both = jnp.where(lane < 64, outs[0], outs[1])
        ctx[pl.ds(row0, nq), at(pair, 128)] = both.astype(BF)

    def long_attend(i):
        pair, block = i >> 1, i & 1
        row0 = pl.multiple_of(block * 256, 256)

        def store(hh, probs):
            plong[2 * pair + hh, pl.ds(row0, 256), :] = probs

        attend(row0, 256, 0, LONG, lens[0], pair, store)

    loop(6, long_attend)

    def short_attend(i):
        seg = jnp.where(i >= 3, 1, 0)
        pair = i - 3 * seg
        row0 = pl.multiple_of(LONG + 128 * seg, 128)

        def store(hh, probs):
            pshort[seg, 2 * pair + hh, :, :] = probs

        attend(row0, 128, row0, SHORT, lens[1 + seg], pair, store)

    loop(6, short_attend)


ERFC = (
    -1.26551223, 1.00002368, 0.37409196, 0.09678418, -0.18628806,
    0.27886807, -1.13520398, 1.48851587, -0.82215223, 0.17087277,
)


def gelu_parts(hidden):
    z = jnp.abs(hidden) * 0.7071067811865476
    t = 1.0 / (1.0 + 0.5 * z)
    series = jnp.full_like(z, ERFC[-1])
    for coefficient in ERFC[-2::-1]:
        series = series * t + coefficient
    square = z * z
    tail = 0.5 * t * jnp.exp(series - square)
    cdf = jnp.where(hidden < 0.0, tail, 1.0 - tail)
    return cdf, jnp.exp(-square) * 0.3989422804014327


def ffn_both(
    lens, xm, ctx, vec, wf, cl, cs,
    ol, os, ga, gone, gctx, gvec,
    wo, wi, wu, res, xhat, grouped, gffn, active, slope, ffn, rstd, acc, ghid, gproj,
):
    for n in range(4):
        for w in range(8):
            wi[w, 96 * n : 96 * n + 96, :] = wf[w, n, 0:96, :]
            wu[4 * (w // 4) + n, 96 * (w % 4) : 96 * (w % 4) + 96, :] = wf[w, n, 96:192, :]
            row = 192 * n + 48 * (w % 4)
            lanes = slice(AH * (w // 4), AH * (w // 4) + AH)
            wo[row : row + 48, lanes] = wf[w, n, 192:240, :]
    gain_one, bias_one = vec[16:17, :], vec[17:18, :]
    gain_two, bias_two = vec[18:19, :], vec[19:20, :]
    gvec[...] = jnp.zeros((8, D), F32)

    def mix(i):
        rows = at(i, 256)
        res[rows, :] = nn(ctx[rows, :], wo[...]) + xm[rows, :].astype(F32)

    loop(3, mix)

    def norm_one(i):
        rows = at(i, 64)
        values = res[rows, :]
        center = values - jnp.mean(values, axis=1, keepdims=True)
        scale = lax.rsqrt(jnp.mean(center * center, axis=1, keepdims=True) + EPS)
        hat = center * scale
        first = hat * gain_one + bias_one
        xhat[rows, :] = hat
        rstd[rows, :] = jnp.broadcast_to(scale, (64, 128))
        res[rows, :] = first
        short = first.astype(BF)
        grouped[0, rows, :] = short[:, 0:AH]
        grouped[1, rows, :] = short[:, AH:D]

    loop(12, norm_one)
    ffn[...] = jnp.zeros((2, ROWS, AH), F32)

    def expand(b):
        acc[...] = nn(grouped[b >> 2], wi[b])

        def act(i):
            rows = at(i, 64)
            hidden = acc[rows, :]
            cdf, density = gelu_parts(hidden)
            active[b, rows, :] = (hidden * cdf).astype(BF)
            slope[b, rows, :] = cdf + hidden * density

        loop(12, act)
        ffn[b >> 2] += nn(active[b], wu[b])

    loop(8, expand)

    def norm_two(cot, out, offset):
        def run(i):
            rows = at(i, 64)
            whole = pl.ds(pl.multiple_of(offset + i * 64, 64), 64)
            values = jnp.concatenate([ffn[0, whole, :], ffn[1, whole, :]], axis=1) + res[whole, :]
            center = values - jnp.mean(values, axis=1, keepdims=True)
            scale = lax.rsqrt(jnp.mean(center * center, axis=1, keepdims=True) + EPS)
            hat = center * scale
            out[rows, :] = (hat * gain_two + bias_two).astype(BF)
            if offset:
                seg, base = 1 + (i >> 1), (i & 1) * 64
            else:
                seg, base = 0, i * 64
            live = base + iota((64, D), 0) < lens[seg]
            up = jnp.where(live, cot[rows, :].astype(F32), 0.0)
            gvec[2:3, :] += jnp.sum(up * hat, axis=0, keepdims=True)
            gvec[3:4, :] += jnp.sum(up, axis=0, keepdims=True)
            up = up * gain_two
            grad = scale * (
                up
                - jnp.mean(up, axis=1, keepdims=True)
                - hat * jnp.mean(up * hat, axis=1, keepdims=True)
            )
            res[whole, :] = grad
            short = grad.astype(BF)
            gffn[0, whole, :] = short[:, 0:AH]
            gffn[1, whole, :] = short[:, AH:D]

        return run

    loop(8, norm_two(cl, ol, 0))
    loop(4, norm_two(cs, os, LONG))
    ffn[...] = jnp.zeros((2, ROWS, AH), F32)

    def contract(b):
        g, n = b >> 2, b & 3
        acc[...] = nt(gffn[g], wu[b])

        def act(i):
            rows = at(i, 64)
            ghid[rows, :] = (acc[rows, :] * slope[b, rows, :]).astype(BF)

        loop(12, act)
        part = tn(active[b], gffn[g]).astype(BF)
        for w in range(4):
            ga[4 * g + w, n, 96:192, :] = part[96 * w : 96 * w + 96, :]
        part = tn(grouped[g], ghid[...]).astype(BF)
        for m in range(4):
            ga[b, m, 0:96, :] = part[96 * m : 96 * m + 96, :]
        ffn[g] += nt(ghid[...], wi[b])

    loop(8, contract)

    def norm_one_back(i):
        rows = at(i, 64)
        up = res[rows, :] + jnp.concatenate([ffn[0, rows, :], ffn[1, rows, :]], axis=1)
        hat = xhat[rows, :]
        gvec[0:1, :] += jnp.sum(up * hat, axis=0, keepdims=True)
        gvec[1:2, :] += jnp.sum(up, axis=0, keepdims=True)
        up = up * gain_one
        grad = rstd[rows, 0:1] * (
            up
            - jnp.mean(up, axis=1, keepdims=True)
            - hat * jnp.mean(up * hat, axis=1, keepdims=True)
        )
        gone[rows, :] = grad
        gproj[rows, :] = grad.astype(BF)

    loop(12, norm_one_back)
    for c in range(2):
        part = tn(ctx[...], gproj[:, AH * c : AH * c + AH]).astype(BF)
        for n in range(4):
            for r in range(4):
                row = 192 * n + 48 * r
                ga[4 * c + r, n, 192:240, :] = part[row : row + 48, :]

    def unmix(i):
        rows = at(i, 256)
        gctx[rows, :] = nt(gproj[rows, :], wo[...]).astype(BF)

    loop(3, unmix)


def mixer_backward(
    lens, xm, packed, plong, pshort, dw, kc, cq, kp, cv, vec, gone, gctx, gvec, wm,
    il, is_, gb,
    xpad, gcp, gdp, grads, gqc, dkv, gkc, glog, gdep, spread, gather, wk,
):
    zero_gaps(xpad)
    zero_gaps(gcp)
    zero_gaps(gdp)
    for start, rows, pstart in SEGS:
        xpad[pstart : pstart + rows, :] = xm[start : start + rows, :].astype(F32)
        gcp[pstart : pstart + rows, :] = gctx[start : start + rows, AH:D].astype(F32)
    spread[...] = head_spread()
    gather[...] = head_gather()
    wk[...] = tap_kernel(wm)
    gdep[...] = jnp.zeros((8 * TAPS, D), F32)

    def dynamic(i):
        rows = at(i, 128)
        ps = padded_start(i)
        wide = pl.ds(pl.multiple_of(ps - 8, 8), 144)
        taps = kp[wide, :]
        grad_wide = gcp[wide, :]
        values = cv[wide, :]
        grad = gcp[pl.ds(ps, 128), :]
        total = jnp.zeros((128, AH), F32)
        gprob = jnp.zeros((128, 128), F32)
        for j in range(TAPS):
            moved = taps if j == 0 else pltpu.roll(taps, 128 - 8 * j, 1)
            part = nn(split_two(moved), spread[...]) * grad_wide
            total = total + part[12 - j : 140 - j, :]
            part = nn((grad * values[4 + j : 132 + j, :]).astype(BF), gather[...])
            gprob = gprob + (part if j == 0 else pltpu.roll(part, 8 * j, 1))
        grads[rows, 3 * AH : 4 * AH] = total.astype(BF)
        probs = kp[pl.ds(ps, 128), :]
        inner = probs * gprob
        for shift in (64, 32, 16, 8):
            inner = inner + pltpu.roll(inner, shift, 1)
        glogits = (probs * (gprob - inner)).astype(BF)
        glog[rows, :] = glogits
        gquery = nt(glogits, wk[...])
        gkc[rows, :] = (gquery * packed[rows, 0:AH].astype(F32)).astype(BF)
        gqc[rows, :] = gquery * kc[rows, :]

    loop(6, dynamic)

    def point_back(c):
        part = nt(gkc[:, 0:256], wm[6, at(c, 256), :])
        part = part + nt(gkc[:, 256:384], wm[7, at(c, 256), 0:128])
        part = part.astype(BF).astype(F32)
        for start, rows, pstart in SEGS:
            gdp[pstart : pstart + rows, at(c, 256)] = part[start : start + rows, :]

    loop(3, point_back)

    def depth(i):
        ps = padded_start(i)
        wide = pl.ds(pl.multiple_of(ps - 8, 8), 144)
        for c in range(3):
            lanes = slice(256 * c, 256 * c + 256)
            tokens = xpad[wide, lanes]
            grad_wide = gdp[wide, lanes]
            grad = gdp[pl.ds(ps, 128), lanes]
            total = gone[at(i, 128), lanes]
            for j in range(TAPS):
                total = total + vec[j : j + 1, lanes] * grad_wide[12 - j : 140 - j, :]
                part = tokens[4 + j : 132 + j, :] * grad
                gdep[8 * j : 8 * j + 8, lanes] += jnp.sum(part.reshape(16, 8, 256), axis=0)
            gone[at(i, 128), lanes] = total

    loop(6, depth)

    def attend(row0, nq, key0, nk, pair, load, first):
        queries = packed[pl.ds(row0, nq), at(pair, 128)].astype(F32)
        keys = packed[pl.ds(key0, nk), pl.ds(pl.multiple_of(AH + pair * 128, 128), 128)]
        vals = packed[pl.ds(key0, nk), pl.ds(pl.multiple_of(2 * AH + pair * 128, 128), 128)]
        up = gctx[pl.ds(row0, nq), at(pair, 128)].astype(F32)
        lane = iota((nq, 128), 1)
        outs = []
        gkeys = jnp.zeros((nk, 128), F32)
        gvals = jnp.zeros((nk, 128), F32)
        for hh in range(2):
            mine = (lane >> 6) == hh
            query = jnp.where(mine, queries, 0.0).astype(BF)
            upper = jnp.where(mine, up, 0.0).astype(BF)
            probs_low = load(hh)
            probs = probs_low.astype(F32)
            gprobs = nt(upper, vals)
            inner = jnp.sum(probs * gprobs, axis=1, keepdims=True)
            gscores = (probs * (gprobs - inner)).astype(BF)
            outs.append(nn(gscores, keys))
            gkeys = gkeys + tn(gscores, query)
            gvals = gvals + tn(probs_low, upper)
        both = jnp.where(lane < 64, outs[0], outs[1]) * 0.125
        both = both + gqc[pl.ds(row0, nq), at(pair, 128)]
        grads[pl.ds(row0, nq), at(pair, 128)] = both.astype(BF)
        span = pl.ds(key0, nk)
        if first:
            dkv[0, span, at(pair, 128)] = gkeys
            dkv[1, span, at(pair, 128)] = gvals
        else:
            dkv[0, span, at(pair, 128)] += gkeys
            dkv[1, span, at(pair, 128)] += gvals

    def long_attend(pair):
        for block in range(2):
            attend(
                256 * block, 256, 0, LONG, pair,
                lambda hh: plong[2 * pair + hh, 256 * block : 256 * block + 256, :],
                block == 0,
            )

    loop(3, long_attend)

    def short_attend(i):
        seg = jnp.where(i >= 3, 1, 0)
        pair = i - 3 * seg
        row0 = pl.multiple_of(LONG + 128 * seg, 128)
        attend(row0, 128, row0, SHORT, pair, lambda hh: pshort[seg, 2 * pair + hh, :, :], True)

    loop(6, short_attend)

    def pack(i):
        rows = at(i, 128)
        grads[rows, AH : 2 * AH] = (dkv[0, rows, :] * 0.125).astype(BF)
        grads[rows, 2 * AH : 3 * AH] = dkv[1, rows, :].astype(BF)

    loop(6, pack)

    def weights(b):
        gb[b] = tn(xm[...], grads[:, at(b, 256)]).astype(BF)

    loop(6, weights)
    gb[6] = tn(dw[...], gkc[:, 0:256]).astype(BF)
    gb[7, :, 0:128] = tn(dw[...], gkc[:, 256:384]).astype(BF)
    taps = [jnp.sum(gdep[8 * j : 8 * j + 8, :], axis=0, keepdims=True) for j in range(TAPS)]
    table = jnp.concatenate(
        taps + [jnp.zeros((7, D), F32), gvec[...], jnp.zeros((104, D), F32)], axis=0
    ).astype(BF)
    misc = tn(table, eye(128, BF))
    gkernel = nt(tn(cq[...], glog[...]).astype(BF), tap_permutation())
    for n in range(4):
        row = 192 * n
        gb[7, row : row + 96, 128:256] = (
            misc[row : row + 96, :] + gkernel[96 * n : 96 * n + 96, :]
        ).astype(BF)
        gb[7, row + 96 : row + 192, 128:256] = misc[row + 96 : row + 192, :].astype(BF)

    def inputs(i):
        rows = at(i, 256)
        total = gone[rows, :]
        for b in range(6):
            total = total + nt(grads[rows, 256 * b : 256 * b + 256], wm[b])
        return total

    def inputs_long(i):
        live = i * 256 + iota((256, D), 0) < lens[0]
        il[at(i, 256), :] = jnp.where(live, inputs(i), 0.0).astype(BF)

    loop(2, inputs_long)
    total = inputs(2)
    row = iota((128, D), 0)
    for seg in range(2):
        part = total[128 * seg : 128 * seg + 128, :]
        is_[128 * seg : 128 * seg + 128, :] = jnp.where(row < lens[1 + seg], part, 0.0).astype(BF)


def call(kernel, n_in, outs, scratch, *args):
    return pl.pallas_call(
        kernel,
        out_shape=[jax.ShapeDtypeStruct(s, d) for s, d in outs],
        in_specs=[pl.BlockSpec(memory_space=pltpu.SMEM)]
        + [pl.BlockSpec(memory_space=pltpu.VMEM)] * (n_in - 1),
        out_specs=[pl.BlockSpec(memory_space=pltpu.VMEM)] * len(outs),
        scratch_shapes=[pltpu.VMEM(s, d) for s, d in scratch],
        compiler_params=pltpu.CompilerParams(vmem_limit_bytes=60 << 20),
        name=kernel.__name__,
    )(*args)


def forward_mixer(lens, xl, xs, wm):
    outs = [
        ((ROWS, D), BF), ((ROWS, 3 * AH), BF),
        ((HEADS, LONG, LONG), BF), ((2, HEADS, SHORT, SHORT), BF),
        ((ROWS, D), BF), ((ROWS, AH), F32), ((ROWS, AH), BF), ((PAD, 128), F32),
        ((PAD, AH), F32), ((ROWS, D), BF), ((24, D), F32),
    ]
    scratch = [((PAD, D), F32), ((256, AH), BF), ((AH, 128), BF)]
    return call(mixer_forward, 4, outs, scratch, lens, xl, xs, wm)


def feed_forward(lens, xm, ctx, vec, wf, cl, cs):
    outs = [
        ((LONG, D), BF), ((2 * SHORT, D), BF), ((SLOTS, 4, 240, AH), BF),
        ((ROWS, D), F32), ((ROWS, D), BF), ((8, D), F32),
    ]
    scratch = [
        ((D, D), BF), ((8, AH, AH), BF), ((8, AH, AH), BF), ((ROWS, D), F32), ((ROWS, D), F32),
        ((2, ROWS, AH), BF), ((2, ROWS, AH), BF), ((8, ROWS, AH), BF), ((8, ROWS, AH), F32),
        ((2, ROWS, AH), F32), ((ROWS, 128), F32), ((ROWS, AH), F32), ((ROWS, AH), BF),
        ((ROWS, D), BF),
    ]
    return call(ffn_both, 7, outs, scratch, lens, xm, ctx, vec, wf, cl, cs)


def backward_mixer(*args):
    outs = [((LONG, D), BF), ((2 * SHORT, D), BF), ((SLOTS, D, 256), BF)]
    scratch = [
        ((PAD, D), F32), ((PAD, AH), F32), ((PAD, D), F32), ((ROWS, 4 * AH), BF),
        ((ROWS, AH), F32), ((2, ROWS, AH), F32), ((ROWS, AH), BF), ((ROWS, 128), BF),
        ((8 * TAPS, D), F32), ((256, AH), BF), ((AH, 128), BF), ((AH, 128), BF),
    ]
    return call(mixer_backward, 15, outs, scratch, *args)


def layer(lens, xl, xs, cl, cs, wm, wf):
    xm, packed, plong, pshort, dw, kc, cq, kp, cv, ctx, vec = forward_mixer(lens, xl, xs, wm)
    ol, os, ga, gone, gctx, gvec = feed_forward(lens, xm, ctx, vec, wf, cl, cs)
    il, is_, gb = backward_mixer(
        lens, xm, packed, plong, pshort, dw, kc, cq, kp, cv, vec, gone, gctx, gvec, wm
    )
    return ol, os, il, is_, ga, gb


def pack_mixer(w_qkv, w_depth, w_point, w_kernel, w_convout, g1, b1, g2, b2):
    rows = w_qkv.shape[0]
    norms = jnp.stack([g1, b1, g2, b2], axis=1)
    left = jnp.concatenate(
        [
            jnp.pad(w_depth.T, ((0, 0), (0, 16 - TAPS))),
            jnp.pad(norms, ((0, 0), (0, 44))),
        ],
        axis=1,
    )
    right = jnp.pad(w_kernel, ((0, rows - w_kernel.shape[0]), (0, 64 - w_kernel.shape[1])))
    return jnp.concatenate([w_qkv, w_convout, w_point, left, right], axis=1)


def pack_ffn(w_out, w_inner, w_outer, slot):
    g, c = slot // 4, slot % 4
    inner = lax.dynamic_slice(w_inner, (g, 0, c * AH), (1, 96, AH))[0]
    outer = lax.dynamic_slice(w_outer, (g, c * 96, 0), (1, 96, AH))[0]
    out = lax.dynamic_slice(w_out, (c * 48, g * AH), (48, AH))
    return jnp.concatenate([inner, outer, out], axis=0)


def body(
    long_tokens, long_lengths, short_tokens, short_lengths,
    w_qkv, w_depth, w_point, w_kernel, w_convout, w_out, norm1_gain, norm1_bias,
    w_inner, w_outer, norm2_gain, norm2_bias, long_cotangent, short_cotangent,
):
    slot = lax.axis_index("wide")
    mixer = pack_mixer(
        w_qkv, w_depth, w_point, w_kernel, w_convout, norm1_gain, norm1_bias, norm2_gain, norm2_bias
    )
    mixer = lax.dynamic_slice(mixer, (0, slot * 256), (192, 256))
    wm = lax.all_gather(mixer, ("wide", "narrow"), axis=0, tiled=False).reshape(SLOTS, D, 256)
    wf = lax.all_gather(pack_ffn(w_out, w_inner, w_outer, slot), ("wide", "narrow"), axis=0)
    wf = wf.reshape(SLOTS, 4, 240, AH)
    lens = jnp.concatenate([long_lengths, short_lengths])
    ol, os, il, is_, ga, gb = layer(
        lens,
        long_tokens.reshape(LONG, D), short_tokens.reshape(2 * SHORT, D),
        long_cotangent.reshape(LONG, D), short_cotangent.reshape(2 * SHORT, D),
        wm, wf,
    )

    def reduce(parts):
        parts = lax.psum_scatter(parts, "wide", scatter_dimension=0, tiled=False)
        parts = lax.psum_scatter(parts, "narrow", scatter_dimension=0, tiled=False)
        parts = lax.psum(parts, "hi")
        return lax.all_gather(parts, "wide", axis=0, tiled=False).astype(F32)

    ga = reduce(ga)
    gb = reduce(gb.reshape(SLOTS, 4, 192, 256))
    inner = ga[:, 0:96].reshape(2, 4, 96, AH).transpose(0, 2, 1, 3).reshape(2, 96, 4 * AH)
    outer = ga[:, 96:192].reshape(2, AH, AH)
    out = ga[:, 192:240].reshape(2, 4, 48, AH).transpose(1, 2, 0, 3).reshape(192, D)
    gb = gb.transpose(1, 0, 2).reshape(192, 2048)
    misc = gb[:, 1920:2048]
    return (
        ol.reshape(long_tokens.shape), os.reshape(short_tokens.shape),
        il.reshape(long_tokens.shape), is_.reshape(short_tokens.shape),
        gb[:, 0:1152], misc[:, 0:TAPS].T, gb[:, 1536:1920], misc[0:96, 64:118], gb[:, 1152:1536],
        out, misc[:, 16], misc[:, 17], inner, outer, misc[:, 18], misc[:, 19],
    )


def solution(mesh):
    wide, narrow = mesh.shape["wide"], mesh.shape["narrow"]
    inner_mesh = Mesh(mesh.devices.reshape(wide // SLOTS, SLOTS, narrow), ("hi", "wide", "narrow"))
    every = ("hi", "wide", "narrow")
    rows = P(every, None, None)
    weights = (
        P("narrow", None), P(None, "narrow"), P("narrow", None), P("narrow", None),
        P("narrow", None), P("narrow", None), P("narrow"), P("narrow"),
        P(None, "narrow", None), P(None, "narrow", None), P("narrow"), P("narrow"),
    )
    return jax.shard_map(
        body,
        mesh=inner_mesh,
        in_specs=(rows, P(every), rows, P(every)) + weights + (rows, rows),
        out_specs=(rows, rows, rows, rows) + weights,
        check_vma=False,
    )
```

time: 730 us -> 398 us (0.55)
  blocking collectives: 196 us -> 10.7 us
  matrix products: 161 us -> 0 us
  Pallas kernels: 0 us -> 133 us
  other arithmetic: 92.5 us -> 1.43 us
  local copies, waits for them, and re-layouts: 105 us -> 17.4 us
  waiting for transfers between devices: 148 us -> 220 us
    dot_general x54 -> x0, matrix products: 161 us -> none  [the longest x2 19.1 us: backward_top(): jnp.einsum('blgd,gfd->blgf', grad_ffn, w_outer, preferred_element_type=jn...]
    pallas_call x0 -> x3, Pallas kernels: none -> 133 us  [call(): pl.pallas_call(kernel, out_shape=[jax.ShapeDtypeStruct(s, d) for s, d in...]
    all_gather x4 -> x3, waiting for transfers between devices: 7.82 us -> 108 us  [the longest x1 58.1 us: body(): lax.all_gather(mixer, ('wide', 'narrow'), axis=0, tiled=False)]
    psum x1 -> x0, blocking collectives: 94.6 us -> none  [body(): lax.psum((grad_parts[0], grad_parts[1], grad_parts[2], grad_parts[3], gra...]
    all_gather x4 -> x1, blocking collectives: 72.4 us -> 10.7 us  [reduce(): return lax.all_gather(parts, 'wide', axis=0, tiled=False).astype(F32)]
    mul x37 -> x0, local copies, waits for them, and re-layouts: 34.2 us -> none  [dynamic_conv(): result = result + kernel_probs[:, :, :, offset][..., None] * window_piece]
    convert_element_type x29 -> x0, other arithmetic: 30.9 us -> none  [the longest x2 6.52 us: forward_bucket(): depth_conv(masked.astype(jnp.float32), w_depth.astype(jnp.float32))]
    unnamed x2 -> x0, blocking collectives: 28.9 us -> none
  transfers between devices with their start and end apart: 12 -> 7, of which waited for: 4 -> 7; matrix products, arithmetic and copies ran while one was open for 26% -> 2% of each run, Pallas kernels for 0% -> 19%
where the time goes in v1:
time: 398 us
  waiting for transfers between devices  220 us (55%)
  Pallas kernels  133 us (33%)
  local copies, waits for them, and re-layouts  17.4 us (4%)
  between operations  14.9 us (4%)
  blocking collectives  10.7 us (3%)
    pallas_call x3, Pallas kernels, call(): pl.pallas_call(kernel, out_shape=[jax.ShapeDtypeStruct(s, d) for s, d in...  133 us
    reduce_scatter x2, waiting for transfers between devices, reduce(): parts = lax.psum_scatter(parts, 'wide', scatter_dimension=0, tiled=False)  65.3 us
    all_gather x1, waiting for transfers between devices, body(): lax.all_gather(mixer, ('wide', 'narrow'), axis=0, tiled=False)  58.1 us
    reduce_scatter x2, waiting for transfers between devices, reduce(): parts = lax.psum_scatter(parts, 'narrow', scatter_dimension=0, tiled=False)  47.1 us
    all_gather x1, waiting for transfers between devices, body(): lax.all_gather(pack_ffn(w_out, w_inner, w_outer, slot), ('wide', 'narrow'...  39.3 us
    all_gather x1, blocking collectives, reduce(): return lax.all_gather(parts, 'wide', axis=0, tiled=False).astype(F32)  10.7 us
    all_gather x1, waiting for transfers between devices, reduce(): return lax.all_gather(parts, 'wide', axis=0, tiled=False).astype(F32)  10.2 us
  transfers between devices with their start and end apart: 7, of which 7 were waited for; matrix products, arithmetic and copies ran while one was open for 2% of the time, Pallas kernels for 19%

profile of v1, /device:TPU:0, one launch (start us, length us, event | category | flops | bytes accessed | tf_op | source)
XLA Modules:
  0.0 398.0 jit_solution(6110271582653784132)
XLA Ops:
  9.9 0.8 copy.66
  10.9 0.8 copy.64
  11.8 1.3 concatenate.10
  13.9 0.8 dynamic_slice.15
  14.7 0.9 dynamic-slice_bitcast_fusion
  17.6 58.1 %all-gather.8.cloned.1.call-done = bf16[6144,256]{1,0:T(8,128)(2,1)} async-done(((bf16[192,256]{1,0:T(8,128)(2,1)}), bf16[6144,256]{1,0:T(8,128)(2,1)}) %all-gather.8.cloned.1.call-update) | async-done | bytes 3145744 | tf_op jit(solution)/shard_map/all_gather | solution.py:618
  75.7 31.1 %mixer_forward.1 = (bf16[768,768]{1,0:T(8,128)(2,1)}, bf16[768,1152]{1,0:T(8,128)(2,1)}, bf16[6,512,512]{2,1,0:T(8,128)(2,1)}, bf16[2,6,128,128]{3,2,1,0:T(8,128...) custom-call(s32[3]{0:T(128)} %pad_add_fusion.lens, ...), custom_call_target="tpu_custom_call" | custom-call | tf_op jit(solution)/shard_map/mixer_forward/pallas_call | solution.py:530
  106.8 39.3 %all-gather.10.cloned.1.call-done = bf16[7680,384]{1,0:T(8,128)(2,1)} async-done(((bf16[240,384]{1,0:T(8,128)(2,1)}), bf16[7680,384]{1,0:T(8,128)(2,1)}) %all-gather.10.cloned.1.call-update) | async-done | bytes 5898256 | tf_op jit(solution)/shard_map/all_gather | solution.py:619
  146.0 59.4 %ffn_both.1 = (bf16[512,768]{1,0:T(8,128)(2,1)}, bf16[256,768]{1,0:T(8,128)(2,1)}, bf16[8,4,240,384]{3,2,1,0:T(8,128)(2,1)}, f32[768,768]{1,0:T(8,128)}, bf16[768,768]{1,0:T(8,128)(2,1)}, /*index=5*/f32[8,768]{1,0:T(8,128)}) custom-call(s32[3]{0:T(128)} %pad_add_fusion.lens, bf16[768,768]{1,0:T(8,128)(2,1)} %get-tuple-element.36.xm, ...), custom_call_target="tpu_custom_call" | custom-call | tf_op jit(solution)/shard_map/ffn_both/pallas_call | solution.py:530
  205.7 42.7 %mixer_backward.1 = (bf16[512,768]{1,0:T(8,128)(2,1)}, bf16[256,768]{1,0:T(8,128)(2,1)}, bf16[8,768,256]{2,1,0:T(8,128)(2,1)}) custom-call(s32[3]{0:T(128)} %pad_add_fusion.lens, bf16[768,768]{1,0:T(8,128)(2,1)} %get-tuple-element.36.xm, bf16[768,1152]{1,0:T(8,128)(2,1)} %get-tuple-element.41.packed, bf16[6,512,512]{2,1,0:T(8,128)(2,1)} %get-tuple-element.42.plong, ...), custom_call_target="tpu_custom_call" | custom-call | tf_op jit(solution)/shard_map/mixer_backward/pallas_call | solution.py:530
  248.4 15.8 %reduce-scatter.9.cloned.1.call-done = bf16[1,4,240,384]{3,2,1,0:T(8,128)(2,1)} async-done(((bf16[8,4,240,384]{3,2,1,0:T(8,128)(2,1)}), bf16[1,4,240,384]{3,2,1,0:T(8,128)(2,1)}) %reduce-scatter.9.cloned.1.call-update) | async-done | bytes 737296 | tf_op jit(solution)/shard_map/reduce_scatter | solution.py:630
  264.3 49.4 %reduce-scatter.5.cloned.1.call-done = bf16[1,4,192,256]{3,2,1,0:T(8,128)(2,1)} async-done(((bf16[8,4,192,256]{3,2,1,0:T(8,128)(2,1)}), bf16[1,4,192,256]{3,2,1,0:T(8,128)(2,1)}) %reduce-scatter.5.cloned.1.call-update) | async-done | bytes 393232 | tf_op jit(solution)/shard_map/reduce_scatter | solution.py:630
  313.8 25.1 %reduce-scatter.11.cloned.1.call-done = bf16[1,240,384]{2,1,0:T(8,128)(2,1)} async-done(((bf16[4,240,384]{2,1,0:T(8,128)(2,1)}), bf16[1,240,384]{2,1,0:T(8,128)(2,1)}) %reduce-scatter.11.cloned.1.call-update) | async-done | bytes 184336 | tf_op jit(solution)/shard_map/reduce_scatter | solution.py:631
  338.9 22.0 %reduce-scatter.7.cloned.1.call-done = bf16[1,192,256]{2,1,0:T(8,128)(2,1)} async-done(((bf16[4,192,256]{2,1,0:T(8,128)(2,1)}), bf16[1,192,256]{2,1,0:T(8,128)(2,1)}) %reduce-scatter.7.cloned.1.call-update) | async-done | bytes 98320 | tf_op jit(solution)/shard_map/reduce_scatter | solution.py:631
  360.9 10.7 %all_gather.24 = bf16[8,192,256]{2,1,0:T(8,128)(2,1)S(1)} all-gather(bf16[1,192,256]{2,1,0:T(8,128)(2,1)} %reduce-scatter.7.cloned.1.call-done), channel_id=1, replica_groups=mesh['wide'=8,'narrow'=4] {'wide'}, dimensions={0}, use_global_device_ids=true | all-gather | bytes 884736 | tf_op jit(solution)/shard_map/all_gather | solution.py:633
  372.0 1.0 slice.55
  373.0 0.7 copy.63
  374.4 0.9 slice_reduce_fusion
  375.3 0.9 fusion
  376.1 10.2 %all-gather.6.cloned.1.call-done = bf16[8,240,384]{2,1,0:T(8,128)(2,1)} async-done(((bf16[1,240,384]{2,1,0:T(8,128)(2,1)}), bf16[8,240,384]{2,1,0:T(8,128)(2,1)}) %all-gather.6.cloned.1.call-update) | async-done | bytes 1474576 | tf_op jit(solution)/shard_map/all_gather | solution.py:633
  386.4 1.1 slice.60
  387.9 0.9 copy.69
  388.8 1.2 fusion.1
  390.0 1.2 copy.68
  (36 shorter events, 6.9 us)
Async XLA Ops:
  7.2 68.5 %all-gather.8.cloned.1.call-start = ((), (), s32[]{:S(2)}) async-start(), calls=%async_computation.9 | async-start | bytes 3244032 | tf_op jit(solution)/shard_map/all_gather | solution.py:618
  10.9 6.1 %copy-start.1 = (s32[2]{0:T(128)S(1)}, s32[2]{0:T(128)}, u32[]{:S(2)}) copy-start(s32[2]{0:T(128)} %param.21) | copy-start | bytes 28
  13.8 132.2 %all-gather.10.cloned.1.call-start = ((), (), s32[]{:S(2)}) async-start(), calls=%async_computation.10 | async-start | bytes 6082560 | tf_op jit(solution)/shard_map/all_gather | solution.py:619
  16.3 247.9 %reduce-scatter.9.cloned.1.call-start = ((), (), s32[]{:S(2)}) async-start(), calls=%async_computation.6 | async-start | bytes 6635520 | tf_op jit(solution)/shard_map/reduce_scatter | solution.py:630
  205.4 108.3 %reduce-scatter.5.cloned.1.call-start = ((), (), s32[]{:S(2)}) async-start(), calls=%async_computation.4 | async-start | bytes 3538944 | tf_op jit(solution)/shard_map/reduce_scatter | solution.py:630
  248.3 90.5 %reduce-scatter.11.cloned.1.call-start = ((), (), s32[]{:S(2)}) async-start(), calls=%async_computation.7 | async-start | bytes 921600 | tf_op jit(solution)/shard_map/reduce_scatter | solution.py:631
  264.3 96.6 %reduce-scatter.7.cloned.1.call-start = ((), (), s32[]{:S(2)}) async-start(), calls=%async_computation.5 | async-start | bytes 491520 | tf_op jit(solution)/shard_map/reduce_scatter | solution.py:631
  313.8 72.6 %all-gather.6.cloned.1.call-start = ((), (), s32[]{:S(2)}) async-start(), calls=%async_computation.8 | async-start | bytes 1658880 | tf_op jit(solution)/shard_map/all_gather | solution.py:633
  386.4 2.4 copy-start
Sparse Core Ops, SparseCore 0:
  13.9 61.7 all-gather.7
  79.1 66.9 all-gather.9
  205.5 58.6 reduce-scatter.8
  267.5 46.2 reduce-scatter.4
  316.0 22.8 reduce-scatter.10
  341.1 19.7 reduce-scatter.6
  362.8 23.5 all-gather.5

commit v2 on v1

--- a/solution.py
+++ b/solution.py
@@ -94,9 +94,24 @@
     return nn(stored, tap_permutation()).astype(BF)
 
 
+def slot_of(where, core, chip):
+    return 2 * ((where >> 1) ^ chip) + ((where & 1) ^ core)
+
+
 def mixer_forward(
-    lens, xl, xs, wm, xm, packed, plong, pshort, dw, kc, cq, kp, cv, ctx, vec, xpad, spread, wk
+    place, llen, slen, xl, xs, p0, p1, p2, p3, p4, p5, p6, p7,
+    xm, packed, plong, pshort, dw, kc, cq, kp, cv, ctx, vec, wm, xpad, spread, wk, sem
 ):
+    for core, pieces in enumerate(((p0, p1, p2, p3), (p4, p5, p6, p7))):
+        for chip, piece in enumerate(pieces):
+            slot = slot_of(place[0], core, chip)
+
+            def fetch(k):
+                rows = pl.ds(pl.multiple_of((place[1] ^ k) * 192, 192), 192)
+                pltpu.make_async_copy(piece.at[k], wm.at[slot, rows, :], sem).start()
+
+            loop(4, fetch)
+    lens = (llen[0], slen[0], slen[1])
     zero_gaps(xpad)
     zero_gaps(cv)
     zero_gaps(kp)
@@ -108,8 +123,9 @@
         values = jnp.where(live, tokens.astype(F32), 0.0)
         xpad[PSTART[i] : PSTART[i] + 128, :] = values
         xm[128 * i : 128 * i + 128, :] = values.astype(BF)
+    spread[...] = head_spread()
+    pltpu.make_async_copy(wm, wm, sem).wait()
     vec[...] = nt(eye(128, BF), wm[7, :, 128:256])[0:24, :]
-    spread[...] = head_spread()
     wk[...] = tap_kernel(wm)
 
     def project(b):
@@ -200,7 +216,7 @@
         def store(hh, probs):
             pshort[seg, 2 * pair + hh, :, :] = probs
 
-        attend(row0, 128, row0, SHORT, lens[1 + seg], pair, store)
+        attend(row0, 128, row0, SHORT, slen[seg], pair, store)
 
     loop(6, short_attend)
 
@@ -224,24 +240,42 @@
 
 
 def ffn_both(
-    lens, xm, ctx, vec, wf, cl, cs,
+    place, llen, slen, xm, ctx, vec, cl, cs, p0, p1, p2, p3, p4, p5, p6, p7,
     ol, os, ga, gone, gctx, gvec,
-    wo, wi, wu, res, xhat, grouped, gffn, active, slope, ffn, rstd, acc, ghid, gproj,
+    wo, wi, wu, res, xhat, grouped, gffn, active, slope, ffn, rstd, acc, ghid, gproj, sems,
 ):
-    for n in range(4):
-        for w in range(8):
-            wi[w, 96 * n : 96 * n + 96, :] = wf[w, n, 0:96, :]
-            wu[4 * (w // 4) + n, 96 * (w % 4) : 96 * (w % 4) + 96, :] = wf[w, n, 96:192, :]
-            row = 192 * n + 48 * (w % 4)
-            lanes = slice(AH * (w // 4), AH * (w // 4) + AH)
-            wo[row : row + 48, lanes] = wf[w, n, 192:240, :]
+    def fetch(part):
+        for core, pieces in enumerate(((p0, p1, p2, p3), (p4, p5, p6, p7))):
+            for chip, piece in enumerate(pieces):
+                slot = slot_of(place[0], core, chip)
+                g, r = slot >> 2, slot & 3
+
+                def one(k):
+                    n = place[1] ^ k
+                    if part == 0:
+                        rows = pl.ds(pl.multiple_of(192 * n + 48 * r, 48), 48)
+                        source, target = pl.ds(192, 48), wo.at[g, rows, :]
+                    elif part == 1:
+                        source, target = pl.ds(0, 96), wi.at[slot, at(n, 96), :]
+                    else:
+                        source, target = pl.ds(96, 96), wu.at[4 * g + n, at(r, 96), :]
+                    pltpu.make_async_copy(piece.at[k, source, :], target, sems.at[part]).start()
+
+                loop(4, one)
+
+    for part in range(3):
+        fetch(part)
     gain_one, bias_one = vec[16:17, :], vec[17:18, :]
     gain_two, bias_two = vec[18:19, :], vec[19:20, :]
     gvec[...] = jnp.zeros((8, D), F32)
 
+    pltpu.make_async_copy(wo, wo, sems.at[0]).wait()
+
     def mix(i):
         rows = at(i, 256)
-        res[rows, :] = nn(ctx[rows, :], wo[...]) + xm[rows, :].astype(F32)
+        for c in range(2):
+            lanes = slice(AH * c, AH * c + AH)
+            res[rows, lanes] = nn(ctx[rows, :], wo[c]) + xm[rows, lanes].astype(F32)
 
     loop(3, mix)
 
@@ -261,6 +295,8 @@
 
     loop(12, norm_one)
     ffn[...] = jnp.zeros((2, ROWS, AH), F32)
+    pltpu.make_async_copy(wi, wi, sems.at[1]).wait()
+    pltpu.make_async_copy(wu, wu, sems.at[2]).wait()
 
     def expand(b):
         acc[...] = nn(grouped[b >> 2], wi[b])
@@ -287,10 +323,10 @@
             hat = center * scale
             out[rows, :] = (hat * gain_two + bias_two).astype(BF)
             if offset:
-                seg, base = 1 + (i >> 1), (i & 1) * 64
+                limit, base = slen[i >> 1], (i & 1) * 64
             else:
-                seg, base = 0, i * 64
-            live = base + iota((64, D), 0) < lens[seg]
+                limit, base = llen[0], i * 64
+            live = base + iota((64, D), 0) < limit
             up = jnp.where(live, cot[rows, :].astype(F32), 0.0)
             gvec[2:3, :] += jnp.sum(up * hat, axis=0, keepdims=True)
             gvec[3:4, :] += jnp.sum(up, axis=0, keepdims=True)
@@ -322,10 +358,10 @@
         loop(12, act)
         part = tn(active[b], gffn[g]).astype(BF)
         for w in range(4):
-            ga[4 * g + w, n, 96:192, :] = part[96 * w : 96 * w + 96, :]
+            ga[(4 * g + w) ^ place[0], n ^ place[1], 96:192, :] = part[96 * w : 96 * w + 96, :]
         part = tn(grouped[g], ghid[...]).astype(BF)
         for m in range(4):
-            ga[b, m, 0:96, :] = part[96 * m : 96 * m + 96, :]
+            ga[b ^ place[0], m ^ place[1], 0:96, :] = part[96 * m : 96 * m + 96, :]
         ffn[g] += nt(ghid[...], wi[b])
 
     loop(8, contract)
@@ -351,17 +387,18 @@
         for n in range(4):
             for r in range(4):
                 row = 192 * n + 48 * r
-                ga[4 * c + r, n, 192:240, :] = part[row : row + 48, :]
+                ga[(4 * c + r) ^ place[0], n ^ place[1], 192:240, :] = part[row : row + 48, :]
 
     def unmix(i):
         rows = at(i, 256)
-        gctx[rows, :] = nt(gproj[rows, :], wo[...]).astype(BF)
+        part = nt(gproj[rows, 0:AH], wo[0]) + nt(gproj[rows, AH:D], wo[1])
+        gctx[rows, :] = part.astype(BF)
 
     loop(3, unmix)
 
 
 def mixer_backward(
-    lens, xm, packed, plong, pshort, dw, kc, cq, kp, cv, vec, gone, gctx, gvec, wm,
+    place, llen, slen, xm, packed, plong, pshort, dw, kc, cq, kp, cv, vec, gone, gctx, gvec, wm,
     il, is_, gb,
     xpad, gcp, gdp, grads, gqc, dkv, gkc, glog, gdep, spread, gather, wk,
 ):
@@ -488,24 +525,28 @@
 
     loop(6, pack)
 
+    def spill(b, values, lanes):
+        for n in range(4):
+            gb[b ^ place[0], n ^ place[1], :, lanes] = values[192 * n : 192 * n + 192, :]
+
     def weights(b):
-        gb[b] = tn(xm[...], grads[:, at(b, 256)]).astype(BF)
+        spill(b, tn(xm[...], grads[:, at(b, 256)]).astype(BF), slice(0, 256))
 
     loop(6, weights)
-    gb[6] = tn(dw[...], gkc[:, 0:256]).astype(BF)
-    gb[7, :, 0:128] = tn(dw[...], gkc[:, 256:384]).astype(BF)
+    spill(6, tn(dw[...], gkc[:, 0:256]).astype(BF), slice(0, 256))
+    spill(7, tn(dw[...], gkc[:, 256:384]).astype(BF), slice(0, 128))
     taps = [jnp.sum(gdep[8 * j : 8 * j + 8, :], axis=0, keepdims=True) for j in range(TAPS)]
     table = jnp.concatenate(
         taps + [jnp.zeros((7, D), F32), gvec[...], jnp.zeros((104, D), F32)], axis=0
     ).astype(BF)
     misc = tn(table, eye(128, BF))
     gkernel = nt(tn(cq[...], glog[...]).astype(BF), tap_permutation())
+    parts = []
     for n in range(4):
         row = 192 * n
-        gb[7, row : row + 96, 128:256] = (
-            misc[row : row + 96, :] + gkernel[96 * n : 96 * n + 96, :]
-        ).astype(BF)
-        gb[7, row + 96 : row + 192, 128:256] = misc[row + 96 : row + 192, :].astype(BF)
+        parts.append(misc[row : row + 96, :] + gkernel[96 * n : 96 * n + 96, :])
+        parts.append(misc[row + 96 : row + 192, :])
+    spill(7, jnp.concatenate(parts, axis=0).astype(BF), slice(128, 256))
 
     def inputs(i):
         rows = at(i, 256)
@@ -515,7 +556,7 @@
         return total
 
     def inputs_long(i):
-        live = i * 256 + iota((256, D), 0) < lens[0]
+        live = i * 256 + iota((256, D), 0) < llen[0]
         il[at(i, 256), :] = jnp.where(live, inputs(i), 0.0).astype(BF)
 
     loop(2, inputs_long)
@@ -523,86 +564,176 @@
     row = iota((128, D), 0)
     for seg in range(2):
         part = total[128 * seg : 128 * seg + 128, :]
-        is_[128 * seg : 128 * seg + 128, :] = jnp.where(row < lens[1 + seg], part, 0.0).astype(BF)
-
-
-def call(kernel, n_in, outs, scratch, *args):
+        is_[128 * seg : 128 * seg + 128, :] = jnp.where(row < slen[seg], part, 0.0).astype(BF)
+
+
+def pack(
+    place, qkv, depth, point, kernel, convout, g1, b1, inner, outer, out, g2, b2, mixer, ffn
+):
+    for w in range(SLOTS):
+
+        @pl.when(place[0] == w)
+        def _():
+            g, r = w // 4, w % 4
+            ffn[0:96, :] = inner[g, :, AH * r : AH * r + AH]
+            ffn[96:192, :] = outer[g, 96 * r : 96 * r + 96, :]
+            ffn[192:240, :] = out[48 * r : 48 * r + 48, AH * g : AH * g + AH]
+            if w < 4:
+                mixer[...] = qkv[:, 256 * w : 256 * w + 256]
+            elif w == 4:
+                mixer[:, 0:128] = qkv[:, 1024:1152]
+                mixer[:, 128:256] = convout[:, 0:128]
+            elif w == 5:
+                mixer[...] = convout[:, 128:384]
+            elif w == 6:
+                mixer[...] = point[:, 0:256]
+            else:
+                mixer[:, 0:128] = point[:, 256:384]
+                rows = [v[...].astype(F32).reshape(1, 192) for v in (g1, b1, g2, b2)]
+                table = jnp.concatenate(
+                    [depth[...].astype(F32), jnp.zeros((7, 192), F32)]
+                    + rows
+                    + [jnp.zeros((108, 192), F32)],
+                    axis=0,
+                )
+                left = tn(table.astype(BF), eye(128, BF))
+                row, col = iota((54, 128), 0), iota((54, 128), 1)
+                right = nn(kernel[...], jnp.where(col == row + 64, 1.0, 0.0).astype(BF))
+                mixer[0:96, 128:256] = (left[0:96, :] + right).astype(BF)
+                mixer[96:192, 128:256] = left[96:192, :].astype(BF)
+
+
+def unpack_ffn(packed, inner, outer, out):
+    for w in range(SLOTS):
+        g, r = w // 4, w % 4
+        inner[g, :, AH * r : AH * r + AH] = packed[w, 0:96, :].astype(F32)
+        outer[g, 96 * r : 96 * r + 96, :] = packed[w, 96:192, :].astype(F32)
+        out[48 * r : 48 * r + 48, AH * g : AH * g + AH] = packed[w, 192:240, :].astype(F32)
+
+
+def unpack_mixer(packed, qkv, depth, point, kernel, convout, g1, b1, g2, b2):
+    for w in range(4):
+        qkv[:, 256 * w : 256 * w + 256] = packed[w].astype(F32)
+    qkv[:, 1024:1152] = packed[4, :, 0:128].astype(F32)
+    convout[:, 0:128] = packed[4, :, 128:256].astype(F32)
+    convout[:, 128:384] = packed[5].astype(F32)
+    point[:, 0:256] = packed[6].astype(F32)
+    point[:, 256:384] = packed[7, :, 0:128].astype(F32)
+    misc = packed[7, :, 128:256]
+    table = nt(eye(128, BF), misc)
+    depth[...] = table[0:TAPS, :]
+    for k, ref in enumerate((g1, b1, g2, b2)):
+        ref[...] = table[16 + k : 17 + k, :].reshape(192)
+    row, col = iota((128, 54), 0), iota((128, 54), 1)
+    kernel[...] = nn(misc[0:96, :], jnp.where(row == col + 64, 1.0, 0.0).astype(BF))
+
+
+SMEM = pl.BlockSpec(memory_space=pltpu.SMEM)
+VMEM = pl.BlockSpec(memory_space=pltpu.VMEM)
+ANY = pl.BlockSpec(memory_space=pl.ANY)
+
+
+def call(kernel, specs, outs, scratch, flops, *args):
     return pl.pallas_call(
         kernel,
         out_shape=[jax.ShapeDtypeStruct(s, d) for s, d in outs],
-        in_specs=[pl.BlockSpec(memory_space=pltpu.SMEM)]
-        + [pl.BlockSpec(memory_space=pltpu.VMEM)] * (n_in - 1),
-        out_specs=[pl.BlockSpec(memory_space=pltpu.VMEM)] * len(outs),
-        scratch_shapes=[pltpu.VMEM(s, d) for s, d in scratch],
+        in_specs=specs,
+        out_specs=[VMEM] * len(outs),
+        scratch_shapes=[pltpu.VMEM(s, d) for s, d in scratch[0]] + list(scratch[1:]),
         compiler_params=pltpu.CompilerParams(vmem_limit_bytes=60 << 20),
+        cost_estimate=pl.CostEstimate(flops=flops, bytes_accessed=1 << 20, transcendentals=0),
         name=kernel.__name__,
     )(*args)
 
 
-def forward_mixer(lens, xl, xs, wm):
+def forward_mixer(scalars, xl, xs, pieces):
     outs = [
         ((ROWS, D), BF), ((ROWS, 3 * AH), BF),
         ((HEADS, LONG, LONG), BF), ((2, HEADS, SHORT, SHORT), BF),
         ((ROWS, D), BF), ((ROWS, AH), F32), ((ROWS, AH), BF), ((PAD, 128), F32),
-        ((PAD, AH), F32), ((ROWS, D), BF), ((24, D), F32),
+        ((PAD, AH), F32), ((ROWS, D), BF), ((24, D), F32), ((SLOTS, D, 256), BF),
     ]
     scratch = [((PAD, D), F32), ((256, AH), BF), ((AH, 128), BF)]
-    return call(mixer_forward, 4, outs, scratch, lens, xl, xs, wm)
-
-
-def feed_forward(lens, xm, ctx, vec, wf, cl, cs):
+    return call(
+        mixer_forward, [SMEM] * 3 + [VMEM] * 2 + [ANY] * 8, outs,
+        (scratch, pltpu.SemaphoreType.DMA), 30 * 10**9, *scalars, xl, xs, *pieces,
+    )
+
+
+def feed_forward(scalars, xm, ctx, vec, cl, cs, pieces):
     outs = [
         ((LONG, D), BF), ((2 * SHORT, D), BF), ((SLOTS, 4, 240, AH), BF),
         ((ROWS, D), F32), ((ROWS, D), BF), ((8, D), F32),
     ]
     scratch = [
-        ((D, D), BF), ((8, AH, AH), BF), ((8, AH, AH), BF), ((ROWS, D), F32), ((ROWS, D), F32),
+        ((2, D, AH), BF), ((8, AH, AH), BF), ((8, AH, AH), BF), ((ROWS, D), F32), ((ROWS, D), F32),
         ((2, ROWS, AH), BF), ((2, ROWS, AH), BF), ((8, ROWS, AH), BF), ((8, ROWS, AH), F32),
         ((2, ROWS, AH), F32), ((ROWS, 128), F32), ((ROWS, AH), F32), ((ROWS, AH), BF),
         ((ROWS, D), BF),
     ]
-    return call(ffn_both, 7, outs, scratch, lens, xm, ctx, vec, wf, cl, cs)
-
-
-def backward_mixer(*args):
-    outs = [((LONG, D), BF), ((2 * SHORT, D), BF), ((SLOTS, D, 256), BF)]
+    return call(
+        ffn_both, [SMEM] * 3 + [VMEM] * 5 + [ANY] * 8, outs,
+        (scratch, pltpu.SemaphoreType.DMA((3,))), 60 * 10**9,
+        *scalars, xm, ctx, vec, cl, cs, *pieces,
+    )
+
+
+def backward_mixer(scalars, *args):
+    outs = [((LONG, D), BF), ((2 * SHORT, D), BF), ((SLOTS, 4, 192, 256), BF)]
     scratch = [
         ((PAD, D), F32), ((PAD, AH), F32), ((PAD, D), F32), ((ROWS, 4 * AH), BF),
         ((ROWS, AH), F32), ((2, ROWS, AH), F32), ((ROWS, AH), BF), ((ROWS, 128), BF),
         ((8 * TAPS, D), F32), ((256, AH), BF), ((AH, 128), BF), ((AH, 128), BF),
     ]
-    return call(mixer_backward, 15, outs, scratch, *args)
-
-
-def layer(lens, xl, xs, cl, cs, wm, wf):
-    xm, packed, plong, pshort, dw, kc, cq, kp, cv, ctx, vec = forward_mixer(lens, xl, xs, wm)
-    ol, os, ga, gone, gctx, gvec = feed_forward(lens, xm, ctx, vec, wf, cl, cs)
-    il, is_, gb = backward_mixer(
-        lens, xm, packed, plong, pshort, dw, kc, cq, kp, cv, vec, gone, gctx, gvec, wm
-    )
-    return ol, os, il, is_, ga, gb
-
-
-def pack_mixer(w_qkv, w_depth, w_point, w_kernel, w_convout, g1, b1, g2, b2):
-    rows = w_qkv.shape[0]
-    norms = jnp.stack([g1, b1, g2, b2], axis=1)
-    left = jnp.concatenate(
-        [
-            jnp.pad(w_depth.T, ((0, 0), (0, 16 - TAPS))),
-            jnp.pad(norms, ((0, 0), (0, 44))),
-        ],
-        axis=1,
-    )
-    right = jnp.pad(w_kernel, ((0, rows - w_kernel.shape[0]), (0, 64 - w_kernel.shape[1])))
-    return jnp.concatenate([w_qkv, w_convout, w_point, left, right], axis=1)
-
-
-def pack_ffn(w_out, w_inner, w_outer, slot):
-    g, c = slot // 4, slot % 4
-    inner = lax.dynamic_slice(w_inner, (g, 0, c * AH), (1, 96, AH))[0]
-    outer = lax.dynamic_slice(w_outer, (g, c * 96, 0), (1, 96, AH))[0]
-    out = lax.dynamic_slice(w_out, (c * 48, g * AH), (48, AH))
-    return jnp.concatenate([inner, outer, out], axis=0)
+    return call(
+        mixer_backward, [SMEM] * 3 + [VMEM] * len(args), outs, (scratch,), 40 * 10**9,
+        *scalars, *args,
+    )
+
+
+def far(values, bit):
+    return lax.ppermute(values, "narrow", [(i, i ^ bit) for i in range(4)])
+
+
+def near(values, bit):
+    return lax.ppermute(values, "wide", [(i, i ^ bit) for i in range(SLOTS)])
+
+
+def gather_narrow(piece):
+    return jnp.stack([piece] + [far(piece, k) for k in (1, 2, 3)])
+
+
+def gather_chips(block):
+    return [block] + [near(block, k) for k in (2, 4, 6)]
+
+
+def gather_cores(blocks):
+    return blocks + [near(block, 1) for block in blocks]
+
+
+def total(first, others):
+    result = first.astype(F32)
+    for other in others:
+        result = result + other.astype(F32)
+    return result.astype(BF)
+
+
+def reduce_cores(parts):
+    parts = parts.reshape((4, 2) + parts.shape[1:])
+    return total(parts[:, 0], [near(parts[:, 1], 1)])
+
+
+def reduce_chips(parts):
+    return total(parts[0], [near(parts[k], 2 * k) for k in (1, 2, 3)])
+
+
+def reduce_narrow(parts):
+    parts = total(parts[0], [far(parts[k], k) for k in (1, 2, 3)])
+    return lax.psum(parts, "hi")
+
+
+def gather_wide(parts):
+    return lax.all_gather(parts, "wide", axis=0, tiled=False)
 
 
 def body(
@@ -610,40 +741,47 @@
     w_qkv, w_depth, w_point, w_kernel, w_convout, w_out, norm1_gain, norm1_bias,
     w_inner, w_outer, norm2_gain, norm2_bias, long_cotangent, short_cotangent,
 ):
-    slot = lax.axis_index("wide")
-    mixer = pack_mixer(
-        w_qkv, w_depth, w_point, w_kernel, w_convout, norm1_gain, norm1_bias, norm2_gain, norm2_bias
-    )
-    mixer = lax.dynamic_slice(mixer, (0, slot * 256), (192, 256))
-    wm = lax.all_gather(mixer, ("wide", "narrow"), axis=0, tiled=False).reshape(SLOTS, D, 256)
-    wf = lax.all_gather(pack_ffn(w_out, w_inner, w_outer, slot), ("wide", "narrow"), axis=0)
-    wf = wf.reshape(SLOTS, 4, 240, AH)
-    lens = jnp.concatenate([long_lengths, short_lengths])
-    ol, os, il, is_, ga, gb = layer(
-        lens,
-        long_tokens.reshape(LONG, D), short_tokens.reshape(2 * SHORT, D),
-        long_cotangent.reshape(LONG, D), short_cotangent.reshape(2 * SHORT, D),
-        wm, wf,
-    )
-
-    def reduce(parts):
-        parts = lax.psum_scatter(parts, "wide", scatter_dimension=0, tiled=False)
-        parts = lax.psum_scatter(parts, "narrow", scatter_dimension=0, tiled=False)
-        parts = lax.psum(parts, "hi")
-        return lax.all_gather(parts, "wide", axis=0, tiled=False).astype(F32)
-
-    ga = reduce(ga)
-    gb = reduce(gb.reshape(SLOTS, 4, 192, 256))
-    inner = ga[:, 0:96].reshape(2, 4, 96, AH).transpose(0, 2, 1, 3).reshape(2, 96, 4 * AH)
-    outer = ga[:, 96:192].reshape(2, AH, AH)
-    out = ga[:, 192:240].reshape(2, 4, 48, AH).transpose(1, 2, 0, 3).reshape(192, D)
-    gb = gb.transpose(1, 0, 2).reshape(192, 2048)
-    misc = gb[:, 1920:2048]
+    place = jnp.stack([lax.axis_index("wide"), lax.axis_index("narrow")]).astype(jnp.int32)
+    scalars = (place, long_lengths, short_lengths)
+    xl, xs = long_tokens.reshape(LONG, D), short_tokens.reshape(2 * SHORT, D)
+    cl, cs = long_cotangent.reshape(LONG, D), short_cotangent.reshape(2 * SHORT, D)
+    mixer, ffn = call(
+        pack, [SMEM] + [VMEM] * 12, [((192, 256), BF), ((240, AH), BF)], ([],), 10**9,
+        place, w_qkv, w_depth, w_point, w_kernel, w_convout, norm1_gain, norm1_bias,
+        w_inner, w_outer, w_out, norm2_gain, norm2_bias,
+    )
+    mixer = gather_narrow(mixer)
+    mixer, ffn = lax.optimization_barrier((mixer, ffn))
+    mixer = gather_chips(mixer)
+    ffn = gather_narrow(ffn)
+    mixer, ffn = lax.optimization_barrier((mixer, ffn))
+    mixer = gather_cores(mixer)
+    ffn = gather_chips(ffn)
+    xm, packed, plong, pshort, dw, kc, cq, kp, cv, ctx, vec, wm = forward_mixer(
+        scalars, xl, xs, mixer
+    )
+    ffn = gather_cores(ffn)
+    ol, os, ga, gone, gctx, gvec = feed_forward(scalars, xm, ctx, vec, cl, cs, ffn)
+    ga = reduce_cores(ga)
+    il, is_, gb = backward_mixer(
+        scalars, xm, packed, plong, pshort, dw, kc, cq, kp, cv, vec, gone, gctx, gvec, wm
+    )
+    ga = reduce_narrow(reduce_chips(ga))
+    gb = reduce_narrow(reduce_chips(reduce_cores(gb)))
+    inner, outer, out = call(
+        unpack_ffn, [VMEM], [((2, 96, 4 * AH), F32), ((2, AH, AH), F32), ((192, D), F32)],
+        ([],), 10**9, gather_wide(ga),
+    )
+    outs = [
+        ((192, 3 * AH), F32), ((TAPS, 192), F32), ((192, AH), F32), ((96, 54), F32), ((192, AH), F32),
+    ] + [((192,), F32)] * 4
+    qkv, depth, point, kernel, convout, g1, b1, g2, b2 = call(
+        unpack_mixer, [VMEM], outs, ([],), 10**9, gather_wide(gb)
+    )
     return (
         ol.reshape(long_tokens.shape), os.reshape(short_tokens.shape),
         il.reshape(long_tokens.shape), is_.reshape(short_tokens.shape),
-        gb[:, 0:1152], misc[:, 0:TAPS].T, gb[:, 1536:1920], misc[0:96, 64:118], gb[:, 1152:1536],
-        out, misc[:, 16], misc[:, 17], inner, outer, misc[:, 18], misc[:, 19],
+        qkv, depth, point, kernel, convout, out, g1, b1, inner, outer, g2, b2,
     )
 
 

time: 398 us -> 322 us (0.81)
  waiting for transfers between devices: 220 us -> 94.1 us
  starting transfers between devices: 0.46 us -> 38.2 us
  Pallas kernels: 133 us -> 142 us
  other arithmetic: 1.43 us -> 8.51 us
  local copies, waits for them, and re-layouts: 17.4 us -> 12.7 us
    reduce_scatter x4 -> x0, waiting for transfers between devices: 112 us -> none  [the longest x2 65.3 us: reduce(): parts = lax.psum_scatter(parts, 'wide', scatter_dimension=0, tiled=False)]
    all_gather x3 -> x1, waiting for transfers between devices: 108 us -> 0.01 us  [gather_wide(): return lax.all_gather(parts, 'wide', axis=0, tiled=False)]
    ppermute x0 -> x34, waiting for transfers between devices: none -> 94.1 us  [the longest x22 57 us: near(): return lax.ppermute(values, 'wide', [(i, i ^ bit) for i in range(SLOTS)])]
    ppermute x0 -> x34, starting transfers between devices: none -> 38.2 us  [the longest x12 22.3 us: far(): return lax.ppermute(values, 'narrow', [(i, i ^ bit) for i in range(4)])]
    pallas_call x3 -> x6, Pallas kernels: 133 us -> 142 us  [call(): pl.pallas_call(kernel, out_shape=[jax.ShapeDtypeStruct(s, d) for s, d in...]
    convert_element_type x0 -> x6, other arithmetic: none -> 5.94 us  [total(): return result.astype(BF)]
    squeeze x1 -> x6, local copies, waits for them, and re-layouts: 0.94 us -> 6.63 us  [the longest x2 5.02 us: reduce_cores(): return total(parts[:, 0], [near(parts[:, 1], 1)])]
    slice x6 -> x0, local copies, waits for them, and re-layouts: 5.14 us -> none  [the longest x1 1.17 us: body(): outer = ga[:, 96:192].reshape(2, AH, AH)]
  transfers between devices with their start and end apart: 7 -> 35, of which waited for: 7 -> 18; matrix products, arithmetic and copies ran while one was open for 2% -> 3% of each run, Pallas kernels for 19% -> 24%
where the time goes in v2:
time: 322 us
  Pallas kernels  142 us (44%)
  waiting for transfers between devices  94.1 us (29%)
  starting transfers between devices  38.2 us (12%)
  between operations  15 us (5%)
  local copies, waits for them, and re-layouts  12.7 us (4%)
  blocking collectives  11.1 us (3%)
  other arithmetic  8.51 us (3%)
    pallas_call x6, Pallas kernels, call(): pl.pallas_call(kernel, out_shape=[jax.ShapeDtypeStruct(s, d) for s, d in...  142 us
    ppermute x22, waiting for transfers between devices, near(): return lax.ppermute(values, 'wide', [(i, i ^ bit) for i in range(SLOTS)])  57 us
    ppermute x12, waiting for transfers between devices, far(): return lax.ppermute(values, 'narrow', [(i, i ^ bit) for i in range(4)])  37 us
    ppermute x12, starting transfers between devices, far(): return lax.ppermute(values, 'narrow', [(i, i ^ bit) for i in range(4)])  22.3 us
    ppermute x22, starting transfers between devices, near(): return lax.ppermute(values, 'wide', [(i, i ^ bit) for i in range(SLOTS)])  15.9 us
    all_gather x1, blocking collectives, gather_wide(): return lax.all_gather(parts, 'wide', axis=0, tiled=False)  11.1 us
  transfers between devices with their start and end apart: 35, of which 18 were waited for; matrix products, arithmetic and copies ran while one was open for 3% of the time, Pallas kernels for 24%

profile of v2, /device:TPU:0, one launch (start us, length us, event | category | flops | bytes accessed | tf_op | source)
XLA Modules:
  0.0 321.6 jit_solution(122134025416769012)
XLA Ops:
  9.2 2.4 pack.1
  11.6 5.0 %collective-permute-start.2 = (bf16[192,256]{1,0:T(8,128)(2,1)}, bf16[192,256]{1,0:T(8,128)(2,1)S(1)}, u32[]{:S(2)}, u32[]{:S(2)}) collective-permute-start(bf16[192,256]{1,0:T(8,128)(2,1)} %get-tuple-element.58), channel_id=1, source_target_pairs={{0,3},{1,2},{2,1},{3,0},{4,7},{5,6},{6,5},{7,4},{8,11},{9,10},{10,... | collective-permute-start | bytes 294920 | tf_op jit(solution)/shard_map/ppermute | solution.py:695
  17.3 3.3 %collective-permute-done.2 = bf16[192,256]{1,0:T(8,128)(2,1)S(1)} collective-permute-done((bf16[192,256]{1,0:T(8,128)(2,1)}, bf16[192,256]{1,0:T(8,128)(2,1)S(1)}, u32[]{:S(2)}, u32[]{:S(2)}) %collective-permute-start.2) | collective-permute-done | bytes 98336 | tf_op jit(solution)/shard_map/ppermute | solution.py:695
  20.6 4.6 %collective-permute-done.1 = bf16[192,256]{1,0:T(8,128)(2,1)S(1)} collective-permute-done((bf16[192,256]{1,0:T(8,128)(2,1)}, bf16[192,256]{1,0:T(8,128)(2,1)S(1)}, u32[]{:S(2)}, u32[]{:S(2)}) %collective-permute-start.1) | collective-permute-done | bytes 98336 | tf_op jit(solution)/shard_map/ppermute | solution.py:695
  26.1 2.6 collective-permute-start.8
  28.7 2.6 collective-permute-start.5
  32.2 3.1 collective-permute-done.8
  35.3 6.9 %collective-permute-start.6 = (bf16[240,384]{1,0:T(8,128)(2,1)}, bf16[240,384]{1,0:T(8,128)(2,1)S(1)}, u32[]{:S(2)}, u32[]{:S(2)}) collective-permute-start(bf16[240,384]{1,0:T(8,128)(2,1)} %get-tuple-element.61), channel_id=1, source_target_pairs={{0,1},{1,0},{2,3},{3,2},{4,5},{5,4},{6,7},{7,6},{8,9},{9,8},{10,11... | collective-permute-start | bytes 552968 | tf_op jit(solution)/shard_map/ppermute | solution.py:695
  54.7 14.1 %collective-permute-done.15.p3 = bf16[4,240,384]{2,1,0:T(8,128)(2,1)S(1)} collective-permute-done((bf16[4,240,384]{2,1,0:T(8,128)(2,1)S(1)}, bf16[4,240,384]{2,1,0:T(8,128)(2,1)S(1)}, u32[]{:S(2)}, u32[]{:S(2)}) %collective-permute-start.15) | collective-permute-done | bytes 737312 | tf_op jit(solution)/shard_map/ppermute | solution.py:699
  68.8 14.9 %collective-permute-done.14.p2 = bf16[4,240,384]{2,1,0:T(8,128)(2,1)S(1)} collective-permute-done((bf16[4,240,384]{2,1,0:T(8,128)(2,1)S(1)}, bf16[4,240,384]{2,1,0:T(8,128)(2,1)S(1)}, u32[]{:S(2)}, u32[]{:S(2)}) %collective-permute-start.14) | collective-permute-done | bytes 737312 | tf_op jit(solution)/shard_map/ppermute | solution.py:699
  85.1 33.0 %mixer_forward.1 = (bf16[768,768]{1,0:T(8,128)(2,1)}, bf16[768,1152]{1,0:T(8,128)(2,1)}, bf16[6,512,512]{2,1,0:T(8,128)(2,1)}, bf16[2,6,128,128]{3,2,1,0:T(8,128...) custom-call(s32[2]{0:T(128)} %pad_add_fusion.place, ...), custom_call_target="tpu_custom_call" | custom-call | flops 30000001024 | bytes 1048576 | tf_op jit(solution)/shard_map/mixer_forward/pallas_call | solution.py:637
  119.0 58.9 %ffn_both.1 = (bf16[512,768]{1,0:T(8,128)(2,1)}, bf16[256,768]{1,0:T(8,128)(2,1)}, bf16[8,4,240,384]{3,2,1,0:T(8,128)(2,1)}, f32[768,768]{1,0:T(8,128)}, bf16[768,768]{1,0:T(8,128)(2,1)}, /*index=5*/f32[8,768]{1,0:T(8,128)}) custom-call(s32[2]{0:T(128)} %pad_add_fusion.place, s32[1]{0:T(128)S(6)} %copy.44.llen, s32[2]{0:T(128)} %slen.5, ...), custom_call_target="tpu_custom_call" | custom-call | flops 60000002048 | bytes 1048576 | tf_op jit(solution)/shard_map/ffn_both/pallas_call | solution.py:637
  180.4 5.3 %collective-permute-done.27 = bf16[4,4,240,384]{3,2,1,0:T(8,128)(2,1)S(1)} collective-permute-done((bf16[4,4,240,384]{3,2,1,0:T(8,128)(2,1)S(1)}, bf16[4,4,240,384]{3,2,1,0:T(8,128)(2,1)S(1)}, u32[]{:S(2)}, u32[]{:S(2)}) %collective-permute-start.27) | collective-permute-done | bytes 2949152 | tf_op jit(solution)/shard_map/ppermute | solution.py:699
  191.4 42.2 %mixer_backward.1 = (bf16[512,768]{1,0:T(8,128)(2,1)}, bf16[256,768]{1,0:T(8,128)(2,1)}, bf16[8,4,192,256]{3,2,1,0:T(8,128)(2,1)}) custom-call(s32[2]{0:T(128)} %pad_add_fusion.place, s32[1]{0:T(128)S(6)} %copy.44.llen, s32[2]{0:T(128)} %slen.5, bf16[768,768]{1,0:T(8,128)(2,1)} %get-tuple-element.66.xm, bf16[768,1152]{1,0:T(8,128)(2,1)} %get-tuple-element.72.packed, ...), custom_call_target="tpu_custom_call" | custom-call | flops 40000000000 | bytes 1048576 | tf_op jit(solution)/shard_map/mixer_backward/pallas_call | solution.py:637
  233.6 2.7 slice_bitcast_fusion.2
  241.7 4.1 %collective-permute-done.31 = bf16[240,384]{1,0:T(8,128)(2,1)S(1)} collective-permute-done((bf16[240,384]{1,0:T(8,128)(2,1)S(1)}, bf16[240,384]{1,0:T(8,128)(2,1)S(1)}, u32[]{:S(2)}, u32[]{:S(2)}) %collective-permute-start.31) | collective-permute-done | bytes 184352 | tf_op jit(solution)/shard_map/ppermute | solution.py:695
  245.9 3.7 %collective-permute-done.33 = bf16[240,384]{1,0:T(8,128)(2,1)S(1)} collective-permute-done((bf16[240,384]{1,0:T(8,128)(2,1)S(1)}, bf16[240,384]{1,0:T(8,128)(2,1)S(1)}, u32[]{:S(2)}, u32[]{:S(2)}) %collective-permute-start.33) | collective-permute-done | bytes 184352 | tf_op jit(solution)/shard_map/ppermute | solution.py:695
  249.6 8.7 %collective-permute-done.32 = bf16[240,384]{1,0:T(8,128)(2,1)S(1)} collective-permute-done((bf16[240,384]{1,0:T(8,128)(2,1)S(1)}, bf16[240,384]{1,0:T(8,128)(2,1)S(1)}, u32[]{:S(2)}, u32[]{:S(2)}) %collective-permute-start.32) | collective-permute-done | bytes 184352 | tf_op jit(solution)/shard_map/ppermute | solution.py:695
  265.2 10.5 %collective-permute-done.21 = bf16[4,192,256]{2,1,0:T(8,128)(2,1)S(1)} collective-permute-done((bf16[4,192,256]{2,1,0:T(8,128)(2,1)S(1)}, bf16[4,192,256]{2,1,0:T(8,128)(2,1)S(1)}, u32[]{:S(2)}, u32[]{:S(2)}) %collective-permute-start.21) | collective-permute-done | bytes 393248 | tf_op jit(solution)/shard_map/ppermute | solution.py:699
  275.7 10.6 %collective-permute-done.23 = bf16[4,192,256]{2,1,0:T(8,128)(2,1)S(1)} collective-permute-done((bf16[4,192,256]{2,1,0:T(8,128)(2,1)S(1)}, bf16[4,192,256]{2,1,0:T(8,128)(2,1)S(1)}, u32[]{:S(2)}, u32[]{:S(2)}) %collective-permute-start.23) | collective-permute-done | bytes 393248 | tf_op jit(solution)/shard_map/ppermute | solution.py:699
  294.0 2.6 collective-permute-done.25
  296.7 11.1 %all-gather = bf16[1536,256]{1,0:T(8,128)(2,1)} all-gather(bf16[192,256]{1,0:T(8,128)(2,1)S(1)} %fusion.13), channel_id=2, replica_groups=mesh['wide'=8,'narrow'=4] {'wide'}, dimensions={0}, use_global_device_ids=true | all-gather | bytes 884736 | tf_op jit(solution)/shard_map/all_gather | solution.py:736
  307.8 2.4 unpack_mixer.1
  311.7 3.0 unpack_ffn.1
  (99 shorter events, 48.0 us)
Async XLA Ops:
  7.2 304.5 %all-gather.4.cloned.1.call-start = ((), (), s32[]{:S(2)}) async-start(), calls=%async_computation | async-start | bytes 1658880 | tf_op jit(solution)/shard_map/all_gather | solution.py:736
  26.1 9.2 %collective-permute-start.8 = (bf16[240,384]{1,0:T(8,128)(2,1)}, bf16[240,384]{1,0:T(8,128)(2,1)S(1)}, u32[]{:S(2)}, u32[]{:S(2)}) collective-permute-start(bf16[240,384]{1,0:T(8,128)(2,1)} %get-tuple-element.61), channel_id=1, source_target_pairs={{0,3},{1,2},{2,1},{3,0},{4,7},{5,6},{6,5},{7,4},{8,11},{9,10},{10,... | collective-permute-start | bytes 552968 | tf_op jit(solution)/shard_map/ppermute | solution.py:695
  28.7 18.3 %collective-permute-start.5 = (bf16[4,192,256]{2,1,0:T(8,128)(2,1)S(1)}, bf16[4,192,256]{2,1,0:T(8,128)(2,1)S(1)}, u32[]{:S(2)}, u32[]{:S(2)}) collective-permute-start(bf16[4,192,256]{2,1,0:T(8,128)(2,1)S(1)} %pad_maximum_fusion.1.p0), channel_id=1, source_target_pairs={{0,24},{4,28},{8,16},{12,20},{16,8},{20,12},{24,0},{28,4},{1,25},{... | collective-permute-start | bytes 1179656 | tf_op jit(solution)/shard_map/ppermute | solution.py:699
  31.3 16.6 %collective-permute-start.4 = (bf16[4,192,256]{2,1,0:T(8,128)(2,1)S(1)}, bf16[4,192,256]{2,1,0:T(8,128)(2,1)S(1)}, u32[]{:S(2)}, u32[]{:S(2)}) collective-permute-start(bf16[4,192,256]{2,1,0:T(8,128)(2,1)S(1)} %pad_maximum_fusion.1.p0), channel_id=1, source_target_pairs={{0,16},{4,20},{8,24},{12,28},{16,0},{20,4},{24,8},{28,12},{1,17},{... | collective-permute-start | bytes 1179656 | tf_op jit(solution)/shard_map/ppermute | solution.py:699
  31.6 16.3 %collective-permute-start.3 = (bf16[4,192,256]{2,1,0:T(8,128)(2,1)S(1)}, bf16[4,192,256]{2,1,0:T(8,128)(2,1)S(1)}, u32[]{:S(2)}, u32[]{:S(2)}) collective-permute-start(bf16[4,192,256]{2,1,0:T(8,128)(2,1)S(1)} %pad_maximum_fusion.1.p0), channel_id=1, source_target_pairs={{0,8},{4,12},{8,0},{12,4},{16,24},{20,28},{24,16},{28,20},{1,9},{5... | collective-permute-start | bytes 1179656 | tf_op jit(solution)/shard_map/ppermute | solution.py:699
  32.2 11.6 %collective-permute-start.7 = (bf16[240,384]{1,0:T(8,128)(2,1)}, bf16[240,384]{1,0:T(8,128)(2,1)S(1)}, u32[]{:S(2)}, u32[]{:S(2)}) collective-permute-start(bf16[240,384]{1,0:T(8,128)(2,1)} %get-tuple-element.61), channel_id=1, source_target_pairs={{0,2},{1,3},{2,0},{3,1},{4,6},{5,7},{6,4},{7,5},{8,10},{9,11},{10,... | collective-permute-start | bytes 552968 | tf_op jit(solution)/shard_map/ppermute | solution.py:695
  35.3 10.6 %collective-permute-start.6 = (bf16[240,384]{1,0:T(8,128)(2,1)}, bf16[240,384]{1,0:T(8,128)(2,1)S(1)}, u32[]{:S(2)}, u32[]{:S(2)}) collective-permute-start(bf16[240,384]{1,0:T(8,128)(2,1)} %get-tuple-element.61), channel_id=1, source_target_pairs={{0,1},{1,0},{2,3},{3,2},{4,5},{5,4},{6,7},{7,6},{8,9},{9,8},{10,11... | collective-permute-start | bytes 552968 | tf_op jit(solution)/shard_map/ppermute | solution.py:695
  48.5 20.3 %collective-permute-start.15 = (bf16[4,240,384]{2,1,0:T(8,128)(2,1)S(1)}, bf16[4,240,384]{2,1,0:T(8,128)(2,1)S(1)}, u32[]{:S(2)}, u32[]{:S(2)}) collective-permute-start(bf16[4,240,384]{2,1,0:T(8,128)(2,1)S(1)} %pad_maximum_fusion.p0), channel_id=1, source_target_pairs={{0,24},{4,28},{8,16},{12,20},{16,8},{20,12},{24,0},{28,4},{1,25},{... | collective-permute-start | bytes 2211848 | tf_op jit(solution)/shard_map/ppermute | solution.py:699
  50.5 33.2 %collective-permute-start.14 = (bf16[4,240,384]{2,1,0:T(8,128)(2,1)S(1)}, bf16[4,240,384]{2,1,0:T(8,128)(2,1)S(1)}, u32[]{:S(2)}, u32[]{:S(2)}) collective-permute-start(bf16[4,240,384]{2,1,0:T(8,128)(2,1)S(1)} %pad_maximum_fusion.p0), channel_id=1, source_target_pairs={{0,16},{4,20},{8,24},{12,28},{16,0},{20,4},{24,8},{28,12},{1,17},{... | collective-permute-start | bytes 2211848 | tf_op jit(solution)/shard_map/ppermute | solution.py:699
  51.7 32.0 %collective-permute-start.13 = (bf16[4,240,384]{2,1,0:T(8,128)(2,1)S(1)}, bf16[4,240,384]{2,1,0:T(8,128)(2,1)S(1)}, u32[]{:S(2)}, u32[]{:S(2)}) collective-permute-start(bf16[4,240,384]{2,1,0:T(8,128)(2,1)S(1)} %pad_maximum_fusion.p0), channel_id=1, source_target_pairs={{0,8},{4,12},{8,0},{12,4},{16,24},{20,28},{24,16},{28,20},{1,9},{5... | collective-permute-start | bytes 2211848 | tf_op jit(solution)/shard_map/ppermute | solution.py:699
  53.5 30.8 %collective-permute-start.12 = (bf16[4,192,256]{2,1,0:T(8,128)(2,1)S(1)}, bf16[4,192,256]{2,1,0:T(8,128)(2,1)S(1)}, u32[]{:S(2)}, u32[]{:S(2)}) collective-permute-start(bf16[4,192,256]{2,1,0:T(8,128)(2,1)S(1)} %collective-permute-done.5.p3), channel_id=1, source_target_pairs={{0,4},{4,0},{8,12},{12,8},{16,20},{20,16},{24,28},{28,24},{1,5},{5... | collective-permute-start | bytes 1179656 | tf_op jit(solution)/shard_map/ppermute | solution.py:699
  54.2 63.9 %collective-permute-start.16 = (bf16[4,240,384]{2,1,0:T(8,128)(2,1)S(1)}, bf16[4,240,384]{2,1,0:T(8,128)(2,1)S(1)}, u32[]{:S(2)}, u32[]{:S(2)}) collective-permute-start(bf16[4,240,384]{2,1,0:T(8,128)(2,1)S(1)} %pad_maximum_fusion.p0), channel_id=1, source_target_pairs={{0,4},{4,0},{8,12},{12,8},{16,20},{20,16},{24,28},{28,24},{1,5},{5... | collective-permute-start | bytes 2211848 | tf_op jit(solution)/shard_map/ppermute | solution.py:699
  68.8 49.3 %collective-permute-start.19 = (bf16[4,240,384]{2,1,0:T(8,128)(2,1)S(1)}, bf16[4,240,384]{2,1,0:T(8,128)(2,1)}, u32[]{:S(2)}, u32[]{:S(2)}) collective-permute-start(bf16[4,240,384]{2,1,0:T(8,128)(2,1)S(1)} %collective-permute-done.15.p3), channel_id=1, source_target_pairs={{0,4},{4,0},{8,12},{12,8},{16,20},{20,16},{24,28},{28,24},{1,5},{5... | collective-permute-start | bytes 2211848 | tf_op jit(solution)/shard_map/ppermute | solution.py:699
  83.7 34.4 %collective-permute-start.18 = (bf16[4,240,384]{2,1,0:T(8,128)(2,1)S(1)}, bf16[4,240,384]{2,1,0:T(8,128)(2,1)}, u32[]{:S(2)}, u32[]{:S(2)}) collective-permute-start(bf16[4,240,384]{2,1,0:T(8,128)(2,1)S(1)} %collective-permute-done.14.p2), channel_id=1, source_target_pairs={{0,4},{4,0},{8,12},{12,8},{16,20},{20,16},{24,28},{28,24},{1,5},{5... | collective-permute-start | bytes 2211848 | tf_op jit(solution)/shard_map/ppermute | solution.py:699
  83.7 34.4 %collective-permute-start.17 = (bf16[4,240,384]{2,1,0:T(8,128)(2,1)S(1)}, bf16[4,240,384]{2,1,0:T(8,128)(2,1)}, u32[]{:S(2)}, u32[]{:S(2)}) collective-permute-start(bf16[4,240,384]{2,1,0:T(8,128)(2,1)S(1)} %collective-permute-done.13.p1), channel_id=1, source_target_pairs={{0,4},{4,0},{8,12},{12,8},{16,20},{20,16},{24,28},{28,24},{1,5},{5... | collective-permute-start | bytes 2211848 | tf_op jit(solution)/shard_map/ppermute | solution.py:699
  187.9 48.5 %collective-permute-start.28 = (bf16[4,240,384]{2,1,0:T(8,128)(2,1)}, bf16[4,240,384]{2,1,0:T(8,128)(2,1)S(1)}, u32[]{:S(2)}, u32[]{:S(2)}) collective-permute-start(bf16[4,240,384]{2,1,0:T(8,128)(2,1)} %get-tuple-element.116), channel_id=1, source_target_pairs={{0,8},{4,12},{8,0},{12,4},{16,24},{20,28},{24,16},{28,20},{1,9},{5... | collective-permute-start | bytes 2211848 | tf_op jit(solution)/shard_map/ppermute | solution.py:699
  189.3 47.1 %collective-permute-start.30 = (bf16[4,240,384]{2,1,0:T(8,128)(2,1)}, bf16[4,240,384]{2,1,0:T(8,128)(2,1)}, u32[]{:S(2)}, u32[]{:S(2)}) collective-permute-start(bf16[4,240,384]{2,1,0:T(8,128)(2,1)} %get-tuple-element.117), channel_id=1, source_target_pairs={{0,24},{4,28},{8,16},{12,20},{16,8},{20,12},{24,0},{28,4},{1,25},{... | collective-permute-start | bytes 2211848 | tf_op jit(solution)/shard_map/ppermute | solution.py:699
  190.4 46.0 %collective-permute-start.29 = (bf16[4,240,384]{2,1,0:T(8,128)(2,1)}, bf16[4,240,384]{2,1,0:T(8,128)(2,1)}, u32[]{:S(2)}, u32[]{:S(2)}) collective-permute-start(bf16[4,240,384]{2,1,0:T(8,128)(2,1)} %get-tuple-element.118), channel_id=1, source_target_pairs={{0,16},{4,20},{8,24},{12,28},{16,0},{20,4},{24,8},{28,12},{1,17},{... | collective-permute-start | bytes 2211848 | tf_op jit(solution)/shard_map/ppermute | solution.py:699
  236.4 22.7 %collective-permute-start.20 = (bf16[4,4,192,256]{3,2,1,0:T(8,128)(2,1)}, bf16[4,4,192,256]{3,2,1,0:T(8,128)(2,1)}, u32[]{:S(2)}, u32[]{:S(2)}) collective-permute-start(bf16[4,4,192,256]{3,2,1,0:T(8,128)(2,1)} %slice_bitcast_fusion.2), channel_id=1, source_target_pairs={{0,4},{4,0},{8,12},{12,8},{16,20},{20,16},{24,28},{28,24},{1,5},{5... | collective-permute-start | bytes 4718600 | tf_op jit(solution)/shard_map/ppermute | solution.py:699
  239.6 10.0 %collective-permute-start.33 = (bf16[240,384]{1,0:T(8,128)(2,1)S(1)}, bf16[240,384]{1,0:T(8,128)(2,1)S(1)}, u32[]{:S(2)}, u32[]{:S(2)}) collective-permute-start(bf16[240,384]{1,0:T(8,128)(2,1)S(1)} %get-tuple-element.123), channel_id=1, source_target_pairs={{0,3},{1,2},{2,1},{3,0},{4,7},{5,6},{6,5},{7,4},{8,11},{9,10},{10,... | collective-permute-start | bytes 552968 | tf_op jit(solution)/shard_map/ppermute | solution.py:695
  240.1 18.2 %collective-permute-start.32 = (bf16[240,384]{1,0:T(8,128)(2,1)S(1)}, bf16[240,384]{1,0:T(8,128)(2,1)S(1)}, u32[]{:S(2)}, u32[]{:S(2)}) collective-permute-start(bf16[240,384]{1,0:T(8,128)(2,1)S(1)} %get-tuple-element.124), channel_id=1, source_target_pairs={{0,2},{1,3},{2,0},{3,1},{4,6},{5,7},{6,4},{7,5},{8,10},{9,11},{10,... | collective-permute-start | bytes 552968 | tf_op jit(solution)/shard_map/ppermute | solution.py:695
  261.6 14.1 %collective-permute-start.21 = (bf16[4,192,256]{2,1,0:T(8,128)(2,1)S(1)}, bf16[4,192,256]{2,1,0:T(8,128)(2,1)S(1)}, u32[]{:S(2)}, u32[]{:S(2)}) collective-permute-start(bf16[4,192,256]{2,1,0:T(8,128)(2,1)S(1)} %get-tuple-element.119), channel_id=1, source_target_pairs={{0,8},{4,12},{8,0},{12,4},{16,24},{20,28},{24,16},{28,20},{1,9},{5... | collective-permute-start | bytes 1179656 | tf_op jit(solution)/shard_map/ppermute | solution.py:699
  263.0 23.3 %collective-permute-start.23 = (bf16[4,192,256]{2,1,0:T(8,128)(2,1)S(1)}, bf16[4,192,256]{2,1,0:T(8,128)(2,1)S(1)}, u32[]{:S(2)}, u32[]{:S(2)}) collective-permute-start(bf16[4,192,256]{2,1,0:T(8,128)(2,1)S(1)} %get-tuple-element.120), channel_id=1, source_target_pairs={{0,24},{4,28},{8,16},{12,20},{16,8},{20,12},{24,0},{28,4},{1,25},{... | collective-permute-start | bytes 1179656 | tf_op jit(solution)/shard_map/ppermute | solution.py:699
  264.2 22.9 %collective-permute-start.22 = (bf16[4,192,256]{2,1,0:T(8,128)(2,1)S(1)}, bf16[4,192,256]{2,1,0:T(8,128)(2,1)S(1)}, u32[]{:S(2)}, u32[]{:S(2)}) collective-permute-start(bf16[4,192,256]{2,1,0:T(8,128)(2,1)S(1)} %get-tuple-element.121), channel_id=1, source_target_pairs={{0,16},{4,20},{8,24},{12,28},{16,0},{20,4},{24,8},{28,12},{1,17},{... | collective-permute-start | bytes 1179656 | tf_op jit(solution)/shard_map/ppermute | solution.py:699
  (25 other events, 466.2 us)
Sparse Core Ops, SparseCore 0:
  259.2 30.7 all-gather.3

commit v3 on v2

--- a/solution.py
+++ b/solution.py
@@ -96,6 +96,19 @@
 
 def slot_of(where, core, chip):
     return 2 * ((where >> 1) ^ chip) + ((where & 1) ^ core)
+
+
+def store_relative(keep, send, place, slot, shard, rows, lanes, values):
+    where = slot ^ place[0]
+    chip, far_off = where >> 1, shard ^ place[1]
+
+    @pl.when((where & 1) == 0)
+    def _():
+        keep[chip, far_off, rows, lanes] = values
+
+    @pl.when((where & 1) == 1)
+    def _():
+        send[chip, far_off, rows, lanes] = values
 
 
 def mixer_forward(
@@ -241,7 +254,7 @@
 
 def ffn_both(
     place, llen, slen, xm, ctx, vec, cl, cs, p0, p1, p2, p3, p4, p5, p6, p7,
-    ol, os, ga, gone, gctx, gvec,
+    ol, os, keep, send, gone, gctx, gvec,
     wo, wi, wu, res, xhat, grouped, gffn, active, slope, ffn, rstd, acc, ghid, gproj, sems,
 ):
     def fetch(part):
@@ -265,6 +278,10 @@
 
     for part in range(3):
         fetch(part)
+
+    def put(slot, shard, rows, values):
+        store_relative(keep, send, place, slot, shard, rows, slice(None), values)
+
     gain_one, bias_one = vec[16:17, :], vec[17:18, :]
     gain_two, bias_two = vec[18:19, :], vec[19:20, :]
     gvec[...] = jnp.zeros((8, D), F32)
@@ -358,10 +375,10 @@
         loop(12, act)
         part = tn(active[b], gffn[g]).astype(BF)
         for w in range(4):
-            ga[(4 * g + w) ^ place[0], n ^ place[1], 96:192, :] = part[96 * w : 96 * w + 96, :]
+            put(4 * g + w, n, slice(96, 192), part[96 * w : 96 * w + 96, :])
         part = tn(grouped[g], ghid[...]).astype(BF)
         for m in range(4):
-            ga[b ^ place[0], m ^ place[1], 0:96, :] = part[96 * m : 96 * m + 96, :]
+            put(b, m, slice(0, 96), part[96 * m : 96 * m + 96, :])
         ffn[g] += nt(ghid[...], wi[b])
 
     loop(8, contract)
@@ -387,7 +404,7 @@
         for n in range(4):
             for r in range(4):
                 row = 192 * n + 48 * r
-                ga[(4 * c + r) ^ place[0], n ^ place[1], 192:240, :] = part[row : row + 48, :]
+                put(4 * c + r, n, slice(192, 240), part[row : row + 48, :])
 
     def unmix(i):
         rows = at(i, 256)
@@ -399,8 +416,8 @@
 
 def mixer_backward(
     place, llen, slen, xm, packed, plong, pshort, dw, kc, cq, kp, cv, vec, gone, gctx, gvec, wm,
-    il, is_, gb,
-    xpad, gcp, gdp, grads, gqc, dkv, gkc, glog, gdep, spread, gather, wk,
+    keep, send, grads, rest,
+    xpad, gcp, gdp, gqc, dkv, gkc, glog, gdep, spread, gather, wk,
 ):
     zero_gaps(xpad)
     zero_gaps(gcp)
@@ -464,7 +481,7 @@
                 total = total + vec[j : j + 1, lanes] * grad_wide[12 - j : 140 - j, :]
                 part = tokens[4 + j : 132 + j, :] * grad
                 gdep[8 * j : 8 * j + 8, lanes] += jnp.sum(part.reshape(16, 8, 256), axis=0)
-            gone[at(i, 128), lanes] = total
+            rest[at(i, 128), lanes] = total
 
     loop(6, depth)
 
@@ -527,7 +544,8 @@
 
     def spill(b, values, lanes):
         for n in range(4):
-            gb[b ^ place[0], n ^ place[1], :, lanes] = values[192 * n : 192 * n + 192, :]
+            part = values[192 * n : 192 * n + 192, :]
+            store_relative(keep, send, place, b, n, slice(None), lanes, part)
 
     def weights(b):
         spill(b, tn(xm[...], grads[:, at(b, 256)]).astype(BF), slice(0, 256))
@@ -548,9 +566,11 @@
         parts.append(misc[row + 96 : row + 192, :])
     spill(7, jnp.concatenate(parts, axis=0).astype(BF), slice(128, 256))
 
+
+def input_gradient(llen, slen, grads, rest, wm, il, is_):
     def inputs(i):
         rows = at(i, 256)
-        total = gone[rows, :]
+        total = rest[rows, :]
         for b in range(6):
             total = total + nt(grads[rows, 256 * b : 256 * b + 256], wm[b])
         return total
@@ -598,7 +618,7 @@
                 )
                 left = tn(table.astype(BF), eye(128, BF))
                 row, col = iota((54, 128), 0), iota((54, 128), 1)
-                right = nn(kernel[...], jnp.where(col == row + 64, 1.0, 0.0).astype(BF))
+                right = tn(kernel[...], jnp.where(col == row + 64, 1.0, 0.0).astype(BF))
                 mixer[0:96, 128:256] = (left[0:96, :] + right).astype(BF)
                 mixer[96:192, 128:256] = left[96:192, :].astype(BF)
 
@@ -624,8 +644,7 @@
     depth[...] = table[0:TAPS, :]
     for k, ref in enumerate((g1, b1, g2, b2)):
         ref[...] = table[16 + k : 17 + k, :].reshape(192)
-    row, col = iota((128, 54), 0), iota((128, 54), 1)
-    kernel[...] = nn(misc[0:96, :], jnp.where(row == col + 64, 1.0, 0.0).astype(BF))
+    kernel[...] = table[64:118, 0:96]
 
 
 SMEM = pl.BlockSpec(memory_space=pltpu.SMEM)
@@ -662,7 +681,7 @@
 
 def feed_forward(scalars, xm, ctx, vec, cl, cs, pieces):
     outs = [
-        ((LONG, D), BF), ((2 * SHORT, D), BF), ((SLOTS, 4, 240, AH), BF),
+        ((LONG, D), BF), ((2 * SHORT, D), BF), ((4, 4, 240, AH), BF), ((4, 4, 240, AH), BF),
         ((ROWS, D), F32), ((ROWS, D), BF), ((8, D), F32),
     ]
     scratch = [
@@ -679,9 +698,11 @@
 
 
 def backward_mixer(scalars, *args):
-    outs = [((LONG, D), BF), ((2 * SHORT, D), BF), ((SLOTS, 4, 192, 256), BF)]
+    outs = [
+        ((4, 4, 192, 256), BF), ((4, 4, 192, 256), BF), ((ROWS, 4 * AH), BF), ((ROWS, D), F32),
+    ]
     scratch = [
-        ((PAD, D), F32), ((PAD, AH), F32), ((PAD, D), F32), ((ROWS, 4 * AH), BF),
+        ((PAD, D), F32), ((PAD, AH), F32), ((PAD, D), F32),
         ((ROWS, AH), F32), ((2, ROWS, AH), F32), ((ROWS, AH), BF), ((ROWS, 128), BF),
         ((8 * TAPS, D), F32), ((256, AH), BF), ((AH, 128), BF), ((AH, 128), BF),
     ]
@@ -691,6 +712,13 @@
     )
 
 
+def backward_inputs(scalars, grads, rest, wm):
+    return call(
+        input_gradient, [SMEM] * 2 + [VMEM] * 3, [((LONG, D), BF), ((2 * SHORT, D), BF)],
+        ([],), 5 * 10**9, *scalars[1:], grads, rest, wm,
+    )
+
+
 def far(values, bit):
     return lax.ppermute(values, "narrow", [(i, i ^ bit) for i in range(4)])
 
@@ -718,18 +746,20 @@
     return result.astype(BF)
 
 
-def reduce_cores(parts):
-    parts = parts.reshape((4, 2) + parts.shape[1:])
-    return total(parts[:, 0], [near(parts[:, 1], 1)])
-
-
-def reduce_chips(parts):
-    return total(parts[0], [near(parts[k], 2 * k) for k in (1, 2, 3)])
-
-
-def reduce_narrow(parts):
-    parts = total(parts[0], [far(parts[k], k) for k in (1, 2, 3)])
-    return lax.psum(parts, "hi")
+def reduce_cores(keep, sent):
+    return [total(keep[k], [sent[k]]) for k in range(4)]
+
+
+def send_chips(parts):
+    return [near(parts[k], 2 * k) for k in (1, 2, 3)]
+
+
+def reduce_chips(first, others):
+    return [total(first[k], [other[k] for other in others]) for k in range(4)]
+
+
+def send_narrow(parts):
+    return [far(parts[k], k) for k in (1, 2, 3)]
 
 
 def gather_wide(parts):
@@ -747,7 +777,7 @@
     cl, cs = long_cotangent.reshape(LONG, D), short_cotangent.reshape(2 * SHORT, D)
     mixer, ffn = call(
         pack, [SMEM] + [VMEM] * 12, [((192, 256), BF), ((240, AH), BF)], ([],), 10**9,
-        place, w_qkv, w_depth, w_point, w_kernel, w_convout, norm1_gain, norm1_bias,
+        place, w_qkv, w_depth, w_point, w_kernel.T, w_convout, norm1_gain, norm1_bias,
         w_inner, w_outer, w_out, norm2_gain, norm2_bias,
     )
     mixer = gather_narrow(mixer)
@@ -760,20 +790,33 @@
     xm, packed, plong, pshort, dw, kc, cq, kp, cv, ctx, vec, wm = forward_mixer(
         scalars, xl, xs, mixer
     )
+    ctx, ffn = lax.optimization_barrier((ctx, ffn))
     ffn = gather_cores(ffn)
-    ol, os, ga, gone, gctx, gvec = feed_forward(scalars, xm, ctx, vec, cl, cs, ffn)
-    ga = reduce_cores(ga)
-    il, is_, gb = backward_mixer(
+    ol, os, keep, send, gone, gctx, gvec = feed_forward(scalars, xm, ctx, vec, cl, cs, ffn)
+    ga = reduce_cores(keep, near(send, 1))
+    ga_sent = send_chips(ga)
+    gone, ga = lax.optimization_barrier((gone, ga))
+    keep, send, grads, rest = backward_mixer(
         scalars, xm, packed, plong, pshort, dw, kc, cq, kp, cv, vec, gone, gctx, gvec, wm
     )
-    ga = reduce_narrow(reduce_chips(ga))
-    gb = reduce_narrow(reduce_chips(reduce_cores(gb)))
+    keep, send, ga_sent = lax.optimization_barrier((keep, send, ga_sent))
+    sent = near(send, 1)
+    ga = reduce_chips(ga[0], ga_sent)
+    ga_sent = send_narrow(ga)
+    gb = reduce_cores(keep, sent)
+    gb_sent = send_chips(gb)
+    rest, gb = lax.optimization_barrier((rest, gb))
+    il, is_ = backward_inputs(scalars, grads, rest, wm)
+    ga_sent, gb_sent, il = lax.optimization_barrier((ga_sent, gb_sent, il))
+    ga = lax.psum(total(ga[0], ga_sent), "hi")
+    gb = reduce_chips(gb[0], gb_sent)
+    gb = lax.psum(total(gb[0], send_narrow(gb)), "hi")
     inner, outer, out = call(
         unpack_ffn, [VMEM], [((2, 96, 4 * AH), F32), ((2, AH, AH), F32), ((192, D), F32)],
         ([],), 10**9, gather_wide(ga),
     )
     outs = [
-        ((192, 3 * AH), F32), ((TAPS, 192), F32), ((192, AH), F32), ((96, 54), F32), ((192, AH), F32),
+        ((192, 3 * AH), F32), ((TAPS, 192), F32), ((192, AH), F32), ((54, 96), F32), ((192, AH), F32),
     ] + [((192,), F32)] * 4
     qkv, depth, point, kernel, convout, g1, b1, g2, b2 = call(
         unpack_mixer, [VMEM], outs, ([],), 10**9, gather_wide(gb)
@@ -781,7 +824,7 @@
     return (
         ol.reshape(long_tokens.shape), os.reshape(short_tokens.shape),
         il.reshape(long_tokens.shape), is_.reshape(short_tokens.shape),
-        qkv, depth, point, kernel, convout, out, g1, b1, inner, outer, g2, b2,
+        qkv, depth, point, kernel.T, convout, out, g1, b1, inner, outer, g2, b2,
     )
 
 

time: 322 us -> 281 us (0.87)
  waiting for transfers between devices: 94.1 us -> 43.5 us
  Pallas kernels: 142 us -> 154 us
  local copies, waits for them, and re-layouts: 12.7 us -> 2.07 us
  other arithmetic: 8.51 us -> 12.8 us
    ppermute x22, waiting for transfers between devices: 57 us -> 17.2 us  [near(): return lax.ppermute(values, 'wide', [(i, i ^ bit) for i in range(SLOTS)])]
    pallas_call x6 -> x7, Pallas kernels: 142 us -> 154 us  [call(): pl.pallas_call(kernel, out_shape=[jax.ShapeDtypeStruct(s, d) for s, d in...]
    ppermute x12, waiting for transfers between devices: 37 us -> 26.3 us  [far(): return lax.ppermute(values, 'narrow', [(i, i ^ bit) for i in range(4)])]
    squeeze x6 -> x0, local copies, waits for them, and re-layouts: 6.63 us -> none  [the longest x2 5.02 us: reduce_cores(): return total(parts[:, 0], [near(parts[:, 1], 1)])]
    unnamed x30 -> x34, local copies, waits for them, and re-layouts: 6.08 us -> 2.07 us
    convert_element_type x6 -> x4, other arithmetic: 5.94 us -> 7.87 us  [total(): return result.astype(BF)]
  transfers between devices with their start and end apart: 35 -> 35, of which waited for: 18 -> 17; matrix products, arithmetic and copies ran while one was open for 3% -> 2% of each run, Pallas kernels for 24% -> 30%
where the time goes in v3:
time: 281 us; the launch traced here: 280 us
  Pallas kernels  154 us (55%)
  waiting for transfers between devices  43.5 us (15%)
  starting transfers between devices  40.6 us (14%)
  between operations  14.9 us (5%)
  other arithmetic  12.8 us (5%)
  blocking collectives  12.4 us (4%)
    pallas_call x7, Pallas kernels, call(): pl.pallas_call(kernel, out_shape=[jax.ShapeDtypeStruct(s, d) for s, d in...  154 us
    ppermute x12, waiting for transfers between devices, far(): return lax.ppermute(values, 'narrow', [(i, i ^ bit) for i in range(4)])  26.3 us
    ppermute x12, starting transfers between devices, far(): return lax.ppermute(values, 'narrow', [(i, i ^ bit) for i in range(4)])  23.1 us
    ppermute x22, starting transfers between devices, near(): return lax.ppermute(values, 'wide', [(i, i ^ bit) for i in range(SLOTS)])  17.5 us
    ppermute x22, waiting for transfers between devices, near(): return lax.ppermute(values, 'wide', [(i, i ^ bit) for i in range(SLOTS)])  17.2 us
    all_gather x1, blocking collectives, gather_wide(): return lax.all_gather(parts, 'wide', axis=0, tiled=False)  12.4 us
    convert_element_type x4, other arithmetic, total(): return result.astype(BF)  7.87 us
  transfers between devices with their start and end apart: 35, of which 17 were waited for; matrix products, arithmetic and copies ran while one was open for 2% of the time, Pallas kernels for 30%

profile of v3, /device:TPU:0, one launch (start us, length us, event | category | flops | bytes accessed | tf_op | source)
XLA Modules:
  0.0 280.1 jit_solution(4402691028178475080)
XLA Ops:
  7.8 2.4 pack.1
  10.2 5.0 %collective-permute-start.2 = (bf16[192,256]{1,0:T(8,128)(2,1)}, bf16[192,256]{1,0:T(8,128)(2,1)S(1)}, u32[]{:S(2)}, u32[]{:S(2)}) collective-permute-start(bf16[192,256]{1,0:T(8,128)(2,1)} %get-tuple-element.83), channel_id=1, source_target_pairs={{0,3},{1,2},{2,1},{3,0},{4,7},{5,6},{6,5},{7,4},{8,11},{9,10},{10,... | collective-permute-start | bytes 294920 | tf_op jit(solution)/shard_map/ppermute | solution.py:723
  15.9 3.3 %collective-permute-done.2 = bf16[192,256]{1,0:T(8,128)(2,1)S(1)} collective-permute-done((bf16[192,256]{1,0:T(8,128)(2,1)}, bf16[192,256]{1,0:T(8,128)(2,1)S(1)}, u32[]{:S(2)}, u32[]{:S(2)}) %collective-permute-start.2) | collective-permute-done | bytes 98336 | tf_op jit(solution)/shard_map/ppermute | solution.py:723
  19.2 4.6 %collective-permute-done.1 = bf16[192,256]{1,0:T(8,128)(2,1)S(1)} collective-permute-done((bf16[192,256]{1,0:T(8,128)(2,1)}, bf16[192,256]{1,0:T(8,128)(2,1)S(1)}, u32[]{:S(2)}, u32[]{:S(2)}) %collective-permute-start.1) | collective-permute-done | bytes 98336 | tf_op jit(solution)/shard_map/ppermute | solution.py:723
  24.7 2.6 collective-permute-start.8
  27.3 2.6 collective-permute-start.5
  30.8 3.1 %collective-permute-done.8 = bf16[240,384]{1,0:T(8,128)(2,1)S(1)} collective-permute-done((bf16[240,384]{1,0:T(8,128)(2,1)}, bf16[240,384]{1,0:T(8,128)(2,1)S(1)}, u32[]{:S(2)}, u32[]{:S(2)}) %collective-permute-start.8) | collective-permute-done | bytes 184352 | tf_op jit(solution)/shard_map/ppermute | solution.py:723
  33.9 6.9 %collective-permute-start.6 = (bf16[240,384]{1,0:T(8,128)(2,1)}, bf16[240,384]{1,0:T(8,128)(2,1)S(1)}, u32[]{:S(2)}, u32[]{:S(2)}) collective-permute-start(bf16[240,384]{1,0:T(8,128)(2,1)} %get-tuple-element.86), channel_id=1, source_target_pairs={{0,1},{1,0},{2,3},{3,2},{4,5},{5,4},{6,7},{7,6},{8,9},{9,8},{10,11... | collective-permute-start | bytes 552968 | tf_op jit(solution)/shard_map/ppermute | solution.py:723
  42.3 2.2 collective-permute-done.6
  48.2 2.1 collective-permute-start.15
  53.0 32.8 %mixer_forward.1 = (bf16[768,768]{1,0:T(8,128)(2,1)}, bf16[768,1152]{1,0:T(8,128)(2,1)}, bf16[6,512,512]{2,1,0:T(8,128)(2,1)}, bf16[2,6,128,128]{3,2,1,0:T(8,128...) custom-call(s32[2]{0:T(128)} %pad_add_fusion.place, ...), custom_call_target="tpu_custom_call" | custom-call | flops 30000001024 | bytes 1048576 | tf_op jit(solution)/shard_map/mixer_forward/pallas_call | solution.py:656
  92.2 63.9 %ffn_both.1 = (bf16[512,768]{1,0:T(8,128)(2,1)}, bf16[256,768]{1,0:T(8,128)(2,1)}, bf16[4,4,240,384]{3,2,1,0:T(8,128)(2,1)}, bf16[4,4,240,384]{3,2,1,0:T(8,128)(...) custom-call(s32[2]{0:T(128)} %pad_add_fusion.place, s32[1]{0:T(128)S(6)} %copy.34.llen, ...), custom_call_target="tpu_custom_call" | custom-call | flops 60000002048 | bytes 1048576 | tf_op jit(solution)/shard_map/ffn_both/pallas_call | solution.py:656
  156.4 5.4 %collective-permute-done.20 = bf16[4,4,240,384]{3,2,1,0:T(8,128)(2,1)S(1)} collective-permute-done((bf16[4,4,240,384]{3,2,1,0:T(8,128)(2,1)}, bf16[4,4,240,384]{3,2,1,0:T(8,128)(2,1)S(1)}, u32[]{:S(2)}, u32[]{:S(2)}) %collective-permute-start.20) | collective-permute-done | bytes 2949152 | tf_op jit(solution)/shard_map/ppermute | solution.py:727
  161.8 3.6 %fusion.3 = (bf16[4,240,384]{2,1,0:T(8,128)(2,1)}, bf16[4,240,384]{2,1,0:T(8,128)(2,1)}, bf16[4,240,384]{2,1,0:T(8,128)(2,1)S(1)}, bf16[4,240,384]{2,1,0:T(8,128)(2,1)S(1)}) fusion(bf16[4,4,240,384]{3,2,1,0:T(8,128)(2,1)S(1)} %collective-permute-done.20, bf16[4,4,240,384]{3,2,1,0:T(8,128)(2,1)} %get-tuple-element.103), kind=kLoop, calls=%fused_computation.11 | loop fusion | flops 5898240 | bytes 8847360 | tf_op jit(solution)/shard_map/convert_element_type | solution.py:746
  168.9 42.8 %mixer_backward.1 = (bf16[4,4,192,256]{3,2,1,0:T(8,128)(2,1)}, bf16[4,4,192,256]{3,2,1,0:T(8,128)(2,1)}, bf16[768,1536]{1,0:T(8,128)(2,1)}, f32[768,768]{1,0:T(8,128)}) custom-call(s32[2]{0:T(128)} %pad_add_fusion.place, s32[1]{0:T(128)S(6)} %copy.34.llen, s32[2]{0:T(128)} %slen.7, bf16[768,768]{1,0:T(8,128)(2,1)} %get-tuple-element.91.xm, ...), custom_call_target="tpu_custom_call" | custom-call | flops 40000000000 | bytes 1048576 | tf_op jit(solution)/shard_map/mixer_backward/pallas_call | solution.py:656
  215.2 2.0 collective-permute-start.24
  223.6 6.5 %input_gradient.1 = (bf16[512,768]{1,0:T(8,128)(2,1)}, bf16[256,768]{1,0:T(8,128)(2,1)}) custom-call(s32[1]{0:T(128)S(6)} %copy.34.llen, s32[2]{0:T(128)} %slen.7, bf16[768,1536]{1,0:T(8,128)(2,1)} %get-tuple-element.125.grads, f32[768,768]{1,0:T(8,128)} %get-tuple-element.127.rest, bf16[8,768,256]{2,1,0:T(8,128)(2,1)} %get-tuple-element.117.wm), custom_call_target="tpu_custom_call" | custom-call | flops 5000000000 | bytes 1048576 | tf_op jit(solution)/shard_map/input_gradient/pallas_call | solution.py:656
  230.1 2.0 collective-permute-done.25
  232.2 6.5 %collective-permute-done.29 = bf16[4,192,256]{2,1,0:T(8,128)(2,1)} collective-permute-done((bf16[4,192,256]{2,1,0:T(8,128)(2,1)S(1)}, bf16[4,192,256]{2,1,0:T(8,128)(2,1)}, u32[]{:S(2)}, u32[]{:S(2)}) %collective-permute-start.29) | collective-permute-done | bytes 393248 | tf_op jit(solution)/shard_map/ppermute | solution.py:727
  247.1 3.1 %collective-permute-done.33 = bf16[192,256]{1,0:T(8,128)(2,1)S(1)} collective-permute-done((bf16[192,256]{1,0:T(8,128)(2,1)S(1)}, bf16[192,256]{1,0:T(8,128)(2,1)S(1)}, u32[]{:S(2)}, u32[]{:S(2)}) %collective-permute-start.33) | collective-permute-done | bytes 98336 | tf_op jit(solution)/shard_map/ppermute | solution.py:723
  250.2 4.1 %collective-permute-done.32 = bf16[192,256]{1,0:T(8,128)(2,1)S(1)} collective-permute-done((bf16[192,256]{1,0:T(8,128)(2,1)S(1)}, bf16[192,256]{1,0:T(8,128)(2,1)S(1)}, u32[]{:S(2)}, u32[]{:S(2)}) %collective-permute-start.32) | collective-permute-done | bytes 98336 | tf_op jit(solution)/shard_map/ppermute | solution.py:723
  255.4 12.4 %all-gather = bf16[1536,256]{1,0:T(8,128)(2,1)} all-gather(bf16[192,256]{1,0:T(8,128)(2,1)S(1)} %fusion.13), channel_id=2, replica_groups=mesh['wide'=8,'narrow'=4] {'wide'}, dimensions={0}, use_global_device_ids=true | all-gather | bytes 884736 | tf_op jit(solution)/shard_map/all_gather | solution.py:766
  267.8 2.4 unpack_mixer.1
  270.2 3.0 %unpack_ffn.1 = (f32[2,96,1536]{2,1,0:T(8,128)}, f32[2,384,384]{2,1,0:T(8,128)}, f32[192,768]{1,0:T(8,128)}) custom-call(bf16[8,240,384]{2,1,0:T(8,128)(2,1)} %bitcast.69), custom_call_target="tpu_custom_call" | custom-call | flops 1000000000 | bytes 1048576 | tf_op jit(solution)/shard_map/unpack_ffn/pallas_call | solution.py:656
  (98 shorter events, 39.8 us)
Async XLA Ops:
  7.2 263.0 %all-gather.4.cloned.1.call-start = ((), (), s32[]{:S(2)}) async-start(), calls=%async_computation | async-start | bytes 1658880 | tf_op jit(solution)/shard_map/all_gather | solution.py:766
  10.2 9.0 %collective-permute-start.2 = (bf16[192,256]{1,0:T(8,128)(2,1)}, bf16[192,256]{1,0:T(8,128)(2,1)S(1)}, u32[]{:S(2)}, u32[]{:S(2)}) collective-permute-start(bf16[192,256]{1,0:T(8,128)(2,1)} %get-tuple-element.83), channel_id=1, source_target_pairs={{0,3},{1,2},{2,1},{3,0},{4,7},{5,6},{6,5},{7,4},{8,11},{9,10},{10,... | collective-permute-start | bytes 294920 | tf_op jit(solution)/shard_map/ppermute | solution.py:723
  15.3 8.5 %collective-permute-start.1 = (bf16[192,256]{1,0:T(8,128)(2,1)}, bf16[192,256]{1,0:T(8,128)(2,1)S(1)}, u32[]{:S(2)}, u32[]{:S(2)}) collective-permute-start(bf16[192,256]{1,0:T(8,128)(2,1)} %get-tuple-element.83), channel_id=1, source_target_pairs={{0,2},{1,3},{2,0},{3,1},{4,6},{5,7},{6,4},{7,5},{8,10},{9,11},{10,... | collective-permute-start | bytes 294920 | tf_op jit(solution)/shard_map/ppermute | solution.py:723
  15.3 8.5 %collective-permute-start = (bf16[192,256]{1,0:T(8,128)(2,1)}, bf16[192,256]{1,0:T(8,128)(2,1)S(1)}, u32[]{:S(2)}, u32[]{:S(2)}) collective-permute-start(bf16[192,256]{1,0:T(8,128)(2,1)} %get-tuple-element.83), channel_id=1, source_target_pairs={{0,1},{1,0},{2,3},{3,2},{4,5},{5,4},{6,7},{7,6},{8,9},{9,8},{10,11... | collective-permute-start | bytes 294920 | tf_op jit(solution)/shard_map/ppermute | solution.py:723
  24.7 9.2 %collective-permute-start.8 = (bf16[240,384]{1,0:T(8,128)(2,1)}, bf16[240,384]{1,0:T(8,128)(2,1)S(1)}, u32[]{:S(2)}, u32[]{:S(2)}) collective-permute-start(bf16[240,384]{1,0:T(8,128)(2,1)} %get-tuple-element.86), channel_id=1, source_target_pairs={{0,3},{1,2},{2,1},{3,0},{4,7},{5,6},{6,5},{7,4},{8,11},{9,10},{10,... | collective-permute-start | bytes 552968 | tf_op jit(solution)/shard_map/ppermute | solution.py:723
  27.3 18.3 %collective-permute-start.5 = (bf16[4,192,256]{2,1,0:T(8,128)(2,1)S(1)}, bf16[4,192,256]{2,1,0:T(8,128)(2,1)S(1)}, u32[]{:S(2)}, u32[]{:S(2)}) collective-permute-start(bf16[4,192,256]{2,1,0:T(8,128)(2,1)S(1)} %pad_maximum_fusion.1.p0), channel_id=1, source_target_pairs={{0,24},{4,28},{8,16},{12,20},{16,8},{20,12},{24,0},{28,4},{1,25},{... | collective-permute-start | bytes 1179656 | tf_op jit(solution)/shard_map/ppermute | solution.py:727
  29.9 16.6 %collective-permute-start.4 = (bf16[4,192,256]{2,1,0:T(8,128)(2,1)S(1)}, bf16[4,192,256]{2,1,0:T(8,128)(2,1)S(1)}, u32[]{:S(2)}, u32[]{:S(2)}) collective-permute-start(bf16[4,192,256]{2,1,0:T(8,128)(2,1)S(1)} %pad_maximum_fusion.1.p0), channel_id=1, source_target_pairs={{0,16},{4,20},{8,24},{12,28},{16,0},{20,4},{24,8},{28,12},{1,17},{... | collective-permute-start | bytes 1179656 | tf_op jit(solution)/shard_map/ppermute | solution.py:727
  30.2 16.3 %collective-permute-start.3 = (bf16[4,192,256]{2,1,0:T(8,128)(2,1)S(1)}, bf16[4,192,256]{2,1,0:T(8,128)(2,1)S(1)}, u32[]{:S(2)}, u32[]{:S(2)}) collective-permute-start(bf16[4,192,256]{2,1,0:T(8,128)(2,1)S(1)} %pad_maximum_fusion.1.p0), channel_id=1, source_target_pairs={{0,8},{4,12},{8,0},{12,4},{16,24},{20,28},{24,16},{28,20},{1,9},{5... | collective-permute-start | bytes 1179656 | tf_op jit(solution)/shard_map/ppermute | solution.py:727
  30.8 11.6 %collective-permute-start.7 = (bf16[240,384]{1,0:T(8,128)(2,1)}, bf16[240,384]{1,0:T(8,128)(2,1)S(1)}, u32[]{:S(2)}, u32[]{:S(2)}) collective-permute-start(bf16[240,384]{1,0:T(8,128)(2,1)} %get-tuple-element.86), channel_id=1, source_target_pairs={{0,2},{1,3},{2,0},{3,1},{4,6},{5,7},{6,4},{7,5},{8,10},{9,11},{10,... | collective-permute-start | bytes 552968 | tf_op jit(solution)/shard_map/ppermute | solution.py:723
  33.9 10.6 %collective-permute-start.6 = (bf16[240,384]{1,0:T(8,128)(2,1)}, bf16[240,384]{1,0:T(8,128)(2,1)S(1)}, u32[]{:S(2)}, u32[]{:S(2)}) collective-permute-start(bf16[240,384]{1,0:T(8,128)(2,1)} %get-tuple-element.86), channel_id=1, source_target_pairs={{0,1},{1,0},{2,3},{3,2},{4,5},{5,4},{6,7},{7,6},{8,9},{9,8},{10,11... | collective-permute-start | bytes 552968 | tf_op jit(solution)/shard_map/ppermute | solution.py:723
  48.2 37.6 %collective-permute-start.15 = (bf16[4,240,384]{2,1,0:T(8,128)(2,1)S(1)}, bf16[4,240,384]{2,1,0:T(8,128)(2,1)S(1)}, u32[]{:S(2)}, u32[]{:S(2)}) collective-permute-start(bf16[4,240,384]{2,1,0:T(8,128)(2,1)S(1)} %pad_maximum_fusion.p0), channel_id=1, source_target_pairs={{0,24},{4,28},{8,16},{12,20},{16,8},{20,12},{24,0},{28,4},{1,25},{... | collective-permute-start | bytes 2211848 | tf_op jit(solution)/shard_map/ppermute | solution.py:727
  50.3 35.5 %collective-permute-start.14 = (bf16[4,240,384]{2,1,0:T(8,128)(2,1)S(1)}, bf16[4,240,384]{2,1,0:T(8,128)(2,1)S(1)}, u32[]{:S(2)}, u32[]{:S(2)}) collective-permute-start(bf16[4,240,384]{2,1,0:T(8,128)(2,1)S(1)} %pad_maximum_fusion.p0), channel_id=1, source_target_pairs={{0,16},{4,20},{8,24},{12,28},{16,0},{20,4},{24,8},{28,12},{1,17},{... | collective-permute-start | bytes 2211848 | tf_op jit(solution)/shard_map/ppermute | solution.py:727
  51.5 34.4 %collective-permute-start.13 = (bf16[4,240,384]{2,1,0:T(8,128)(2,1)S(1)}, bf16[4,240,384]{2,1,0:T(8,128)(2,1)S(1)}, u32[]{:S(2)}, u32[]{:S(2)}) collective-permute-start(bf16[4,240,384]{2,1,0:T(8,128)(2,1)S(1)} %pad_maximum_fusion.p0), channel_id=1, source_target_pairs={{0,8},{4,12},{8,0},{12,4},{16,24},{20,28},{24,16},{28,20},{1,9},{5... | collective-permute-start | bytes 2211848 | tf_op jit(solution)/shard_map/ppermute | solution.py:727
  165.4 46.2 %collective-permute-start.23 = (bf16[4,240,384]{2,1,0:T(8,128)(2,1)}, bf16[4,240,384]{2,1,0:T(8,128)(2,1)S(1)}, u32[]{:S(2)}, u32[]{:S(2)}) collective-permute-start(bf16[4,240,384]{2,1,0:T(8,128)(2,1)} %get-tuple-element.150), channel_id=1, source_target_pairs={{0,24},{4,28},{8,16},{12,20},{16,8},{20,12},{24,0},{28,4},{1,25},{... | collective-permute-start | bytes 2211848 | tf_op jit(solution)/shard_map/ppermute | solution.py:727
  167.2 44.5 %collective-permute-start.22 = (bf16[4,240,384]{2,1,0:T(8,128)(2,1)}, bf16[4,240,384]{2,1,0:T(8,128)(2,1)S(1)}, u32[]{:S(2)}, u32[]{:S(2)}) collective-permute-start(bf16[4,240,384]{2,1,0:T(8,128)(2,1)} %get-tuple-element.151), channel_id=1, source_target_pairs={{0,16},{4,20},{8,24},{12,28},{16,0},{20,4},{24,8},{28,12},{1,17},{... | collective-permute-start | bytes 2211848 | tf_op jit(solution)/shard_map/ppermute | solution.py:727
  168.3 43.3 %collective-permute-start.21 = (bf16[4,240,384]{2,1,0:T(8,128)(2,1)S(1)}, bf16[4,240,384]{2,1,0:T(8,128)(2,1)S(1)}, u32[]{:S(2)}, u32[]{:S(2)}) collective-permute-start(bf16[4,240,384]{2,1,0:T(8,128)(2,1)S(1)} %get-tuple-element.152), channel_id=1, source_target_pairs={{0,8},{4,12},{8,0},{12,4},{16,24},{20,28},{24,16},{28,20},{1,9},{5... | collective-permute-start | bytes 2211848 | tf_op jit(solution)/shard_map/ppermute | solution.py:727
  212.8 9.4 %collective-permute-start.26 = (bf16[240,384]{1,0:T(8,128)(2,1)S(1)}, bf16[240,384]{1,0:T(8,128)(2,1)S(1)}, u32[]{:S(2)}, u32[]{:S(2)}) collective-permute-start(bf16[240,384]{1,0:T(8,128)(2,1)S(1)} %get-tuple-element.158), channel_id=1, source_target_pairs={{0,3},{1,2},{2,1},{3,0},{4,7},{5,6},{6,5},{7,4},{8,11},{9,10},{10,... | collective-permute-start | bytes 552968 | tf_op jit(solution)/shard_map/ppermute | solution.py:723
  214.1 18.0 %collective-permute-start.25 = (bf16[240,384]{1,0:T(8,128)(2,1)}, bf16[240,384]{1,0:T(8,128)(2,1)}, u32[]{:S(2)}, u32[]{:S(2)}) collective-permute-start(bf16[240,384]{1,0:T(8,128)(2,1)} %get-tuple-element.159), channel_id=1, source_target_pairs={{0,2},{1,3},{2,0},{3,1},{4,6},{5,7},{6,4},{7,5},{8,10},{9,11},{10,... | collective-permute-start | bytes 552968 | tf_op jit(solution)/shard_map/ppermute | solution.py:723
  215.2 17.0 %collective-permute-start.24 = (bf16[240,384]{1,0:T(8,128)(2,1)}, bf16[240,384]{1,0:T(8,128)(2,1)}, u32[]{:S(2)}, u32[]{:S(2)}) collective-permute-start(bf16[240,384]{1,0:T(8,128)(2,1)} %get-tuple-element.160), channel_id=1, source_target_pairs={{0,1},{1,0},{2,3},{3,2},{4,5},{5,4},{6,7},{7,6},{8,9},{9,8},{10,11... | collective-permute-start | bytes 552968 | tf_op jit(solution)/shard_map/ppermute | solution.py:723
  218.4 13.8 %collective-permute-start.30 = (bf16[4,192,256]{2,1,0:T(8,128)(2,1)}, bf16[4,192,256]{2,1,0:T(8,128)(2,1)}, u32[]{:S(2)}, u32[]{:S(2)}) collective-permute-start(bf16[4,192,256]{2,1,0:T(8,128)(2,1)} %get-tuple-element.155), channel_id=1, source_target_pairs={{0,24},{4,28},{8,16},{12,20},{16,8},{20,12},{24,0},{28,4},{1,25},{... | collective-permute-start | bytes 1179656 | tf_op jit(solution)/shard_map/ppermute | solution.py:727
  220.2 18.5 %collective-permute-start.29 = (bf16[4,192,256]{2,1,0:T(8,128)(2,1)S(1)}, bf16[4,192,256]{2,1,0:T(8,128)(2,1)}, u32[]{:S(2)}, u32[]{:S(2)}) collective-permute-start(bf16[4,192,256]{2,1,0:T(8,128)(2,1)S(1)} %get-tuple-element.156), channel_id=1, source_target_pairs={{0,16},{4,20},{8,24},{12,28},{16,0},{20,4},{24,8},{28,12},{1,17},{... | collective-permute-start | bytes 1179656 | tf_op jit(solution)/shard_map/ppermute | solution.py:727
  222.2 16.5 %collective-permute-start.28 = (bf16[4,192,256]{2,1,0:T(8,128)(2,1)S(1)}, bf16[4,192,256]{2,1,0:T(8,128)(2,1)}, u32[]{:S(2)}, u32[]{:S(2)}) collective-permute-start(bf16[4,192,256]{2,1,0:T(8,128)(2,1)S(1)} %get-tuple-element.157), channel_id=1, source_target_pairs={{0,8},{4,12},{8,0},{12,4},{16,24},{20,28},{24,16},{28,20},{1,9},{5... | collective-permute-start | bytes 1179656 | tf_op jit(solution)/shard_map/ppermute | solution.py:727
  243.1 7.2 %collective-permute-start.33 = (bf16[192,256]{1,0:T(8,128)(2,1)S(1)}, bf16[192,256]{1,0:T(8,128)(2,1)S(1)}, u32[]{:S(2)}, u32[]{:S(2)}) collective-permute-start(bf16[192,256]{1,0:T(8,128)(2,1)S(1)} %get-tuple-element.162), channel_id=1, source_target_pairs={{0,3},{1,2},{2,1},{3,0},{4,7},{5,6},{6,5},{7,4},{8,11},{9,10},{10,... | collective-permute-start | bytes 294920 | tf_op jit(solution)/shard_map/ppermute | solution.py:723
  244.4 9.9 %collective-permute-start.32 = (bf16[192,256]{1,0:T(8,128)(2,1)S(1)}, bf16[192,256]{1,0:T(8,128)(2,1)S(1)}, u32[]{:S(2)}, u32[]{:S(2)}) collective-permute-start(bf16[192,256]{1,0:T(8,128)(2,1)S(1)} %get-tuple-element.163), channel_id=1, source_target_pairs={{0,2},{1,3},{2,0},{3,1},{4,6},{5,7},{6,4},{7,5},{8,10},{9,11},{10,... | collective-permute-start | bytes 294920 | tf_op jit(solution)/shard_map/ppermute | solution.py:723
  (28 other events, 172.6 us)
Sparse Core Ops, SparseCore 0:
  240.8 25.9 all-gather.3

commit v4 on v3

v4 whole, which is shorter than its diff:
```python
import jax
import jax.numpy as jnp
from jax import lax
from jax.experimental import pallas as pl
from jax.experimental.pallas import tpu as pltpu
from jax.sharding import Mesh
from jax.sharding import PartitionSpec as P

BF = jnp.bfloat16
F32 = jnp.float32
EPS = 1e-12
D = 768
AH = 384
HEADS = 6
TAPS = 9
LONG = 512
SHORT = 128
ROWS = 768
PAD = 800
SLOTS = 8
NEG = -1000000000.0
PSTART = tuple(8 + 128 * i + 8 * max(i - 3, 0) for i in range(6))
SEGS = ((0, 512, 8), (512, 128, 528), (640, 128, 664))


def nn(a, b):
    return lax.dot_general(a, b, (((1,), (0,)), ((), ())), preferred_element_type=F32)


def nt(a, b):
    return lax.dot_general(a, b, (((1,), (1,)), ((), ())), preferred_element_type=F32)


def tn(a, b):
    return lax.dot_general(a, b, (((0,), (0,)), ((), ())), preferred_element_type=F32)


def iota(shape, axis):
    return lax.broadcasted_iota(jnp.int32, shape, axis)


def loop(count, body):
    def step(i, carry):
        body(i)
        return carry

    lax.fori_loop(0, count, step, 0)


def at(i, size):
    if isinstance(i, int):
        return pl.ds(i * size, size)
    return pl.ds(pl.multiple_of(i * size, size), size)


def padded_start(i):
    return pl.multiple_of(8 + 128 * i + 8 * jnp.maximum(i - 3, 0), 8)


def zero_gaps(ref):
    for start in (0, 520, 656, 792):
        ref[start : start + 8, :] = jnp.zeros((8, ref.shape[1]), ref.dtype)


def eye(n, dtype):
    return jnp.where(iota((n, n), 0) == iota((n, n), 1), 1.0, 0.0).astype(dtype)


def tap_permutation():
    row, col = iota((128, 128), 0), iota((128, 128), 1)
    head, tap = col & 7, col >> 3
    keep = (head < HEADS) & (tap < TAPS) & (row == 64 + head * TAPS + tap)
    return jnp.where(keep, 1.0, 0.0).astype(BF)


def head_spread():
    row, col = iota((256, AH), 0), iota((256, AH), 1)
    return jnp.where((row & 127) == (col >> 6), 1.0, 0.0).astype(BF)


def head_gather():
    row, col = iota((AH, 128), 0), iota((AH, 128), 1)
    return jnp.where((row >> 6) == col, 1.0, 0.0).astype(BF)


def split_two(values):
    high = values.astype(BF)
    low = (values - high.astype(F32)).astype(BF)
    return jnp.concatenate([high, low], axis=1)


def spread_taps(probs):
    moved = [probs] + [pltpu.roll(probs, 128 - 8 * j, 1) for j in range(1, TAPS)]
    return split_two(jnp.concatenate(moved, axis=0))


def tap_kernel(wm):
    stored = jnp.concatenate([wm[7, 192 * n : 192 * n + 96, 128:256] for n in range(4)], axis=0)
    return nn(stored, tap_permutation()).astype(BF)


def slot_of(where, core, chip):
    return 2 * ((where >> 1) ^ chip) + ((where & 1) ^ core)


def fetch_mixer(place, pieces, wm, sem):
    for at_core in range(2):
        for chip in range(4):
            piece = pieces[4 * at_core + chip]
            slot = slot_of(place[0], at_core, chip)

            def fetch(k):
                pltpu.make_async_copy(piece.at[k], wm.at[slot, at(place[1] ^ k, 192), :], sem).start()

            loop(4, fetch)


def mixer_forward(
    place, llen, slen, xl, xs, p0, p1, p2, p3, p4, p5, p6, p7,
    xm_any, packed_any, plong_any, pshort_any, dw_any, kc_any, cq_any, kp_any, cv_any, ctx_any, vec,
    wm, xpad, spread, wk, xm, packed, plong, pshort, dw, kc, cq, kp, cv, ctx, sem, sems
):
    fetch_mixer(place, (p0, p1, p2, p3, p4, p5, p6, p7), wm, sem)
    lens = (llen[0], slen[0], slen[1])
    zero_gaps(xpad)
    zero_gaps(cv)
    zero_gaps(kp)
    for i in range(6):
        seg = max(i - 3, 0)
        base = 128 * i if i < 4 else 0
        tokens = xl[128 * i : 128 * i + 128, :] if i < 4 else xs[128 * (i - 4) : 128 * (i - 3), :]
        live = base + iota((128, D), 0) < lens[seg]
        values = jnp.where(live, tokens.astype(F32), 0.0)
        xpad[PSTART[i] : PSTART[i] + 128, :] = values
        xm[128 * i : 128 * i + 128, :] = values.astype(BF)
    stores = [start_copy(xm, xm_any, sems.at[0])]
    spread[...] = head_spread()
    pltpu.make_async_copy(wm, wm, sem).wait()
    vec[...] = nt(eye(128, BF), wm[7, :, 128:256])[0:24, :]
    wk[...] = tap_kernel(wm)

    def depth(i):
        ps = padded_start(i)
        for c in range(3):
            lanes = slice(256 * c, 256 * c + 256)
            window = xpad[pl.ds(pl.multiple_of(ps - 8, 8), 144), lanes]
            total = jnp.zeros((128, 256), F32)
            for j in range(TAPS):
                total = total + vec[j : j + 1, lanes] * window[4 + j : 132 + j, :]
            dw[at(i, 128), lanes] = total.astype(BF)

    def project(b):
        packed[:, at(b, 256)] = nn(xm[...], wm[b]).astype(BF)
        depth(b)

    loop(4, project)
    depth(jnp.int32(4))
    part = nn(xm[...], wm[4])
    packed[:, 1024:1152] = part[:, 0:128].astype(BF)
    for start, rows, pstart in SEGS:
        cv[pstart : pstart + rows, 0:128] = part[start : start + rows, 128:256]
    depth(jnp.int32(5))
    part = nn(xm[...], wm[5])
    for start, rows, pstart in SEGS:
        cv[pstart : pstart + rows, 128:384] = part[start : start + rows, :]
    stores += [
        start_copy(packed, packed_any, sems.at[1]), start_copy(dw, dw_any, sems.at[2]),
        start_copy(cv, cv_any, sems.at[3]),
    ]
    kc[:, 0:256] = nn(dw[...], wm[6])
    kc[:, 256:384] = nn(dw[...], wm[7, :, 0:128])
    stores.append(start_copy(kc, kc_any, sems.at[4]))

    def dynamic(i):
        rows = at(i, 128)
        ps = padded_start(i)
        query = (kc[rows, :] * packed[rows, 0:AH].astype(F32)).astype(BF)
        cq[rows, :] = query
        logits = nn(query, wk[...])
        real = iota((128, 128), 1) < 8 * TAPS
        top = jnp.where(real, logits, NEG * 1e20)
        for shift in (64, 32, 16, 8):
            top = jnp.maximum(top, pltpu.roll(top, shift, 1))
        ex = jnp.where(real, jnp.exp(logits - top), 0.0)
        total = ex
        for shift in (64, 32, 16, 8):
            total = total + pltpu.roll(total, shift, 1)
        probs = ex / total
        kp[pl.ds(ps, 128), :] = probs
        window = cv[pl.ds(pl.multiple_of(ps - 8, 8), 144), :]
        weights = nn(spread_taps(probs), spread[...])
        out = jnp.zeros((128, AH), F32)
        for j in range(TAPS):
            out = out + weights[128 * j : 128 * j + 128, :] * window[4 + j : 132 + j, :]
        ctx[rows, AH:D] = out.astype(BF)

    loop(6, dynamic)
    stores += [start_copy(cq, cq_any, sems.at[5]), start_copy(kp, kp_any, sems.at[6])]

    def attend(row0, nq, key0, nk, limit, pair, store):
        queries = packed[pl.ds(row0, nq), at(pair, 128)].astype(F32) * 0.125
        keys = packed[pl.ds(key0, nk), at(3 + pair, 128)].astype(F32)
        vals = packed[pl.ds(key0, nk), at(6 + pair, 128)]
        lane, key_lane = iota((nq, 128), 1), iota((nk, 128), 1)
        bias = jnp.where(iota((nk, 128), 0) < limit, 0.0, NEG)
        outs = []
        for hh in range(2):
            spare = 64 * (1 - hh)
            query = jnp.where((lane >> 6) == hh, queries, jnp.where(lane == spare, 1.0, 0.0))
            scores = nt(query.astype(BF), jnp.where(key_lane == spare, bias, keys).astype(BF))
            ex = jnp.exp(scores - jnp.max(scores, axis=1, keepdims=True))
            probs = (ex * (1.0 / jnp.sum(ex, axis=1, keepdims=True))).astype(BF)
            store(hh, probs)
            outs.append(nn(probs, vals))
        both = jnp.where(lane < 64, outs[0], outs[1])
        ctx[pl.ds(row0, nq), at(pair, 128)] = both.astype(BF)

    def long_attend(i):
        pair, block = i >> 1, i & 1
        row0 = pl.multiple_of(block * 256, 256)

        def store(hh, probs):
            plong[2 * pair + hh, pl.ds(row0, 256), :] = probs

        attend(row0, 256, 0, LONG, lens[0], pair, store)

    loop(6, long_attend)
    stores.append(start_copy(plong, plong_any, sems.at[7]))
    for seg in range(2):
        for pair in range(3):

            def store(hh, probs):
                pshort[seg, 2 * pair + hh, :, :] = probs

            row0 = LONG + 128 * seg
            attend(row0, 128, row0, SHORT, lens[1 + seg], pair, store)
    stores += [start_copy(pshort, pshort_any, sems.at[8]), start_copy(ctx, ctx_any, sems.at[9])]
    for copy in stores:
        copy.wait()


def gelu_parts(hidden):
    cdf = 0.5 + 0.5 * lax.erf(hidden * 0.7071067811865476)
    return cdf, jnp.exp(hidden * hidden * -0.5) * 0.3989422804014327


def fold(values):
    return jnp.sum(values.reshape(values.shape[0] // 8, 8, values.shape[1]), axis=0)


def start_copy(source, target, sem):
    copy = pltpu.make_async_copy(source, target, sem)
    copy.start()
    return copy


def ship(keep, send, place, slot, shard, rows, source, sem):
    where = slot ^ place[0]
    chip, far_off = where >> 1, shard ^ place[1]

    @pl.when((where & 1) == 0)
    def _():
        pltpu.make_async_copy(source, keep.at[chip, far_off, rows, :], sem).start()

    @pl.when((where & 1) == 1)
    def _():
        pltpu.make_async_copy(source, send.at[chip, far_off, rows, :], sem).start()


def ffn_both(
    place, llen, slen, vec, xm_any, ctx_any, cl, cs, p0, p1, p2, p3, p4, p5, p6, p7,
    ol, os, keep, send, gone_any, gctx_any, gvec,
    wo, wi, wu, xm, ctx, cot, out, res, xhat, grouped, gffn, active, slope, ffn, rstd,
    hid_a, hid_b, ghid_a, ghid_b, gproj, gout, ginner, gouter, gone, gctx, sums, sems,
):
    loads = [start_copy(ctx_any, ctx, sems.at[3]), start_copy(xm_any, xm, sems.at[4])]

    def fetch(part):
        for core, pieces in enumerate(((p0, p1, p2, p3), (p4, p5, p6, p7))):
            for chip, piece in enumerate(pieces):
                slot = slot_of(place[0], core, chip)
                g, r = slot >> 2, slot & 3

                def one(k):
                    n = place[1] ^ k
                    if part == 0:
                        rows = pl.ds(pl.multiple_of(192 * n + 48 * r, 48), 48)
                        source, target = pl.ds(192, 48), wo.at[g, rows, :]
                    elif part == 1:
                        source, target = pl.ds(0, 96), wi.at[slot, at(n, 96), :]
                    else:
                        source, target = pl.ds(96, 96), wu.at[4 * g + n, at(r, 96), :]
                    pltpu.make_async_copy(piece.at[k, source, :], target, sems.at[part]).start()

                loop(4, one)

    for part in range(3):
        fetch(part)
    cots = [
        start_copy(cl, cot.at[0:LONG], sems.at[5]), start_copy(cs, cot.at[LONG:ROWS], sems.at[6])
    ]
    gain_one, bias_one = vec[16:17, :], vec[17:18, :]
    gain_two, bias_two = vec[18:19, :], vec[19:20, :]
    sums[...] = jnp.zeros((32, D), F32)
    ffn[...] = jnp.zeros((2, ROWS, AH), F32)
    for copy in loads:
        copy.wait()
    pltpu.make_async_copy(wo, wo, sems.at[0]).wait()

    def mix(i):
        rows = at(i, 256)
        for c in range(2):
            lanes = slice(AH * c, AH * c + AH)
            res[rows, lanes] = nn(ctx[rows, :], wo[c]) + xm[rows, lanes].astype(F32)

    loop(3, mix)

    def norm_one(i):
        for half in range(2):
            rows = at(2 * i + half, 32)
            values = res[rows, :]
            center = values - jnp.mean(values, axis=1, keepdims=True)
            scale = lax.rsqrt(jnp.mean(center * center, axis=1, keepdims=True) + EPS)
            hat = center * scale
            first = hat * gain_one + bias_one
            xhat[rows, :] = hat
            rstd[rows, :] = jnp.broadcast_to(scale, (32, 128))
            res[rows, :] = first
            short = first.astype(BF)
            grouped[0, rows, :] = short[:, 0:AH]
            grouped[1, rows, :] = short[:, AH:D]

    loop(12, norm_one)
    pltpu.make_async_copy(wi, wi, sems.at[1]).wait()
    pltpu.make_async_copy(wu, wu, sems.at[2]).wait()

    def hidden(t, target):
        b = lax.div(t, 3)
        target[...] = nn(grouped[b >> 2, at(t - 3 * b, 256), :], wi[b])

    def outward(t):
        b = lax.div(t, 3)
        rows = at(t - 3 * b, 256)
        ffn[b >> 2, rows, :] += nn(active[b, rows, :], wu[b])

    def act(t, source):
        b = lax.div(t, 3)
        m = t - 3 * b
        for part in range(8):
            values = source[32 * part : 32 * part + 32, :]
            rows = pl.ds(pl.multiple_of(m * 256 + 32 * part, 32), 32)
            cdf, density = gelu_parts(values)
            active[b, rows, :] = (values * cdf).astype(BF)
            slope[b, rows, :] = cdf + values * density

    def pair(u, first=False):
        t = 2 * u
        if not first:
            outward(t - 1)
        hidden(t + 1, hid_b)
        act(t, hid_a)
        outward(t)
        hidden(jnp.minimum(t + 2, 23), hid_a)
        act(t + 1, hid_b)

    hidden(jnp.int32(0), hid_a)
    pair(jnp.int32(0), True)
    loop(11, lambda u: pair(u + 1))
    outward(jnp.int32(23))
    for copy in cots:
        copy.wait()

    def norm_two(i):
        limit = jnp.where(i < 8, llen[0], slen[jnp.clip((i - 8) >> 1, 0, 1)])
        base = jnp.where(i < 8, 64 * i, 64 * (i & 1))
        for half in range(2):
            rows = at(2 * i + half, 32)
            values = jnp.concatenate([ffn[0, rows, :], ffn[1, rows, :]], axis=1) + res[rows, :]
            center = values - jnp.mean(values, axis=1, keepdims=True)
            scale = lax.rsqrt(jnp.mean(center * center, axis=1, keepdims=True) + EPS)
            hat = center * scale
            out[rows, :] = (hat * gain_two + bias_two).astype(BF)
            live = base + 32 * half + iota((32, D), 0) < limit
            up = jnp.where(live, cot[rows, :].astype(F32), 0.0)
            sums[16:24, :] += fold(up * hat)
            sums[24:32, :] += fold(up)
            up = up * gain_two
            grad = scale * (
                up
                - jnp.mean(up, axis=1, keepdims=True)
                - hat * jnp.mean(up * hat, axis=1, keepdims=True)
            )
            res[rows, :] = grad
            short = grad.astype(BF)
            gffn[0, rows, :] = short[:, 0:AH]
            gffn[1, rows, :] = short[:, AH:D]

    loop(12, norm_two)
    stores = [
        start_copy(out.at[0:LONG], ol, sems.at[3]), start_copy(out.at[LONG:ROWS], os, sems.at[4])
    ]
    ffn[...] = jnp.zeros((2, ROWS, AH), F32)

    def slopes(b, target):
        for part in range(6):
            rows = slice(128 * part, 128 * part + 128)
            back = nt(gffn[b >> 2, rows, :], wu[b])
            target[rows, :] = (back * slope[b, rows, :]).astype(BF)

    def gradients(b, source):
        g, n = b >> 2, b & 3
        gouter[b] = tn(active[b], gffn[g]).astype(BF)
        ginner[b] = tn(grouped[g], source[...]).astype(BF)
        ffn[g] += nt(source[...], wi[b])
        for w in range(4):
            rows = pl.ds(96 * w, 96)
            ship(keep, send, place, 4 * g + w, n, pl.ds(96, 96), gouter.at[b, rows, :], sems.at[0])
            ship(keep, send, place, b, w, pl.ds(0, 96), ginner.at[b, rows, :], sems.at[1])

    slopes(jnp.int32(0), ghid_a)

    def contract(u):
        b = 2 * u
        slopes(b + 1, ghid_b)
        gradients(b, ghid_a)
        slopes(jnp.minimum(b + 2, 7), ghid_a)
        gradients(b + 1, ghid_b)

    loop(4, contract)

    def norm_one_back(i):
        for half in range(2):
            rows = at(2 * i + half, 32)
            up = res[rows, :] + jnp.concatenate([ffn[0, rows, :], ffn[1, rows, :]], axis=1)
            hat = xhat[rows, :]
            sums[0:8, :] += fold(up * hat)
            sums[8:16, :] += fold(up)
            up = up * gain_one
            grad = rstd[rows, 0:1] * (
                up
                - jnp.mean(up, axis=1, keepdims=True)
                - hat * jnp.mean(up * hat, axis=1, keepdims=True)
            )
            gone[rows, :] = grad
            gproj[rows, :] = grad.astype(BF)

    loop(12, norm_one_back)
    stores.append(start_copy(gone, gone_any, sems.at[5]))
    for k in range(4):
        gvec[k : k + 1, :] = jnp.sum(sums[8 * k : 8 * k + 8, :], axis=0, keepdims=True)
    gvec[4:8, :] = jnp.zeros((4, D), F32)
    for c in range(2):
        gout[c] = tn(ctx[...], gproj[:, AH * c : AH * c + AH]).astype(BF)
        for n in range(4):
            for r in range(4):
                source = gout.at[c, pl.ds(192 * n + 48 * r, 48), :]
                ship(keep, send, place, 4 * c + r, n, pl.ds(192, 48), source, sems.at[2])

    def unmix(i):
        rows = at(i, 256)
        part = nt(gproj[rows, 0:AH], wo[0]) + nt(gproj[rows, AH:D], wo[1])
        gctx[rows, :] = part.astype(BF)

    loop(3, unmix)
    stores.append(start_copy(gctx, gctx_any, sems.at[6]))
    for copy in stores:
        copy.wait()
    pltpu.make_async_copy(gouter, gouter, sems.at[0]).wait()
    pltpu.make_async_copy(ginner, ginner, sems.at[1]).wait()
    pltpu.make_async_copy(gout, gout, sems.at[2]).wait()


def mixer_backward(
    place, vec, gvec, xm_any, packed_any, plong_any, pshort_any, dw_any, kc_any, cq_any, kp_any,
    cv_any, gctx_any, p0, p1, p2, p3, p4, p5, p6, p7,
    keep, send, grads_any, gdep_any,
    wm, xm, packed, plong, pshort, dw, kc, cq, kp, cv, gctx,
    xpad, gcp, gdp, grads, gqc, dkv, gkc, glog, gdep, gb, spread, gather, wk, sem, sems, out_sem,
):
    arrays = (
        (gctx_any, gctx), (kp_any, kp), (cv_any, cv), (packed_any, packed), (kc_any, kc),
        (xm_any, xm), (plong_any, plong), (pshort_any, pshort), (dw_any, dw), (cq_any, cq),
    )
    loads = [start_copy(a, b, sems.at[k]) for k, (a, b) in enumerate(arrays[0:5])]
    fetch_mixer(place, (p0, p1, p2, p3, p4, p5, p6, p7), wm, sem)
    late = [start_copy(a, b, sems.at[5 + k]) for k, (a, b) in enumerate(arrays[5:])]
    zero_gaps(xpad)
    zero_gaps(gcp)
    zero_gaps(gdp)
    spread[...] = head_spread()
    gather[...] = head_gather()
    gdep[...] = jnp.zeros((8 * TAPS, D), F32)
    for copy in loads:
        copy.wait()
    for start, rows, pstart in SEGS:
        gcp[pstart : pstart + rows, :] = gctx[start : start + rows, AH:D].astype(F32)
    pltpu.make_async_copy(wm, wm, sem).wait()
    wk[...] = tap_kernel(wm)

    def dynamic(i):
        rows = at(i, 128)
        ps = padded_start(i)
        wide = pl.ds(pl.multiple_of(ps - 8, 8), 144)
        grad_wide = gcp[wide, :]
        values = cv[wide, :]
        grad = gcp[pl.ds(ps, 128), :]
        weights = nn(spread_taps(kp[wide, :]), spread[...])
        total = jnp.zeros((128, AH), F32)
        parts = []
        for j in range(TAPS):
            part = weights[144 * j : 144 * j + 144, :] * grad_wide
            total = total + part[12 - j : 140 - j, :]
            parts.append((grad * values[4 + j : 132 + j, :]).astype(BF))
        grads[rows, 3 * AH : 4 * AH] = total.astype(BF)
        sums = nn(jnp.concatenate(parts, axis=0), gather[...])
        gprob = sums[0:128, :]
        for j in range(1, TAPS):
            gprob = gprob + pltpu.roll(sums[128 * j : 128 * j + 128, :], 8 * j, 1)
        probs = kp[pl.ds(ps, 128), :]
        inner = probs * gprob
        for shift in (64, 32, 16, 8):
            inner = inner + pltpu.roll(inner, shift, 1)
        glogits = (probs * (gprob - inner)).astype(BF)
        glog[rows, :] = glogits
        gquery = nt(glogits, wk[...])
        gkc[rows, :] = (gquery * packed[rows, 0:AH].astype(F32)).astype(BF)
        gqc[rows, :] = gquery * kc[rows, :]

    loop(6, dynamic)
    for copy in late:
        copy.wait()

    def point_back(c):
        part = nt(gkc[:, 0:256], wm[6, at(c, 256), :])
        part = part + nt(gkc[:, 256:384], wm[7, at(c, 256), 0:128])
        part = part.astype(BF).astype(F32)
        for start, rows, pstart in SEGS:
            gdp[pstart : pstart + rows, at(c, 256)] = part[start : start + rows, :]

    loop(3, point_back)
    copy_depth = start_copy(gdp, gdep_any, out_sem.at[1])

    def attend(row0, nq, key0, nk, pair, load, first):
        queries = packed[pl.ds(row0, nq), at(pair, 128)].astype(F32) * 0.125
        keys = packed[pl.ds(key0, nk), at(3 + pair, 128)]
        vals = packed[pl.ds(key0, nk), at(6 + pair, 128)]
        up = gctx[pl.ds(row0, nq), at(pair, 128)].astype(F32)
        lane = iota((nq, 128), 1)
        outs = []
        gkeys = jnp.zeros((nk, 128), F32)
        gvals = jnp.zeros((nk, 128), F32)
        for hh in range(2):
            mine = (lane >> 6) == hh
            query = jnp.where(mine, queries, 0.0).astype(BF)
            upper = jnp.where(mine, up, 0.0).astype(BF)
            probs_low = load(hh)
            probs = probs_low.astype(F32)
            gprobs = nt(upper, vals)
            inner = jnp.sum(probs * gprobs, axis=1, keepdims=True)
            gscores = (probs * (gprobs - inner)).astype(BF)
            outs.append(nn(gscores, keys))
            gkeys = gkeys + tn(gscores, query)
            gvals = gvals + tn(probs_low, upper)
        both = jnp.where(lane < 64, outs[0], outs[1]) * 0.125
        both = both + gqc[pl.ds(row0, nq), at(pair, 128)]
        grads[pl.ds(row0, nq), at(pair, 128)] = both.astype(BF)
        span = pl.ds(key0, nk)
        if nq == nk:
            grads[span, at(3 + pair, 128)] = gkeys.astype(BF)
            grads[span, at(6 + pair, 128)] = gvals.astype(BF)
        elif first:
            dkv[0] = gkeys
            dkv[1] = gvals
        else:
            grads[span, at(3 + pair, 128)] = (dkv[0] + gkeys).astype(BF)
            grads[span, at(6 + pair, 128)] = (dkv[1] + gvals).astype(BF)

    def long_attend(pair):
        for block in range(2):
            attend(
                256 * block, 256, 0, LONG, pair,
                lambda hh: plong[2 * pair + hh, 256 * block : 256 * block + 256, :],
                block == 0,
            )

    loop(3, long_attend)
    for seg in range(2):
        for pair in range(3):
            row0 = LONG + 128 * seg
            attend(row0, 128, row0, SHORT, pair, lambda hh: pshort[seg, 2 * pair + hh, :, :], True)
    copy_grads = start_copy(grads, grads_any, out_sem.at[2])
    for start, rows, pstart in SEGS:
        xpad[pstart : pstart + rows, :] = xm[start : start + rows, :].astype(F32)

    def release(b):
        for n in range(4):
            where = b ^ place[0]
            chip, far_off = where >> 1, n ^ place[1]
            source = gb.at[b, pl.ds(192 * n, 192), :]

            @pl.when((where & 1) == 0)
            def _():
                pltpu.make_async_copy(source, keep.at[chip, far_off], out_sem.at[0]).start()

            @pl.when((where & 1) == 1)
            def _():
                pltpu.make_async_copy(source, send.at[chip, far_off], out_sem.at[0]).start()

    gb[6] = tn(dw[...], gkc[:, 0:256]).astype(BF)
    release(6)

    def depth(i):
        ps = padded_start(i)
        wide = pl.ds(pl.multiple_of(ps - 8, 8), 144)
        for c in range(3):
            lanes = slice(256 * c, 256 * c + 256)
            tokens = xpad[pl.ds(ps, 128), lanes]
            grad_wide = gdp[wide, lanes]
            for j in range(TAPS):
                gdep[8 * j : 8 * j + 8, lanes] += fold(tokens * grad_wide[12 - j : 140 - j, :])

    def weights(b):
        gb[b] = tn(xm[...], grads[:, at(b, 256)]).astype(BF)
        depth(b)
        release(b)

    loop(6, weights)
    gb[7, :, 0:128] = tn(dw[...], gkc[:, 256:384]).astype(BF)
    taps = [jnp.sum(gdep[8 * j : 8 * j + 8, :], axis=0, keepdims=True) for j in range(TAPS)]
    table = jnp.concatenate(
        taps + [jnp.zeros((7, D), F32), gvec[...], jnp.zeros((104, D), F32)], axis=0
    ).astype(BF)
    misc = tn(table, eye(128, BF))
    gkernel = nt(tn(cq[...], glog[...]).astype(BF), tap_permutation())
    for n in range(4):
        row = 192 * n
        part = misc[row : row + 96, :] + gkernel[96 * n : 96 * n + 96, :]
        gb[7, row : row + 96, 128:256] = part.astype(BF)
        gb[7, row + 96 : row + 192, 128:256] = misc[row + 96 : row + 192, :].astype(BF)
    release(7)
    copy_depth.wait()
    copy_grads.wait()
    pltpu.make_async_copy(gb, gb, out_sem.at[0]).wait()


def input_gradient(
    place, llen, slen, vec, grads_any, gdp_any, gone_any, p0, p1, p2, p3, p4, p5, p6, p7,
    il, is_, wm, grads, gdp, rest, sem, sems
):
    arrays = ((gone_any, rest), (gdp_any, gdp), (grads_any, grads))
    loads = [start_copy(a, b, sems.at[k]) for k, (a, b) in enumerate(arrays)]
    fetch_mixer(place, (p0, p1, p2, p3, p4, p5, p6, p7), wm, sem)
    for copy in loads:
        copy.wait()

    def depth(i):
        ps = padded_start(i)
        for c in range(3):
            lanes = slice(256 * c, 256 * c + 256)
            window = gdp[pl.ds(pl.multiple_of(ps - 8, 8), 144), lanes]
            total = rest[at(i, 128), lanes]
            for j in range(TAPS):
                total = total + vec[j : j + 1, lanes] * window[12 - j : 140 - j, :]
            rest[at(i, 128), lanes] = total

    loop(6, depth)
    pltpu.make_async_copy(wm, wm, sem).wait()

    def inputs(i):
        rows = at(i, 256)
        total = rest[rows, :]
        for b in range(6):
            total = total + nt(grads[rows, 256 * b : 256 * b + 256], wm[b])
        return total

    def inputs_long(i):
        live = i * 256 + iota((256, D), 0) < llen[0]
        il[at(i, 256), :] = jnp.where(live, inputs(i), 0.0).astype(BF)

    loop(2, inputs_long)
    total = inputs(2)
    row = iota((128, D), 0)
    for seg in range(2):
        part = total[128 * seg : 128 * seg + 128, :]
        is_[128 * seg : 128 * seg + 128, :] = jnp.where(row < slen[seg], part, 0.0).astype(BF)


def pack(
    place, qkv, depth, point, kernel, convout, g1, b1, inner, outer, out, g2, b2, mixer, ffn
):
    for w in range(SLOTS):

        @pl.when(place[0] == w)
        def _():
            g, r = w // 4, w % 4
            ffn[0:96, :] = inner[g, :, AH * r : AH * r + AH]
            ffn[96:192, :] = outer[g, 96 * r : 96 * r + 96, :]
            ffn[192:240, :] = out[48 * r : 48 * r + 48, AH * g : AH * g + AH]
            if w < 4:
                mixer[...] = qkv[:, 256 * w : 256 * w + 256]
            elif w == 4:
                mixer[:, 0:128] = qkv[:, 1024:1152]
                mixer[:, 128:256] = convout[:, 0:128]
            elif w == 5:
                mixer[...] = convout[:, 128:384]
            elif w == 6:
                mixer[...] = point[:, 0:256]
            else:
                mixer[:, 0:128] = point[:, 256:384]
                rows = [v[...].astype(F32).reshape(1, 192) for v in (g1, b1, g2, b2)]
                table = jnp.concatenate(
                    [depth[...].astype(F32), jnp.zeros((7, 192), F32)]
                    + rows
                    + [jnp.zeros((108, 192), F32)],
                    axis=0,
                )
                left = tn(table.astype(BF), eye(128, BF))
                row, col = iota((54, 128), 0), iota((54, 128), 1)
                right = tn(kernel[...], jnp.where(col == row + 64, 1.0, 0.0).astype(BF))
                mixer[0:96, 128:256] = (left[0:96, :] + right).astype(BF)
                mixer[96:192, 128:256] = left[96:192, :].astype(BF)


def unpack_ffn(packed, inner, outer, out):
    for w in range(SLOTS):
        g, r = w // 4, w % 4
        inner[g, :, AH * r : AH * r + AH] = packed[w, 0:96, :].astype(F32)
        outer[g, 96 * r : 96 * r + 96, :] = packed[w, 96:192, :].astype(F32)
        out[48 * r : 48 * r + 48, AH * g : AH * g + AH] = packed[w, 192:240, :].astype(F32)


def unpack_mixer(packed, qkv, depth, point, kernel, convout, g1, b1, g2, b2):
    for w in range(4):
        qkv[:, 256 * w : 256 * w + 256] = packed[w].astype(F32)
    qkv[:, 1024:1152] = packed[4, :, 0:128].astype(F32)
    convout[:, 0:128] = packed[4, :, 128:256].astype(F32)
    convout[:, 128:384] = packed[5].astype(F32)
    point[:, 0:256] = packed[6].astype(F32)
    point[:, 256:384] = packed[7, :, 0:128].astype(F32)
    misc = packed[7, :, 128:256]
    table = nt(eye(128, BF), misc)
    depth[...] = table[0:TAPS, :]
    for k, ref in enumerate((g1, b1, g2, b2)):
        ref[...] = table[16 + k : 17 + k, :].reshape(192)
    kernel[...] = table[64:118, 0:96]


SMEM = pl.BlockSpec(memory_space=pltpu.SMEM)
VMEM = pl.BlockSpec(memory_space=pltpu.VMEM)
ANY = pl.BlockSpec(memory_space=pl.ANY)


def call(kernel, specs, outs, scratch, flops, *args, out_specs=None):
    return pl.pallas_call(
        kernel,
        out_shape=[jax.ShapeDtypeStruct(s, d) for s, d in outs],
        in_specs=specs,
        out_specs=out_specs or [VMEM] * len(outs),
        scratch_shapes=[pltpu.VMEM(s, d) for s, d in scratch[0]] + list(scratch[1:]),
        compiler_params=pltpu.CompilerParams(vmem_limit_bytes=60 << 20),
        cost_estimate=pl.CostEstimate(flops=flops, bytes_accessed=1 << 20, transcendentals=0),
        name=kernel.__name__,
    )(*args)


def forward_mixer(scalars, xl, xs, pieces):
    outs = [
        ((ROWS, D), BF), ((ROWS, 3 * AH), BF),
        ((HEADS, LONG, LONG), BF), ((2, HEADS, SHORT, SHORT), BF),
        ((ROWS, D), BF), ((ROWS, AH), F32), ((ROWS, AH), BF), ((PAD, 128), F32),
        ((PAD, AH), F32), ((ROWS, D), BF), ((24, D), F32),
    ]
    scratch = [((SLOTS, D, 256), BF), ((PAD, D), F32), ((256, AH), BF), ((AH, 128), BF)]
    return call(
        mixer_forward, [SMEM] * 3 + [VMEM] * 2 + [ANY] * 8, outs,
        (scratch + outs[:-1], pltpu.SemaphoreType.DMA, pltpu.SemaphoreType.DMA((10,))), 30 * 10**9,
        *scalars, xl, xs, *pieces, out_specs=[ANY] * 10 + [VMEM],
    )


def feed_forward(scalars, xm, ctx, vec, cl, cs, pieces):
    outs = [
        ((LONG, D), BF), ((2 * SHORT, D), BF), ((4, 4, 240, AH), BF), ((4, 4, 240, AH), BF),
        ((ROWS, D), F32), ((ROWS, D), BF), ((8, D), F32),
    ]
    scratch = [
        ((2, D, AH), BF), ((8, AH, AH), BF), ((8, AH, AH), BF), ((ROWS, D), BF), ((ROWS, D), BF),
        ((ROWS, D), BF), ((ROWS, D), BF), ((ROWS, D), F32), ((ROWS, D), F32),
        ((2, ROWS, AH), BF), ((2, ROWS, AH), BF), ((8, ROWS, AH), BF), ((8, ROWS, AH), F32),
        ((2, ROWS, AH), F32), ((ROWS, 128), F32), ((256, AH), F32), ((256, AH), F32),
        ((ROWS, AH), BF), ((ROWS, AH), BF), ((ROWS, D), BF), ((2, ROWS, AH), BF),
        ((8, AH, AH), BF), ((8, AH, AH), BF), ((ROWS, D), F32), ((ROWS, D), BF), ((32, D), F32),
    ]
    return call(
        ffn_both, [SMEM] * 3 + [VMEM] + [ANY] * 12, outs,
        (scratch, pltpu.SemaphoreType.DMA((7,))), 60 * 10**9,
        *scalars, vec, xm, ctx, cl, cs, *pieces, out_specs=[ANY] * 6 + [VMEM],
    )


def backward_mixer(place, vec, gvec, arrays, pieces):
    outs = [
        ((4, 4, 192, 256), BF), ((4, 4, 192, 256), BF), ((ROWS, 4 * AH), BF), ((PAD, D), F32),
    ]
    scratch = [((SLOTS, D, 256), BF)] + [(a.shape, a.dtype) for a in arrays] + [
        ((PAD, D), F32), ((PAD, AH), F32), ((PAD, D), F32), ((ROWS, 4 * AH), BF),
        ((ROWS, AH), F32), ((2, LONG, 128), F32), ((ROWS, AH), BF), ((ROWS, 128), BF),
        ((8 * TAPS, D), F32), ((SLOTS, D, 256), BF), ((256, AH), BF), ((AH, 128), BF),
        ((AH, 128), BF),
    ]
    dma = pltpu.SemaphoreType.DMA
    return call(
        mixer_backward, [SMEM] + [VMEM] * 2 + [ANY] * 18, outs,
        (scratch, dma, dma((10,)), dma((3,))), 40 * 10**9,
        place, vec, gvec, *arrays, *pieces, out_specs=[ANY] * 4,
    )


def backward_inputs(scalars, vec, grads, gdp, gone, pieces):
    scratch = [
        ((SLOTS, D, 256), BF), ((ROWS, 4 * AH), BF), ((PAD, D), F32), ((ROWS, D), F32),
    ]
    dma = pltpu.SemaphoreType.DMA
    return call(
        input_gradient, [SMEM] * 3 + [VMEM] + [ANY] * 11, [((LONG, D), BF), ((2 * SHORT, D), BF)],
        (scratch, dma, dma((3,))), 5 * 10**9, *scalars, vec, grads, gdp, gone, *pieces,
    )


def far(values, bit):
    return lax.ppermute(values, "narrow", [(i, i ^ bit) for i in range(4)])


def near(values, bit):
    return lax.ppermute(values, "wide", [(i, i ^ bit) for i in range(SLOTS)])


def gather_narrow(piece):
    return jnp.stack([piece] + [far(piece, k) for k in (1, 2, 3)])


def gather_chips(block):
    return [block] + [near(block, k) for k in (2, 4, 6)]


def gather_cores(blocks):
    return blocks + [near(block, 1) for block in blocks]


def total(first, others):
    result = first.astype(F32)
    for other in others:
        result = result + other.astype(F32)
    return result.astype(BF)


def reduce_cores(keep, sent):
    return [total(keep[k], [sent[k]]) for k in range(4)]


def send_chips(parts):
    return [near(parts[k], 2 * k) for k in (1, 2, 3)]


def reduce_chips(first, others):
    return [total(first[k], [other[k] for other in others]) for k in range(4)]


def send_narrow(parts):
    return [far(parts[k], k) for k in (1, 2, 3)]


def gather_wide(parts):
    return lax.all_gather(parts, "wide", axis=0, tiled=False)


def body(
    long_tokens, long_lengths, short_tokens, short_lengths,
    w_qkv, w_depth, w_point, w_kernel, w_convout, w_out, norm1_gain, norm1_bias,
    w_inner, w_outer, norm2_gain, norm2_bias, long_cotangent, short_cotangent,
):
    place = jnp.stack([lax.axis_index("wide"), lax.axis_index("narrow")]).astype(jnp.int32)
    scalars = (place, long_lengths, short_lengths)
    xl, xs = long_tokens.reshape(LONG, D), short_tokens.reshape(2 * SHORT, D)
    cl, cs = long_cotangent.reshape(LONG, D), short_cotangent.reshape(2 * SHORT, D)
    mixer, ffn = call(
        pack, [SMEM] + [VMEM] * 12, [((192, 256), BF), ((240, AH), BF)], ([],), 10**9,
        place, w_qkv, w_depth, w_point, w_kernel.T, w_convout, norm1_gain, norm1_bias,
        w_inner, w_outer, w_out, norm2_gain, norm2_bias,
    )
    mixer = gather_narrow(mixer)
    mixer, ffn = lax.optimization_barrier((mixer, ffn))
    mixer = gather_chips(mixer)
    ffn = gather_narrow(ffn)
    mixer, ffn = lax.optimization_barrier((mixer, ffn))
    mixer = gather_cores(mixer)
    ffn = gather_chips(ffn)
    xm, packed, plong, pshort, dw, kc, cq, kp, cv, ctx, vec = forward_mixer(scalars, xl, xs, mixer)
    ctx, ffn = lax.optimization_barrier((ctx, ffn))
    ffn = gather_cores(ffn)
    ol, os, keep, send, gone, gctx, gvec = feed_forward(scalars, xm, ctx, vec, cl, cs, ffn)
    ga = reduce_cores(keep, near(send, 1))
    ga_sent = send_chips(ga)
    gctx, ga = lax.optimization_barrier((gctx, ga))
    keep, send, grads, gdp = backward_mixer(
        place, vec, gvec, (xm, packed, plong, pshort, dw, kc, cq, kp, cv, gctx), mixer
    )
    keep, send, ga_sent = lax.optimization_barrier((keep, send, ga_sent))
    sent = near(send, 1)
    ga = reduce_chips(ga[0], ga_sent)
    ga_sent = send_narrow(ga)
    gb = reduce_cores(keep, sent)
    gb_sent = send_chips(gb)
    grads, gb = lax.optimization_barrier((grads, gb))
    il, is_ = backward_inputs(scalars, vec, grads, gdp, gone, mixer)
    ga_sent, gb_sent, il = lax.optimization_barrier((ga_sent, gb_sent, il))
    ga = lax.psum(total(ga[0], ga_sent), "hi")
    gb = reduce_chips(gb[0], gb_sent)
    gb = lax.psum(total(gb[0], send_narrow(gb)), "hi")
    inner, outer, out = call(
        unpack_ffn, [VMEM], [((2, 96, 4 * AH), F32), ((2, AH, AH), F32), ((192, D), F32)],
        ([],), 10**9, gather_wide(ga),
    )
    outs = [
        ((192, 3 * AH), F32), ((TAPS, 192), F32), ((192, AH), F32), ((54, 96), F32), ((192, AH), F32),
    ] + [((192,), F32)] * 4
    qkv, depth, point, kernel, convout, g1, b1, g2, b2 = call(
        unpack_mixer, [VMEM], outs, ([],), 10**9, gather_wide(gb)
    )
    return (
        ol.reshape(long_tokens.shape), os.reshape(short_tokens.shape),
        il.reshape(long_tokens.shape), is_.reshape(short_tokens.shape),
        qkv, depth, point, kernel.T, convout, out, g1, b1, inner, outer, g2, b2,
    )


def solution(mesh):
    wide, narrow = mesh.shape["wide"], mesh.shape["narrow"]
    inner_mesh = Mesh(mesh.devices.reshape(wide // SLOTS, SLOTS, narrow), ("hi", "wide", "narrow"))
    every = ("hi", "wide", "narrow")
    rows = P(every, None, None)
    weights = (
        P("narrow", None), P(None, "narrow"), P("narrow", None), P("narrow", None),
        P("narrow", None), P("narrow", None), P("narrow"), P("narrow"),
        P(None, "narrow", None), P(None, "narrow", None), P("narrow"), P("narrow"),
    )
    return jax.shard_map(
        body,
        mesh=inner_mesh,
        in_specs=(rows, P(every), rows, P(every)) + weights + (rows, rows),
        out_specs=(rows, rows, rows, rows) + weights,
        check_vma=False,
    )
```

time: 281 us -> 250 us (0.89)
  Pallas kernels: 154 us -> 124 us
    pallas_call x7, Pallas kernels: 154 us -> 124 us  [call(): pl.pallas_call(kernel, out_shape=[jax.ShapeDtypeStruct(s, d) for s, d in...]
  transfers between devices with their start and end apart: 35 -> 35, of which waited for: 17 -> 18; matrix products, arithmetic and copies ran while one was open for 2% -> 2% of each run, Pallas kernels for 30% -> 29%
where the time goes in v4:
time: 250 us
  Pallas kernels  124 us (50%)
  waiting for transfers between devices  43 us (17%)
  starting transfers between devices  41.1 us (16%)
  between operations  14.9 us (6%)
  other arithmetic  12.8 us (5%)
  blocking collectives  11.8 us (5%)
    pallas_call x7, Pallas kernels, call(): pl.pallas_call(kernel, out_shape=[jax.ShapeDtypeStruct(s, d) for s, d in...  124 us
    ppermute x12, waiting for transfers between devices, far(): return lax.ppermute(values, 'narrow', [(i, i ^ bit) for i in range(4)])  24.6 us
    ppermute x12, starting transfers between devices, far(): return lax.ppermute(values, 'narrow', [(i, i ^ bit) for i in range(4)])  23.9 us
    ppermute x22, waiting for transfers between devices, near(): return lax.ppermute(values, 'wide', [(i, i ^ bit) for i in range(SLOTS)])  18.4 us
    ppermute x22, starting transfers between devices, near(): return lax.ppermute(values, 'wide', [(i, i ^ bit) for i in range(SLOTS)])  17.1 us
    all_gather x1, blocking collectives, gather_wide(): return lax.all_gather(parts, 'wide', axis=0, tiled=False)  11.8 us
    convert_element_type x4, other arithmetic, total(): return result.astype(BF)  7.87 us
  transfers between devices with their start and end apart: 35, of which 18 were waited for; matrix products, arithmetic and copies ran while one was open for 2% of the time, Pallas kernels for 29%

profile of v4, /device:TPU:0, one launch (start us, length us, event | category | flops | bytes accessed | tf_op | source)
XLA Modules:
  0.0 249.7 jit_solution(4347494742472643162)
XLA Ops:
  7.8 2.4 pack.1
  10.2 5.0 %collective-permute-start.2 = (bf16[192,256]{1,0:T(8,128)(2,1)}, bf16[192,256]{1,0:T(8,128)(2,1)S(1)}, u32[]{:S(2)}, u32[]{:S(2)}) collective-permute-start(bf16[192,256]{1,0:T(8,128)(2,1)} %get-tuple-element.82), channel_id=1, source_target_pairs={{0,3},{1,2},{2,1},{3,0},{4,7},{5,6},{6,5},{7,4},{8,11},{9,10},{10,... | collective-permute-start | bytes 294920 | tf_op jit(solution)/shard_map/ppermute | solution.py:831
  15.9 3.3 %collective-permute-done.2 = bf16[192,256]{1,0:T(8,128)(2,1)S(1)} collective-permute-done((bf16[192,256]{1,0:T(8,128)(2,1)}, bf16[192,256]{1,0:T(8,128)(2,1)S(1)}, u32[]{:S(2)}, u32[]{:S(2)}) %collective-permute-start.2) | collective-permute-done | bytes 98336 | tf_op jit(solution)/shard_map/ppermute | solution.py:831
  19.2 4.6 %collective-permute-done.1 = bf16[192,256]{1,0:T(8,128)(2,1)S(1)} collective-permute-done((bf16[192,256]{1,0:T(8,128)(2,1)}, bf16[192,256]{1,0:T(8,128)(2,1)S(1)}, u32[]{:S(2)}, u32[]{:S(2)}) %collective-permute-start.1) | collective-permute-done | bytes 98336 | tf_op jit(solution)/shard_map/ppermute | solution.py:831
  24.7 2.6 %collective-permute-start.8 = (bf16[240,384]{1,0:T(8,128)(2,1)}, bf16[240,384]{1,0:T(8,128)(2,1)S(1)}, u32[]{:S(2)}, u32[]{:S(2)}) collective-permute-start(bf16[240,384]{1,0:T(8,128)(2,1)} %get-tuple-element.85), channel_id=1, source_target_pairs={{0,3},{1,2},{2,1},{3,0},{4,7},{5,6},{6,5},{7,4},{8,11},{9,10},{10,... | collective-permute-start | bytes 552968 | tf_op jit(solution)/shard_map/ppermute | solution.py:831
  27.3 2.6 %collective-permute-start.5 = (bf16[4,192,256]{2,1,0:T(8,128)(2,1)S(1)}, bf16[4,192,256]{2,1,0:T(8,128)(2,1)S(1)}, u32[]{:S(2)}, u32[]{:S(2)}) collective-permute-start(bf16[4,192,256]{2,1,0:T(8,128)(2,1)S(1)} %pad_maximum_fusion.1.p0), channel_id=1, source_target_pairs={{0,24},{4,28},{8,16},{12,20},{16,8},{20,12},{24,0},{28,4},{1,25},{... | collective-permute-start | bytes 1179656 | tf_op jit(solution)/shard_map/ppermute | solution.py:835
  30.8 3.1 %collective-permute-done.8 = bf16[240,384]{1,0:T(8,128)(2,1)S(1)} collective-permute-done((bf16[240,384]{1,0:T(8,128)(2,1)}, bf16[240,384]{1,0:T(8,128)(2,1)S(1)}, u32[]{:S(2)}, u32[]{:S(2)}) %collective-permute-start.8) | collective-permute-done | bytes 184352 | tf_op jit(solution)/shard_map/ppermute | solution.py:831
  33.9 6.9 %collective-permute-start.6 = (bf16[240,384]{1,0:T(8,128)(2,1)}, bf16[240,384]{1,0:T(8,128)(2,1)S(1)}, u32[]{:S(2)}, u32[]{:S(2)}) collective-permute-start(bf16[240,384]{1,0:T(8,128)(2,1)} %get-tuple-element.85), channel_id=1, source_target_pairs={{0,1},{1,0},{2,3},{3,2},{4,5},{5,4},{6,7},{7,6},{8,9},{9,8},{10,11... | collective-permute-start | bytes 552968 | tf_op jit(solution)/shard_map/ppermute | solution.py:831
  42.3 2.2 collective-permute-done.6
  48.2 2.1 collective-permute-start.15
  53.0 28.8 %mixer_forward.1 = (bf16[768,768]{1,0:T(8,128)(2,1)}, bf16[768,1152]{1,0:T(8,128)(2,1)}, bf16[6,512,512]{2,1,0:T(8,128)(2,1)}, bf16[2,6,128,128]{3,2,1,0:T(8,128...) custom-call(s32[2]{0:T(128)} %pad_add_fusion.place, ...), custom_call_target="tpu_custom_call" | custom-call | flops 30000001024 | bytes 1048576 | tf_op jit(solution)/shard_map/mixer_forward/pallas_call | solution.py:754
  89.8 46.5 %ffn_both.1 = (bf16[512,768]{1,0:T(8,128)(2,1)}, bf16[256,768]{1,0:T(8,128)(2,1)}, bf16[4,4,240,384]{3,2,1,0:T(8,128)(2,1)}, bf16[4,4,240,384]{3,2,1,0:T(8,128)(...) custom-call(s32[2]{0:T(128)} %pad_add_fusion.place, s32[1]{0:T(128)S(6)} %copy.34.llen, ...), custom_call_target="tpu_custom_call" | custom-call | flops 60000002048 | bytes 1048576 | tf_op jit(solution)/shard_map/ffn_both/pallas_call | solution.py:754
  136.5 5.4 %collective-permute-done.20 = bf16[4,4,240,384]{3,2,1,0:T(8,128)(2,1)S(1)} collective-permute-done((bf16[4,4,240,384]{3,2,1,0:T(8,128)(2,1)}, bf16[4,4,240,384]{3,2,1,0:T(8,128)(2,1)S(1)}, u32[]{:S(2)}, u32[]{:S(2)}) %collective-permute-start.20) | collective-permute-done | bytes 2949152 | tf_op jit(solution)/shard_map/ppermute | solution.py:835
  141.9 3.6 %fusion.3 = (bf16[4,240,384]{2,1,0:T(8,128)(2,1)}, bf16[4,240,384]{2,1,0:T(8,128)(2,1)}, bf16[4,240,384]{2,1,0:T(8,128)(2,1)S(1)}, bf16[4,240,384]{2,1,0:T(8,128)(2,1)S(1)}) fusion(bf16[4,4,240,384]{3,2,1,0:T(8,128)(2,1)S(1)} %collective-permute-done.20, bf16[4,4,240,384]{3,2,1,0:T(8,128)(2,1)} %get-tuple-element.102), kind=kLoop, calls=%fused_computation.11 | loop fusion | flops 5898240 | bytes 8847360 | tf_op jit(solution)/shard_map/convert_element_type | solution.py:854
  149.1 30.7 %mixer_backward.1 = (bf16[4,4,192,256]{3,2,1,0:T(8,128)(2,1)}, bf16[4,4,192,256]{3,2,1,0:T(8,128)(2,1)}, bf16[768,1536]{1,0:T(8,128)(2,1)}, f32[800,768]{1,0:T(8,128)}) custom-call(s32[2]{0:T(128)} %pad_add_fusion.place, f32[24,768]{1,0:T(8,128)} %get-tuple-element.90.vec, f32[8,768]{1,0:T(8,128)} %get-tuple-element.105.gvec, ...), custom_call_target="tpu_custom_call" | custom-call | flops 40000000000 | bytes 1048576 | tf_op jit(solution)/shard_map/mixer_backward/pallas_call | solution.py:754
  192.8 10.3 %input_gradient.1 = (bf16[512,768]{1,0:T(8,128)(2,1)}, bf16[256,768]{1,0:T(8,128)(2,1)}) custom-call(s32[2]{0:T(128)} %pad_add_fusion.place, s32[1]{0:T(128)S(6)} %copy.34.llen, s32[2]{0:T(128)} %slen.5, f32[24,768]{1,0:T(8,128)} %get-tuple-element.90.vec, bf16[768,1536]{1,0:T(8,128)(2,1)} %get-tuple-element.123.grads_any, ...), custom_call_target="tpu_custom_call" | custom-call | flops 5000000000 | bytes 1048576 | tf_op jit(solution)/shard_map/input_gradient/pallas_call | solution.py:754
  203.1 4.9 %collective-permute-done.29 = bf16[4,192,256]{2,1,0:T(8,128)(2,1)} collective-permute-done((bf16[4,192,256]{2,1,0:T(8,128)(2,1)S(1)}, bf16[4,192,256]{2,1,0:T(8,128)(2,1)}, u32[]{:S(2)}, u32[]{:S(2)}) %collective-permute-start.29) | collective-permute-done | bytes 393248 | tf_op jit(solution)/shard_map/ppermute | solution.py:835
  208.0 1.9 fusion.10
  211.3 2.8 %collective-permute-start.31 = (bf16[192,256]{1,0:T(8,128)(2,1)S(1)}, bf16[192,256]{1,0:T(8,128)(2,1)S(1)}, u32[]{:S(2)}, u32[]{:S(2)}) collective-permute-start(bf16[192,256]{1,0:T(8,128)(2,1)S(1)} %get-tuple-element.159), channel_id=1, source_target_pairs={{0,1},{1,0},{2,3},{3,2},{4,5},{5,4},{6,7},{7,6},{8,9},{9,8},{10,11... | collective-permute-start | bytes 294920 | tf_op jit(solution)/shard_map/ppermute | solution.py:831
  217.3 3.6 %collective-permute-done.33 = bf16[192,256]{1,0:T(8,128)(2,1)S(1)} collective-permute-done((bf16[192,256]{1,0:T(8,128)(2,1)S(1)}, bf16[192,256]{1,0:T(8,128)(2,1)S(1)}, u32[]{:S(2)}, u32[]{:S(2)}) %collective-permute-start.33) | collective-permute-done | bytes 98336 | tf_op jit(solution)/shard_map/ppermute | solution.py:831
  220.9 3.7 %collective-permute-done.32 = bf16[192,256]{1,0:T(8,128)(2,1)S(1)} collective-permute-done((bf16[192,256]{1,0:T(8,128)(2,1)S(1)}, bf16[192,256]{1,0:T(8,128)(2,1)S(1)}, u32[]{:S(2)}, u32[]{:S(2)}) %collective-permute-start.32) | collective-permute-done | bytes 98336 | tf_op jit(solution)/shard_map/ppermute | solution.py:831
  225.7 11.8 %all-gather = bf16[1536,256]{1,0:T(8,128)(2,1)} all-gather(bf16[192,256]{1,0:T(8,128)(2,1)S(1)} %fusion.13), channel_id=2, replica_groups=mesh['wide'=8,'narrow'=4] {'wide'}, dimensions={0}, use_global_device_ids=true | all-gather | bytes 884736 | tf_op jit(solution)/shard_map/all_gather | solution.py:874
  237.4 2.4 unpack_mixer.1
  239.8 3.0 %unpack_ffn.1 = (f32[2,96,1536]{2,1,0:T(8,128)}, f32[2,384,384]{2,1,0:T(8,128)}, f32[192,768]{1,0:T(8,128)}) custom-call(bf16[8,240,384]{2,1,0:T(8,128)(2,1)} %bitcast.69), custom_call_target="tpu_custom_call" | custom-call | flops 1000000000 | bytes 1048576 | tf_op jit(solution)/shard_map/unpack_ffn/pallas_call | solution.py:754
  (98 shorter events, 40.6 us)
Async XLA Ops:
  7.2 232.6 %all-gather.4.cloned.1.call-start = ((), (), s32[]{:S(2)}) async-start(), calls=%async_computation | async-start | bytes 1658880 | tf_op jit(solution)/shard_map/all_gather | solution.py:874
  10.2 9.0 %collective-permute-start.2 = (bf16[192,256]{1,0:T(8,128)(2,1)}, bf16[192,256]{1,0:T(8,128)(2,1)S(1)}, u32[]{:S(2)}, u32[]{:S(2)}) collective-permute-start(bf16[192,256]{1,0:T(8,128)(2,1)} %get-tuple-element.82), channel_id=1, source_target_pairs={{0,3},{1,2},{2,1},{3,0},{4,7},{5,6},{6,5},{7,4},{8,11},{9,10},{10,... | collective-permute-start | bytes 294920 | tf_op jit(solution)/shard_map/ppermute | solution.py:831
  15.3 8.5 %collective-permute-start.1 = (bf16[192,256]{1,0:T(8,128)(2,1)}, bf16[192,256]{1,0:T(8,128)(2,1)S(1)}, u32[]{:S(2)}, u32[]{:S(2)}) collective-permute-start(bf16[192,256]{1,0:T(8,128)(2,1)} %get-tuple-element.82), channel_id=1, source_target_pairs={{0,2},{1,3},{2,0},{3,1},{4,6},{5,7},{6,4},{7,5},{8,10},{9,11},{10,... | collective-permute-start | bytes 294920 | tf_op jit(solution)/shard_map/ppermute | solution.py:831
  15.3 8.5 %collective-permute-start = (bf16[192,256]{1,0:T(8,128)(2,1)}, bf16[192,256]{1,0:T(8,128)(2,1)S(1)}, u32[]{:S(2)}, u32[]{:S(2)}) collective-permute-start(bf16[192,256]{1,0:T(8,128)(2,1)} %get-tuple-element.82), channel_id=1, source_target_pairs={{0,1},{1,0},{2,3},{3,2},{4,5},{5,4},{6,7},{7,6},{8,9},{9,8},{10,11... | collective-permute-start | bytes 294920 | tf_op jit(solution)/shard_map/ppermute | solution.py:831
  24.7 9.2 %collective-permute-start.8 = (bf16[240,384]{1,0:T(8,128)(2,1)}, bf16[240,384]{1,0:T(8,128)(2,1)S(1)}, u32[]{:S(2)}, u32[]{:S(2)}) collective-permute-start(bf16[240,384]{1,0:T(8,128)(2,1)} %get-tuple-element.85), channel_id=1, source_target_pairs={{0,3},{1,2},{2,1},{3,0},{4,7},{5,6},{6,5},{7,4},{8,11},{9,10},{10,... | collective-permute-start | bytes 552968 | tf_op jit(solution)/shard_map/ppermute | solution.py:831
  27.3 18.3 %collective-permute-start.5 = (bf16[4,192,256]{2,1,0:T(8,128)(2,1)S(1)}, bf16[4,192,256]{2,1,0:T(8,128)(2,1)S(1)}, u32[]{:S(2)}, u32[]{:S(2)}) collective-permute-start(bf16[4,192,256]{2,1,0:T(8,128)(2,1)S(1)} %pad_maximum_fusion.1.p0), channel_id=1, source_target_pairs={{0,24},{4,28},{8,16},{12,20},{16,8},{20,12},{24,0},{28,4},{1,25},{... | collective-permute-start | bytes 1179656 | tf_op jit(solution)/shard_map/ppermute | solution.py:835
  29.9 16.6 %collective-permute-start.4 = (bf16[4,192,256]{2,1,0:T(8,128)(2,1)S(1)}, bf16[4,192,256]{2,1,0:T(8,128)(2,1)S(1)}, u32[]{:S(2)}, u32[]{:S(2)}) collective-permute-start(bf16[4,192,256]{2,1,0:T(8,128)(2,1)S(1)} %pad_maximum_fusion.1.p0), channel_id=1, source_target_pairs={{0,16},{4,20},{8,24},{12,28},{16,0},{20,4},{24,8},{28,12},{1,17},{... | collective-permute-start | bytes 1179656 | tf_op jit(solution)/shard_map/ppermute | solution.py:835
  30.2 16.3 %collective-permute-start.3 = (bf16[4,192,256]{2,1,0:T(8,128)(2,1)S(1)}, bf16[4,192,256]{2,1,0:T(8,128)(2,1)S(1)}, u32[]{:S(2)}, u32[]{:S(2)}) collective-permute-start(bf16[4,192,256]{2,1,0:T(8,128)(2,1)S(1)} %pad_maximum_fusion.1.p0), channel_id=1, source_target_pairs={{0,8},{4,12},{8,0},{12,4},{16,24},{20,28},{24,16},{28,20},{1,9},{5... | collective-permute-start | bytes 1179656 | tf_op jit(solution)/shard_map/ppermute | solution.py:835
  30.8 11.6 %collective-permute-start.7 = (bf16[240,384]{1,0:T(8,128)(2,1)}, bf16[240,384]{1,0:T(8,128)(2,1)S(1)}, u32[]{:S(2)}, u32[]{:S(2)}) collective-permute-start(bf16[240,384]{1,0:T(8,128)(2,1)} %get-tuple-element.85), channel_id=1, source_target_pairs={{0,2},{1,3},{2,0},{3,1},{4,6},{5,7},{6,4},{7,5},{8,10},{9,11},{10,... | collective-permute-start | bytes 552968 | tf_op jit(solution)/shard_map/ppermute | solution.py:831
  33.9 10.6 %collective-permute-start.6 = (bf16[240,384]{1,0:T(8,128)(2,1)}, bf16[240,384]{1,0:T(8,128)(2,1)S(1)}, u32[]{:S(2)}, u32[]{:S(2)}) collective-permute-start(bf16[240,384]{1,0:T(8,128)(2,1)} %get-tuple-element.85), channel_id=1, source_target_pairs={{0,1},{1,0},{2,3},{3,2},{4,5},{5,4},{6,7},{7,6},{8,9},{9,8},{10,11... | collective-permute-start | bytes 552968 | tf_op jit(solution)/shard_map/ppermute | solution.py:831
  48.2 33.6 %collective-permute-start.15 = (bf16[4,240,384]{2,1,0:T(8,128)(2,1)S(1)}, bf16[4,240,384]{2,1,0:T(8,128)(2,1)S(1)}, u32[]{:S(2)}, u32[]{:S(2)}) collective-permute-start(bf16[4,240,384]{2,1,0:T(8,128)(2,1)S(1)} %pad_maximum_fusion.p0), channel_id=1, source_target_pairs={{0,24},{4,28},{8,16},{12,20},{16,8},{20,12},{24,0},{28,4},{1,25},{... | collective-permute-start | bytes 2211848 | tf_op jit(solution)/shard_map/ppermute | solution.py:835
  50.3 33.1 %collective-permute-start.14 = (bf16[4,240,384]{2,1,0:T(8,128)(2,1)S(1)}, bf16[4,240,384]{2,1,0:T(8,128)(2,1)S(1)}, u32[]{:S(2)}, u32[]{:S(2)}) collective-permute-start(bf16[4,240,384]{2,1,0:T(8,128)(2,1)S(1)} %pad_maximum_fusion.p0), channel_id=1, source_target_pairs={{0,16},{4,20},{8,24},{12,28},{16,0},{20,4},{24,8},{28,12},{1,17},{... | collective-permute-start | bytes 2211848 | tf_op jit(solution)/shard_map/ppermute | solution.py:835
  51.5 32.0 %collective-permute-start.13 = (bf16[4,240,384]{2,1,0:T(8,128)(2,1)S(1)}, bf16[4,240,384]{2,1,0:T(8,128)(2,1)S(1)}, u32[]{:S(2)}, u32[]{:S(2)}) collective-permute-start(bf16[4,240,384]{2,1,0:T(8,128)(2,1)S(1)} %pad_maximum_fusion.p0), channel_id=1, source_target_pairs={{0,8},{4,12},{8,0},{12,4},{16,24},{20,28},{24,16},{28,20},{1,9},{5... | collective-permute-start | bytes 2211848 | tf_op jit(solution)/shard_map/ppermute | solution.py:835
  145.6 34.2 %collective-permute-start.23 = (bf16[4,240,384]{2,1,0:T(8,128)(2,1)}, bf16[4,240,384]{2,1,0:T(8,128)(2,1)S(1)}, u32[]{:S(2)}, u32[]{:S(2)}) collective-permute-start(bf16[4,240,384]{2,1,0:T(8,128)(2,1)} %get-tuple-element.148), channel_id=1, source_target_pairs={{0,24},{4,28},{8,16},{12,20},{16,8},{20,12},{24,0},{28,4},{1,25},{... | collective-permute-start | bytes 2211848 | tf_op jit(solution)/shard_map/ppermute | solution.py:835
  147.3 33.7 %collective-permute-start.22 = (bf16[4,240,384]{2,1,0:T(8,128)(2,1)}, bf16[4,240,384]{2,1,0:T(8,128)(2,1)S(1)}, u32[]{:S(2)}, u32[]{:S(2)}) collective-permute-start(bf16[4,240,384]{2,1,0:T(8,128)(2,1)} %get-tuple-element.149), channel_id=1, source_target_pairs={{0,16},{4,20},{8,24},{12,28},{16,0},{20,4},{24,8},{28,12},{1,17},{... | collective-permute-start | bytes 2211848 | tf_op jit(solution)/shard_map/ppermute | solution.py:835
  148.6 32.5 %collective-permute-start.21 = (bf16[4,240,384]{2,1,0:T(8,128)(2,1)S(1)}, bf16[4,240,384]{2,1,0:T(8,128)(2,1)S(1)}, u32[]{:S(2)}, u32[]{:S(2)}) collective-permute-start(bf16[4,240,384]{2,1,0:T(8,128)(2,1)S(1)} %get-tuple-element.150), channel_id=1, source_target_pairs={{0,8},{4,12},{8,0},{12,4},{16,24},{20,28},{24,16},{28,20},{1,9},{5... | collective-permute-start | bytes 2211848 | tf_op jit(solution)/shard_map/ppermute | solution.py:835
  182.0 9.4 %collective-permute-start.26 = (bf16[240,384]{1,0:T(8,128)(2,1)S(1)}, bf16[240,384]{1,0:T(8,128)(2,1)S(1)}, u32[]{:S(2)}, u32[]{:S(2)}) collective-permute-start(bf16[240,384]{1,0:T(8,128)(2,1)S(1)} %get-tuple-element.156), channel_id=1, source_target_pairs={{0,3},{1,2},{2,1},{3,0},{4,7},{5,6},{6,5},{7,4},{8,11},{9,10},{10,... | collective-permute-start | bytes 552968 | tf_op jit(solution)/shard_map/ppermute | solution.py:831
  183.5 19.6 %collective-permute-start.25 = (bf16[240,384]{1,0:T(8,128)(2,1)}, bf16[240,384]{1,0:T(8,128)(2,1)}, u32[]{:S(2)}, u32[]{:S(2)}) collective-permute-start(bf16[240,384]{1,0:T(8,128)(2,1)} %get-tuple-element.157), channel_id=1, source_target_pairs={{0,2},{1,3},{2,0},{3,1},{4,6},{5,7},{6,4},{7,5},{8,10},{9,11},{10,... | collective-permute-start | bytes 552968 | tf_op jit(solution)/shard_map/ppermute | solution.py:831
  184.9 18.2 %collective-permute-start.24 = (bf16[240,384]{1,0:T(8,128)(2,1)}, bf16[240,384]{1,0:T(8,128)(2,1)}, u32[]{:S(2)}, u32[]{:S(2)}) collective-permute-start(bf16[240,384]{1,0:T(8,128)(2,1)} %get-tuple-element.158), channel_id=1, source_target_pairs={{0,1},{1,0},{2,3},{3,2},{4,5},{5,4},{6,7},{7,6},{8,9},{9,8},{10,11... | collective-permute-start | bytes 552968 | tf_op jit(solution)/shard_map/ppermute | solution.py:831
  187.7 15.5 %collective-permute-start.30 = (bf16[4,192,256]{2,1,0:T(8,128)(2,1)}, bf16[4,192,256]{2,1,0:T(8,128)(2,1)}, u32[]{:S(2)}, u32[]{:S(2)}) collective-permute-start(bf16[4,192,256]{2,1,0:T(8,128)(2,1)} %get-tuple-element.153), channel_id=1, source_target_pairs={{0,24},{4,28},{8,16},{12,20},{16,8},{20,12},{24,0},{28,4},{1,25},{... | collective-permute-start | bytes 1179656 | tf_op jit(solution)/shard_map/ppermute | solution.py:835
  189.4 18.6 %collective-permute-start.29 = (bf16[4,192,256]{2,1,0:T(8,128)(2,1)S(1)}, bf16[4,192,256]{2,1,0:T(8,128)(2,1)}, u32[]{:S(2)}, u32[]{:S(2)}) collective-permute-start(bf16[4,192,256]{2,1,0:T(8,128)(2,1)S(1)} %get-tuple-element.154), channel_id=1, source_target_pairs={{0,16},{4,20},{8,24},{12,28},{16,0},{20,4},{24,8},{28,12},{1,17},{... | collective-permute-start | bytes 1179656 | tf_op jit(solution)/shard_map/ppermute | solution.py:835
  191.4 16.5 %collective-permute-start.28 = (bf16[4,192,256]{2,1,0:T(8,128)(2,1)S(1)}, bf16[4,192,256]{2,1,0:T(8,128)(2,1)}, u32[]{:S(2)}, u32[]{:S(2)}) collective-permute-start(bf16[4,192,256]{2,1,0:T(8,128)(2,1)S(1)} %get-tuple-element.155), channel_id=1, source_target_pairs={{0,8},{4,12},{8,0},{12,4},{16,24},{20,28},{24,16},{28,20},{1,9},{5... | collective-permute-start | bytes 1179656 | tf_op jit(solution)/shard_map/ppermute | solution.py:835
  214.1 6.7 %collective-permute-start.33 = (bf16[192,256]{1,0:T(8,128)(2,1)S(1)}, bf16[192,256]{1,0:T(8,128)(2,1)S(1)}, u32[]{:S(2)}, u32[]{:S(2)}) collective-permute-start(bf16[192,256]{1,0:T(8,128)(2,1)S(1)} %get-tuple-element.160), channel_id=1, source_target_pairs={{0,3},{1,2},{2,1},{3,0},{4,7},{5,6},{6,5},{7,4},{8,11},{9,10},{10,... | collective-permute-start | bytes 294920 | tf_op jit(solution)/shard_map/ppermute | solution.py:831
  215.1 9.5 %collective-permute-start.32 = (bf16[192,256]{1,0:T(8,128)(2,1)S(1)}, bf16[192,256]{1,0:T(8,128)(2,1)S(1)}, u32[]{:S(2)}, u32[]{:S(2)}) collective-permute-start(bf16[192,256]{1,0:T(8,128)(2,1)S(1)} %get-tuple-element.161), channel_id=1, source_target_pairs={{0,2},{1,3},{2,0},{3,1},{4,6},{5,7},{6,4},{7,5},{8,10},{9,11},{10,... | collective-permute-start | bytes 294920 | tf_op jit(solution)/shard_map/ppermute | solution.py:831
  (28 other events, 173.5 us)
Sparse Core Ops, SparseCore 0:
  210.1 25.8 all-gather.3

commit v5 on v4

--- a/solution.py
+++ b/solution.py
@@ -287,9 +287,10 @@
                         rows = pl.ds(pl.multiple_of(192 * n + 48 * r, 48), 48)
                         source, target = pl.ds(192, 48), wo.at[g, rows, :]
                     elif part == 1:
-                        source, target = pl.ds(0, 96), wi.at[slot, at(n, 96), :]
+                        source, target = pl.ds(0, 96), wi.at[slot >> 1, at(n, 96), at(slot & 1, AH)]
                     else:
-                        source, target = pl.ds(96, 96), wu.at[4 * g + n, at(r, 96), :]
+                        rows = at(4 * (n & 1) + r, 96)
+                        source, target = pl.ds(96, 96), wu.at[2 * g + (n >> 1), rows, :]
                     pltpu.make_async_copy(piece.at[k, source, :], target, sems.at[part]).start()
 
                 loop(4, one)
@@ -315,14 +316,18 @@
 
     loop(3, mix)
 
+    def several(i):
+        return [at(4 * i + k, 32) for k in range(4)]
+
     def norm_one(i):
-        for half in range(2):
-            rows = at(2 * i + half, 32)
-            values = res[rows, :]
+        spots = several(i)
+        done = []
+        for values in [res[rows, :] for rows in spots]:
             center = values - jnp.mean(values, axis=1, keepdims=True)
             scale = lax.rsqrt(jnp.mean(center * center, axis=1, keepdims=True) + EPS)
             hat = center * scale
-            first = hat * gain_one + bias_one
+            done.append((hat, scale, hat * gain_one + bias_one))
+        for rows, (hat, scale, first) in zip(spots, done):
             xhat[rows, :] = hat
             rstd[rows, :] = jnp.broadcast_to(scale, (32, 128))
             res[rows, :] = first
@@ -330,25 +335,25 @@
             grouped[0, rows, :] = short[:, 0:AH]
             grouped[1, rows, :] = short[:, AH:D]
 
-    loop(12, norm_one)
+    loop(6, norm_one)
     pltpu.make_async_copy(wi, wi, sems.at[1]).wait()
     pltpu.make_async_copy(wu, wu, sems.at[2]).wait()
 
     def hidden(t, target):
         b = lax.div(t, 3)
-        target[...] = nn(grouped[b >> 2, at(t - 3 * b, 256), :], wi[b])
+        target[...] = nn(grouped[b >> 1, at(t - 3 * b, 256), :], wi[b])
 
     def outward(t):
         b = lax.div(t, 3)
         rows = at(t - 3 * b, 256)
-        ffn[b >> 2, rows, :] += nn(active[b, rows, :], wu[b])
+        ffn[b >> 1, rows, :] += nn(active[b, rows, :], wu[b])
 
     def act(t, source):
         b = lax.div(t, 3)
         m = t - 3 * b
-        for part in range(8):
-            values = source[32 * part : 32 * part + 32, :]
-            rows = pl.ds(pl.multiple_of(m * 256 + 32 * part, 32), 32)
+        for part in range(16):
+            values = source[16 * part : 16 * part + 16, :]
+            rows = pl.ds(pl.multiple_of(m * 256 + 16 * part, 16), 16)
             cdf, density = gelu_parts(values)
             active[b, rows, :] = (values * cdf).astype(BF)
             slope[b, rows, :] = cdf + values * density
@@ -360,42 +365,53 @@
         hidden(t + 1, hid_b)
         act(t, hid_a)
         outward(t)
-        hidden(jnp.minimum(t + 2, 23), hid_a)
+        hidden(jnp.minimum(t + 2, 11), hid_a)
         act(t + 1, hid_b)
 
     hidden(jnp.int32(0), hid_a)
     pair(jnp.int32(0), True)
-    loop(11, lambda u: pair(u + 1))
-    outward(jnp.int32(23))
+    loop(5, lambda u: pair(u + 1))
+    outward(jnp.int32(11))
     for copy in cots:
         copy.wait()
 
     def norm_two(i):
-        limit = jnp.where(i < 8, llen[0], slen[jnp.clip((i - 8) >> 1, 0, 1)])
-        base = jnp.where(i < 8, 64 * i, 64 * (i & 1))
-        for half in range(2):
-            rows = at(2 * i + half, 32)
-            values = jnp.concatenate([ffn[0, rows, :], ffn[1, rows, :]], axis=1) + res[rows, :]
+        limit = jnp.where(i < 4, llen[0], slen[jnp.clip(i - 4, 0, 1)])
+        base = jnp.where(i < 4, 128 * i, 0)
+        spots = several(i)
+        loaded = [
+            (
+                jnp.concatenate([ffn[0, rows, :], ffn[1, rows, :]], axis=1) + res[rows, :],
+                cot[rows, :].astype(F32),
+            )
+            for rows in spots
+        ]
+        done = []
+        for k, (values, up) in enumerate(loaded):
             center = values - jnp.mean(values, axis=1, keepdims=True)
             scale = lax.rsqrt(jnp.mean(center * center, axis=1, keepdims=True) + EPS)
             hat = center * scale
-            out[rows, :] = (hat * gain_two + bias_two).astype(BF)
-            live = base + 32 * half + iota((32, D), 0) < limit
-            up = jnp.where(live, cot[rows, :].astype(F32), 0.0)
-            sums[16:24, :] += fold(up * hat)
-            sums[24:32, :] += fold(up)
+            result = (hat * gain_two + bias_two).astype(BF)
+            live = base + 32 * k + iota((32, D), 0) < limit
+            up = jnp.where(live, up, 0.0)
+            gain_part, bias_part = fold(up * hat), fold(up)
             up = up * gain_two
             grad = scale * (
                 up
                 - jnp.mean(up, axis=1, keepdims=True)
                 - hat * jnp.mean(up * hat, axis=1, keepdims=True)
             )
+            done.append((result, gain_part, bias_part, grad))
+        for rows, (result, _, _, grad) in zip(spots, done):
+            out[rows, :] = result
             res[rows, :] = grad
             short = grad.astype(BF)
             gffn[0, rows, :] = short[:, 0:AH]
             gffn[1, rows, :] = short[:, AH:D]
-
-    loop(12, norm_two)
+        sums[16:24, :] += done[0][1] + done[1][1] + done[2][1] + done[3][1]
+        sums[24:32, :] += done[0][2] + done[1][2] + done[2][2] + done[3][2]
+
+    loop(6, norm_two)
     stores = [
         start_copy(out.at[0:LONG], ol, sems.at[3]), start_copy(out.at[LONG:ROWS], os, sems.at[4])
     ]
@@ -404,18 +420,21 @@
     def slopes(b, target):
         for part in range(6):
             rows = slice(128 * part, 128 * part + 128)
-            back = nt(gffn[b >> 2, rows, :], wu[b])
+            back = nt(gffn[b >> 1, rows, :], wu[b])
             target[rows, :] = (back * slope[b, rows, :]).astype(BF)
 
     def gradients(b, source):
-        g, n = b >> 2, b & 3
+        g = b >> 1
         gouter[b] = tn(active[b], gffn[g]).astype(BF)
         ginner[b] = tn(grouped[g], source[...]).astype(BF)
         ffn[g] += nt(source[...], wi[b])
-        for w in range(4):
-            rows = pl.ds(96 * w, 96)
-            ship(keep, send, place, 4 * g + w, n, pl.ds(96, 96), gouter.at[b, rows, :], sems.at[0])
-            ship(keep, send, place, b, w, pl.ds(0, 96), ginner.at[b, rows, :], sems.at[1])
+        for half in range(2):
+            n = 2 * (b & 1) + half
+            for w in range(4):
+                outer = gouter.at[b, pl.ds(AH * half + 96 * w, 96), :]
+                ship(keep, send, place, 4 * g + w, n, pl.ds(96, 96), outer, sems.at[0])
+                inner = ginner.at[b, pl.ds(96 * w, 96), pl.ds(AH * half, AH)]
+                ship(keep, send, place, 2 * b + half, w, pl.ds(0, 96), inner, sems.at[1])
 
     slopes(jnp.int32(0), ghid_a)
 
@@ -423,28 +442,37 @@
         b = 2 * u
         slopes(b + 1, ghid_b)
         gradients(b, ghid_a)
-        slopes(jnp.minimum(b + 2, 7), ghid_a)
+        slopes(jnp.minimum(b + 2, 3), ghid_a)
         gradients(b + 1, ghid_b)
 
-    loop(4, contract)
+    loop(2, contract)
 
     def norm_one_back(i):
-        for half in range(2):
-            rows = at(2 * i + half, 32)
-            up = res[rows, :] + jnp.concatenate([ffn[0, rows, :], ffn[1, rows, :]], axis=1)
-            hat = xhat[rows, :]
-            sums[0:8, :] += fold(up * hat)
-            sums[8:16, :] += fold(up)
+        spots = several(i)
+        loaded = [
+            (
+                res[rows, :] + jnp.concatenate([ffn[0, rows, :], ffn[1, rows, :]], axis=1),
+                xhat[rows, :], rstd[rows, 0:1],
+            )
+            for rows in spots
+        ]
+        done = []
+        for up, hat, scale in loaded:
+            gain_part, bias_part = fold(up * hat), fold(up)
             up = up * gain_one
-            grad = rstd[rows, 0:1] * (
+            grad = scale * (
                 up
                 - jnp.mean(up, axis=1, keepdims=True)
                 - hat * jnp.mean(up * hat, axis=1, keepdims=True)
             )
+            done.append((gain_part, bias_part, grad))
+        for rows, (_, _, grad) in zip(spots, done):
             gone[rows, :] = grad
             gproj[rows, :] = grad.astype(BF)
-
-    loop(12, norm_one_back)
+        sums[0:8, :] += done[0][0] + done[1][0] + done[2][0] + done[3][0]
+        sums[8:16, :] += done[0][1] + done[1][1] + done[2][1] + done[3][1]
+
+    loop(6, norm_one_back)
     stores.append(start_copy(gone, gone_any, sems.at[5]))
     for k in range(4):
         gvec[k : k + 1, :] = jnp.sum(sums[8 * k : 8 * k + 8, :], axis=0, keepdims=True)
@@ -721,12 +749,14 @@
                 mixer[96:192, 128:256] = left[96:192, :].astype(BF)
 
 
-def unpack_ffn(packed, inner, outer, out):
-    for w in range(SLOTS):
-        g, r = w // 4, w % 4
-        inner[g, :, AH * r : AH * r + AH] = packed[w, 0:96, :].astype(F32)
-        outer[g, 96 * r : 96 * r + 96, :] = packed[w, 96:192, :].astype(F32)
-        out[48 * r : 48 * r + 48, AH * g : AH * g + AH] = packed[w, 192:240, :].astype(F32)
+def unpack_ffn(place, p0, p1, p2, p3, p4, p5, p6, p7, inner, outer, out):
+    for core, pieces in enumerate(((p0, p1, p2, p3), (p4, p5, p6, p7))):
+        for chip, piece in enumerate(pieces):
+            slot = slot_of(place[0], core, chip)
+            g, r = slot >> 2, slot & 3
+            inner[g, :, at(r, AH)] = piece[0:96, :].astype(F32)
+            outer[g, at(r, 96), :] = piece[96:192, :].astype(F32)
+            out[at(r, 48), at(g, AH)] = piece[192:240, :].astype(F32)
 
 
 def unpack_mixer(packed, qkv, depth, point, kernel, convout, g1, b1, g2, b2):
@@ -784,12 +814,12 @@
         ((ROWS, D), F32), ((ROWS, D), BF), ((8, D), F32),
     ]
     scratch = [
-        ((2, D, AH), BF), ((8, AH, AH), BF), ((8, AH, AH), BF), ((ROWS, D), BF), ((ROWS, D), BF),
+        ((2, D, AH), BF), ((4, AH, D), BF), ((4, D, AH), BF), ((ROWS, D), BF), ((ROWS, D), BF),
         ((ROWS, D), BF), ((ROWS, D), BF), ((ROWS, D), F32), ((ROWS, D), F32),
-        ((2, ROWS, AH), BF), ((2, ROWS, AH), BF), ((8, ROWS, AH), BF), ((8, ROWS, AH), F32),
-        ((2, ROWS, AH), F32), ((ROWS, 128), F32), ((256, AH), F32), ((256, AH), F32),
-        ((ROWS, AH), BF), ((ROWS, AH), BF), ((ROWS, D), BF), ((2, ROWS, AH), BF),
-        ((8, AH, AH), BF), ((8, AH, AH), BF), ((ROWS, D), F32), ((ROWS, D), BF), ((32, D), F32),
+        ((2, ROWS, AH), BF), ((2, ROWS, AH), BF), ((4, ROWS, D), BF), ((4, ROWS, D), F32),
+        ((2, ROWS, AH), F32), ((ROWS, 128), F32), ((256, D), F32), ((256, D), F32),
+        ((ROWS, D), BF), ((ROWS, D), BF), ((ROWS, D), BF), ((2, ROWS, AH), BF),
+        ((4, AH, D), BF), ((4, D, AH), BF), ((ROWS, D), F32), ((ROWS, D), BF), ((32, D), F32),
     ]
     return call(
         ffn_both, [SMEM] * 3 + [VMEM] + [ANY] * 12, outs,
@@ -918,8 +948,9 @@
     gb = reduce_chips(gb[0], gb_sent)
     gb = lax.psum(total(gb[0], send_narrow(gb)), "hi")
     inner, outer, out = call(
-        unpack_ffn, [VMEM], [((2, 96, 4 * AH), F32), ((2, AH, AH), F32), ((192, D), F32)],
-        ([],), 10**9, gather_wide(ga),
+        unpack_ffn, [SMEM] + [VMEM] * 8,
+        [((2, 96, 4 * AH), F32), ((2, AH, AH), F32), ((192, D), F32)],
+        ([],), 10**9, place, *gather_cores(gather_chips(ga)),
     )
     outs = [
         ((192, 3 * AH), F32), ((TAPS, 192), F32), ((192, AH), F32), ((54, 96), F32), ((192, AH), F32),

time: 250 us -> 229 us (0.916)
  between operations: 14.9 us -> 1.62 us
  Pallas kernels: 124 us -> 114 us
  starting transfers between devices: 41.1 us -> 44.6 us
    pallas_call x7, Pallas kernels: 124 us -> 114 us  [call(): pl.pallas_call(kernel, out_shape=[jax.ShapeDtypeStruct(s, d) for s, d in...]
    ppermute x12, waiting for transfers between devices: 24.6 us -> 20.4 us  [far(): return lax.ppermute(values, 'narrow', [(i, i ^ bit) for i in range(4)])]
    ppermute x22 -> x29, starting transfers between devices: 17.1 us -> 20.7 us  [near(): return lax.ppermute(values, 'wide', [(i, i ^ bit) for i in range(SLOTS)])]
    ppermute x22 -> x29, waiting for transfers between devices: 18.4 us -> 21.5 us  [near(): return lax.ppermute(values, 'wide', [(i, i ^ bit) for i in range(SLOTS)])]
  transfers between devices with their start and end apart: 35 -> 41, of which waited for: 18 -> 18; matrix products, arithmetic and copies ran while one was open for 2% -> 2% of each run, Pallas kernels for 29% -> 32%
where the time goes in v5:
time: 229 us; the launch traced here: 228 us
  Pallas kernels  114 us (50%)
  starting transfers between devices  44.6 us (19%)
  waiting for transfers between devices  41.9 us (18%)
  other arithmetic  12.1 us (5%)
  blocking collectives  10.5 us (5%)
  local copies, waits for them, and re-layouts  3.56 us (2%)
    pallas_call x7, Pallas kernels, call(): pl.pallas_call(kernel, out_shape=[jax.ShapeDtypeStruct(s, d) for s, d in...  114 us
    ppermute x12, starting transfers between devices, far(): return lax.ppermute(values, 'narrow', [(i, i ^ bit) for i in range(4)])  23.9 us
    ppermute x29, waiting for transfers between devices, near(): return lax.ppermute(values, 'wide', [(i, i ^ bit) for i in range(SLOTS)])  21.5 us
    ppermute x29, starting transfers between devices, near(): return lax.ppermute(values, 'wide', [(i, i ^ bit) for i in range(SLOTS)])  20.7 us
    ppermute x12, waiting for transfers between devices, far(): return lax.ppermute(values, 'narrow', [(i, i ^ bit) for i in range(4)])  20.4 us
    all_gather x1, blocking collectives, gather_wide(): return lax.all_gather(parts, 'wide', axis=0, tiled=False)  10.5 us
    convert_element_type x4, other arithmetic, total(): return result.astype(BF)  7.11 us
  transfers between devices with their start and end apart: 41, of which 18 were waited for; matrix products, arithmetic and copies ran while one was open for 2% of the time, Pallas kernels for 32%

profile of v5, /device:TPU:0, one launch (start us, length us, event | category | flops | bytes accessed | tf_op | source)
XLA Modules:
  0.0 227.9 jit_solution(6556298015210892569)
XLA Ops:
  1.3 2.4 %pack.1 = (bf16[192,256]{1,0:T(8,128)(2,1)}, bf16[240,384]{1,0:T(8,128)(2,1)}) custom-call(s32[2]{0:T(128)} %pad_add_fusion.place, bf16[192,1152]{1,0:T(8,128)(2,1)} %qkv.1, bf16[9,192]{1,0:T(8,128)(2,1)} %depth.1, bf16[192,384]{1,0:T(8,128)(2,1)} %point.1, bf16[54,96]{1,0:T(8,128)(2,1)} %bitcast.72, bf16[192,384]{1,0:T(8,128)(2,1)} %convout.1, ...), custom_call_target="tpu_custom_call" | custom-call | flops 1000000000 | bytes 1048576 | tf_op jit(solution)/shard_map/pack/pallas_call | solution.py:784
  3.7 5.0 %collective-permute-start.2 = (bf16[192,256]{1,0:T(8,128)(2,1)}, bf16[192,256]{1,0:T(8,128)(2,1)S(1)}, u32[]{:S(2)}, u32[]{:S(2)}) collective-permute-start(bf16[192,256]{1,0:T(8,128)(2,1)} %get-tuple-element.82), channel_id=1, source_target_pairs={{0,3},{1,2},{2,1},{3,0},{4,7},{5,6},{6,5},{7,4},{8,11},{9,10},{10,... | collective-permute-start | bytes 294920 | tf_op jit(solution)/shard_map/ppermute | solution.py:861
  9.3 3.3 %collective-permute-done.2 = bf16[192,256]{1,0:T(8,128)(2,1)S(1)} collective-permute-done((bf16[192,256]{1,0:T(8,128)(2,1)}, bf16[192,256]{1,0:T(8,128)(2,1)S(1)}, u32[]{:S(2)}, u32[]{:S(2)}) %collective-permute-start.2) | collective-permute-done | bytes 98336 | tf_op jit(solution)/shard_map/ppermute | solution.py:861
  12.6 4.6 %collective-permute-done.1 = bf16[192,256]{1,0:T(8,128)(2,1)S(1)} collective-permute-done((bf16[192,256]{1,0:T(8,128)(2,1)}, bf16[192,256]{1,0:T(8,128)(2,1)S(1)}, u32[]{:S(2)}, u32[]{:S(2)}) %collective-permute-start.1) | collective-permute-done | bytes 98336 | tf_op jit(solution)/shard_map/ppermute | solution.py:861
  18.2 2.6 %collective-permute-start.8 = (bf16[240,384]{1,0:T(8,128)(2,1)}, bf16[240,384]{1,0:T(8,128)(2,1)S(1)}, u32[]{:S(2)}, u32[]{:S(2)}) collective-permute-start(bf16[240,384]{1,0:T(8,128)(2,1)} %get-tuple-element.85), channel_id=1, source_target_pairs={{0,3},{1,2},{2,1},{3,0},{4,7},{5,6},{6,5},{7,4},{8,11},{9,10},{10,... | collective-permute-start | bytes 552968 | tf_op jit(solution)/shard_map/ppermute | solution.py:861
  20.7 2.6 %collective-permute-start.5 = (bf16[4,192,256]{2,1,0:T(8,128)(2,1)S(1)}, bf16[4,192,256]{2,1,0:T(8,128)(2,1)S(1)}, u32[]{:S(2)}, u32[]{:S(2)}) collective-permute-start(bf16[4,192,256]{2,1,0:T(8,128)(2,1)S(1)} %pad_maximum_fusion.1.p0), channel_id=1, source_target_pairs={{0,24},{4,28},{8,16},{12,20},{16,8},{20,12},{24,0},{28,4},{1,25},{... | collective-permute-start | bytes 1179656 | tf_op jit(solution)/shard_map/ppermute | solution.py:865
  24.2 3.1 %collective-permute-done.8 = bf16[240,384]{1,0:T(8,128)(2,1)S(1)} collective-permute-done((bf16[240,384]{1,0:T(8,128)(2,1)}, bf16[240,384]{1,0:T(8,128)(2,1)S(1)}, u32[]{:S(2)}, u32[]{:S(2)}) %collective-permute-start.8) | collective-permute-done | bytes 184352 | tf_op jit(solution)/shard_map/ppermute | solution.py:861
  27.3 6.9 %collective-permute-start.6 = (bf16[240,384]{1,0:T(8,128)(2,1)}, bf16[240,384]{1,0:T(8,128)(2,1)S(1)}, u32[]{:S(2)}, u32[]{:S(2)}) collective-permute-start(bf16[240,384]{1,0:T(8,128)(2,1)} %get-tuple-element.85), channel_id=1, source_target_pairs={{0,1},{1,0},{2,3},{3,2},{4,5},{5,4},{6,7},{7,6},{8,9},{9,8},{10,11... | collective-permute-start | bytes 552968 | tf_op jit(solution)/shard_map/ppermute | solution.py:861
  35.8 2.2 collective-permute-done.6
  41.7 2.1 collective-permute-start.15
  46.5 28.8 %mixer_forward.1 = (bf16[768,768]{1,0:T(8,128)(2,1)}, bf16[768,1152]{1,0:T(8,128)(2,1)}, bf16[6,512,512]{2,1,0:T(8,128)(2,1)}, bf16[2,6,128,128]{3,2,1,0:T(8,128...) custom-call(s32[2]{0:T(128)} %pad_add_fusion.place, ...), custom_call_target="tpu_custom_call" | custom-call | flops 30000001024 | bytes 1048576 | tf_op jit(solution)/shard_map/mixer_forward/pallas_call | solution.py:784
  83.3 35.8 %ffn_both.1 = (bf16[512,768]{1,0:T(8,128)(2,1)}, bf16[256,768]{1,0:T(8,128)(2,1)}, bf16[4,4,240,384]{3,2,1,0:T(8,128)(2,1)}, bf16[4,4,240,384]{3,2,1,0:T(8,128)(...) custom-call(s32[2]{0:T(128)} %pad_add_fusion.place, s32[1]{0:T(128)S(6)} %copy.34.llen, ...), custom_call_target="tpu_custom_call" | custom-call | flops 60000002048 | bytes 1048576 | tf_op jit(solution)/shard_map/ffn_both/pallas_call | solution.py:784
  119.3 5.5 %collective-permute-done.20 = bf16[4,4,240,384]{3,2,1,0:T(8,128)(2,1)S(1)} collective-permute-done((bf16[4,4,240,384]{3,2,1,0:T(8,128)(2,1)}, bf16[4,4,240,384]{3,2,1,0:T(8,128)(2,1)S(1)}, u32[]{:S(2)}, u32[]{:S(2)}) %collective-permute-start.20) | collective-permute-done | bytes 2949152 | tf_op jit(solution)/shard_map/ppermute | solution.py:865
  124.7 3.6 %fusion.3 = (bf16[4,240,384]{2,1,0:T(8,128)(2,1)}, bf16[4,240,384]{2,1,0:T(8,128)(2,1)}, bf16[4,240,384]{2,1,0:T(8,128)(2,1)S(1)}, bf16[4,240,384]{2,1,0:T(8,128)(2,1)S(1)}) fusion(bf16[4,4,240,384]{3,2,1,0:T(8,128)(2,1)S(1)} %collective-permute-done.20, bf16[4,4,240,384]{3,2,1,0:T(8,128)(2,1)} %get-tuple-element.102), kind=kLoop, calls=%fused_computation.11 | loop fusion | flops 5898240 | bytes 8847360 | tf_op jit(solution)/shard_map/convert_element_type | solution.py:884
  128.4 1.7 collective-permute-start.23
  131.9 30.7 %mixer_backward.1 = (bf16[4,4,192,256]{3,2,1,0:T(8,128)(2,1)}, bf16[4,4,192,256]{3,2,1,0:T(8,128)(2,1)}, bf16[768,1536]{1,0:T(8,128)(2,1)}, f32[800,768]{1,0:T(8,128)}) custom-call(s32[2]{0:T(128)} %pad_add_fusion.place, f32[24,768]{1,0:T(8,128)} %get-tuple-element.90.vec, f32[8,768]{1,0:T(8,128)} %get-tuple-element.105.gvec, ...), custom_call_target="tpu_custom_call" | custom-call | flops 40000000000 | bytes 1048576 | tf_op jit(solution)/shard_map/mixer_backward/pallas_call | solution.py:784
  175.6 10.3 %input_gradient.1 = (bf16[512,768]{1,0:T(8,128)(2,1)}, bf16[256,768]{1,0:T(8,128)(2,1)}) custom-call(s32[2]{0:T(128)} %pad_add_fusion.place, s32[1]{0:T(128)S(6)} %copy.34.llen, s32[2]{0:T(128)} %slen.5, f32[24,768]{1,0:T(8,128)} %get-tuple-element.90.vec, bf16[768,1536]{1,0:T(8,128)(2,1)} %get-tuple-element.123.grads_any, ...), custom_call_target="tpu_custom_call" | custom-call | flops 5000000000 | bytes 1048576 | tf_op jit(solution)/shard_map/input_gradient/pallas_call | solution.py:784
  185.9 4.8 %collective-permute-done.29 = bf16[4,192,256]{2,1,0:T(8,128)(2,1)} collective-permute-done((bf16[4,192,256]{2,1,0:T(8,128)(2,1)S(1)}, bf16[4,192,256]{2,1,0:T(8,128)(2,1)}, u32[]{:S(2)}, u32[]{:S(2)}) %collective-permute-start.29) | collective-permute-done | bytes 393248 | tf_op jit(solution)/shard_map/ppermute | solution.py:865
  192.2 2.8 %collective-permute-start.31 = (bf16[192,256]{1,0:T(8,128)(2,1)S(1)}, bf16[192,256]{1,0:T(8,128)(2,1)S(1)}, u32[]{:S(2)}, u32[]{:S(2)}) collective-permute-start(bf16[192,256]{1,0:T(8,128)(2,1)S(1)} %get-tuple-element.159), channel_id=1, source_target_pairs={{0,1},{1,0},{2,3},{3,2},{4,5},{5,4},{6,7},{7,6},{8,9},{9,8},{10,11... | collective-permute-start | bytes 294920 | tf_op jit(solution)/shard_map/ppermute | solution.py:861
  202.5 3.0 %collective-permute-done.32 = bf16[192,256]{1,0:T(8,128)(2,1)S(1)} collective-permute-done((bf16[192,256]{1,0:T(8,128)(2,1)S(1)}, bf16[192,256]{1,0:T(8,128)(2,1)S(1)}, u32[]{:S(2)}, u32[]{:S(2)}) %collective-permute-start.32) | collective-permute-done | bytes 98336 | tf_op jit(solution)/shard_map/ppermute | solution.py:861
  206.6 3.1 %collective-permute-done.35.p2 = bf16[240,384]{1,0:T(8,128)(2,1)S(1)} collective-permute-done((bf16[240,384]{1,0:T(8,128)(2,1)S(1)}, bf16[240,384]{1,0:T(8,128)(2,1)S(1)}, u32[]{:S(2)}, u32[]{:S(2)}) %collective-permute-start.35) | collective-permute-done | bytes 184352 | tf_op jit(solution)/shard_map/ppermute | solution.py:865
  210.2 10.5 %all-gather = bf16[1536,256]{1,0:T(8,128)(2,1)} all-gather(bf16[192,256]{1,0:T(8,128)(2,1)S(1)} %fusion.13), channel_id=2, replica_groups=mesh['wide'=8,'narrow'=4] {'wide'}, dimensions={0}, use_global_device_ids=true | all-gather | bytes 884736 | tf_op jit(solution)/shard_map/all_gather | solution.py:904
  220.8 2.4 %unpack_mixer.1 = (f32[192,1152]{1,0:T(8,128)}, f32[9,192]{1,0:T(8,128)}, f32[192,384]{1,0:T(8,128)}, f32[54,96]{1,0:T(8,128)}, f32[192,384]{1,0:T(8,128)}, /*in...) custom-call(bf16[8,192,256]{2,1,0:T(8,128)(2,1)} %bitcast.59), custom_call_target="tpu_custom_call" | custom-call | flops 1000000000 | bytes 1048576 | tf_op jit(solution)/shard_map/unpack_mixer/pallas_call | solution.py:784
  224.7 3.2 %unpack_ffn.1 = (f32[2,96,1536]{2,1,0:T(8,128)}, f32[2,384,384]{2,1,0:T(8,128)}, f32[192,768]{1,0:T(8,128)}) custom-call(s32[2]{0:T(128)} %pad_add_fusion.place, bf16[240,384]{1,0:T(8,128)(2,1)} %copy-done.5, bf16[240,384]{1,0:T(8,128)(2,1)} %copy-done.22, bf16[240,384]{1,0:T(8,128)(2,1)} %copy-done.21, bf16[240,384]{1,0:T(8,128)(2,1)} %copy-done.20, ...), custom_call_target="tpu_custom_call" | custom-call | flops 1000000000 | bytes 1048576 | tf_op jit(solution)/shard_map/unpack_ffn/pallas_call | solution.py:784
  (127 shorter events, 45.2 us)
Async XLA Ops:
  18.2 9.2 %collective-permute-start.8 = (bf16[240,384]{1,0:T(8,128)(2,1)}, bf16[240,384]{1,0:T(8,128)(2,1)S(1)}, u32[]{:S(2)}, u32[]{:S(2)}) collective-permute-start(bf16[240,384]{1,0:T(8,128)(2,1)} %get-tuple-element.85), channel_id=1, source_target_pairs={{0,3},{1,2},{2,1},{3,0},{4,7},{5,6},{6,5},{7,4},{8,11},{9,10},{10,... | collective-permute-start | bytes 552968 | tf_op jit(solution)/shard_map/ppermute | solution.py:861
  20.7 18.3 %collective-permute-start.5 = (bf16[4,192,256]{2,1,0:T(8,128)(2,1)S(1)}, bf16[4,192,256]{2,1,0:T(8,128)(2,1)S(1)}, u32[]{:S(2)}, u32[]{:S(2)}) collective-permute-start(bf16[4,192,256]{2,1,0:T(8,128)(2,1)S(1)} %pad_maximum_fusion.1.p0), channel_id=1, source_target_pairs={{0,24},{4,28},{8,16},{12,20},{16,8},{20,12},{24,0},{28,4},{1,25},{... | collective-permute-start | bytes 1179656 | tf_op jit(solution)/shard_map/ppermute | solution.py:865
  23.3 16.6 %collective-permute-start.4 = (bf16[4,192,256]{2,1,0:T(8,128)(2,1)S(1)}, bf16[4,192,256]{2,1,0:T(8,128)(2,1)S(1)}, u32[]{:S(2)}, u32[]{:S(2)}) collective-permute-start(bf16[4,192,256]{2,1,0:T(8,128)(2,1)S(1)} %pad_maximum_fusion.1.p0), channel_id=1, source_target_pairs={{0,16},{4,20},{8,24},{12,28},{16,0},{20,4},{24,8},{28,12},{1,17},{... | collective-permute-start | bytes 1179656 | tf_op jit(solution)/shard_map/ppermute | solution.py:865
  23.7 16.3 %collective-permute-start.3 = (bf16[4,192,256]{2,1,0:T(8,128)(2,1)S(1)}, bf16[4,192,256]{2,1,0:T(8,128)(2,1)S(1)}, u32[]{:S(2)}, u32[]{:S(2)}) collective-permute-start(bf16[4,192,256]{2,1,0:T(8,128)(2,1)S(1)} %pad_maximum_fusion.1.p0), channel_id=1, source_target_pairs={{0,8},{4,12},{8,0},{12,4},{16,24},{20,28},{24,16},{28,20},{1,9},{5... | collective-permute-start | bytes 1179656 | tf_op jit(solution)/shard_map/ppermute | solution.py:865
  24.2 11.6 %collective-permute-start.7 = (bf16[240,384]{1,0:T(8,128)(2,1)}, bf16[240,384]{1,0:T(8,128)(2,1)S(1)}, u32[]{:S(2)}, u32[]{:S(2)}) collective-permute-start(bf16[240,384]{1,0:T(8,128)(2,1)} %get-tuple-element.85), channel_id=1, source_target_pairs={{0,2},{1,3},{2,0},{3,1},{4,6},{5,7},{6,4},{7,5},{8,10},{9,11},{10,... | collective-permute-start | bytes 552968 | tf_op jit(solution)/shard_map/ppermute | solution.py:861
  27.3 10.6 %collective-permute-start.6 = (bf16[240,384]{1,0:T(8,128)(2,1)}, bf16[240,384]{1,0:T(8,128)(2,1)S(1)}, u32[]{:S(2)}, u32[]{:S(2)}) collective-permute-start(bf16[240,384]{1,0:T(8,128)(2,1)} %get-tuple-element.85), channel_id=1, source_target_pairs={{0,1},{1,0},{2,3},{3,2},{4,5},{5,4},{6,7},{7,6},{8,9},{9,8},{10,11... | collective-permute-start | bytes 552968 | tf_op jit(solution)/shard_map/ppermute | solution.py:861
  41.7 33.6 %collective-permute-start.15 = (bf16[4,240,384]{2,1,0:T(8,128)(2,1)S(1)}, bf16[4,240,384]{2,1,0:T(8,128)(2,1)S(1)}, u32[]{:S(2)}, u32[]{:S(2)}) collective-permute-start(bf16[4,240,384]{2,1,0:T(8,128)(2,1)S(1)} %pad_maximum_fusion.p0), channel_id=1, source_target_pairs={{0,24},{4,28},{8,16},{12,20},{16,8},{20,12},{24,0},{28,4},{1,25},{... | collective-permute-start | bytes 2211848 | tf_op jit(solution)/shard_map/ppermute | solution.py:865
  43.7 33.2 %collective-permute-start.14 = (bf16[4,240,384]{2,1,0:T(8,128)(2,1)S(1)}, bf16[4,240,384]{2,1,0:T(8,128)(2,1)S(1)}, u32[]{:S(2)}, u32[]{:S(2)}) collective-permute-start(bf16[4,240,384]{2,1,0:T(8,128)(2,1)S(1)} %pad_maximum_fusion.p0), channel_id=1, source_target_pairs={{0,16},{4,20},{8,24},{12,28},{16,0},{20,4},{24,8},{28,12},{1,17},{... | collective-permute-start | bytes 2211848 | tf_op jit(solution)/shard_map/ppermute | solution.py:865
  44.9 32.0 %collective-permute-start.13 = (bf16[4,240,384]{2,1,0:T(8,128)(2,1)S(1)}, bf16[4,240,384]{2,1,0:T(8,128)(2,1)S(1)}, u32[]{:S(2)}, u32[]{:S(2)}) collective-permute-start(bf16[4,240,384]{2,1,0:T(8,128)(2,1)S(1)} %pad_maximum_fusion.p0), channel_id=1, source_target_pairs={{0,8},{4,12},{8,0},{12,4},{16,24},{20,28},{24,16},{28,20},{1,9},{5... | collective-permute-start | bytes 2211848 | tf_op jit(solution)/shard_map/ppermute | solution.py:865
  128.4 34.2 %collective-permute-start.23 = (bf16[4,240,384]{2,1,0:T(8,128)(2,1)}, bf16[4,240,384]{2,1,0:T(8,128)(2,1)S(1)}, u32[]{:S(2)}, u32[]{:S(2)}) collective-permute-start(bf16[4,240,384]{2,1,0:T(8,128)(2,1)} %get-tuple-element.148), channel_id=1, source_target_pairs={{0,24},{4,28},{8,16},{12,20},{16,8},{20,12},{24,0},{28,4},{1,25},{... | collective-permute-start | bytes 2211848 | tf_op jit(solution)/shard_map/ppermute | solution.py:865
  130.1 33.7 %collective-permute-start.22 = (bf16[4,240,384]{2,1,0:T(8,128)(2,1)}, bf16[4,240,384]{2,1,0:T(8,128)(2,1)S(1)}, u32[]{:S(2)}, u32[]{:S(2)}) collective-permute-start(bf16[4,240,384]{2,1,0:T(8,128)(2,1)} %get-tuple-element.149), channel_id=1, source_target_pairs={{0,16},{4,20},{8,24},{12,28},{16,0},{20,4},{24,8},{28,12},{1,17},{... | collective-permute-start | bytes 2211848 | tf_op jit(solution)/shard_map/ppermute | solution.py:865
  131.4 32.5 %collective-permute-start.21 = (bf16[4,240,384]{2,1,0:T(8,128)(2,1)S(1)}, bf16[4,240,384]{2,1,0:T(8,128)(2,1)S(1)}, u32[]{:S(2)}, u32[]{:S(2)}) collective-permute-start(bf16[4,240,384]{2,1,0:T(8,128)(2,1)S(1)} %get-tuple-element.150), channel_id=1, source_target_pairs={{0,8},{4,12},{8,0},{12,4},{16,24},{20,28},{24,16},{28,20},{1,9},{5... | collective-permute-start | bytes 2211848 | tf_op jit(solution)/shard_map/ppermute | solution.py:865
  164.8 9.4 %collective-permute-start.26 = (bf16[240,384]{1,0:T(8,128)(2,1)S(1)}, bf16[240,384]{1,0:T(8,128)(2,1)S(1)}, u32[]{:S(2)}, u32[]{:S(2)}) collective-permute-start(bf16[240,384]{1,0:T(8,128)(2,1)S(1)} %get-tuple-element.156), channel_id=1, source_target_pairs={{0,3},{1,2},{2,1},{3,0},{4,7},{5,6},{6,5},{7,4},{8,11},{9,10},{10,... | collective-permute-start | bytes 552968 | tf_op jit(solution)/shard_map/ppermute | solution.py:861
  166.2 19.6 %collective-permute-start.25 = (bf16[240,384]{1,0:T(8,128)(2,1)}, bf16[240,384]{1,0:T(8,128)(2,1)}, u32[]{:S(2)}, u32[]{:S(2)}) collective-permute-start(bf16[240,384]{1,0:T(8,128)(2,1)} %get-tuple-element.157), channel_id=1, source_target_pairs={{0,2},{1,3},{2,0},{3,1},{4,6},{5,7},{6,4},{7,5},{8,10},{9,11},{10,... | collective-permute-start | bytes 552968 | tf_op jit(solution)/shard_map/ppermute | solution.py:861
  167.6 18.2 %collective-permute-start.24 = (bf16[240,384]{1,0:T(8,128)(2,1)}, bf16[240,384]{1,0:T(8,128)(2,1)}, u32[]{:S(2)}, u32[]{:S(2)}) collective-permute-start(bf16[240,384]{1,0:T(8,128)(2,1)} %get-tuple-element.158), channel_id=1, source_target_pairs={{0,1},{1,0},{2,3},{3,2},{4,5},{5,4},{6,7},{7,6},{8,9},{9,8},{10,11... | collective-permute-start | bytes 552968 | tf_op jit(solution)/shard_map/ppermute | solution.py:861
  170.4 15.5 %collective-permute-start.30 = (bf16[4,192,256]{2,1,0:T(8,128)(2,1)}, bf16[4,192,256]{2,1,0:T(8,128)(2,1)}, u32[]{:S(2)}, u32[]{:S(2)}) collective-permute-start(bf16[4,192,256]{2,1,0:T(8,128)(2,1)} %get-tuple-element.153), channel_id=1, source_target_pairs={{0,24},{4,28},{8,16},{12,20},{16,8},{20,12},{24,0},{28,4},{1,25},{... | collective-permute-start | bytes 1179656 | tf_op jit(solution)/shard_map/ppermute | solution.py:865
  172.2 18.6 %collective-permute-start.29 = (bf16[4,192,256]{2,1,0:T(8,128)(2,1)S(1)}, bf16[4,192,256]{2,1,0:T(8,128)(2,1)}, u32[]{:S(2)}, u32[]{:S(2)}) collective-permute-start(bf16[4,192,256]{2,1,0:T(8,128)(2,1)S(1)} %get-tuple-element.154), channel_id=1, source_target_pairs={{0,16},{4,20},{8,24},{12,28},{16,0},{20,4},{24,8},{28,12},{1,17},{... | collective-permute-start | bytes 1179656 | tf_op jit(solution)/shard_map/ppermute | solution.py:865
  174.2 16.5 %collective-permute-start.28 = (bf16[4,192,256]{2,1,0:T(8,128)(2,1)S(1)}, bf16[4,192,256]{2,1,0:T(8,128)(2,1)}, u32[]{:S(2)}, u32[]{:S(2)}) collective-permute-start(bf16[4,192,256]{2,1,0:T(8,128)(2,1)S(1)} %get-tuple-element.155), channel_id=1, source_target_pairs={{0,8},{4,12},{8,0},{12,4},{16,24},{20,28},{24,16},{28,20},{1,9},{5... | collective-permute-start | bytes 1179656 | tf_op jit(solution)/shard_map/ppermute | solution.py:865
  196.0 9.5 %collective-permute-start.32 = (bf16[192,256]{1,0:T(8,128)(2,1)S(1)}, bf16[192,256]{1,0:T(8,128)(2,1)S(1)}, u32[]{:S(2)}, u32[]{:S(2)}) collective-permute-start(bf16[192,256]{1,0:T(8,128)(2,1)S(1)} %get-tuple-element.161), channel_id=1, source_target_pairs={{0,2},{1,3},{2,0},{3,1},{4,6},{5,7},{6,4},{7,5},{8,10},{9,11},{10,... | collective-permute-start | bytes 294920 | tf_op jit(solution)/shard_map/ppermute | solution.py:861
  197.7 25.4 %collective-permute-start.37 = (bf16[240,384]{1,0:T(8,128)(2,1)S(1)}, bf16[240,384]{1,0:T(8,128)(2,1)S(1)}, u32[]{:S(2)}, u32[]{:S(2)}) collective-permute-start(bf16[240,384]{1,0:T(8,128)(2,1)S(1)} %fusion.10.p0), channel_id=1, source_target_pairs={{0,4},{4,0},{8,12},{12,8},{16,20},{20,16},{24,28},{28,24},{1,5},{5... | collective-permute-start | bytes 552968 | tf_op jit(solution)/shard_map/ppermute | solution.py:865
  199.1 10.6 %collective-permute-start.35 = (bf16[240,384]{1,0:T(8,128)(2,1)S(1)}, bf16[240,384]{1,0:T(8,128)(2,1)S(1)}, u32[]{:S(2)}, u32[]{:S(2)}) collective-permute-start(bf16[240,384]{1,0:T(8,128)(2,1)S(1)} %fusion.10.p0), channel_id=1, source_target_pairs={{0,16},{4,20},{8,24},{12,28},{16,0},{20,4},{24,8},{28,12},{1,17},{... | collective-permute-start | bytes 552968 | tf_op jit(solution)/shard_map/ppermute | solution.py:865
  206.6 16.6 %collective-permute-start.40 = (bf16[240,384]{1,0:T(8,128)(2,1)S(1)}, bf16[240,384]{1,0:T(8,128)(2,1)S(1)}, u32[]{:S(2)}, u32[]{:S(2)}) collective-permute-start(bf16[240,384]{1,0:T(8,128)(2,1)S(1)} %collective-permute-done.36.p3), channel_id=1, source_target_pairs={{0,4},{4,0},{8,12},{12,8},{16,20},{20,16},{24,28},{28,24},{1,5},{5... | collective-permute-start | bytes 552968 | tf_op jit(solution)/shard_map/ppermute | solution.py:865
  209.7 13.5 %collective-permute-start.39 = (bf16[240,384]{1,0:T(8,128)(2,1)S(1)}, bf16[240,384]{1,0:T(8,128)(2,1)S(1)}, u32[]{:S(2)}, u32[]{:S(2)}) collective-permute-start(bf16[240,384]{1,0:T(8,128)(2,1)S(1)} %collective-permute-done.35.p2), channel_id=1, source_target_pairs={{0,4},{4,0},{8,12},{12,8},{16,20},{20,16},{24,28},{28,24},{1,5},{5... | collective-permute-start | bytes 552968 | tf_op jit(solution)/shard_map/ppermute | solution.py:865
  209.8 13.5 %collective-permute-start.38 = (bf16[240,384]{1,0:T(8,128)(2,1)S(1)}, bf16[240,384]{1,0:T(8,128)(2,1)S(1)}, u32[]{:S(2)}, u32[]{:S(2)}) collective-permute-start(bf16[240,384]{1,0:T(8,128)(2,1)S(1)} %collective-permute-done.34.p1), channel_id=1, source_target_pairs={{0,4},{4,0},{8,12},{12,8},{16,20},{20,16},{24,28},{28,24},{1,5},{5... | collective-permute-start | bytes 552968 | tf_op jit(solution)/shard_map/ppermute | solution.py:865
  (43 other events, 306.5 us)

commit v6 on v5

--- a/solution.py
+++ b/solution.py
@@ -141,10 +141,10 @@
 
     def depth(i):
         ps = padded_start(i)
-        for c in range(3):
-            lanes = slice(256 * c, 256 * c + 256)
+        for c in range(6):
+            lanes = slice(128 * c, 128 * c + 128)
             window = xpad[pl.ds(pl.multiple_of(ps - 8, 8), 144), lanes]
-            total = jnp.zeros((128, 256), F32)
+            total = jnp.zeros((128, 128), F32)
             for j in range(TAPS):
                 total = total + vec[j : j + 1, lanes] * window[4 + j : 132 + j, :]
             dw[at(i, 128), lanes] = total.astype(BF)
@@ -171,13 +171,12 @@
     kc[:, 256:384] = nn(dw[...], wm[7, :, 0:128])
     stores.append(start_copy(kc, kc_any, sems.at[4]))
 
-    def dynamic(i):
-        rows = at(i, 128)
-        ps = padded_start(i)
+    def tap_softmax(i):
+        rows = at(i, 384)
         query = (kc[rows, :] * packed[rows, 0:AH].astype(F32)).astype(BF)
         cq[rows, :] = query
         logits = nn(query, wk[...])
-        real = iota((128, 128), 1) < 8 * TAPS
+        real = iota((384, 128), 1) < 8 * TAPS
         top = jnp.where(real, logits, NEG * 1e20)
         for shift in (64, 32, 16, 8):
             top = jnp.maximum(top, pltpu.roll(top, shift, 1))
@@ -185,16 +184,25 @@
         total = ex
         for shift in (64, 32, 16, 8):
             total = total + pltpu.roll(total, shift, 1)
-        probs = ex / total
-        kp[pl.ds(ps, 128), :] = probs
-        window = cv[pl.ds(pl.multiple_of(ps - 8, 8), 144), :]
-        weights = nn(spread_taps(probs), spread[...])
-        out = jnp.zeros((128, AH), F32)
-        for j in range(TAPS):
-            out = out + weights[128 * j : 128 * j + 128, :] * window[4 + j : 132 + j, :]
-        ctx[rows, AH:D] = out.astype(BF)
-
-    loop(6, dynamic)
+        probs = ex * (1.0 / total)
+        for k in range(3):
+            kp[pl.ds(padded_start(3 * i + k), 128), :] = probs[128 * k : 128 * k + 128, :]
+
+    loop(2, tap_softmax)
+
+    def dynamic(u):
+        for i in (2 * u, 2 * u + 1):
+            ps = padded_start(i)
+            weights = nn(spread_taps(kp[pl.ds(ps, 128), :]), spread[...])
+            for c in range(3):
+                lanes = slice(128 * c, 128 * c + 128)
+                window = cv[pl.ds(pl.multiple_of(ps - 8, 8), 144), lanes]
+                out = jnp.zeros((128, 128), F32)
+                for j in range(TAPS):
+                    out = out + weights[128 * j : 128 * j + 128, lanes] * window[4 + j : 132 + j, :]
+                ctx[at(i, 128), AH + 128 * c : AH + 128 * c + 128] = out.astype(BF)
+
+    loop(3, dynamic)
     stores += [start_copy(cq, cq_any, sems.at[5]), start_copy(kp, kp_any, sems.at[6])]
 
     def attend(row0, nq, key0, nk, limit, pair, store):
@@ -208,8 +216,13 @@
             spare = 64 * (1 - hh)
             query = jnp.where((lane >> 6) == hh, queries, jnp.where(lane == spare, 1.0, 0.0))
             scores = nt(query.astype(BF), jnp.where(key_lane == spare, bias, keys).astype(BF))
-            ex = jnp.exp(scores - jnp.max(scores, axis=1, keepdims=True))
-            probs = (ex * (1.0 / jnp.sum(ex, axis=1, keepdims=True))).astype(BF)
+            parts = []
+            for r in range(0, nq, 32):
+                part = scores[r : r + 32, :]
+                part = jnp.exp(part - jnp.max(part, axis=1, keepdims=True))
+                part = part * (1.0 / jnp.sum(part, axis=1, keepdims=True))
+                parts.append(part.astype(BF))
+            probs = jnp.concatenate(parts, axis=0)
             store(hh, probs)
             outs.append(nn(probs, vals))
         both = jnp.where(lane < 64, outs[0], outs[1])
@@ -295,11 +308,7 @@
 
                 loop(4, one)
 
-    for part in range(3):
-        fetch(part)
-    cots = [
-        start_copy(cl, cot.at[0:LONG], sems.at[5]), start_copy(cs, cot.at[LONG:ROWS], sems.at[6])
-    ]
+    fetch(0)
     gain_one, bias_one = vec[16:17, :], vec[17:18, :]
     gain_two, bias_two = vec[18:19, :], vec[19:20, :]
     sums[...] = jnp.zeros((32, D), F32)
@@ -307,14 +316,17 @@
     for copy in loads:
         copy.wait()
     pltpu.make_async_copy(wo, wo, sems.at[0]).wait()
+    fetch(1)
+    fetch(2)
+    cots = [
+        start_copy(cl, cot.at[0:LONG], sems.at[5]), start_copy(cs, cot.at[LONG:ROWS], sems.at[6])
+    ]
 
     def mix(i):
         rows = at(i, 256)
         for c in range(2):
             lanes = slice(AH * c, AH * c + AH)
             res[rows, lanes] = nn(ctx[rows, :], wo[c]) + xm[rows, lanes].astype(F32)
-
-    loop(3, mix)
 
     def several(i):
         return [at(4 * i + k, 32) for k in range(4)]
@@ -335,7 +347,12 @@
             grouped[0, rows, :] = short[:, 0:AH]
             grouped[1, rows, :] = short[:, AH:D]
 
-    loop(6, norm_one)
+    mix(0)
+    for tile in range(3):
+        if tile < 2:
+            mix(tile + 1)
+        norm_one(2 * tile)
+        norm_one(2 * tile + 1)
     pltpu.make_async_copy(wi, wi, sems.at[1]).wait()
     pltpu.make_async_copy(wu, wu, sems.at[2]).wait()
 
@@ -472,24 +489,24 @@
         sums[0:8, :] += done[0][0] + done[1][0] + done[2][0] + done[3][0]
         sums[8:16, :] += done[0][1] + done[1][1] + done[2][1] + done[3][1]
 
+    def unmix(i):
+        rows = at(i, 256)
+        part = nt(gproj[rows, 0:AH], wo[0]) + nt(gproj[rows, AH:D], wo[1])
+        gctx[rows, :] = part.astype(BF)
+
     loop(6, norm_one_back)
+    loop(2, unmix)
     stores.append(start_copy(gone, gone_any, sems.at[5]))
-    for k in range(4):
-        gvec[k : k + 1, :] = jnp.sum(sums[8 * k : 8 * k + 8, :], axis=0, keepdims=True)
-    gvec[4:8, :] = jnp.zeros((4, D), F32)
     for c in range(2):
         gout[c] = tn(ctx[...], gproj[:, AH * c : AH * c + AH]).astype(BF)
         for n in range(4):
             for r in range(4):
                 source = gout.at[c, pl.ds(192 * n + 48 * r, 48), :]
                 ship(keep, send, place, 4 * c + r, n, pl.ds(192, 48), source, sems.at[2])
-
-    def unmix(i):
-        rows = at(i, 256)
-        part = nt(gproj[rows, 0:AH], wo[0]) + nt(gproj[rows, AH:D], wo[1])
-        gctx[rows, :] = part.astype(BF)
-
-    loop(3, unmix)
+    unmix(2)
+    for k in range(4):
+        gvec[k : k + 1, :] = jnp.sum(sums[8 * k : 8 * k + 8, :], axis=0, keepdims=True)
+    gvec[4:8, :] = jnp.zeros((4, D), F32)
     stores.append(start_copy(gctx, gctx_any, sems.at[6]))
     for copy in stores:
         copy.wait()
@@ -503,15 +520,17 @@
     cv_any, gctx_any, p0, p1, p2, p3, p4, p5, p6, p7,
     keep, send, grads_any, gdep_any,
     wm, xm, packed, plong, pshort, dw, kc, cq, kp, cv, gctx,
-    xpad, gcp, gdp, grads, gqc, dkv, gkc, glog, gdep, gb, spread, gather, wk, sem, sems, out_sem,
+    xpad, gcp, gdp, grads, gqc, dkv, gkc, glog, gprob, gdep, gb, spread, gather, wk, sem, sems,
+    out_sem,
 ):
     arrays = (
         (gctx_any, gctx), (kp_any, kp), (cv_any, cv), (packed_any, packed), (kc_any, kc),
         (xm_any, xm), (plong_any, plong), (pshort_any, pshort), (dw_any, dw), (cq_any, cq),
     )
-    loads = [start_copy(a, b, sems.at[k]) for k, (a, b) in enumerate(arrays[0:5])]
-    fetch_mixer(place, (p0, p1, p2, p3, p4, p5, p6, p7), wm, sem)
-    late = [start_copy(a, b, sems.at[5 + k]) for k, (a, b) in enumerate(arrays[5:])]
+    def begin(first, last):
+        return [start_copy(*arrays[k], sems.at[k]) for k in range(first, last)]
+
+    loads = begin(0, 3)
     zero_gaps(xpad)
     zero_gaps(gcp)
     zero_gaps(gdp)
@@ -520,43 +539,59 @@
     gdep[...] = jnp.zeros((8 * TAPS, D), F32)
     for copy in loads:
         copy.wait()
+    loads = begin(3, 6)
+    fetch_mixer(place, (p0, p1, p2, p3, p4, p5, p6, p7), wm, sem)
+    late = begin(6, 10)
     for start, rows, pstart in SEGS:
         gcp[pstart : pstart + rows, :] = gctx[start : start + rows, AH:D].astype(F32)
-    pltpu.make_async_copy(wm, wm, sem).wait()
-    wk[...] = tap_kernel(wm)
 
     def dynamic(i):
         rows = at(i, 128)
         ps = padded_start(i)
         wide = pl.ds(pl.multiple_of(ps - 8, 8), 144)
-        grad_wide = gcp[wide, :]
-        values = cv[wide, :]
-        grad = gcp[pl.ds(ps, 128), :]
         weights = nn(spread_taps(kp[wide, :]), spread[...])
-        total = jnp.zeros((128, AH), F32)
-        parts = []
-        for j in range(TAPS):
-            part = weights[144 * j : 144 * j + 144, :] * grad_wide
-            total = total + part[12 - j : 140 - j, :]
-            parts.append((grad * values[4 + j : 132 + j, :]).astype(BF))
-        grads[rows, 3 * AH : 4 * AH] = total.astype(BF)
-        sums = nn(jnp.concatenate(parts, axis=0), gather[...])
-        gprob = sums[0:128, :]
+        columns = []
+        for c in range(3):
+            lanes = slice(128 * c, 128 * c + 128)
+            grad_wide = gcp[wide, lanes]
+            values = cv[wide, lanes]
+            grad = gcp[pl.ds(ps, 128), lanes]
+            total = jnp.zeros((128, 128), F32)
+            parts = []
+            for j in range(TAPS):
+                part = weights[144 * j : 144 * j + 144, lanes] * grad_wide
+                total = total + part[12 - j : 140 - j, :]
+                parts.append((grad * values[4 + j : 132 + j, :]).astype(BF))
+            grads[rows, 3 * AH + 128 * c : 3 * AH + 128 * c + 128] = total.astype(BF)
+            columns.append(jnp.concatenate(parts, axis=0))
+        sums = nn(jnp.concatenate(columns, axis=1), gather[...])
+        total = sums[0:128, :]
         for j in range(1, TAPS):
-            gprob = gprob + pltpu.roll(sums[128 * j : 128 * j + 128, :], 8 * j, 1)
-        probs = kp[pl.ds(ps, 128), :]
-        inner = probs * gprob
+            total = total + pltpu.roll(sums[128 * j : 128 * j + 128, :], 8 * j, 1)
+        gprob[rows, :] = total
+
+    loop(6, dynamic)
+    for copy in loads:
+        copy.wait()
+    pltpu.make_async_copy(wm, wm, sem).wait()
+    wk[...] = tap_kernel(wm)
+
+    def tap_softmax_back(i):
+        rows = at(i, 384)
+        probs = jnp.concatenate([kp[pl.ds(padded_start(3 * i + k), 128), :] for k in range(3)], axis=0)
+        upper = gprob[rows, :]
+        inner = probs * upper
         for shift in (64, 32, 16, 8):
             inner = inner + pltpu.roll(inner, shift, 1)
-        glogits = (probs * (gprob - inner)).astype(BF)
+        glogits = (probs * (upper - inner)).astype(BF)
         glog[rows, :] = glogits
         gquery = nt(glogits, wk[...])
         gkc[rows, :] = (gquery * packed[rows, 0:AH].astype(F32)).astype(BF)
         gqc[rows, :] = gquery * kc[rows, :]
 
-    loop(6, dynamic)
-    for copy in late:
-        copy.wait()
+    loop(2, tap_softmax_back)
+    for start, rows, pstart in SEGS:
+        xpad[pstart : pstart + rows, :] = xm[start : start + rows, :].astype(F32)
 
     def point_back(c):
         part = nt(gkc[:, 0:256], wm[6, at(c, 256), :])
@@ -567,6 +602,49 @@
 
     loop(3, point_back)
     copy_depth = start_copy(gdp, gdep_any, out_sem.at[1])
+
+    def release(b):
+        for n in range(4):
+            where = b ^ place[0]
+            chip, far_off = where >> 1, n ^ place[1]
+            source = gb.at[b, pl.ds(192 * n, 192), :]
+
+            @pl.when((where & 1) == 0)
+            def _():
+                pltpu.make_async_copy(source, keep.at[chip, far_off], out_sem.at[0]).start()
+
+            @pl.when((where & 1) == 1)
+            def _():
+                pltpu.make_async_copy(source, send.at[chip, far_off], out_sem.at[0]).start()
+
+    def depth(i):
+        ps = padded_start(i)
+        wide = pl.ds(pl.multiple_of(ps - 8, 8), 144)
+        for c in range(6):
+            lanes = slice(128 * c, 128 * c + 128)
+            tokens = xpad[pl.ds(ps, 128), lanes]
+            grad_wide = gdp[wide, lanes]
+            for j in range(TAPS):
+                gdep[8 * j : 8 * j + 8, lanes] += fold(tokens * grad_wide[12 - j : 140 - j, :])
+
+    loop(6, depth)
+    for copy in late:
+        copy.wait()
+    gb[6] = tn(dw[...], gkc[:, 0:256]).astype(BF)
+    gb[7, :, 0:128] = tn(dw[...], gkc[:, 256:384]).astype(BF)
+    taps = [jnp.sum(gdep[8 * j : 8 * j + 8, :], axis=0, keepdims=True) for j in range(TAPS)]
+    table = jnp.concatenate(
+        taps + [jnp.zeros((7, D), F32), gvec[...], jnp.zeros((104, D), F32)], axis=0
+    ).astype(BF)
+    misc = tn(table, eye(128, BF))
+    gkernel = nt(tn(cq[...], glog[...]).astype(BF), tap_permutation())
+    for n in range(4):
+        row = 192 * n
+        part = misc[row : row + 96, :] + gkernel[96 * n : 96 * n + 96, :]
+        gb[7, row : row + 96, 128:256] = part.astype(BF)
+        gb[7, row + 96 : row + 192, 128:256] = misc[row + 96 : row + 192, :].astype(BF)
+    release(6)
+    release(7)
 
     def attend(row0, nq, key0, nk, pair, load, first):
         queries = packed[pl.ds(row0, nq), at(pair, 128)].astype(F32) * 0.125
@@ -582,10 +660,13 @@
             query = jnp.where(mine, queries, 0.0).astype(BF)
             upper = jnp.where(mine, up, 0.0).astype(BF)
             probs_low = load(hh)
-            probs = probs_low.astype(F32)
             gprobs = nt(upper, vals)
-            inner = jnp.sum(probs * gprobs, axis=1, keepdims=True)
-            gscores = (probs * (gprobs - inner)).astype(BF)
+            parts = []
+            for r in range(0, nq, 32):
+                probs, part = probs_low[r : r + 32, :].astype(F32), gprobs[r : r + 32, :]
+                inner = jnp.sum(probs * part, axis=1, keepdims=True)
+                parts.append((probs * (part - inner)).astype(BF))
+            gscores = jnp.concatenate(parts, axis=0)
             outs.append(nn(gscores, keys))
             gkeys = gkeys + tn(gscores, query)
             gvals = gvals + tn(probs_low, upper)
@@ -617,55 +698,12 @@
             row0 = LONG + 128 * seg
             attend(row0, 128, row0, SHORT, pair, lambda hh: pshort[seg, 2 * pair + hh, :, :], True)
     copy_grads = start_copy(grads, grads_any, out_sem.at[2])
-    for start, rows, pstart in SEGS:
-        xpad[pstart : pstart + rows, :] = xm[start : start + rows, :].astype(F32)
-
-    def release(b):
-        for n in range(4):
-            where = b ^ place[0]
-            chip, far_off = where >> 1, n ^ place[1]
-            source = gb.at[b, pl.ds(192 * n, 192), :]
-
-            @pl.when((where & 1) == 0)
-            def _():
-                pltpu.make_async_copy(source, keep.at[chip, far_off], out_sem.at[0]).start()
-
-            @pl.when((where & 1) == 1)
-            def _():
-                pltpu.make_async_copy(source, send.at[chip, far_off], out_sem.at[0]).start()
-
-    gb[6] = tn(dw[...], gkc[:, 0:256]).astype(BF)
-    release(6)
-
-    def depth(i):
-        ps = padded_start(i)
-        wide = pl.ds(pl.multiple_of(ps - 8, 8), 144)
-        for c in range(3):
-            lanes = slice(256 * c, 256 * c + 256)
-            tokens = xpad[pl.ds(ps, 128), lanes]
-            grad_wide = gdp[wide, lanes]
-            for j in range(TAPS):
-                gdep[8 * j : 8 * j + 8, lanes] += fold(tokens * grad_wide[12 - j : 140 - j, :])
 
     def weights(b):
         gb[b] = tn(xm[...], grads[:, at(b, 256)]).astype(BF)
-        depth(b)
         release(b)
 
     loop(6, weights)
-    gb[7, :, 0:128] = tn(dw[...], gkc[:, 256:384]).astype(BF)
-    taps = [jnp.sum(gdep[8 * j : 8 * j + 8, :], axis=0, keepdims=True) for j in range(TAPS)]
-    table = jnp.concatenate(
-        taps + [jnp.zeros((7, D), F32), gvec[...], jnp.zeros((104, D), F32)], axis=0
-    ).astype(BF)
-    misc = tn(table, eye(128, BF))
-    gkernel = nt(tn(cq[...], glog[...]).astype(BF), tap_permutation())
-    for n in range(4):
-        row = 192 * n
-        part = misc[row : row + 96, :] + gkernel[96 * n : 96 * n + 96, :]
-        gb[7, row : row + 96, 128:256] = part.astype(BF)
-        gb[7, row + 96 : row + 192, 128:256] = misc[row + 96 : row + 192, :].astype(BF)
-    release(7)
     copy_depth.wait()
     copy_grads.wait()
     pltpu.make_async_copy(gb, gb, out_sem.at[0]).wait()
@@ -683,8 +721,8 @@
 
     def depth(i):
         ps = padded_start(i)
-        for c in range(3):
-            lanes = slice(256 * c, 256 * c + 256)
+        for c in range(6):
+            lanes = slice(128 * c, 128 * c + 128)
             window = gdp[pl.ds(pl.multiple_of(ps - 8, 8), 144), lanes]
             total = rest[at(i, 128), lanes]
             for j in range(TAPS):
@@ -759,7 +797,13 @@
             out[at(r, 48), at(g, AH)] = piece[192:240, :].astype(F32)
 
 
-def unpack_mixer(packed, qkv, depth, point, kernel, convout, g1, b1, g2, b2):
+def unpack_mixer(
+    place, p0, p1, p2, p3, p4, p5, p6, p7,
+    qkv, depth, point, kernel, convout, g1, b1, g2, b2, packed,
+):
+    for core, pieces in enumerate(((p0, p1, p2, p3), (p4, p5, p6, p7))):
+        for chip, piece in enumerate(pieces):
+            packed[slot_of(place[0], core, chip)] = piece[...]
     for w in range(4):
         qkv[:, 256 * w : 256 * w + 256] = packed[w].astype(F32)
     qkv[:, 1024:1152] = packed[4, :, 0:128].astype(F32)
@@ -780,6 +824,9 @@
 ANY = pl.BlockSpec(memory_space=pl.ANY)
 
 
+VMEM_MIB = {'unpack_ffn': 12, 'unpack_mixer': 12, 'input_gradient': 24}
+
+
 def call(kernel, specs, outs, scratch, flops, *args, out_specs=None):
     return pl.pallas_call(
         kernel,
@@ -787,7 +834,7 @@
         in_specs=specs,
         out_specs=out_specs or [VMEM] * len(outs),
         scratch_shapes=[pltpu.VMEM(s, d) for s, d in scratch[0]] + list(scratch[1:]),
-        compiler_params=pltpu.CompilerParams(vmem_limit_bytes=60 << 20),
+        compiler_params=pltpu.CompilerParams(vmem_limit_bytes=VMEM_MIB.get(kernel.__name__, 60) << 20),
         cost_estimate=pl.CostEstimate(flops=flops, bytes_accessed=1 << 20, transcendentals=0),
         name=kernel.__name__,
     )(*args)
@@ -835,6 +882,7 @@
     scratch = [((SLOTS, D, 256), BF)] + [(a.shape, a.dtype) for a in arrays] + [
         ((PAD, D), F32), ((PAD, AH), F32), ((PAD, D), F32), ((ROWS, 4 * AH), BF),
         ((ROWS, AH), F32), ((2, LONG, 128), F32), ((ROWS, AH), BF), ((ROWS, 128), BF),
+        ((ROWS, 128), F32),
         ((8 * TAPS, D), F32), ((SLOTS, D, 256), BF), ((256, AH), BF), ((AH, 128), BF),
         ((AH, 128), BF),
     ]
@@ -898,10 +946,6 @@
 
 def send_narrow(parts):
     return [far(parts[k], k) for k in (1, 2, 3)]
-
-
-def gather_wide(parts):
-    return lax.all_gather(parts, "wide", axis=0, tiled=False)
 
 
 def body(
@@ -936,27 +980,31 @@
         place, vec, gvec, (xm, packed, plong, pshort, dw, kc, cq, kp, cv, gctx), mixer
     )
     keep, send, ga_sent = lax.optimization_barrier((keep, send, ga_sent))
-    sent = near(send, 1)
+    gb = reduce_cores(keep, near(send, 1))
+    gb_sent = send_chips(gb)
+    ga_sent, gb = lax.optimization_barrier((ga_sent, gb))
     ga = reduce_chips(ga[0], ga_sent)
-    ga_sent = send_narrow(ga)
-    gb = reduce_cores(keep, sent)
-    gb_sent = send_chips(gb)
-    grads, gb = lax.optimization_barrier((grads, gb))
+    ga_sent = [far(ga[1], 1), far(ga[2], 2)]
+    grads, ga = lax.optimization_barrier((grads, ga))
     il, is_ = backward_inputs(scalars, vec, grads, gdp, gone, mixer)
+    last, il = lax.optimization_barrier((ga[3], il))
     ga_sent, gb_sent, il = lax.optimization_barrier((ga_sent, gb_sent, il))
-    ga = lax.psum(total(ga[0], ga_sent), "hi")
+    ga_sent.append(far(last, 3))
+    ga = gather_chips(lax.psum(total(ga[0], ga_sent), "hi"))
     gb = reduce_chips(gb[0], gb_sent)
-    gb = lax.psum(total(gb[0], send_narrow(gb)), "hi")
+    gb = gather_chips(lax.psum(total(gb[0], send_narrow(gb)), "hi"))
     inner, outer, out = call(
         unpack_ffn, [SMEM] + [VMEM] * 8,
         [((2, 96, 4 * AH), F32), ((2, AH, AH), F32), ((192, D), F32)],
-        ([],), 10**9, place, *gather_cores(gather_chips(ga)),
-    )
+        ([],), 10**9, place, *gather_cores(ga),
+    )
+    gb, inner = lax.optimization_barrier((gb, inner))
     outs = [
         ((192, 3 * AH), F32), ((TAPS, 192), F32), ((192, AH), F32), ((54, 96), F32), ((192, AH), F32),
     ] + [((192,), F32)] * 4
     qkv, depth, point, kernel, convout, g1, b1, g2, b2 = call(
-        unpack_mixer, [VMEM], outs, ([],), 10**9, gather_wide(gb)
+        unpack_mixer, [SMEM] + [VMEM] * 8, outs, ([((SLOTS, 192, 256), BF)],), 10**9,
+        place, *gather_cores(gb),
     )
     return (
         ol.reshape(long_tokens.shape), os.reshape(short_tokens.shape),

time: 229 us -> 222 us (0.969)
  blocking collectives: 10.5 us -> 0 us
  waiting for transfers between devices: 41.9 us -> 51.1 us
  Pallas kernels: 114 us -> 108 us
  starting transfers between devices: 44.6 us -> 49.3 us
  other arithmetic: 12.1 us -> 8.9 us
    all_gather x1 -> x0, blocking collectives: 10.5 us -> none  [gather_wide(): return lax.all_gather(parts, 'wide', axis=0, tiled=False)]
    pallas_call x7, Pallas kernels: 114 us -> 108 us  [call(): pl.pallas_call(kernel, out_shape=[jax.ShapeDtypeStruct(s, d) for s, d in...]
    ppermute x12, waiting for transfers between devices: 20.4 us -> 25.2 us  [far(): return lax.ppermute(values, 'narrow', [(i, i ^ bit) for i in range(4)])]
    ppermute x29 -> x36, starting transfers between devices: 20.7 us -> 25.6 us  [near(): return lax.ppermute(values, 'wide', [(i, i ^ bit) for i in range(SLOTS)])]
    ppermute x29 -> x36, waiting for transfers between devices: 21.5 us -> 25.9 us  [near(): return lax.ppermute(values, 'wide', [(i, i ^ bit) for i in range(SLOTS)])]
  transfers between devices with their start and end apart: 41 -> 48, of which waited for: 18 -> 23; matrix products, arithmetic and copies ran while one was open for 2% -> 1% of each run, Pallas kernels for 32% -> 31%
where the time goes in v6:
time: 222 us
  Pallas kernels  108 us (49%)
  waiting for transfers between devices  51.1 us (23%)
  starting transfers between devices  49.3 us (22%)
  other arithmetic  8.9 us (4%)
  local copies, waits for them, and re-layouts  3.43 us (2%)
    pallas_call x7, Pallas kernels, call(): pl.pallas_call(kernel, out_shape=[jax.ShapeDtypeStruct(s, d) for s, d in...  108 us
    ppermute x36, waiting for transfers between devices, near(): return lax.ppermute(values, 'wide', [(i, i ^ bit) for i in range(SLOTS)])  25.9 us
    ppermute x36, starting transfers between devices, near(): return lax.ppermute(values, 'wide', [(i, i ^ bit) for i in range(SLOTS)])  25.6 us
    ppermute x12, waiting for transfers between devices, far(): return lax.ppermute(values, 'narrow', [(i, i ^ bit) for i in range(4)])  25.2 us
    ppermute x12, starting transfers between devices, far(): return lax.ppermute(values, 'narrow', [(i, i ^ bit) for i in range(4)])  23.8 us
    convert_element_type x4, other arithmetic, total(): return result.astype(BF)  5.8 us
  transfers between devices with their start and end apart: 48, of which 23 were waited for; matrix products, arithmetic and copies ran while one was open for 1% of the time, Pallas kernels for 31%

profile of v6, /device:TPU:0, one launch (start us, length us, event | category | flops | bytes accessed | tf_op | source)
XLA Modules:
  0.0 222.0 jit_solution(6154667902873829746)
XLA Ops:
  1.2 2.4 %pack.1 = (bf16[192,256]{1,0:T(8,128)(2,1)}, bf16[240,384]{1,0:T(8,128)(2,1)}) custom-call(s32[2]{0:T(128)} %pad_add_fusion.place, bf16[192,1152]{1,0:T(8,128)(2,1)} %qkv.1, bf16[9,192]{1,0:T(8,128)(2,1)} %depth.1, bf16[192,384]{1,0:T(8,128)(2,1)} %point.1, bf16[54,96]{1,0:T(8,128)(2,1)} %bitcast.67, bf16[192,384]{1,0:T(8,128)(2,1)} %convout.1, ...), custom_call_target="tpu_custom_call" | custom-call | flops 1000000000 | bytes 1048576 | tf_op jit(solution)/shard_map/pack/pallas_call | solution.py:831
  3.6 5.0 %collective-permute-start.2 = (bf16[192,256]{1,0:T(8,128)(2,1)}, bf16[192,256]{1,0:T(8,128)(2,1)S(1)}, u32[]{:S(2)}, u32[]{:S(2)}) collective-permute-start(bf16[192,256]{1,0:T(8,128)(2,1)} %get-tuple-element.93), channel_id=1, source_target_pairs={{0,3},{1,2},{2,1},{3,0},{4,7},{5,6},{6,5},{7,4},{8,11},{9,10},{10,... | collective-permute-start | bytes 294920 | tf_op jit(solution)/shard_map/ppermute | solution.py:909
  9.3 3.3 %collective-permute-done.2 = bf16[192,256]{1,0:T(8,128)(2,1)S(1)} collective-permute-done((bf16[192,256]{1,0:T(8,128)(2,1)}, bf16[192,256]{1,0:T(8,128)(2,1)S(1)}, u32[]{:S(2)}, u32[]{:S(2)}) %collective-permute-start.2) | collective-permute-done | bytes 98336 | tf_op jit(solution)/shard_map/ppermute | solution.py:909
  12.6 4.6 %collective-permute-done.1 = bf16[192,256]{1,0:T(8,128)(2,1)S(1)} collective-permute-done((bf16[192,256]{1,0:T(8,128)(2,1)}, bf16[192,256]{1,0:T(8,128)(2,1)S(1)}, u32[]{:S(2)}, u32[]{:S(2)}) %collective-permute-start.1) | collective-permute-done | bytes 98336 | tf_op jit(solution)/shard_map/ppermute | solution.py:909
  18.1 2.6 %collective-permute-start.8 = (bf16[240,384]{1,0:T(8,128)(2,1)}, bf16[240,384]{1,0:T(8,128)(2,1)S(1)}, u32[]{:S(2)}, u32[]{:S(2)}) collective-permute-start(bf16[240,384]{1,0:T(8,128)(2,1)} %get-tuple-element.96), channel_id=1, source_target_pairs={{0,3},{1,2},{2,1},{3,0},{4,7},{5,6},{6,5},{7,4},{8,11},{9,10},{10,... | collective-permute-start | bytes 552968 | tf_op jit(solution)/shard_map/ppermute | solution.py:909
  20.7 2.6 %collective-permute-start.5 = (bf16[4,192,256]{2,1,0:T(8,128)(2,1)S(1)}, bf16[4,192,256]{2,1,0:T(8,128)(2,1)S(1)}, u32[]{:S(2)}, u32[]{:S(2)}) collective-permute-start(bf16[4,192,256]{2,1,0:T(8,128)(2,1)S(1)} %pad_maximum_fusion.1.p0), channel_id=1, source_target_pairs={{0,24},{4,28},{8,16},{12,20},{16,8},{20,12},{24,0},{28,4},{1,25},{... | collective-permute-start | bytes 1179656 | tf_op jit(solution)/shard_map/ppermute | solution.py:913
  24.2 3.1 %collective-permute-done.8 = bf16[240,384]{1,0:T(8,128)(2,1)S(1)} collective-permute-done((bf16[240,384]{1,0:T(8,128)(2,1)}, bf16[240,384]{1,0:T(8,128)(2,1)S(1)}, u32[]{:S(2)}, u32[]{:S(2)}) %collective-permute-start.8) | collective-permute-done | bytes 184352 | tf_op jit(solution)/shard_map/ppermute | solution.py:909
  27.3 6.9 %collective-permute-start.6 = (bf16[240,384]{1,0:T(8,128)(2,1)}, bf16[240,384]{1,0:T(8,128)(2,1)S(1)}, u32[]{:S(2)}, u32[]{:S(2)}) collective-permute-start(bf16[240,384]{1,0:T(8,128)(2,1)} %get-tuple-element.96), channel_id=1, source_target_pairs={{0,1},{1,0},{2,3},{3,2},{4,5},{5,4},{6,7},{7,6},{8,9},{9,8},{10,11... | collective-permute-start | bytes 552968 | tf_op jit(solution)/shard_map/ppermute | solution.py:909
  35.8 2.2 collective-permute-done.6
  41.7 2.1 collective-permute-start.15
  46.1 25.5 %mixer_forward.1 = (bf16[768,768]{1,0:T(8,128)(2,1)}, bf16[768,1152]{1,0:T(8,128)(2,1)}, bf16[6,512,512]{2,1,0:T(8,128)(2,1)}, bf16[2,6,128,128]{3,2,1,0:T(8,128...) custom-call(s32[2]{0:T(128)} %pad_add_fusion.place, ...), custom_call_target="tpu_custom_call" | custom-call | flops 30000001024 | bytes 1048576 | tf_op jit(solution)/shard_map/mixer_forward/pallas_call | solution.py:831
  71.7 5.3 %collective-permute-done.14.p2 = bf16[4,240,384]{2,1,0:T(8,128)(2,1)} collective-permute-done((bf16[4,240,384]{2,1,0:T(8,128)(2,1)S(1)}, bf16[4,240,384]{2,1,0:T(8,128)(2,1)}, u32[]{:S(2)}, u32[]{:S(2)}) %collective-permute-start.14) | collective-permute-done | bytes 737312 | tf_op jit(solution)/shard_map/ppermute | solution.py:913
  83.4 35.1 %ffn_both.1 = (bf16[512,768]{1,0:T(8,128)(2,1)}, bf16[256,768]{1,0:T(8,128)(2,1)}, bf16[4,4,240,384]{3,2,1,0:T(8,128)(2,1)}, bf16[4,4,240,384]{3,2,1,0:T(8,128)(...) custom-call(s32[2]{0:T(128)} %pad_add_fusion.place, s32[1]{0:T(128)S(6)} %copy.34.llen, ...), custom_call_target="tpu_custom_call" | custom-call | flops 60000002048 | bytes 1048576 | tf_op jit(solution)/shard_map/ffn_both/pallas_call | solution.py:831
  118.7 5.5 %collective-permute-done.20 = bf16[4,4,240,384]{3,2,1,0:T(8,128)(2,1)S(1)} collective-permute-done((bf16[4,4,240,384]{3,2,1,0:T(8,128)(2,1)}, bf16[4,4,240,384]{3,2,1,0:T(8,128)(2,1)S(1)}, u32[]{:S(2)}, u32[]{:S(2)}) %collective-permute-start.20) | collective-permute-done | bytes 2949152 | tf_op jit(solution)/shard_map/ppermute | solution.py:913
  124.2 3.6 %fusion.3 = (bf16[4,240,384]{2,1,0:T(8,128)(2,1)}, bf16[4,240,384]{2,1,0:T(8,128)(2,1)}, bf16[4,240,384]{2,1,0:T(8,128)(2,1)S(1)}, bf16[4,240,384]{2,1,0:T(8,128)(2,1)S(1)}) fusion(bf16[4,4,240,384]{3,2,1,0:T(8,128)(2,1)S(1)} %collective-permute-done.20, bf16[4,4,240,384]{3,2,1,0:T(8,128)(2,1)} %get-tuple-element.113), kind=kLoop, calls=%fused_computation.11 | loop fusion | flops 5898240 | bytes 8847360 | tf_op jit(solution)/shard_map/convert_element_type | solution.py:932
  131.3 28.8 %mixer_backward.1 = (bf16[4,4,192,256]{3,2,1,0:T(8,128)(2,1)}, bf16[4,4,192,256]{3,2,1,0:T(8,128)(2,1)}, bf16[768,1536]{1,0:T(8,128)(2,1)}, f32[800,768]{1,0:T(8,128)}) custom-call(s32[2]{0:T(128)} %pad_add_fusion.place, f32[24,768]{1,0:T(8,128)} %get-tuple-element.101.vec, f32[8,768]{1,0:T(8,128)} %get-tuple-element.116.gvec, ...), custom_call_target="tpu_custom_call" | custom-call | flops 40000000000 | bytes 1048576 | tf_op jit(solution)/shard_map/mixer_backward/pallas_call | solution.py:831
  160.2 3.1 %collective-permute-done.22 = bf16[4,240,384]{2,1,0:T(8,128)(2,1)S(1)} collective-permute-done((bf16[4,240,384]{2,1,0:T(8,128)(2,1)}, bf16[4,240,384]{2,1,0:T(8,128)(2,1)S(1)}, u32[]{:S(2)}, u32[]{:S(2)}) %collective-permute-start.22) | collective-permute-done | bytes 737312 | tf_op jit(solution)/shard_map/ppermute | solution.py:913
  163.3 3.6 %collective-permute-done.24 = bf16[4,4,192,256]{3,2,1,0:T(8,128)(2,1)S(1)} collective-permute-done((bf16[4,4,192,256]{3,2,1,0:T(8,128)(2,1)}, bf16[4,4,192,256]{3,2,1,0:T(8,128)(2,1)S(1)}, u32[]{:S(2)}, u32[]{:S(2)}) %collective-permute-start.24) | collective-permute-done | bytes 1572896 | tf_op jit(solution)/shard_map/ppermute | solution.py:913
  176.7 11.5 %input_gradient.1 = (bf16[512,768]{1,0:T(8,128)(2,1)}, bf16[256,768]{1,0:T(8,128)(2,1)}) custom-call(s32[2]{0:T(128)S(1)} %copy-done.17, s32[1]{0:T(128)S(6)} %copy.34.llen, s32[2]{0:T(128)S(1)} %copy-done.16, f32[24,768]{1,0:T(8,128)S(1)} %copy-done.21, bf16[768,1536]{1,0:T(8,128)(2,1)S(1)} %copy-done.20, f32[800,768]{1,0:T(8,128)S(1)} %copy-done.18, ...), custom_call_target="tpu_custom_call" | custom-call | flops 5000000000 | bytes 1048576 | tf_op jit(solution)/shard_map/input_gradient/pallas_call | solution.py:831
  188.2 2.5 %collective-permute-start.36 = (bf16[240,384]{1,0:T(8,128)(2,1)S(1)}, bf16[240,384]{1,0:T(8,128)(2,1)S(1)}, u32[]{:S(2)}, u32[]{:S(2)}) collective-permute-start(bf16[240,384]{1,0:T(8,128)(2,1)S(1)} %get-tuple-element.152), channel_id=1, source_target_pairs={{0,3},{1,2},{2,1},{3,0},{4,7},{5,6},{6,5},{7,4},{8,11},{9,10},{10,... | collective-permute-start | bytes 552968 | tf_op jit(solution)/shard_map/ppermute | solution.py:909
  191.4 5.2 %collective-permute-done.36 = bf16[240,384]{1,0:T(8,128)(2,1)S(1)} collective-permute-done((bf16[240,384]{1,0:T(8,128)(2,1)S(1)}, bf16[240,384]{1,0:T(8,128)(2,1)S(1)}, u32[]{:S(2)}, u32[]{:S(2)}) %collective-permute-start.36) | collective-permute-done | bytes 184352 | tf_op jit(solution)/shard_map/ppermute | solution.py:909
  200.2 2.4 %collective-permute-start.32 = (bf16[192,256]{1,0:T(8,128)(2,1)S(1)}, bf16[192,256]{1,0:T(8,128)(2,1)S(1)}, u32[]{:S(2)}, u32[]{:S(2)}) collective-permute-start(bf16[192,256]{1,0:T(8,128)(2,1)S(1)} %get-tuple-element.183), channel_id=1, source_target_pairs={{0,3},{1,2},{2,1},{3,0},{4,7},{5,6},{6,5},{7,4},{8,11},{9,10},{10,... | collective-permute-start | bytes 294920 | tf_op jit(solution)/shard_map/ppermute | solution.py:909
  203.8 3.3 %collective-permute-done.32 = bf16[192,256]{1,0:T(8,128)(2,1)S(1)} collective-permute-done((bf16[192,256]{1,0:T(8,128)(2,1)S(1)}, bf16[192,256]{1,0:T(8,128)(2,1)S(1)}, u32[]{:S(2)}, u32[]{:S(2)}) %collective-permute-start.32) | collective-permute-done | bytes 98336 | tf_op jit(solution)/shard_map/ppermute | solution.py:909
  213.8 2.3 %unpack_ffn.1 = (f32[2,96,1536]{2,1,0:T(8,128)}, f32[2,384,384]{2,1,0:T(8,128)}, f32[192,768]{1,0:T(8,128)}) custom-call(s32[2]{0:T(128)S(1)} %copy-done.17, bf16[240,384]{1,0:T(8,128)(2,1)S(1)} %add_convert_fusion.8.p0, bf16[240,384]{1,0:T(8,128)(2,1)S(1)} %collective-permute-done.37.p1, bf16[240,384]{1,0:T(8,128)(2,1)S(1)} %collective-permute-done.38.p2, ...), custom_call_target="tpu_custom_call" | custom-call | flops 1000000000 | bytes 1048576 | tf_op jit(solution)/shard_map/unpack_ffn/pallas_call | solution.py:831
  (142 shorter events, 47.7 us)
Async XLA Ops:
  3.6 9.0 %collective-permute-start.2 = (bf16[192,256]{1,0:T(8,128)(2,1)}, bf16[192,256]{1,0:T(8,128)(2,1)S(1)}, u32[]{:S(2)}, u32[]{:S(2)}) collective-permute-start(bf16[192,256]{1,0:T(8,128)(2,1)} %get-tuple-element.93), channel_id=1, source_target_pairs={{0,3},{1,2},{2,1},{3,0},{4,7},{5,6},{6,5},{7,4},{8,11},{9,10},{10,... | collective-permute-start | bytes 294920 | tf_op jit(solution)/shard_map/ppermute | solution.py:909
  8.7 8.5 %collective-permute-start.1 = (bf16[192,256]{1,0:T(8,128)(2,1)}, bf16[192,256]{1,0:T(8,128)(2,1)S(1)}, u32[]{:S(2)}, u32[]{:S(2)}) collective-permute-start(bf16[192,256]{1,0:T(8,128)(2,1)} %get-tuple-element.93), channel_id=1, source_target_pairs={{0,2},{1,3},{2,0},{3,1},{4,6},{5,7},{6,4},{7,5},{8,10},{9,11},{10,... | collective-permute-start | bytes 294920 | tf_op jit(solution)/shard_map/ppermute | solution.py:909
  8.7 8.5 %collective-permute-start = (bf16[192,256]{1,0:T(8,128)(2,1)}, bf16[192,256]{1,0:T(8,128)(2,1)S(1)}, u32[]{:S(2)}, u32[]{:S(2)}) collective-permute-start(bf16[192,256]{1,0:T(8,128)(2,1)} %get-tuple-element.93), channel_id=1, source_target_pairs={{0,1},{1,0},{2,3},{3,2},{4,5},{5,4},{6,7},{7,6},{8,9},{9,8},{10,11... | collective-permute-start | bytes 294920 | tf_op jit(solution)/shard_map/ppermute | solution.py:909
  18.1 9.2 %collective-permute-start.8 = (bf16[240,384]{1,0:T(8,128)(2,1)}, bf16[240,384]{1,0:T(8,128)(2,1)S(1)}, u32[]{:S(2)}, u32[]{:S(2)}) collective-permute-start(bf16[240,384]{1,0:T(8,128)(2,1)} %get-tuple-element.96), channel_id=1, source_target_pairs={{0,3},{1,2},{2,1},{3,0},{4,7},{5,6},{6,5},{7,4},{8,11},{9,10},{10,... | collective-permute-start | bytes 552968 | tf_op jit(solution)/shard_map/ppermute | solution.py:909
  20.7 18.3 %collective-permute-start.5 = (bf16[4,192,256]{2,1,0:T(8,128)(2,1)S(1)}, bf16[4,192,256]{2,1,0:T(8,128)(2,1)S(1)}, u32[]{:S(2)}, u32[]{:S(2)}) collective-permute-start(bf16[4,192,256]{2,1,0:T(8,128)(2,1)S(1)} %pad_maximum_fusion.1.p0), channel_id=1, source_target_pairs={{0,24},{4,28},{8,16},{12,20},{16,8},{20,12},{24,0},{28,4},{1,25},{... | collective-permute-start | bytes 1179656 | tf_op jit(solution)/shard_map/ppermute | solution.py:913
  23.3 16.6 %collective-permute-start.4 = (bf16[4,192,256]{2,1,0:T(8,128)(2,1)S(1)}, bf16[4,192,256]{2,1,0:T(8,128)(2,1)S(1)}, u32[]{:S(2)}, u32[]{:S(2)}) collective-permute-start(bf16[4,192,256]{2,1,0:T(8,128)(2,1)S(1)} %pad_maximum_fusion.1.p0), channel_id=1, source_target_pairs={{0,16},{4,20},{8,24},{12,28},{16,0},{20,4},{24,8},{28,12},{1,17},{... | collective-permute-start | bytes 1179656 | tf_op jit(solution)/shard_map/ppermute | solution.py:913
  23.7 16.3 %collective-permute-start.3 = (bf16[4,192,256]{2,1,0:T(8,128)(2,1)S(1)}, bf16[4,192,256]{2,1,0:T(8,128)(2,1)S(1)}, u32[]{:S(2)}, u32[]{:S(2)}) collective-permute-start(bf16[4,192,256]{2,1,0:T(8,128)(2,1)S(1)} %pad_maximum_fusion.1.p0), channel_id=1, source_target_pairs={{0,8},{4,12},{8,0},{12,4},{16,24},{20,28},{24,16},{28,20},{1,9},{5... | collective-permute-start | bytes 1179656 | tf_op jit(solution)/shard_map/ppermute | solution.py:913
  24.2 11.6 %collective-permute-start.7 = (bf16[240,384]{1,0:T(8,128)(2,1)}, bf16[240,384]{1,0:T(8,128)(2,1)S(1)}, u32[]{:S(2)}, u32[]{:S(2)}) collective-permute-start(bf16[240,384]{1,0:T(8,128)(2,1)} %get-tuple-element.96), channel_id=1, source_target_pairs={{0,2},{1,3},{2,0},{3,1},{4,6},{5,7},{6,4},{7,5},{8,10},{9,11},{10,... | collective-permute-start | bytes 552968 | tf_op jit(solution)/shard_map/ppermute | solution.py:909
  27.3 10.6 %collective-permute-start.6 = (bf16[240,384]{1,0:T(8,128)(2,1)}, bf16[240,384]{1,0:T(8,128)(2,1)S(1)}, u32[]{:S(2)}, u32[]{:S(2)}) collective-permute-start(bf16[240,384]{1,0:T(8,128)(2,1)} %get-tuple-element.96), channel_id=1, source_target_pairs={{0,1},{1,0},{2,3},{3,2},{4,5},{5,4},{6,7},{7,6},{8,9},{9,8},{10,11... | collective-permute-start | bytes 552968 | tf_op jit(solution)/shard_map/ppermute | solution.py:909
  41.7 30.0 %collective-permute-start.15 = (bf16[4,240,384]{2,1,0:T(8,128)(2,1)S(1)}, bf16[4,240,384]{2,1,0:T(8,128)(2,1)}, u32[]{:S(2)}, u32[]{:S(2)}) collective-permute-start(bf16[4,240,384]{2,1,0:T(8,128)(2,1)S(1)} %pad_maximum_fusion.p0), channel_id=1, source_target_pairs={{0,24},{4,28},{8,16},{12,20},{16,8},{20,12},{24,0},{28,4},{1,25},{... | collective-permute-start | bytes 2211848 | tf_op jit(solution)/shard_map/ppermute | solution.py:913
  43.7 33.3 %collective-permute-start.14 = (bf16[4,240,384]{2,1,0:T(8,128)(2,1)S(1)}, bf16[4,240,384]{2,1,0:T(8,128)(2,1)}, u32[]{:S(2)}, u32[]{:S(2)}) collective-permute-start(bf16[4,240,384]{2,1,0:T(8,128)(2,1)S(1)} %pad_maximum_fusion.p0), channel_id=1, source_target_pairs={{0,16},{4,20},{8,24},{12,28},{16,0},{20,4},{24,8},{28,12},{1,17},{... | collective-permute-start | bytes 2211848 | tf_op jit(solution)/shard_map/ppermute | solution.py:913
  44.9 32.1 %collective-permute-start.13 = (bf16[4,240,384]{2,1,0:T(8,128)(2,1)S(1)}, bf16[4,240,384]{2,1,0:T(8,128)(2,1)}, u32[]{:S(2)}, u32[]{:S(2)}) collective-permute-start(bf16[4,240,384]{2,1,0:T(8,128)(2,1)S(1)} %pad_maximum_fusion.p0), channel_id=1, source_target_pairs={{0,8},{4,12},{8,0},{12,4},{16,24},{20,28},{24,16},{28,20},{1,9},{5... | collective-permute-start | bytes 2211848 | tf_op jit(solution)/shard_map/ppermute | solution.py:913
  127.8 32.3 %collective-permute-start.23 = (bf16[4,240,384]{2,1,0:T(8,128)(2,1)}, bf16[4,240,384]{2,1,0:T(8,128)(2,1)S(1)}, u32[]{:S(2)}, u32[]{:S(2)}) collective-permute-start(bf16[4,240,384]{2,1,0:T(8,128)(2,1)} %get-tuple-element.170), channel_id=1, source_target_pairs={{0,24},{4,28},{8,16},{12,20},{16,8},{20,12},{24,0},{28,4},{1,25},{... | collective-permute-start | bytes 2211848 | tf_op jit(solution)/shard_map/ppermute | solution.py:913
  129.5 33.7 %collective-permute-start.22 = (bf16[4,240,384]{2,1,0:T(8,128)(2,1)}, bf16[4,240,384]{2,1,0:T(8,128)(2,1)S(1)}, u32[]{:S(2)}, u32[]{:S(2)}) collective-permute-start(bf16[4,240,384]{2,1,0:T(8,128)(2,1)} %get-tuple-element.171), channel_id=1, source_target_pairs={{0,16},{4,20},{8,24},{12,28},{16,0},{20,4},{24,8},{28,12},{1,17},{... | collective-permute-start | bytes 2211848 | tf_op jit(solution)/shard_map/ppermute | solution.py:913
  130.6 32.7 %collective-permute-start.21 = (bf16[4,240,384]{2,1,0:T(8,128)(2,1)S(1)}, bf16[4,240,384]{2,1,0:T(8,128)(2,1)S(1)}, u32[]{:S(2)}, u32[]{:S(2)}) collective-permute-start(bf16[4,240,384]{2,1,0:T(8,128)(2,1)S(1)} %get-tuple-element.172), channel_id=1, source_target_pairs={{0,8},{4,12},{8,0},{12,4},{16,24},{20,28},{24,16},{28,20},{1,9},{5... | collective-permute-start | bytes 2211848 | tf_op jit(solution)/shard_map/ppermute | solution.py:913
  168.9 21.9 %collective-permute-start.29 = (bf16[4,192,256]{2,1,0:T(8,128)(2,1)S(1)}, bf16[4,192,256]{2,1,0:T(8,128)(2,1)S(1)}, u32[]{:S(2)}, u32[]{:S(2)}) collective-permute-start(bf16[4,192,256]{2,1,0:T(8,128)(2,1)S(1)} %get-tuple-element.174), channel_id=1, source_target_pairs={{0,24},{4,28},{8,16},{12,20},{16,8},{20,12},{24,0},{28,4},{1,25},{... | collective-permute-start | bytes 1179656 | tf_op jit(solution)/shard_map/ppermute | solution.py:913
  170.7 20.1 %collective-permute-start.28 = (bf16[4,192,256]{2,1,0:T(8,128)(2,1)S(1)}, bf16[4,192,256]{2,1,0:T(8,128)(2,1)S(1)}, u32[]{:S(2)}, u32[]{:S(2)}) collective-permute-start(bf16[4,192,256]{2,1,0:T(8,128)(2,1)S(1)} %get-tuple-element.175), channel_id=1, source_target_pairs={{0,16},{4,20},{8,24},{12,28},{16,0},{20,4},{24,8},{28,12},{1,17},{... | collective-permute-start | bytes 1179656 | tf_op jit(solution)/shard_map/ppermute | solution.py:913
  171.7 19.0 %collective-permute-start.27 = (bf16[4,192,256]{2,1,0:T(8,128)(2,1)S(1)}, bf16[4,192,256]{2,1,0:T(8,128)(2,1)S(1)}, u32[]{:S(2)}, u32[]{:S(2)}) collective-permute-start(bf16[4,192,256]{2,1,0:T(8,128)(2,1)S(1)} %get-tuple-element.176), channel_id=1, source_target_pairs={{0,8},{4,12},{8,0},{12,4},{16,24},{20,28},{24,16},{28,20},{1,9},{5... | collective-permute-start | bytes 1179656 | tf_op jit(solution)/shard_map/ppermute | solution.py:913
  172.9 15.3 %collective-permute-start.26 = (bf16[240,384]{1,0:T(8,128)(2,1)S(1)}, bf16[240,384]{1,0:T(8,128)(2,1)S(1)}, u32[]{:S(2)}, u32[]{:S(2)}) collective-permute-start(bf16[240,384]{1,0:T(8,128)(2,1)S(1)} %get-tuple-element.180), channel_id=1, source_target_pairs={{0,2},{1,3},{2,0},{3,1},{4,6},{5,7},{6,4},{7,5},{8,10},{9,11},{10,... | collective-permute-start | bytes 552968 | tf_op jit(solution)/shard_map/ppermute | solution.py:909
  173.4 17.4 %collective-permute-start.25 = (bf16[240,384]{1,0:T(8,128)(2,1)S(1)}, bf16[240,384]{1,0:T(8,128)(2,1)S(1)}, u32[]{:S(2)}, u32[]{:S(2)}) collective-permute-start(bf16[240,384]{1,0:T(8,128)(2,1)S(1)} %get-tuple-element.181), channel_id=1, source_target_pairs={{0,1},{1,0},{2,3},{3,2},{4,5},{5,4},{6,7},{7,6},{8,9},{9,8},{10,11... | collective-permute-start | bytes 552968 | tf_op jit(solution)/shard_map/ppermute | solution.py:909
  188.2 8.4 %collective-permute-start.36 = (bf16[240,384]{1,0:T(8,128)(2,1)S(1)}, bf16[240,384]{1,0:T(8,128)(2,1)S(1)}, u32[]{:S(2)}, u32[]{:S(2)}) collective-permute-start(bf16[240,384]{1,0:T(8,128)(2,1)S(1)} %get-tuple-element.152), channel_id=1, source_target_pairs={{0,3},{1,2},{2,1},{3,0},{4,7},{5,6},{6,5},{7,4},{8,11},{9,10},{10,... | collective-permute-start | bytes 552968 | tf_op jit(solution)/shard_map/ppermute | solution.py:909
  190.9 11.8 %collective-permute-start.30 = (bf16[192,256]{1,0:T(8,128)(2,1)S(1)}, bf16[192,256]{1,0:T(8,128)(2,1)S(1)}, u32[]{:S(2)}, u32[]{:S(2)}) collective-permute-start(bf16[192,256]{1,0:T(8,128)(2,1)S(1)} %get-tuple-element.182), channel_id=1, source_target_pairs={{0,1},{1,0},{2,3},{3,2},{4,5},{5,4},{6,7},{7,6},{8,9},{9,8},{10,11... | collective-permute-start | bytes 294920 | tf_op jit(solution)/shard_map/ppermute | solution.py:909
  196.7 10.4 %collective-permute-start.39 = (bf16[240,384]{1,0:T(8,128)(2,1)S(1)}, bf16[240,384]{1,0:T(8,128)(2,1)S(1)}, u32[]{:S(2)}, u32[]{:S(2)}) collective-permute-start(bf16[240,384]{1,0:T(8,128)(2,1)S(1)} %add_convert_fusion.8.p0), channel_id=1, source_target_pairs={{0,24},{4,28},{8,16},{12,20},{16,8},{20,12},{24,0},{28,4},{1,25},{... | collective-permute-start | bytes 552968 | tf_op jit(solution)/shard_map/ppermute | solution.py:913
  198.4 9.2 %collective-permute-start.38 = (bf16[240,384]{1,0:T(8,128)(2,1)S(1)}, bf16[240,384]{1,0:T(8,128)(2,1)S(1)}, u32[]{:S(2)}, u32[]{:S(2)}) collective-permute-start(bf16[240,384]{1,0:T(8,128)(2,1)S(1)} %add_convert_fusion.8.p0), channel_id=1, source_target_pairs={{0,16},{4,20},{8,24},{12,28},{16,0},{20,4},{24,8},{28,12},{1,17},{... | collective-permute-start | bytes 552968 | tf_op jit(solution)/shard_map/ppermute | solution.py:913
  (51 other events, 247.6 us)

commit v7 on v6

--- a/solution.py
+++ b/solution.py
@@ -518,7 +518,7 @@
 def mixer_backward(
     place, vec, gvec, xm_any, packed_any, plong_any, pshort_any, dw_any, kc_any, cq_any, kp_any,
     cv_any, gctx_any, p0, p1, p2, p3, p4, p5, p6, p7,
-    keep, send, grads_any, gdep_any,
+    keep, send0, send1, send2, send3, grads_any, gdep_any,
     wm, xm, packed, plong, pshort, dw, kc, cq, kp, cv, gctx,
     xpad, gcp, gdp, grads, gqc, dkv, gkc, glog, gprob, gdep, gb, spread, gather, wk, sem, sems,
     out_sem,
@@ -613,9 +613,11 @@
             def _():
                 pltpu.make_async_copy(source, keep.at[chip, far_off], out_sem.at[0]).start()
 
-            @pl.when((where & 1) == 1)
-            def _():
-                pltpu.make_async_copy(source, send.at[chip, far_off], out_sem.at[0]).start()
+            for k, send in enumerate((send0, send1, send2, send3)):
+
+                @pl.when(where == 2 * k + 1)
+                def _():
+                    pltpu.make_async_copy(source, send.at[far_off], out_sem.at[0]).start()
 
     def depth(i):
         ps = padded_start(i)
@@ -824,7 +826,7 @@
 ANY = pl.BlockSpec(memory_space=pl.ANY)
 
 
-VMEM_MIB = {'unpack_ffn': 12, 'unpack_mixer': 12, 'input_gradient': 24}
+VMEM_MIB = {'unpack_ffn': 12, 'unpack_mixer': 12}
 
 
 def call(kernel, specs, outs, scratch, flops, *args, out_specs=None):
@@ -876,9 +878,8 @@
 
 
 def backward_mixer(place, vec, gvec, arrays, pieces):
-    outs = [
-        ((4, 4, 192, 256), BF), ((4, 4, 192, 256), BF), ((ROWS, 4 * AH), BF), ((PAD, D), F32),
-    ]
+    outs = [((4, 4, 192, 256), BF)] + [((4, 192, 256), BF)] * 4
+    outs += [((ROWS, 4 * AH), BF), ((PAD, D), F32)]
     scratch = [((SLOTS, D, 256), BF)] + [(a.shape, a.dtype) for a in arrays] + [
         ((PAD, D), F32), ((PAD, AH), F32), ((PAD, D), F32), ((ROWS, 4 * AH), BF),
         ((ROWS, AH), F32), ((2, LONG, 128), F32), ((ROWS, AH), BF), ((ROWS, 128), BF),
@@ -890,7 +891,7 @@
     return call(
         mixer_backward, [SMEM] + [VMEM] * 2 + [ANY] * 18, outs,
         (scratch, dma, dma((10,)), dma((3,))), 40 * 10**9,
-        place, vec, gvec, *arrays, *pieces, out_specs=[ANY] * 4,
+        place, vec, gvec, *arrays, *pieces, out_specs=[ANY] * 7,
     )
 
 
@@ -976,12 +977,15 @@
     ga = reduce_cores(keep, near(send, 1))
     ga_sent = send_chips(ga)
     gctx, ga = lax.optimization_barrier((gctx, ga))
-    keep, send, grads, gdp = backward_mixer(
+    keep, s0, s1, s2, s3, grads, gdp = backward_mixer(
         place, vec, gvec, (xm, packed, plong, pshort, dw, kc, cq, kp, cv, gctx), mixer
     )
-    keep, send, ga_sent = lax.optimization_barrier((keep, send, ga_sent))
-    gb = reduce_cores(keep, near(send, 1))
-    gb_sent = send_chips(gb)
+    gb = [total(keep[1], [near(s1, 1)]), total(keep[2], [near(s2, 1)])]
+    keep, s0, s3, gb, ga_sent = lax.optimization_barrier((keep, s0, s3, gb, ga_sent))
+    gb_sent = [near(gb[0], 2), near(gb[1], 4)]
+    gb3 = total(keep[3], [near(s3, 1)])
+    gb_sent.append(near(gb3, 6))
+    gb = [total(keep[0], [near(s0, 1)]), gb[0], gb[1], gb3]
     ga_sent, gb = lax.optimization_barrier((ga_sent, gb))
     ga = reduce_chips(ga[0], ga_sent)
     ga_sent = [far(ga[1], 1), far(ga[2], 2)]

time: 222 us -> 218 us (0.982)
  waiting for transfers between devices: 51.1 us -> 43.2 us
  other arithmetic: 8.9 us -> 12.9 us
  starting transfers between devices: 49.3 us -> 51.8 us
    ppermute x36 -> x39, waiting for transfers between devices: 25.9 us -> 20.7 us  [near(): return lax.ppermute(values, 'wide', [(i, i ^ bit) for i in range(SLOTS)])]
    ppermute x12, waiting for transfers between devices: 25.2 us -> 22.5 us  [far(): return lax.ppermute(values, 'narrow', [(i, i ^ bit) for i in range(4)])]
    convert_element_type x4 -> x5, other arithmetic: 5.8 us -> 7.83 us  [total(): return result.astype(BF)]
    ppermute x36 -> x39, starting transfers between devices: 25.6 us -> 26.7 us  [near(): return lax.ppermute(values, 'wide', [(i, i ^ bit) for i in range(SLOTS)])]
  transfers between devices with their start and end apart: 48 -> 51, of which waited for: 23 -> 24; matrix products, arithmetic and copies ran while one was open for 1% -> 4% of each run, Pallas kernels for 31% -> 31%
where the time goes in v7:
time: 218 us
  Pallas kernels  106 us (49%)
  starting transfers between devices  51.8 us (24%)
  waiting for transfers between devices  43.2 us (20%)
  other arithmetic  12.9 us (6%)
    pallas_call x7, Pallas kernels, call(): pl.pallas_call(kernel, out_shape=[jax.ShapeDtypeStruct(s, d) for s, d in...  106 us
    ppermute x39, starting transfers between devices, near(): return lax.ppermute(values, 'wide', [(i, i ^ bit) for i in range(SLOTS)])  26.7 us
    ppermute x12, starting transfers between devices, far(): return lax.ppermute(values, 'narrow', [(i, i ^ bit) for i in range(4)])  25.1 us
    ppermute x12, waiting for transfers between devices, far(): return lax.ppermute(values, 'narrow', [(i, i ^ bit) for i in range(4)])  22.5 us
    ppermute x39, waiting for transfers between devices, near(): return lax.ppermute(values, 'wide', [(i, i ^ bit) for i in range(SLOTS)])  20.7 us
    convert_element_type x5, other arithmetic, total(): return result.astype(BF)  7.83 us
  transfers between devices with their start and end apart: 51, of which 24 were waited for; matrix products, arithmetic and copies ran while one was open for 4% of the time, Pallas kernels for 31%

profile of v7, /device:TPU:0, one launch (start us, length us, event | category | flops | bytes accessed | tf_op | source)
XLA Modules:
  0.0 217.6 jit_solution(16534389209342346231)
XLA Ops:
  1.2 2.4 %pack.1 = (bf16[192,256]{1,0:T(8,128)(2,1)}, bf16[240,384]{1,0:T(8,128)(2,1)}) custom-call(s32[2]{0:T(128)} %pad_add_fusion.place, bf16[192,1152]{1,0:T(8,128)(2,1)} %qkv.1, bf16[9,192]{1,0:T(8,128)(2,1)} %depth.1, bf16[192,384]{1,0:T(8,128)(2,1)} %point.1, bf16[54,96]{1,0:T(8,128)(2,1)} %bitcast.71, bf16[192,384]{1,0:T(8,128)(2,1)} %convout.1, ...), custom_call_target="tpu_custom_call" | custom-call | flops 1000000000 | bytes 1048576 | tf_op jit(solution)/shard_map/pack/pallas_call | solution.py:833
  3.6 5.0 %collective-permute-start.2 = (bf16[192,256]{1,0:T(8,128)(2,1)}, bf16[192,256]{1,0:T(8,128)(2,1)S(1)}, u32[]{:S(2)}, u32[]{:S(2)}) collective-permute-start(bf16[192,256]{1,0:T(8,128)(2,1)} %get-tuple-element.99), channel_id=1, source_target_pairs={{0,3},{1,2},{2,1},{3,0},{4,7},{5,6},{6,5},{7,4},{8,11},{9,10},{10,... | collective-permute-start | bytes 294920 | tf_op jit(solution)/shard_map/ppermute | solution.py:910
  9.3 3.3 %collective-permute-done.2 = bf16[192,256]{1,0:T(8,128)(2,1)S(1)} collective-permute-done((bf16[192,256]{1,0:T(8,128)(2,1)}, bf16[192,256]{1,0:T(8,128)(2,1)S(1)}, u32[]{:S(2)}, u32[]{:S(2)}) %collective-permute-start.2) | collective-permute-done | bytes 98336 | tf_op jit(solution)/shard_map/ppermute | solution.py:910
  12.6 4.6 %collective-permute-done.1 = bf16[192,256]{1,0:T(8,128)(2,1)S(1)} collective-permute-done((bf16[192,256]{1,0:T(8,128)(2,1)}, bf16[192,256]{1,0:T(8,128)(2,1)S(1)}, u32[]{:S(2)}, u32[]{:S(2)}) %collective-permute-start.1) | collective-permute-done | bytes 98336 | tf_op jit(solution)/shard_map/ppermute | solution.py:910
  18.1 2.6 %collective-permute-start.8 = (bf16[240,384]{1,0:T(8,128)(2,1)}, bf16[240,384]{1,0:T(8,128)(2,1)S(1)}, u32[]{:S(2)}, u32[]{:S(2)}) collective-permute-start(bf16[240,384]{1,0:T(8,128)(2,1)} %get-tuple-element.102), channel_id=1, source_target_pairs={{0,3},{1,2},{2,1},{3,0},{4,7},{5,6},{6,5},{7,4},{8,11},{9,10},{10,... | collective-permute-start | bytes 552968 | tf_op jit(solution)/shard_map/ppermute | solution.py:910
  20.7 2.6 %collective-permute-start.5 = (bf16[4,192,256]{2,1,0:T(8,128)(2,1)S(1)}, bf16[4,192,256]{2,1,0:T(8,128)(2,1)S(1)}, u32[]{:S(2)}, u32[]{:S(2)}) collective-permute-start(bf16[4,192,256]{2,1,0:T(8,128)(2,1)S(1)} %pad_maximum_fusion.1.p0), channel_id=1, source_target_pairs={{0,24},{4,28},{8,16},{12,20},{16,8},{20,12},{24,0},{28,4},{1,25},{... | collective-permute-start | bytes 1179656 | tf_op jit(solution)/shard_map/ppermute | solution.py:914
  24.2 3.1 %collective-permute-done.8 = bf16[240,384]{1,0:T(8,128)(2,1)S(1)} collective-permute-done((bf16[240,384]{1,0:T(8,128)(2,1)}, bf16[240,384]{1,0:T(8,128)(2,1)S(1)}, u32[]{:S(2)}, u32[]{:S(2)}) %collective-permute-start.8) | collective-permute-done | bytes 184352 | tf_op jit(solution)/shard_map/ppermute | solution.py:910
  27.3 6.9 %collective-permute-start.6 = (bf16[240,384]{1,0:T(8,128)(2,1)}, bf16[240,384]{1,0:T(8,128)(2,1)S(1)}, u32[]{:S(2)}, u32[]{:S(2)}) collective-permute-start(bf16[240,384]{1,0:T(8,128)(2,1)} %get-tuple-element.102), channel_id=1, source_target_pairs={{0,1},{1,0},{2,3},{3,2},{4,5},{5,4},{6,7},{7,6},{8,9},{9,8},{10,11... | collective-permute-start | bytes 552968 | tf_op jit(solution)/shard_map/ppermute | solution.py:910
  35.8 2.2 %collective-permute-done.6 = bf16[240,384]{1,0:T(8,128)(2,1)S(1)} collective-permute-done((bf16[240,384]{1,0:T(8,128)(2,1)}, bf16[240,384]{1,0:T(8,128)(2,1)S(1)}, u32[]{:S(2)}, u32[]{:S(2)}) %collective-permute-start.6) | collective-permute-done | bytes 184352 | tf_op jit(solution)/shard_map/ppermute | solution.py:910
  41.7 2.1 collective-permute-start.15
  46.5 25.5 %mixer_forward.1 = (bf16[768,768]{1,0:T(8,128)(2,1)}, bf16[768,1152]{1,0:T(8,128)(2,1)}, bf16[6,512,512]{2,1,0:T(8,128)(2,1)}, bf16[2,6,128,128]{3,2,1,0:T(8,128...) custom-call(s32[2]{0:T(128)} %pad_add_fusion.place, ...), custom_call_target="tpu_custom_call" | custom-call | flops 30000001024 | bytes 1048576 | tf_op jit(solution)/shard_map/mixer_forward/pallas_call | solution.py:833
  72.0 4.9 %collective-permute-done.14.p2 = bf16[4,240,384]{2,1,0:T(8,128)(2,1)S(1)} collective-permute-done((bf16[4,240,384]{2,1,0:T(8,128)(2,1)S(1)}, bf16[4,240,384]{2,1,0:T(8,128)(2,1)S(1)}, u32[]{:S(2)}, u32[]{:S(2)}) %collective-permute-start.14) | collective-permute-done | bytes 737312 | tf_op jit(solution)/shard_map/ppermute | solution.py:914
  83.3 35.1 %ffn_both.1 = (bf16[512,768]{1,0:T(8,128)(2,1)}, bf16[256,768]{1,0:T(8,128)(2,1)}, bf16[4,4,240,384]{3,2,1,0:T(8,128)(2,1)}, bf16[4,4,240,384]{3,2,1,0:T(8,128)(...) custom-call(s32[2]{0:T(128)} %pad_add_fusion.place, s32[1]{0:T(128)S(6)} %copy.34.llen, ...), custom_call_target="tpu_custom_call" | custom-call | flops 60000002048 | bytes 1048576 | tf_op jit(solution)/shard_map/ffn_both/pallas_call | solution.py:833
  118.6 5.5 %collective-permute-done.20 = bf16[4,4,240,384]{3,2,1,0:T(8,128)(2,1)S(1)} collective-permute-done((bf16[4,4,240,384]{3,2,1,0:T(8,128)(2,1)}, bf16[4,4,240,384]{3,2,1,0:T(8,128)(2,1)S(1)}, u32[]{:S(2)}, u32[]{:S(2)}) %collective-permute-start.20) | collective-permute-done | bytes 2949152 | tf_op jit(solution)/shard_map/ppermute | solution.py:914
  124.0 3.7 %fusion.7 = (bf16[4,240,384]{2,1,0:T(8,128)(2,1)}, bf16[4,240,384]{2,1,0:T(8,128)(2,1)}, bf16[4,240,384]{2,1,0:T(8,128)(2,1)}, bf16[4,240,384]{2,1,0:T(8,128)(2,1)S(1)}) fusion(bf16[4,4,240,384]{3,2,1,0:T(8,128)(2,1)S(1)} %collective-permute-done.20, bf16[4,4,240,384]{3,2,1,0:T(8,128)(2,1)} %get-tuple-element.119), kind=kLoop, calls=%fused_computation.15 | loop fusion | flops 5898240 | bytes 8847360 | tf_op jit(solution)/shard_map/convert_element_type | solution.py:933
  131.2 28.9 %mixer_backward.1 = (bf16[4,4,192,256]{3,2,1,0:T(8,128)(2,1)}, bf16[4,192,256]{2,1,0:T(8,128)(2,1)}, bf16[4,192,256]{2,1,0:T(8,128)(2,1)}, bf16[4,192,256]{2,1,0...) custom-call(s32[2]{0:T(128)} %pad_add_fusion.place, ...), custom_call_target="tpu_custom_call" | custom-call | flops 40000000000 | bytes 1048576 | tf_op jit(solution)/shard_map/mixer_backward/pallas_call | solution.py:833
  162.7 2.0 fusion.2
  172.8 10.0 %input_gradient.1 = (bf16[512,768]{1,0:T(8,128)(2,1)}, bf16[256,768]{1,0:T(8,128)(2,1)}) custom-call(s32[2]{0:T(128)} %pad_add_fusion.place, s32[1]{0:T(128)S(6)} %copy.34.llen, s32[2]{0:T(128)} %slen.5, f32[24,768]{1,0:T(8,128)} %get-tuple-element.107.vec, bf16[768,1536]{1,0:T(8,128)(2,1)} %get-tuple-element.150.grads_any, ...), custom_call_target="tpu_custom_call" | custom-call | flops 5000000000 | bytes 1048576 | tf_op jit(solution)/shard_map/input_gradient/pallas_call | solution.py:833
  182.8 2.5 %collective-permute-start.39 = (bf16[240,384]{1,0:T(8,128)(2,1)S(1)}, bf16[240,384]{1,0:T(8,128)(2,1)S(1)}, u32[]{:S(2)}, u32[]{:S(2)}) collective-permute-start(bf16[240,384]{1,0:T(8,128)(2,1)S(1)} %get-tuple-element.164), channel_id=1, source_target_pairs={{0,3},{1,2},{2,1},{3,0},{4,7},{5,6},{6,5},{7,4},{8,11},{9,10},{10,... | collective-permute-start | bytes 552968 | tf_op jit(solution)/shard_map/ppermute | solution.py:910
  189.2 2.3 %collective-permute-done.39 = bf16[240,384]{1,0:T(8,128)(2,1)S(1)} collective-permute-done((bf16[240,384]{1,0:T(8,128)(2,1)S(1)}, bf16[240,384]{1,0:T(8,128)(2,1)S(1)}, u32[]{:S(2)}, u32[]{:S(2)}) %collective-permute-start.39) | collective-permute-done | bytes 184352 | tf_op jit(solution)/shard_map/ppermute | solution.py:910
  197.0 2.1 collective-permute-start.34
  199.1 3.4 %collective-permute-done.35 = bf16[192,256]{1,0:T(8,128)(2,1)S(1)} collective-permute-done((bf16[192,256]{1,0:T(8,128)(2,1)S(1)}, bf16[192,256]{1,0:T(8,128)(2,1)S(1)}, u32[]{:S(2)}, u32[]{:S(2)}) %collective-permute-start.35) | collective-permute-done | bytes 98336 | tf_op jit(solution)/shard_map/ppermute | solution.py:910
  203.6 2.0 collective-permute-done.34
  210.3 2.3 %unpack_ffn.1 = (f32[2,96,1536]{2,1,0:T(8,128)}, f32[2,384,384]{2,1,0:T(8,128)}, f32[192,768]{1,0:T(8,128)}) custom-call(s32[2]{0:T(128)S(1)} %copy-done, bf16[240,384]{1,0:T(8,128)(2,1)S(1)} %add_convert_fusion.4.p0, bf16[240,384]{1,0:T(8,128)(2,1)S(1)} %collective-permute-done.40.p1, bf16[240,384]{1,0:T(8,128)(2,1)S(1)} %collective-permute-done.41.p2, ...), custom_call_target="tpu_custom_call" | custom-call | flops 1000000000 | bytes 1048576 | tf_op jit(solution)/shard_map/unpack_ffn/pallas_call | solution.py:833
  (133 shorter events, 51.0 us)
Async XLA Ops:
  3.6 9.0 %collective-permute-start.2 = (bf16[192,256]{1,0:T(8,128)(2,1)}, bf16[192,256]{1,0:T(8,128)(2,1)S(1)}, u32[]{:S(2)}, u32[]{:S(2)}) collective-permute-start(bf16[192,256]{1,0:T(8,128)(2,1)} %get-tuple-element.99), channel_id=1, source_target_pairs={{0,3},{1,2},{2,1},{3,0},{4,7},{5,6},{6,5},{7,4},{8,11},{9,10},{10,... | collective-permute-start | bytes 294920 | tf_op jit(solution)/shard_map/ppermute | solution.py:910
  18.1 9.2 %collective-permute-start.8 = (bf16[240,384]{1,0:T(8,128)(2,1)}, bf16[240,384]{1,0:T(8,128)(2,1)S(1)}, u32[]{:S(2)}, u32[]{:S(2)}) collective-permute-start(bf16[240,384]{1,0:T(8,128)(2,1)} %get-tuple-element.102), channel_id=1, source_target_pairs={{0,3},{1,2},{2,1},{3,0},{4,7},{5,6},{6,5},{7,4},{8,11},{9,10},{10,... | collective-permute-start | bytes 552968 | tf_op jit(solution)/shard_map/ppermute | solution.py:910
  20.7 18.3 %collective-permute-start.5 = (bf16[4,192,256]{2,1,0:T(8,128)(2,1)S(1)}, bf16[4,192,256]{2,1,0:T(8,128)(2,1)S(1)}, u32[]{:S(2)}, u32[]{:S(2)}) collective-permute-start(bf16[4,192,256]{2,1,0:T(8,128)(2,1)S(1)} %pad_maximum_fusion.1.p0), channel_id=1, source_target_pairs={{0,24},{4,28},{8,16},{12,20},{16,8},{20,12},{24,0},{28,4},{1,25},{... | collective-permute-start | bytes 1179656 | tf_op jit(solution)/shard_map/ppermute | solution.py:914
  23.3 16.6 %collective-permute-start.4 = (bf16[4,192,256]{2,1,0:T(8,128)(2,1)S(1)}, bf16[4,192,256]{2,1,0:T(8,128)(2,1)S(1)}, u32[]{:S(2)}, u32[]{:S(2)}) collective-permute-start(bf16[4,192,256]{2,1,0:T(8,128)(2,1)S(1)} %pad_maximum_fusion.1.p0), channel_id=1, source_target_pairs={{0,16},{4,20},{8,24},{12,28},{16,0},{20,4},{24,8},{28,12},{1,17},{... | collective-permute-start | bytes 1179656 | tf_op jit(solution)/shard_map/ppermute | solution.py:914
  23.7 16.3 %collective-permute-start.3 = (bf16[4,192,256]{2,1,0:T(8,128)(2,1)S(1)}, bf16[4,192,256]{2,1,0:T(8,128)(2,1)S(1)}, u32[]{:S(2)}, u32[]{:S(2)}) collective-permute-start(bf16[4,192,256]{2,1,0:T(8,128)(2,1)S(1)} %pad_maximum_fusion.1.p0), channel_id=1, source_target_pairs={{0,8},{4,12},{8,0},{12,4},{16,24},{20,28},{24,16},{28,20},{1,9},{5... | collective-permute-start | bytes 1179656 | tf_op jit(solution)/shard_map/ppermute | solution.py:914
  24.2 11.6 %collective-permute-start.7 = (bf16[240,384]{1,0:T(8,128)(2,1)}, bf16[240,384]{1,0:T(8,128)(2,1)S(1)}, u32[]{:S(2)}, u32[]{:S(2)}) collective-permute-start(bf16[240,384]{1,0:T(8,128)(2,1)} %get-tuple-element.102), channel_id=1, source_target_pairs={{0,2},{1,3},{2,0},{3,1},{4,6},{5,7},{6,4},{7,5},{8,10},{9,11},{10,... | collective-permute-start | bytes 552968 | tf_op jit(solution)/shard_map/ppermute | solution.py:910
  27.3 10.6 %collective-permute-start.6 = (bf16[240,384]{1,0:T(8,128)(2,1)}, bf16[240,384]{1,0:T(8,128)(2,1)S(1)}, u32[]{:S(2)}, u32[]{:S(2)}) collective-permute-start(bf16[240,384]{1,0:T(8,128)(2,1)} %get-tuple-element.102), channel_id=1, source_target_pairs={{0,1},{1,0},{2,3},{3,2},{4,5},{5,4},{6,7},{7,6},{8,9},{9,8},{10,11... | collective-permute-start | bytes 552968 | tf_op jit(solution)/shard_map/ppermute | solution.py:910
  41.7 30.3 %collective-permute-start.15 = (bf16[4,240,384]{2,1,0:T(8,128)(2,1)S(1)}, bf16[4,240,384]{2,1,0:T(8,128)(2,1)S(1)}, u32[]{:S(2)}, u32[]{:S(2)}) collective-permute-start(bf16[4,240,384]{2,1,0:T(8,128)(2,1)S(1)} %pad_maximum_fusion.p0), channel_id=1, source_target_pairs={{0,24},{4,28},{8,16},{12,20},{16,8},{20,12},{24,0},{28,4},{1,25},{... | collective-permute-start | bytes 2211848 | tf_op jit(solution)/shard_map/ppermute | solution.py:914
  43.7 33.2 %collective-permute-start.14 = (bf16[4,240,384]{2,1,0:T(8,128)(2,1)S(1)}, bf16[4,240,384]{2,1,0:T(8,128)(2,1)S(1)}, u32[]{:S(2)}, u32[]{:S(2)}) collective-permute-start(bf16[4,240,384]{2,1,0:T(8,128)(2,1)S(1)} %pad_maximum_fusion.p0), channel_id=1, source_target_pairs={{0,16},{4,20},{8,24},{12,28},{16,0},{20,4},{24,8},{28,12},{1,17},{... | collective-permute-start | bytes 2211848 | tf_op jit(solution)/shard_map/ppermute | solution.py:914
  44.9 32.0 %collective-permute-start.13 = (bf16[4,240,384]{2,1,0:T(8,128)(2,1)S(1)}, bf16[4,240,384]{2,1,0:T(8,128)(2,1)S(1)}, u32[]{:S(2)}, u32[]{:S(2)}) collective-permute-start(bf16[4,240,384]{2,1,0:T(8,128)(2,1)S(1)} %pad_maximum_fusion.p0), channel_id=1, source_target_pairs={{0,8},{4,12},{8,0},{12,4},{16,24},{20,28},{24,16},{28,20},{1,9},{5... | collective-permute-start | bytes 2211848 | tf_op jit(solution)/shard_map/ppermute | solution.py:914
  127.7 37.0 %collective-permute-start.25 = (bf16[4,240,384]{2,1,0:T(8,128)(2,1)}, bf16[4,240,384]{2,1,0:T(8,128)(2,1)S(1)}, u32[]{:S(2)}, u32[]{:S(2)}) collective-permute-start(bf16[4,240,384]{2,1,0:T(8,128)(2,1)} %get-tuple-element.182), channel_id=1, source_target_pairs={{0,24},{4,28},{8,16},{12,20},{16,8},{20,12},{24,0},{28,4},{1,25},{... | collective-permute-start | bytes 2211848 | tf_op jit(solution)/shard_map/ppermute | solution.py:914
  129.4 35.3 %collective-permute-start.24 = (bf16[4,240,384]{2,1,0:T(8,128)(2,1)}, bf16[4,240,384]{2,1,0:T(8,128)(2,1)S(1)}, u32[]{:S(2)}, u32[]{:S(2)}) collective-permute-start(bf16[4,240,384]{2,1,0:T(8,128)(2,1)} %get-tuple-element.183), channel_id=1, source_target_pairs={{0,16},{4,20},{8,24},{12,28},{16,0},{20,4},{24,8},{28,12},{1,17},{... | collective-permute-start | bytes 2211848 | tf_op jit(solution)/shard_map/ppermute | solution.py:914
  130.7 34.1 %collective-permute-start.23 = (bf16[4,240,384]{2,1,0:T(8,128)(2,1)}, bf16[4,240,384]{2,1,0:T(8,128)(2,1)S(1)}, u32[]{:S(2)}, u32[]{:S(2)}) collective-permute-start(bf16[4,240,384]{2,1,0:T(8,128)(2,1)} %get-tuple-element.184), channel_id=1, source_target_pairs={{0,8},{4,12},{8,0},{12,4},{16,24},{20,28},{24,16},{28,20},{1,9},{5... | collective-permute-start | bytes 2211848 | tf_op jit(solution)/shard_map/ppermute | solution.py:914
  165.3 17.5 %collective-permute-start.30 = (bf16[4,192,256]{2,1,0:T(8,128)(2,1)}, bf16[4,192,256]{2,1,0:T(8,128)(2,1)}, u32[]{:S(2)}, u32[]{:S(2)}) collective-permute-start(bf16[4,192,256]{2,1,0:T(8,128)(2,1)} %get-tuple-element.142), channel_id=1, source_target_pairs={{0,8},{4,12},{8,0},{12,4},{16,24},{20,28},{24,16},{28,20},{1,9},{5... | collective-permute-start | bytes 1179656 | tf_op jit(solution)/shard_map/ppermute | solution.py:914
  166.8 19.4 %collective-permute-start.31 = (bf16[4,192,256]{2,1,0:T(8,128)(2,1)S(1)}, bf16[4,192,256]{2,1,0:T(8,128)(2,1)}, u32[]{:S(2)}, u32[]{:S(2)}) collective-permute-start(bf16[4,192,256]{2,1,0:T(8,128)(2,1)S(1)} %get-tuple-element.143), channel_id=1, source_target_pairs={{0,16},{4,20},{8,24},{12,28},{16,0},{20,4},{24,8},{28,12},{1,17},{... | collective-permute-start | bytes 1179656 | tf_op jit(solution)/shard_map/ppermute | solution.py:914
  168.5 17.7 %collective-permute-start.32 = (bf16[4,192,256]{2,1,0:T(8,128)(2,1)}, bf16[4,192,256]{2,1,0:T(8,128)(2,1)}, u32[]{:S(2)}, u32[]{:S(2)}) collective-permute-start(bf16[4,192,256]{2,1,0:T(8,128)(2,1)} %get-tuple-element.193), channel_id=1, source_target_pairs={{0,24},{4,28},{8,16},{12,20},{16,8},{20,12},{24,0},{28,4},{1,25},{... | collective-permute-start | bytes 1179656 | tf_op jit(solution)/shard_map/ppermute | solution.py:914
  170.9 15.3 %collective-permute-start.29 = (bf16[240,384]{1,0:T(8,128)(2,1)}, bf16[240,384]{1,0:T(8,128)(2,1)S(1)}, u32[]{:S(2)}, u32[]{:S(2)}) collective-permute-start(bf16[240,384]{1,0:T(8,128)(2,1)} %get-tuple-element.188), channel_id=1, source_target_pairs={{0,2},{1,3},{2,0},{3,1},{4,6},{5,7},{6,4},{7,5},{8,10},{9,11},{10,... | collective-permute-start | bytes 552968 | tf_op jit(solution)/shard_map/ppermute | solution.py:910
  171.5 14.7 %collective-permute-start.28 = (bf16[240,384]{1,0:T(8,128)(2,1)}, bf16[240,384]{1,0:T(8,128)(2,1)S(1)}, u32[]{:S(2)}, u32[]{:S(2)}) collective-permute-start(bf16[240,384]{1,0:T(8,128)(2,1)} %get-tuple-element.189), channel_id=1, source_target_pairs={{0,1},{1,0},{2,3},{3,2},{4,5},{5,4},{6,7},{7,6},{8,9},{9,8},{10,11... | collective-permute-start | bytes 552968 | tf_op jit(solution)/shard_map/ppermute | solution.py:910
  182.8 8.8 %collective-permute-start.39 = (bf16[240,384]{1,0:T(8,128)(2,1)S(1)}, bf16[240,384]{1,0:T(8,128)(2,1)S(1)}, u32[]{:S(2)}, u32[]{:S(2)}) collective-permute-start(bf16[240,384]{1,0:T(8,128)(2,1)S(1)} %get-tuple-element.164), channel_id=1, source_target_pairs={{0,3},{1,2},{2,1},{3,0},{4,7},{5,6},{6,5},{7,4},{8,11},{9,10},{10,... | collective-permute-start | bytes 552968 | tf_op jit(solution)/shard_map/ppermute | solution.py:910
  187.6 9.4 %collective-permute-start.33 = (bf16[192,256]{1,0:T(8,128)(2,1)S(1)}, bf16[192,256]{1,0:T(8,128)(2,1)S(1)}, u32[]{:S(2)}, u32[]{:S(2)}) collective-permute-start(bf16[192,256]{1,0:T(8,128)(2,1)S(1)} %get-tuple-element.190), channel_id=1, source_target_pairs={{0,1},{1,0},{2,3},{3,2},{4,5},{5,4},{6,7},{7,6},{8,9},{9,8},{10,11... | collective-permute-start | bytes 294920 | tf_op jit(solution)/shard_map/ppermute | solution.py:910
  191.7 10.8 %collective-permute-start.42 = (bf16[240,384]{1,0:T(8,128)(2,1)S(1)}, bf16[240,384]{1,0:T(8,128)(2,1)S(1)}, u32[]{:S(2)}, u32[]{:S(2)}) collective-permute-start(bf16[240,384]{1,0:T(8,128)(2,1)S(1)} %add_convert_fusion.4.p0), channel_id=1, source_target_pairs={{0,24},{4,28},{8,16},{12,20},{16,8},{20,12},{24,0},{28,4},{1,25},{... | collective-permute-start | bytes 552968 | tf_op jit(solution)/shard_map/ppermute | solution.py:914
  192.9 10.1 %collective-permute-start.41 = (bf16[240,384]{1,0:T(8,128)(2,1)S(1)}, bf16[240,384]{1,0:T(8,128)(2,1)S(1)}, u32[]{:S(2)}, u32[]{:S(2)}) collective-permute-start(bf16[240,384]{1,0:T(8,128)(2,1)S(1)} %add_convert_fusion.4.p0), channel_id=1, source_target_pairs={{0,16},{4,20},{8,24},{12,28},{16,0},{20,4},{24,8},{28,12},{1,17},{... | collective-permute-start | bytes 552968 | tf_op jit(solution)/shard_map/ppermute | solution.py:914
  194.6 8.6 %collective-permute-start.40 = (bf16[240,384]{1,0:T(8,128)(2,1)S(1)}, bf16[240,384]{1,0:T(8,128)(2,1)S(1)}, u32[]{:S(2)}, u32[]{:S(2)}) collective-permute-start(bf16[240,384]{1,0:T(8,128)(2,1)S(1)} %add_convert_fusion.4.p0), channel_id=1, source_target_pairs={{0,8},{4,12},{8,0},{12,4},{16,24},{20,28},{24,16},{28,20},{1,9},{5... | collective-permute-start | bytes 552968 | tf_op jit(solution)/shard_map/ppermute | solution.py:914
  197.0 8.5 %collective-permute-start.34 = (bf16[192,256]{1,0:T(8,128)(2,1)S(1)}, bf16[192,256]{1,0:T(8,128)(2,1)S(1)}, u32[]{:S(2)}, u32[]{:S(2)}) collective-permute-start(bf16[192,256]{1,0:T(8,128)(2,1)S(1)} %get-tuple-element.192), channel_id=1, source_target_pairs={{0,2},{1,3},{2,0},{3,1},{4,6},{5,7},{6,4},{7,5},{8,10},{9,11},{10,... | collective-permute-start | bytes 294920 | tf_op jit(solution)/shard_map/ppermute | solution.py:910
  (46 other events, 284.1 us)

commit v8 on v7

--- a/solution.py
+++ b/solution.py
@@ -988,12 +988,12 @@
     gb = [total(keep[0], [near(s0, 1)]), gb[0], gb[1], gb3]
     ga_sent, gb = lax.optimization_barrier((ga_sent, gb))
     ga = reduce_chips(ga[0], ga_sent)
-    ga_sent = [far(ga[1], 1), far(ga[2], 2)]
+    ga_sent = [far(ga[3], 3), far(ga[2], 2)]
     grads, ga = lax.optimization_barrier((grads, ga))
     il, is_ = backward_inputs(scalars, vec, grads, gdp, gone, mixer)
-    last, il = lax.optimization_barrier((ga[3], il))
+    last, il = lax.optimization_barrier((ga[1], il))
     ga_sent, gb_sent, il = lax.optimization_barrier((ga_sent, gb_sent, il))
-    ga_sent.append(far(last, 3))
+    ga_sent.append(far(last, 1))
     ga = gather_chips(lax.psum(total(ga[0], ga_sent), "hi"))
     gb = reduce_chips(gb[0], gb_sent)
     gb = gather_chips(lax.psum(total(gb[0], send_narrow(gb)), "hi"))

time: 218 us -> 218 us (level)
  transfers between devices with their start and end apart: 51 -> 51, of which waited for: 24 -> 25; matrix products, arithmetic and copies ran while one was open for 4% -> 4% of each run, Pallas kernels for 31% -> 31%
where the time goes in v8:
time: 218 us
  Pallas kernels  106 us (49%)
  starting transfers between devices  50.8 us (23%)
  waiting for transfers between devices  44.1 us (20%)
  other arithmetic  12.9 us (6%)
    pallas_call x7, Pallas kernels, call(): pl.pallas_call(kernel, out_shape=[jax.ShapeDtypeStruct(s, d) for s, d in...  106 us
    ppermute x39, starting transfers between devices, near(): return lax.ppermute(values, 'wide', [(i, i ^ bit) for i in range(SLOTS)])  26.7 us
    ppermute x12, starting transfers between devices, far(): return lax.ppermute(values, 'narrow', [(i, i ^ bit) for i in range(4)])  24.1 us
    ppermute x12, waiting for transfers between devices, far(): return lax.ppermute(values, 'narrow', [(i, i ^ bit) for i in range(4)])  23 us
    ppermute x39, waiting for transfers between devices, near(): return lax.ppermute(values, 'wide', [(i, i ^ bit) for i in range(SLOTS)])  21.1 us
    convert_element_type x5, other arithmetic, total(): return result.astype(BF)  7.83 us
  transfers between devices with their start and end apart: 51, of which 25 were waited for; matrix products, arithmetic and copies ran while one was open for 4% of the time, Pallas kernels for 31%

profile of v8, /device:TPU:0, one launch (start us, length us, event | category | flops | bytes accessed | tf_op | source)
XLA Modules:
  0.0 217.5 jit_solution(7730685472468856290)
XLA Ops:
  1.2 2.4 %pack.1 = (bf16[192,256]{1,0:T(8,128)(2,1)}, bf16[240,384]{1,0:T(8,128)(2,1)}) custom-call(s32[2]{0:T(128)} %pad_add_fusion.place, bf16[192,1152]{1,0:T(8,128)(2,1)} %qkv.1, bf16[9,192]{1,0:T(8,128)(2,1)} %depth.1, bf16[192,384]{1,0:T(8,128)(2,1)} %point.1, bf16[54,96]{1,0:T(8,128)(2,1)} %bitcast.71, bf16[192,384]{1,0:T(8,128)(2,1)} %convout.1, ...), custom_call_target="tpu_custom_call" | custom-call | flops 1000000000 | bytes 1048576 | tf_op jit(solution)/shard_map/pack/pallas_call | solution.py:833
  3.6 5.0 %collective-permute-start.2 = (bf16[192,256]{1,0:T(8,128)(2,1)}, bf16[192,256]{1,0:T(8,128)(2,1)S(1)}, u32[]{:S(2)}, u32[]{:S(2)}) collective-permute-start(bf16[192,256]{1,0:T(8,128)(2,1)} %get-tuple-element.99), channel_id=1, source_target_pairs={{0,3},{1,2},{2,1},{3,0},{4,7},{5,6},{6,5},{7,4},{8,11},{9,10},{10,... | collective-permute-start | bytes 294920 | tf_op jit(solution)/shard_map/ppermute | solution.py:910
  9.3 3.3 %collective-permute-done.2 = bf16[192,256]{1,0:T(8,128)(2,1)S(1)} collective-permute-done((bf16[192,256]{1,0:T(8,128)(2,1)}, bf16[192,256]{1,0:T(8,128)(2,1)S(1)}, u32[]{:S(2)}, u32[]{:S(2)}) %collective-permute-start.2) | collective-permute-done | bytes 98336 | tf_op jit(solution)/shard_map/ppermute | solution.py:910
  12.6 4.6 %collective-permute-done.1 = bf16[192,256]{1,0:T(8,128)(2,1)S(1)} collective-permute-done((bf16[192,256]{1,0:T(8,128)(2,1)}, bf16[192,256]{1,0:T(8,128)(2,1)S(1)}, u32[]{:S(2)}, u32[]{:S(2)}) %collective-permute-start.1) | collective-permute-done | bytes 98336 | tf_op jit(solution)/shard_map/ppermute | solution.py:910
  18.1 2.6 %collective-permute-start.8 = (bf16[240,384]{1,0:T(8,128)(2,1)}, bf16[240,384]{1,0:T(8,128)(2,1)S(1)}, u32[]{:S(2)}, u32[]{:S(2)}) collective-permute-start(bf16[240,384]{1,0:T(8,128)(2,1)} %get-tuple-element.102), channel_id=1, source_target_pairs={{0,3},{1,2},{2,1},{3,0},{4,7},{5,6},{6,5},{7,4},{8,11},{9,10},{10,... | collective-permute-start | bytes 552968 | tf_op jit(solution)/shard_map/ppermute | solution.py:910
  20.7 2.6 %collective-permute-start.5 = (bf16[4,192,256]{2,1,0:T(8,128)(2,1)S(1)}, bf16[4,192,256]{2,1,0:T(8,128)(2,1)S(1)}, u32[]{:S(2)}, u32[]{:S(2)}) collective-permute-start(bf16[4,192,256]{2,1,0:T(8,128)(2,1)S(1)} %pad_maximum_fusion.1.p0), channel_id=1, source_target_pairs={{0,24},{4,28},{8,16},{12,20},{16,8},{20,12},{24,0},{28,4},{1,25},{... | collective-permute-start | bytes 1179656 | tf_op jit(solution)/shard_map/ppermute | solution.py:914
  24.2 3.1 %collective-permute-done.8 = bf16[240,384]{1,0:T(8,128)(2,1)S(1)} collective-permute-done((bf16[240,384]{1,0:T(8,128)(2,1)}, bf16[240,384]{1,0:T(8,128)(2,1)S(1)}, u32[]{:S(2)}, u32[]{:S(2)}) %collective-permute-start.8) | collective-permute-done | bytes 184352 | tf_op jit(solution)/shard_map/ppermute | solution.py:910
  27.3 6.9 %collective-permute-start.6 = (bf16[240,384]{1,0:T(8,128)(2,1)}, bf16[240,384]{1,0:T(8,128)(2,1)S(1)}, u32[]{:S(2)}, u32[]{:S(2)}) collective-permute-start(bf16[240,384]{1,0:T(8,128)(2,1)} %get-tuple-element.102), channel_id=1, source_target_pairs={{0,1},{1,0},{2,3},{3,2},{4,5},{5,4},{6,7},{7,6},{8,9},{9,8},{10,11... | collective-permute-start | bytes 552968 | tf_op jit(solution)/shard_map/ppermute | solution.py:910
  35.8 2.2 %collective-permute-done.6 = bf16[240,384]{1,0:T(8,128)(2,1)S(1)} collective-permute-done((bf16[240,384]{1,0:T(8,128)(2,1)}, bf16[240,384]{1,0:T(8,128)(2,1)S(1)}, u32[]{:S(2)}, u32[]{:S(2)}) %collective-permute-start.6) | collective-permute-done | bytes 184352 | tf_op jit(solution)/shard_map/ppermute | solution.py:910
  41.7 2.1 collective-permute-start.15
  46.5 25.5 %mixer_forward.1 = (bf16[768,768]{1,0:T(8,128)(2,1)}, bf16[768,1152]{1,0:T(8,128)(2,1)}, bf16[6,512,512]{2,1,0:T(8,128)(2,1)}, bf16[2,6,128,128]{3,2,1,0:T(8,128...) custom-call(s32[2]{0:T(128)} %pad_add_fusion.place, ...), custom_call_target="tpu_custom_call" | custom-call | flops 30000001024 | bytes 1048576 | tf_op jit(solution)/shard_map/mixer_forward/pallas_call | solution.py:833
  72.0 4.9 %collective-permute-done.14.p2 = bf16[4,240,384]{2,1,0:T(8,128)(2,1)S(1)} collective-permute-done((bf16[4,240,384]{2,1,0:T(8,128)(2,1)S(1)}, bf16[4,240,384]{2,1,0:T(8,128)(2,1)S(1)}, u32[]{:S(2)}, u32[]{:S(2)}) %collective-permute-start.14) | collective-permute-done | bytes 737312 | tf_op jit(solution)/shard_map/ppermute | solution.py:914
  83.3 35.1 %ffn_both.1 = (bf16[512,768]{1,0:T(8,128)(2,1)}, bf16[256,768]{1,0:T(8,128)(2,1)}, bf16[4,4,240,384]{3,2,1,0:T(8,128)(2,1)}, bf16[4,4,240,384]{3,2,1,0:T(8,128)(...) custom-call(s32[2]{0:T(128)} %pad_add_fusion.place, s32[1]{0:T(128)S(6)} %copy.34.llen, ...), custom_call_target="tpu_custom_call" | custom-call | flops 60000002048 | bytes 1048576 | tf_op jit(solution)/shard_map/ffn_both/pallas_call | solution.py:833
  118.6 5.5 %collective-permute-done.20 = bf16[4,4,240,384]{3,2,1,0:T(8,128)(2,1)S(1)} collective-permute-done((bf16[4,4,240,384]{3,2,1,0:T(8,128)(2,1)}, bf16[4,4,240,384]{3,2,1,0:T(8,128)(2,1)S(1)}, u32[]{:S(2)}, u32[]{:S(2)}) %collective-permute-start.20) | collective-permute-done | bytes 2949152 | tf_op jit(solution)/shard_map/ppermute | solution.py:914
  124.0 3.7 %fusion.7 = (bf16[4,240,384]{2,1,0:T(8,128)(2,1)}, bf16[4,240,384]{2,1,0:T(8,128)(2,1)}, bf16[4,240,384]{2,1,0:T(8,128)(2,1)}, bf16[4,240,384]{2,1,0:T(8,128)(2,1)S(1)}) fusion(bf16[4,4,240,384]{3,2,1,0:T(8,128)(2,1)S(1)} %collective-permute-done.20, bf16[4,4,240,384]{3,2,1,0:T(8,128)(2,1)} %get-tuple-element.119), kind=kLoop, calls=%fused_computation.15 | loop fusion | flops 5898240 | bytes 8847360 | tf_op jit(solution)/shard_map/convert_element_type | solution.py:933
  131.2 28.9 %mixer_backward.1 = (bf16[4,4,192,256]{3,2,1,0:T(8,128)(2,1)}, bf16[4,192,256]{2,1,0:T(8,128)(2,1)}, bf16[4,192,256]{2,1,0:T(8,128)(2,1)}, bf16[4,192,256]{2,1,0...) custom-call(s32[2]{0:T(128)} %pad_add_fusion.place, ...), custom_call_target="tpu_custom_call" | custom-call | flops 40000000000 | bytes 1048576 | tf_op jit(solution)/shard_map/mixer_backward/pallas_call | solution.py:833
  162.7 2.0 fusion.2
  171.5 3.3 %collective-permute-start.28 = (bf16[240,384]{1,0:T(8,128)(2,1)}, bf16[240,384]{1,0:T(8,128)(2,1)S(1)}, u32[]{:S(2)}, u32[]{:S(2)}) collective-permute-start(bf16[240,384]{1,0:T(8,128)(2,1)} %get-tuple-element.189), channel_id=1, source_target_pairs={{0,3},{1,2},{2,1},{3,0},{4,7},{5,6},{6,5},{7,4},{8,11},{9,10},{10,... | collective-permute-start | bytes 552968 | tf_op jit(solution)/shard_map/ppermute | solution.py:910
  174.8 10.0 %input_gradient.1 = (bf16[512,768]{1,0:T(8,128)(2,1)}, bf16[256,768]{1,0:T(8,128)(2,1)}) custom-call(s32[2]{0:T(128)} %pad_add_fusion.place, s32[1]{0:T(128)S(6)} %copy.34.llen, s32[2]{0:T(128)} %slen.5, f32[24,768]{1,0:T(8,128)} %get-tuple-element.107.vec, bf16[768,1536]{1,0:T(8,128)(2,1)} %get-tuple-element.150.grads_any, ...), custom_call_target="tpu_custom_call" | custom-call | flops 5000000000 | bytes 1048576 | tf_op jit(solution)/shard_map/input_gradient/pallas_call | solution.py:833
  188.8 3.5 %collective-permute-start.33 = (bf16[192,256]{1,0:T(8,128)(2,1)S(1)}, bf16[192,256]{1,0:T(8,128)(2,1)S(1)}, u32[]{:S(2)}, u32[]{:S(2)}) collective-permute-start(bf16[192,256]{1,0:T(8,128)(2,1)S(1)} %get-tuple-element.190), channel_id=1, source_target_pairs={{0,1},{1,0},{2,3},{3,2},{4,5},{5,4},{6,7},{7,6},{8,9},{9,8},{10,11... | collective-permute-start | bytes 294920 | tf_op jit(solution)/shard_map/ppermute | solution.py:910
  197.4 5.0 %collective-permute-done.35 = bf16[192,256]{1,0:T(8,128)(2,1)S(1)} collective-permute-done((bf16[192,256]{1,0:T(8,128)(2,1)S(1)}, bf16[192,256]{1,0:T(8,128)(2,1)S(1)}, u32[]{:S(2)}, u32[]{:S(2)}) %collective-permute-start.35) | collective-permute-done | bytes 98336 | tf_op jit(solution)/shard_map/ppermute | solution.py:910
  203.5 2.1 collective-permute-done.34
  210.2 2.3 %unpack_ffn.1 = (f32[2,96,1536]{2,1,0:T(8,128)}, f32[2,384,384]{2,1,0:T(8,128)}, f32[192,768]{1,0:T(8,128)}) custom-call(s32[2]{0:T(128)S(1)} %copy-done, bf16[240,384]{1,0:T(8,128)(2,1)S(1)} %add_convert_fusion.4.p0, bf16[240,384]{1,0:T(8,128)(2,1)S(1)} %collective-permute-done.40.p1, bf16[240,384]{1,0:T(8,128)(2,1)S(1)} %collective-permute-done.41.p2, ...), custom_call_target="tpu_custom_call" | custom-call | flops 1000000000 | bytes 1048576 | tf_op jit(solution)/shard_map/unpack_ffn/pallas_call | solution.py:833
  215.7 1.8 unpack_mixer.1
  (133 shorter events, 47.6 us)
Async XLA Ops:
  3.6 9.0 %collective-permute-start.2 = (bf16[192,256]{1,0:T(8,128)(2,1)}, bf16[192,256]{1,0:T(8,128)(2,1)S(1)}, u32[]{:S(2)}, u32[]{:S(2)}) collective-permute-start(bf16[192,256]{1,0:T(8,128)(2,1)} %get-tuple-element.99), channel_id=1, source_target_pairs={{0,3},{1,2},{2,1},{3,0},{4,7},{5,6},{6,5},{7,4},{8,11},{9,10},{10,... | collective-permute-start | bytes 294920 | tf_op jit(solution)/shard_map/ppermute | solution.py:910
  8.7 8.5 %collective-permute-start.1 = (bf16[192,256]{1,0:T(8,128)(2,1)}, bf16[192,256]{1,0:T(8,128)(2,1)S(1)}, u32[]{:S(2)}, u32[]{:S(2)}) collective-permute-start(bf16[192,256]{1,0:T(8,128)(2,1)} %get-tuple-element.99), channel_id=1, source_target_pairs={{0,2},{1,3},{2,0},{3,1},{4,6},{5,7},{6,4},{7,5},{8,10},{9,11},{10,... | collective-permute-start | bytes 294920 | tf_op jit(solution)/shard_map/ppermute | solution.py:910
  8.7 8.5 %collective-permute-start = (bf16[192,256]{1,0:T(8,128)(2,1)}, bf16[192,256]{1,0:T(8,128)(2,1)S(1)}, u32[]{:S(2)}, u32[]{:S(2)}) collective-permute-start(bf16[192,256]{1,0:T(8,128)(2,1)} %get-tuple-element.99), channel_id=1, source_target_pairs={{0,1},{1,0},{2,3},{3,2},{4,5},{5,4},{6,7},{7,6},{8,9},{9,8},{10,11... | collective-permute-start | bytes 294920 | tf_op jit(solution)/shard_map/ppermute | solution.py:910
  18.1 9.2 %collective-permute-start.8 = (bf16[240,384]{1,0:T(8,128)(2,1)}, bf16[240,384]{1,0:T(8,128)(2,1)S(1)}, u32[]{:S(2)}, u32[]{:S(2)}) collective-permute-start(bf16[240,384]{1,0:T(8,128)(2,1)} %get-tuple-element.102), channel_id=1, source_target_pairs={{0,3},{1,2},{2,1},{3,0},{4,7},{5,6},{6,5},{7,4},{8,11},{9,10},{10,... | collective-permute-start | bytes 552968 | tf_op jit(solution)/shard_map/ppermute | solution.py:910
  20.7 18.3 %collective-permute-start.5 = (bf16[4,192,256]{2,1,0:T(8,128)(2,1)S(1)}, bf16[4,192,256]{2,1,0:T(8,128)(2,1)S(1)}, u32[]{:S(2)}, u32[]{:S(2)}) collective-permute-start(bf16[4,192,256]{2,1,0:T(8,128)(2,1)S(1)} %pad_maximum_fusion.1.p0), channel_id=1, source_target_pairs={{0,24},{4,28},{8,16},{12,20},{16,8},{20,12},{24,0},{28,4},{1,25},{... | collective-permute-start | bytes 1179656 | tf_op jit(solution)/shard_map/ppermute | solution.py:914
  23.3 16.6 %collective-permute-start.4 = (bf16[4,192,256]{2,1,0:T(8,128)(2,1)S(1)}, bf16[4,192,256]{2,1,0:T(8,128)(2,1)S(1)}, u32[]{:S(2)}, u32[]{:S(2)}) collective-permute-start(bf16[4,192,256]{2,1,0:T(8,128)(2,1)S(1)} %pad_maximum_fusion.1.p0), channel_id=1, source_target_pairs={{0,16},{4,20},{8,24},{12,28},{16,0},{20,4},{24,8},{28,12},{1,17},{... | collective-permute-start | bytes 1179656 | tf_op jit(solution)/shard_map/ppermute | solution.py:914
  23.7 16.3 %collective-permute-start.3 = (bf16[4,192,256]{2,1,0:T(8,128)(2,1)S(1)}, bf16[4,192,256]{2,1,0:T(8,128)(2,1)S(1)}, u32[]{:S(2)}, u32[]{:S(2)}) collective-permute-start(bf16[4,192,256]{2,1,0:T(8,128)(2,1)S(1)} %pad_maximum_fusion.1.p0), channel_id=1, source_target_pairs={{0,8},{4,12},{8,0},{12,4},{16,24},{20,28},{24,16},{28,20},{1,9},{5... | collective-permute-start | bytes 1179656 | tf_op jit(solution)/shard_map/ppermute | solution.py:914
  24.2 11.6 %collective-permute-start.7 = (bf16[240,384]{1,0:T(8,128)(2,1)}, bf16[240,384]{1,0:T(8,128)(2,1)S(1)}, u32[]{:S(2)}, u32[]{:S(2)}) collective-permute-start(bf16[240,384]{1,0:T(8,128)(2,1)} %get-tuple-element.102), channel_id=1, source_target_pairs={{0,2},{1,3},{2,0},{3,1},{4,6},{5,7},{6,4},{7,5},{8,10},{9,11},{10,... | collective-permute-start | bytes 552968 | tf_op jit(solution)/shard_map/ppermute | solution.py:910
  27.3 10.6 %collective-permute-start.6 = (bf16[240,384]{1,0:T(8,128)(2,1)}, bf16[240,384]{1,0:T(8,128)(2,1)S(1)}, u32[]{:S(2)}, u32[]{:S(2)}) collective-permute-start(bf16[240,384]{1,0:T(8,128)(2,1)} %get-tuple-element.102), channel_id=1, source_target_pairs={{0,1},{1,0},{2,3},{3,2},{4,5},{5,4},{6,7},{7,6},{8,9},{9,8},{10,11... | collective-permute-start | bytes 552968 | tf_op jit(solution)/shard_map/ppermute | solution.py:910
  41.7 30.3 %collective-permute-start.15 = (bf16[4,240,384]{2,1,0:T(8,128)(2,1)S(1)}, bf16[4,240,384]{2,1,0:T(8,128)(2,1)S(1)}, u32[]{:S(2)}, u32[]{:S(2)}) collective-permute-start(bf16[4,240,384]{2,1,0:T(8,128)(2,1)S(1)} %pad_maximum_fusion.p0), channel_id=1, source_target_pairs={{0,24},{4,28},{8,16},{12,20},{16,8},{20,12},{24,0},{28,4},{1,25},{... | collective-permute-start | bytes 2211848 | tf_op jit(solution)/shard_map/ppermute | solution.py:914
  43.7 33.2 %collective-permute-start.14 = (bf16[4,240,384]{2,1,0:T(8,128)(2,1)S(1)}, bf16[4,240,384]{2,1,0:T(8,128)(2,1)S(1)}, u32[]{:S(2)}, u32[]{:S(2)}) collective-permute-start(bf16[4,240,384]{2,1,0:T(8,128)(2,1)S(1)} %pad_maximum_fusion.p0), channel_id=1, source_target_pairs={{0,16},{4,20},{8,24},{12,28},{16,0},{20,4},{24,8},{28,12},{1,17},{... | collective-permute-start | bytes 2211848 | tf_op jit(solution)/shard_map/ppermute | solution.py:914
  44.9 32.0 %collective-permute-start.13 = (bf16[4,240,384]{2,1,0:T(8,128)(2,1)S(1)}, bf16[4,240,384]{2,1,0:T(8,128)(2,1)S(1)}, u32[]{:S(2)}, u32[]{:S(2)}) collective-permute-start(bf16[4,240,384]{2,1,0:T(8,128)(2,1)S(1)} %pad_maximum_fusion.p0), channel_id=1, source_target_pairs={{0,8},{4,12},{8,0},{12,4},{16,24},{20,28},{24,16},{28,20},{1,9},{5... | collective-permute-start | bytes 2211848 | tf_op jit(solution)/shard_map/ppermute | solution.py:914
  127.7 37.0 %collective-permute-start.25 = (bf16[4,240,384]{2,1,0:T(8,128)(2,1)}, bf16[4,240,384]{2,1,0:T(8,128)(2,1)S(1)}, u32[]{:S(2)}, u32[]{:S(2)}) collective-permute-start(bf16[4,240,384]{2,1,0:T(8,128)(2,1)} %get-tuple-element.182), channel_id=1, source_target_pairs={{0,24},{4,28},{8,16},{12,20},{16,8},{20,12},{24,0},{28,4},{1,25},{... | collective-permute-start | bytes 2211848 | tf_op jit(solution)/shard_map/ppermute | solution.py:914
  129.4 35.3 %collective-permute-start.24 = (bf16[4,240,384]{2,1,0:T(8,128)(2,1)}, bf16[4,240,384]{2,1,0:T(8,128)(2,1)S(1)}, u32[]{:S(2)}, u32[]{:S(2)}) collective-permute-start(bf16[4,240,384]{2,1,0:T(8,128)(2,1)} %get-tuple-element.183), channel_id=1, source_target_pairs={{0,16},{4,20},{8,24},{12,28},{16,0},{20,4},{24,8},{28,12},{1,17},{... | collective-permute-start | bytes 2211848 | tf_op jit(solution)/shard_map/ppermute | solution.py:914
  130.7 34.1 %collective-permute-start.23 = (bf16[4,240,384]{2,1,0:T(8,128)(2,1)}, bf16[4,240,384]{2,1,0:T(8,128)(2,1)S(1)}, u32[]{:S(2)}, u32[]{:S(2)}) collective-permute-start(bf16[4,240,384]{2,1,0:T(8,128)(2,1)} %get-tuple-element.184), channel_id=1, source_target_pairs={{0,8},{4,12},{8,0},{12,4},{16,24},{20,28},{24,16},{28,20},{1,9},{5... | collective-permute-start | bytes 2211848 | tf_op jit(solution)/shard_map/ppermute | solution.py:914
  165.3 19.4 %collective-permute-start.30 = (bf16[4,192,256]{2,1,0:T(8,128)(2,1)}, bf16[4,192,256]{2,1,0:T(8,128)(2,1)}, u32[]{:S(2)}, u32[]{:S(2)}) collective-permute-start(bf16[4,192,256]{2,1,0:T(8,128)(2,1)} %get-tuple-element.142), channel_id=1, source_target_pairs={{0,8},{4,12},{8,0},{12,4},{16,24},{20,28},{24,16},{28,20},{1,9},{5... | collective-permute-start | bytes 1179656 | tf_op jit(solution)/shard_map/ppermute | solution.py:914
  166.8 19.4 %collective-permute-start.31 = (bf16[4,192,256]{2,1,0:T(8,128)(2,1)S(1)}, bf16[4,192,256]{2,1,0:T(8,128)(2,1)}, u32[]{:S(2)}, u32[]{:S(2)}) collective-permute-start(bf16[4,192,256]{2,1,0:T(8,128)(2,1)S(1)} %get-tuple-element.143), channel_id=1, source_target_pairs={{0,16},{4,20},{8,24},{12,28},{16,0},{20,4},{24,8},{28,12},{1,17},{... | collective-permute-start | bytes 1179656 | tf_op jit(solution)/shard_map/ppermute | solution.py:914
  168.5 18.8 %collective-permute-start.32 = (bf16[4,192,256]{2,1,0:T(8,128)(2,1)}, bf16[4,192,256]{2,1,0:T(8,128)(2,1)}, u32[]{:S(2)}, u32[]{:S(2)}) collective-permute-start(bf16[4,192,256]{2,1,0:T(8,128)(2,1)} %get-tuple-element.193), channel_id=1, source_target_pairs={{0,24},{4,28},{8,16},{12,20},{16,8},{20,12},{24,0},{28,4},{1,25},{... | collective-permute-start | bytes 1179656 | tf_op jit(solution)/shard_map/ppermute | solution.py:914
  170.9 16.5 %collective-permute-start.29 = (bf16[240,384]{1,0:T(8,128)(2,1)}, bf16[240,384]{1,0:T(8,128)(2,1)S(1)}, u32[]{:S(2)}, u32[]{:S(2)}) collective-permute-start(bf16[240,384]{1,0:T(8,128)(2,1)} %get-tuple-element.188), channel_id=1, source_target_pairs={{0,2},{1,3},{2,0},{3,1},{4,6},{5,7},{6,4},{7,5},{8,10},{9,11},{10,... | collective-permute-start | bytes 552968 | tf_op jit(solution)/shard_map/ppermute | solution.py:910
  171.5 15.9 %collective-permute-start.28 = (bf16[240,384]{1,0:T(8,128)(2,1)}, bf16[240,384]{1,0:T(8,128)(2,1)S(1)}, u32[]{:S(2)}, u32[]{:S(2)}) collective-permute-start(bf16[240,384]{1,0:T(8,128)(2,1)} %get-tuple-element.189), channel_id=1, source_target_pairs={{0,3},{1,2},{2,1},{3,0},{4,7},{5,6},{6,5},{7,4},{8,11},{9,10},{10,... | collective-permute-start | bytes 552968 | tf_op jit(solution)/shard_map/ppermute | solution.py:910
  188.8 8.5 %collective-permute-start.33 = (bf16[192,256]{1,0:T(8,128)(2,1)S(1)}, bf16[192,256]{1,0:T(8,128)(2,1)S(1)}, u32[]{:S(2)}, u32[]{:S(2)}) collective-permute-start(bf16[192,256]{1,0:T(8,128)(2,1)S(1)} %get-tuple-element.190), channel_id=1, source_target_pairs={{0,1},{1,0},{2,3},{3,2},{4,5},{5,4},{6,7},{7,6},{8,9},{9,8},{10,11... | collective-permute-start | bytes 294920 | tf_op jit(solution)/shard_map/ppermute | solution.py:910
  192.3 10.1 %collective-permute-start.42 = (bf16[240,384]{1,0:T(8,128)(2,1)S(1)}, bf16[240,384]{1,0:T(8,128)(2,1)S(1)}, u32[]{:S(2)}, u32[]{:S(2)}) collective-permute-start(bf16[240,384]{1,0:T(8,128)(2,1)S(1)} %add_convert_fusion.4.p0), channel_id=1, source_target_pairs={{0,24},{4,28},{8,16},{12,20},{16,8},{20,12},{24,0},{28,4},{1,25},{... | collective-permute-start | bytes 552968 | tf_op jit(solution)/shard_map/ppermute | solution.py:914
  193.6 9.3 %collective-permute-start.41 = (bf16[240,384]{1,0:T(8,128)(2,1)S(1)}, bf16[240,384]{1,0:T(8,128)(2,1)S(1)}, u32[]{:S(2)}, u32[]{:S(2)}) collective-permute-start(bf16[240,384]{1,0:T(8,128)(2,1)S(1)} %add_convert_fusion.4.p0), channel_id=1, source_target_pairs={{0,16},{4,20},{8,24},{12,28},{16,0},{20,4},{24,8},{28,12},{1,17},{... | collective-permute-start | bytes 552968 | tf_op jit(solution)/shard_map/ppermute | solution.py:914
  197.3 8.3 %collective-permute-start.34 = (bf16[192,256]{1,0:T(8,128)(2,1)S(1)}, bf16[192,256]{1,0:T(8,128)(2,1)S(1)}, u32[]{:S(2)}, u32[]{:S(2)}) collective-permute-start(bf16[192,256]{1,0:T(8,128)(2,1)S(1)} %get-tuple-element.192), channel_id=1, source_target_pairs={{0,2},{1,3},{2,0},{3,1},{4,6},{5,7},{6,4},{7,5},{8,10},{9,11},{10,... | collective-permute-start | bytes 294920 | tf_op jit(solution)/shard_map/ppermute | solution.py:910
  (46 other events, 280.7 us)

commit v9 on v7

--- a/solution.py
+++ b/solution.py
@@ -267,7 +267,7 @@
     return copy
 
 
-def ship(keep, send, place, slot, shard, rows, source, sem):
+def ship(keep, sends, place, slot, shard, rows, source, sem):
     where = slot ^ place[0]
     chip, far_off = where >> 1, shard ^ place[1]
 
@@ -275,17 +275,20 @@
     def _():
         pltpu.make_async_copy(source, keep.at[chip, far_off, rows, :], sem).start()
 
-    @pl.when((where & 1) == 1)
-    def _():
-        pltpu.make_async_copy(source, send.at[chip, far_off, rows, :], sem).start()
+    for k, send in enumerate(sends):
+
+        @pl.when(where == 2 * k + 1)
+        def _():
+            pltpu.make_async_copy(source, send.at[far_off, rows, :], sem).start()
 
 
 def ffn_both(
     place, llen, slen, vec, xm_any, ctx_any, cl, cs, p0, p1, p2, p3, p4, p5, p6, p7,
-    ol, os, keep, send, gone_any, gctx_any, gvec,
+    ol, os, keep, send0, send1, send2, send3, gone_any, gctx_any, gvec,
     wo, wi, wu, xm, ctx, cot, out, res, xhat, grouped, gffn, active, slope, ffn, rstd,
     hid_a, hid_b, ghid_a, ghid_b, gproj, gout, ginner, gouter, gone, gctx, sums, sems,
 ):
+    sends = (send0, send1, send2, send3)
     loads = [start_copy(ctx_any, ctx, sems.at[3]), start_copy(xm_any, xm, sems.at[4])]
 
     def fetch(part):
@@ -347,12 +350,8 @@
             grouped[0, rows, :] = short[:, 0:AH]
             grouped[1, rows, :] = short[:, AH:D]
 
-    mix(0)
-    for tile in range(3):
-        if tile < 2:
-            mix(tile + 1)
-        norm_one(2 * tile)
-        norm_one(2 * tile + 1)
+    loop(3, mix)
+    loop(6, norm_one)
     pltpu.make_async_copy(wi, wi, sems.at[1]).wait()
     pltpu.make_async_copy(wu, wu, sems.at[2]).wait()
 
@@ -449,9 +448,9 @@
             n = 2 * (b & 1) + half
             for w in range(4):
                 outer = gouter.at[b, pl.ds(AH * half + 96 * w, 96), :]
-                ship(keep, send, place, 4 * g + w, n, pl.ds(96, 96), outer, sems.at[0])
+                ship(keep, sends, place, 4 * g + w, n, pl.ds(96, 96), outer, sems.at[0])
                 inner = ginner.at[b, pl.ds(96 * w, 96), pl.ds(AH * half, AH)]
-                ship(keep, send, place, 2 * b + half, w, pl.ds(0, 96), inner, sems.at[1])
+                ship(keep, sends, place, 2 * b + half, w, pl.ds(0, 96), inner, sems.at[1])
 
     slopes(jnp.int32(0), ghid_a)
 
@@ -502,7 +501,7 @@
         for n in range(4):
             for r in range(4):
                 source = gout.at[c, pl.ds(192 * n + 48 * r, 48), :]
-                ship(keep, send, place, 4 * c + r, n, pl.ds(192, 48), source, sems.at[2])
+                ship(keep, sends, place, 4 * c + r, n, pl.ds(192, 48), source, sems.at[2])
     unmix(2)
     for k in range(4):
         gvec[k : k + 1, :] = jnp.sum(sums[8 * k : 8 * k + 8, :], axis=0, keepdims=True)
@@ -754,27 +753,33 @@
 
 
 def pack(
-    place, qkv, depth, point, kernel, convout, g1, b1, inner, outer, out, g2, b2, mixer, ffn
+    place, qkv, point, convout, inner, outer, out, depth, kernel, g1, b1, g2, b2, mixer, ffn, sems
 ):
     for w in range(SLOTS):
 
         @pl.when(place[0] == w)
         def _():
             g, r = w // 4, w % 4
-            ffn[0:96, :] = inner[g, :, AH * r : AH * r + AH]
-            ffn[96:192, :] = outer[g, 96 * r : 96 * r + 96, :]
-            ffn[192:240, :] = out[48 * r : 48 * r + 48, AH * g : AH * g + AH]
             if w < 4:
-                mixer[...] = qkv[:, 256 * w : 256 * w + 256]
+                parts = [(qkv.at[:, 256 * w : 256 * w + 256], mixer)]
             elif w == 4:
-                mixer[:, 0:128] = qkv[:, 1024:1152]
-                mixer[:, 128:256] = convout[:, 0:128]
+                parts = [
+                    (qkv.at[:, 1024:1152], mixer.at[:, 0:128]),
+                    (convout.at[:, 0:128], mixer.at[:, 128:256]),
+                ]
             elif w == 5:
-                mixer[...] = convout[:, 128:384]
+                parts = [(convout.at[:, 128:384], mixer)]
             elif w == 6:
-                mixer[...] = point[:, 0:256]
+                parts = [(point.at[:, 0:256], mixer)]
             else:
-                mixer[:, 0:128] = point[:, 256:384]
+                parts = [(point.at[:, 256:384], mixer.at[:, 0:128])]
+            parts += [
+                (inner.at[g, :, AH * r : AH * r + AH], ffn.at[0:96]),
+                (outer.at[g, 96 * r : 96 * r + 96, :], ffn.at[96:192]),
+                (out.at[48 * r : 48 * r + 48, AH * g : AH * g + AH], ffn.at[192:240]),
+            ]
+            copies = [start_copy(a, b, sems.at[k]) for k, (a, b) in enumerate(parts)]
+            if w == 7:
                 rows = [v[...].astype(F32).reshape(1, 192) for v in (g1, b1, g2, b2)]
                 table = jnp.concatenate(
                     [depth[...].astype(F32), jnp.zeros((7, 192), F32)]
@@ -787,6 +792,8 @@
                 right = tn(kernel[...], jnp.where(col == row + 64, 1.0, 0.0).astype(BF))
                 mixer[0:96, 128:256] = (left[0:96, :] + right).astype(BF)
                 mixer[96:192, 128:256] = left[96:192, :].astype(BF)
+            for copy in copies:
+                copy.wait()
 
 
 def unpack_ffn(place, p0, p1, p2, p3, p4, p5, p6, p7, inner, outer, out):
@@ -859,7 +866,8 @@
 
 def feed_forward(scalars, xm, ctx, vec, cl, cs, pieces):
     outs = [
-        ((LONG, D), BF), ((2 * SHORT, D), BF), ((4, 4, 240, AH), BF), ((4, 4, 240, AH), BF),
+        ((LONG, D), BF), ((2 * SHORT, D), BF), ((4, 4, 240, AH), BF), ((4, 240, AH), BF),
+        ((4, 240, AH), BF), ((4, 240, AH), BF), ((4, 240, AH), BF),
         ((ROWS, D), F32), ((ROWS, D), BF), ((8, D), F32),
     ]
     scratch = [
@@ -873,7 +881,7 @@
     return call(
         ffn_both, [SMEM] * 3 + [VMEM] + [ANY] * 12, outs,
         (scratch, pltpu.SemaphoreType.DMA((7,))), 60 * 10**9,
-        *scalars, vec, xm, ctx, cl, cs, *pieces, out_specs=[ANY] * 6 + [VMEM],
+        *scalars, vec, xm, ctx, cl, cs, *pieces, out_specs=[ANY] * 9 + [VMEM],
     )
 
 
@@ -959,9 +967,10 @@
     xl, xs = long_tokens.reshape(LONG, D), short_tokens.reshape(2 * SHORT, D)
     cl, cs = long_cotangent.reshape(LONG, D), short_cotangent.reshape(2 * SHORT, D)
     mixer, ffn = call(
-        pack, [SMEM] + [VMEM] * 12, [((192, 256), BF), ((240, AH), BF)], ([],), 10**9,
-        place, w_qkv, w_depth, w_point, w_kernel.T, w_convout, norm1_gain, norm1_bias,
-        w_inner, w_outer, w_out, norm2_gain, norm2_bias,
+        pack, [SMEM] + [ANY] * 6 + [VMEM] * 6, [((192, 256), BF), ((240, AH), BF)],
+        ([], pltpu.SemaphoreType.DMA((5,))), 10**9,
+        place, w_qkv, w_point, w_convout, w_inner, w_outer, w_out,
+        w_depth, w_kernel.T, norm1_gain, norm1_bias, norm2_gain, norm2_bias,
     )
     mixer = gather_narrow(mixer)
     mixer, ffn = lax.optimization_barrier((mixer, ffn))
@@ -973,8 +982,13 @@
     xm, packed, plong, pshort, dw, kc, cq, kp, cv, ctx, vec = forward_mixer(scalars, xl, xs, mixer)
     ctx, ffn = lax.optimization_barrier((ctx, ffn))
     ffn = gather_cores(ffn)
-    ol, os, keep, send, gone, gctx, gvec = feed_forward(scalars, xm, ctx, vec, cl, cs, ffn)
-    ga = reduce_cores(keep, near(send, 1))
+    ol, os, keep, s0, s1, s2, s3, gone, gctx, gvec = feed_forward(
+        scalars, xm, ctx, vec, cl, cs, ffn
+    )
+    swapped = [near(s3, 1), near(s1, 1), near(s2, 1), near(s0, 1)]
+    ga = [total(keep[3], swapped[0:1]), total(keep[1], swapped[1:2])]
+    rest, _ = lax.optimization_barrier((swapped[2:4], ga))
+    ga = [total(keep[0], rest[1:2]), ga[1], total(keep[2], rest[0:1]), ga[0]]
     ga_sent = send_chips(ga)
     gctx, ga = lax.optimization_barrier((gctx, ga))
     keep, s0, s1, s2, s3, grads, gdp = backward_mixer(

time: 218 us -> 218 us (level)
  waiting for transfers between devices: 43.2 us -> 40.8 us
    ppermute x39 -> x42, waiting for transfers between devices: 20.7 us -> 17.9 us  [near(): return lax.ppermute(values, 'wide', [(i, i ^ bit) for i in range(SLOTS)])]
    ppermute x39 -> x42, starting transfers between devices: 26.7 us -> 27.5 us  [near(): return lax.ppermute(values, 'wide', [(i, i ^ bit) for i in range(SLOTS)])]
    convert_element_type x5 -> x6, other arithmetic: 7.83 us -> 8.46 us  [total(): return result.astype(BF)]
  transfers between devices with their start and end apart: 51 -> 54, of which waited for: 24 -> 27; matrix products, arithmetic and copies ran while one was open for 4% -> 6% of each run, Pallas kernels for 31% -> 31%
where the time goes in v9:
time: 218 us; the launch traced here: 217 us
  Pallas kernels  107 us (49%)
  starting transfers between devices  52.5 us (24%)
  waiting for transfers between devices  40.8 us (19%)
  other arithmetic  13.5 us (6%)
    pallas_call x7, Pallas kernels, call(): pl.pallas_call(kernel, out_shape=[jax.ShapeDtypeStruct(s, d) for s, d in...  107 us
    ppermute x42, starting transfers between devices, near(): return lax.ppermute(values, 'wide', [(i, i ^ bit) for i in range(SLOTS)])  27.5 us
    ppermute x12, starting transfers between devices, far(): return lax.ppermute(values, 'narrow', [(i, i ^ bit) for i in range(4)])  25 us
    ppermute x12, waiting for transfers between devices, far(): return lax.ppermute(values, 'narrow', [(i, i ^ bit) for i in range(4)])  22.9 us
    ppermute x42, waiting for transfers between devices, near(): return lax.ppermute(values, 'wide', [(i, i ^ bit) for i in range(SLOTS)])  17.9 us
    convert_element_type x6, other arithmetic, total(): return result.astype(BF)  8.46 us
  transfers between devices with their start and end apart: 54, of which 27 were waited for; matrix products, arithmetic and copies ran while one was open for 6% of the time, Pallas kernels for 31%

profile of v9, /device:TPU:0, one launch (start us, length us, event | category | flops | bytes accessed | tf_op | source)
XLA Modules:
  0.0 217.4 jit_solution(14494495269925450056)
XLA Ops:
  1.2 2.5 %pack.1 = (bf16[192,256]{1,0:T(8,128)(2,1)}, bf16[240,384]{1,0:T(8,128)(2,1)}) custom-call(s32[2]{0:T(128)} %pad_add_fusion.place, bf16[192,1152]{1,0:T(8,128)(2,1)} %qkv.1, bf16[192,384]{1,0:T(8,128)(2,1)} %point.1, bf16[192,384]{1,0:T(8,128)(2,1)} %convout.1, bf16[2,96,1536]{2,1,0:T(8,128)(2,1)} %inner.1, bf16[2,384,384]{2,1,0:T(8,128)(2,1)} %outer.1, ...), custom_call_target="tpu_custom_call" | custom-call | flops 1000000000 | bytes 1048576 | tf_op jit(solution)/shard_map/pack/pallas_call | solution.py:840
  3.8 5.1 %collective-permute-start.2 = (bf16[192,256]{1,0:T(8,128)(2,1)}, bf16[192,256]{1,0:T(8,128)(2,1)S(1)}, u32[]{:S(2)}, u32[]{:S(2)}) collective-permute-start(bf16[192,256]{1,0:T(8,128)(2,1)} %get-tuple-element.104), channel_id=1, source_target_pairs={{0,3},{1,2},{2,1},{3,0},{4,7},{5,6},{6,5},{7,4},{8,11},{9,10},{10,... | collective-permute-start | bytes 294920 | tf_op jit(solution)/shard_map/ppermute | solution.py:918
  9.5 3.3 %collective-permute-done.2 = bf16[192,256]{1,0:T(8,128)(2,1)S(1)} collective-permute-done((bf16[192,256]{1,0:T(8,128)(2,1)}, bf16[192,256]{1,0:T(8,128)(2,1)S(1)}, u32[]{:S(2)}, u32[]{:S(2)}) %collective-permute-start.2) | collective-permute-done | bytes 98336 | tf_op jit(solution)/shard_map/ppermute | solution.py:918
  12.8 4.6 %collective-permute-done.1 = bf16[192,256]{1,0:T(8,128)(2,1)S(1)} collective-permute-done((bf16[192,256]{1,0:T(8,128)(2,1)}, bf16[192,256]{1,0:T(8,128)(2,1)S(1)}, u32[]{:S(2)}, u32[]{:S(2)}) %collective-permute-start.1) | collective-permute-done | bytes 98336 | tf_op jit(solution)/shard_map/ppermute | solution.py:918
  18.3 2.6 %collective-permute-start.8 = (bf16[240,384]{1,0:T(8,128)(2,1)}, bf16[240,384]{1,0:T(8,128)(2,1)S(1)}, u32[]{:S(2)}, u32[]{:S(2)}) collective-permute-start(bf16[240,384]{1,0:T(8,128)(2,1)} %get-tuple-element.107), channel_id=1, source_target_pairs={{0,3},{1,2},{2,1},{3,0},{4,7},{5,6},{6,5},{7,4},{8,11},{9,10},{10,... | collective-permute-start | bytes 552968 | tf_op jit(solution)/shard_map/ppermute | solution.py:918
  20.9 2.5 %collective-permute-start.5 = (bf16[4,192,256]{2,1,0:T(8,128)(2,1)S(1)}, bf16[4,192,256]{2,1,0:T(8,128)(2,1)S(1)}, u32[]{:S(2)}, u32[]{:S(2)}) collective-permute-start(bf16[4,192,256]{2,1,0:T(8,128)(2,1)S(1)} %pad_maximum_fusion.1.p0), channel_id=1, source_target_pairs={{0,24},{4,28},{8,16},{12,20},{16,8},{20,12},{24,0},{28,4},{1,25},{... | collective-permute-start | bytes 1179656 | tf_op jit(solution)/shard_map/ppermute | solution.py:922
  24.4 3.2 %collective-permute-done.8 = bf16[240,384]{1,0:T(8,128)(2,1)S(1)} collective-permute-done((bf16[240,384]{1,0:T(8,128)(2,1)}, bf16[240,384]{1,0:T(8,128)(2,1)S(1)}, u32[]{:S(2)}, u32[]{:S(2)}) %collective-permute-start.8) | collective-permute-done | bytes 184352 | tf_op jit(solution)/shard_map/ppermute | solution.py:918
  27.6 6.9 %collective-permute-start.6 = (bf16[240,384]{1,0:T(8,128)(2,1)}, bf16[240,384]{1,0:T(8,128)(2,1)S(1)}, u32[]{:S(2)}, u32[]{:S(2)}) collective-permute-start(bf16[240,384]{1,0:T(8,128)(2,1)} %get-tuple-element.107), channel_id=1, source_target_pairs={{0,1},{1,0},{2,3},{3,2},{4,5},{5,4},{6,7},{7,6},{8,9},{9,8},{10,11... | collective-permute-start | bytes 552968 | tf_op jit(solution)/shard_map/ppermute | solution.py:918
  36.0 2.2 %collective-permute-done.6 = bf16[240,384]{1,0:T(8,128)(2,1)S(1)} collective-permute-done((bf16[240,384]{1,0:T(8,128)(2,1)}, bf16[240,384]{1,0:T(8,128)(2,1)S(1)}, u32[]{:S(2)}, u32[]{:S(2)}) %collective-permute-start.6) | collective-permute-done | bytes 184352 | tf_op jit(solution)/shard_map/ppermute | solution.py:918
  41.5 2.1 collective-permute-start.15
  46.1 25.6 %mixer_forward.1 = (bf16[768,768]{1,0:T(8,128)(2,1)}, bf16[768,1152]{1,0:T(8,128)(2,1)}, bf16[6,512,512]{2,1,0:T(8,128)(2,1)}, bf16[2,6,128,128]{3,2,1,0:T(8,128...) custom-call(s32[2]{0:T(128)} %pad_add_fusion.place, ...), custom_call_target="tpu_custom_call" | custom-call | flops 30000001024 | bytes 1048576 | tf_op jit(solution)/shard_map/mixer_forward/pallas_call | solution.py:840
  71.7 5.0 %collective-permute-done.14.p2 = bf16[4,240,384]{2,1,0:T(8,128)(2,1)S(1)} collective-permute-done((bf16[4,240,384]{2,1,0:T(8,128)(2,1)S(1)}, bf16[4,240,384]{2,1,0:T(8,128)(2,1)S(1)}, u32[]{:S(2)}, u32[]{:S(2)}) %collective-permute-start.14) | collective-permute-done | bytes 737312 | tf_op jit(solution)/shard_map/ppermute | solution.py:922
  83.1 36.2 %ffn_both.1 = (bf16[512,768]{1,0:T(8,128)(2,1)}, bf16[256,768]{1,0:T(8,128)(2,1)}, bf16[4,4,240,384]{3,2,1,0:T(8,128)(2,1)}, bf16[4,240,384]{2,1,0:T(8,128)(2,1)...) custom-call(s32[2]{0:T(128)} %pad_add_fusion.place, ...), custom_call_target="tpu_custom_call" | custom-call | flops 60000002048 | bytes 1048576 | tf_op jit(solution)/shard_map/ffn_both/pallas_call | solution.py:840
  122.8 3.0 %fusion.1 = (bf16[4,240,384]{2,1,0:T(8,128)(2,1)}, bf16[4,240,384]{2,1,0:T(8,128)(2,1)}) fusion(bf16[4,240,384]{2,1,0:T(8,128)(2,1)S(1)} %collective-permute-done.23, bf16[4,4,240,384]{3,2,1,0:T(8,128)(2,1)} %get-tuple-element.124, bf16[4,240,384]{2,1,0:T(8,128)(2,1)S(1)} %collective-permute-done.22), kind=kLoop, calls=%fused_computation.3 | loop fusion | flops 2949120 | bytes 4423680 | tf_op jit(solution)/shard_map/convert_element_type | solution.py:941
  130.6 28.9 %mixer_backward.1 = (bf16[4,4,192,256]{3,2,1,0:T(8,128)(2,1)}, bf16[4,192,256]{2,1,0:T(8,128)(2,1)}, bf16[4,192,256]{2,1,0:T(8,128)(2,1)}, bf16[4,192,256]{2,1,0...) custom-call(s32[2]{0:T(128)} %pad_add_fusion.place, ...), custom_call_target="tpu_custom_call" | custom-call | flops 40000000000 | bytes 1048576 | tf_op jit(solution)/shard_map/mixer_backward/pallas_call | solution.py:840
  162.0 2.0 fusion.6
  172.6 9.9 %input_gradient.1 = (bf16[512,768]{1,0:T(8,128)(2,1)}, bf16[256,768]{1,0:T(8,128)(2,1)}) custom-call(s32[2]{0:T(128)} %pad_add_fusion.place, s32[1]{0:T(128)S(6)} %copy.34.llen, s32[2]{0:T(128)} %slen.5, f32[24,768]{1,0:T(8,128)} %get-tuple-element.112.vec, bf16[768,1536]{1,0:T(8,128)(2,1)} %get-tuple-element.160.grads_any, ...), custom_call_target="tpu_custom_call" | custom-call | flops 5000000000 | bytes 1048576 | tf_op jit(solution)/shard_map/input_gradient/pallas_call | solution.py:840
  182.6 2.1 collective-permute-start.42
  188.7 2.7 %collective-permute-done.42 = bf16[240,384]{1,0:T(8,128)(2,1)S(1)} collective-permute-done((bf16[240,384]{1,0:T(8,128)(2,1)S(1)}, bf16[240,384]{1,0:T(8,128)(2,1)S(1)}, u32[]{:S(2)}, u32[]{:S(2)}) %collective-permute-start.42) | collective-permute-done | bytes 184352 | tf_op jit(solution)/shard_map/ppermute | solution.py:918
  196.2 2.4 %collective-permute-start.37 = (bf16[192,256]{1,0:T(8,128)(2,1)S(1)}, bf16[192,256]{1,0:T(8,128)(2,1)S(1)}, u32[]{:S(2)}, u32[]{:S(2)}) collective-permute-start(bf16[192,256]{1,0:T(8,128)(2,1)S(1)} %get-tuple-element.202), channel_id=1, source_target_pairs={{0,2},{1,3},{2,0},{3,1},{4,6},{5,7},{6,4},{7,5},{8,10},{9,11},{10,... | collective-permute-start | bytes 294920 | tf_op jit(solution)/shard_map/ppermute | solution.py:918
  198.6 3.5 %collective-permute-done.38 = bf16[192,256]{1,0:T(8,128)(2,1)S(1)} collective-permute-done((bf16[192,256]{1,0:T(8,128)(2,1)S(1)}, bf16[192,256]{1,0:T(8,128)(2,1)S(1)}, u32[]{:S(2)}, u32[]{:S(2)}) %collective-permute-start.38) | collective-permute-done | bytes 98336 | tf_op jit(solution)/shard_map/ppermute | solution.py:918
  203.1 2.0 collective-permute-done.37
  209.8 2.3 %unpack_ffn.1 = (f32[2,96,1536]{2,1,0:T(8,128)}, f32[2,384,384]{2,1,0:T(8,128)}, f32[192,768]{1,0:T(8,128)}) custom-call(s32[2]{0:T(128)S(1)} %copy-done, bf16[240,384]{1,0:T(8,128)(2,1)S(1)} %add_convert_fusion.p0, bf16[240,384]{1,0:T(8,128)(2,1)S(1)} %collective-permute-done.43.p1, bf16[240,384]{1,0:T(8,128)(2,1)S(1)} %collective-permute-done.44.p2, ...), custom_call_target="tpu_custom_call" | custom-call | flops 1000000000 | bytes 1048576 | tf_op jit(solution)/shard_map/unpack_ffn/pallas_call | solution.py:840
  215.6 1.8 unpack_mixer.1
  (142 shorter events, 53.5 us)
Async XLA Ops:
  3.8 9.0 %collective-permute-start.2 = (bf16[192,256]{1,0:T(8,128)(2,1)}, bf16[192,256]{1,0:T(8,128)(2,1)S(1)}, u32[]{:S(2)}, u32[]{:S(2)}) collective-permute-start(bf16[192,256]{1,0:T(8,128)(2,1)} %get-tuple-element.104), channel_id=1, source_target_pairs={{0,3},{1,2},{2,1},{3,0},{4,7},{5,6},{6,5},{7,4},{8,11},{9,10},{10,... | collective-permute-start | bytes 294920 | tf_op jit(solution)/shard_map/ppermute | solution.py:918
  18.3 9.2 %collective-permute-start.8 = (bf16[240,384]{1,0:T(8,128)(2,1)}, bf16[240,384]{1,0:T(8,128)(2,1)S(1)}, u32[]{:S(2)}, u32[]{:S(2)}) collective-permute-start(bf16[240,384]{1,0:T(8,128)(2,1)} %get-tuple-element.107), channel_id=1, source_target_pairs={{0,3},{1,2},{2,1},{3,0},{4,7},{5,6},{6,5},{7,4},{8,11},{9,10},{10,... | collective-permute-start | bytes 552968 | tf_op jit(solution)/shard_map/ppermute | solution.py:918
  20.9 18.3 %collective-permute-start.5 = (bf16[4,192,256]{2,1,0:T(8,128)(2,1)S(1)}, bf16[4,192,256]{2,1,0:T(8,128)(2,1)S(1)}, u32[]{:S(2)}, u32[]{:S(2)}) collective-permute-start(bf16[4,192,256]{2,1,0:T(8,128)(2,1)S(1)} %pad_maximum_fusion.1.p0), channel_id=1, source_target_pairs={{0,24},{4,28},{8,16},{12,20},{16,8},{20,12},{24,0},{28,4},{1,25},{... | collective-permute-start | bytes 1179656 | tf_op jit(solution)/shard_map/ppermute | solution.py:922
  23.4 16.3 %collective-permute-start.4 = (bf16[4,192,256]{2,1,0:T(8,128)(2,1)S(1)}, bf16[4,192,256]{2,1,0:T(8,128)(2,1)S(1)}, u32[]{:S(2)}, u32[]{:S(2)}) collective-permute-start(bf16[4,192,256]{2,1,0:T(8,128)(2,1)S(1)} %pad_maximum_fusion.1.p0), channel_id=1, source_target_pairs={{0,16},{4,20},{8,24},{12,28},{16,0},{20,4},{24,8},{28,12},{1,17},{... | collective-permute-start | bytes 1179656 | tf_op jit(solution)/shard_map/ppermute | solution.py:922
  23.9 15.9 %collective-permute-start.3 = (bf16[4,192,256]{2,1,0:T(8,128)(2,1)S(1)}, bf16[4,192,256]{2,1,0:T(8,128)(2,1)S(1)}, u32[]{:S(2)}, u32[]{:S(2)}) collective-permute-start(bf16[4,192,256]{2,1,0:T(8,128)(2,1)S(1)} %pad_maximum_fusion.1.p0), channel_id=1, source_target_pairs={{0,8},{4,12},{8,0},{12,4},{16,24},{20,28},{24,16},{28,20},{1,9},{5... | collective-permute-start | bytes 1179656 | tf_op jit(solution)/shard_map/ppermute | solution.py:922
  24.4 11.6 %collective-permute-start.7 = (bf16[240,384]{1,0:T(8,128)(2,1)}, bf16[240,384]{1,0:T(8,128)(2,1)S(1)}, u32[]{:S(2)}, u32[]{:S(2)}) collective-permute-start(bf16[240,384]{1,0:T(8,128)(2,1)} %get-tuple-element.107), channel_id=1, source_target_pairs={{0,2},{1,3},{2,0},{3,1},{4,6},{5,7},{6,4},{7,5},{8,10},{9,11},{10,... | collective-permute-start | bytes 552968 | tf_op jit(solution)/shard_map/ppermute | solution.py:918
  27.6 10.6 %collective-permute-start.6 = (bf16[240,384]{1,0:T(8,128)(2,1)}, bf16[240,384]{1,0:T(8,128)(2,1)S(1)}, u32[]{:S(2)}, u32[]{:S(2)}) collective-permute-start(bf16[240,384]{1,0:T(8,128)(2,1)} %get-tuple-element.107), channel_id=1, source_target_pairs={{0,1},{1,0},{2,3},{3,2},{4,5},{5,4},{6,7},{7,6},{8,9},{9,8},{10,11... | collective-permute-start | bytes 552968 | tf_op jit(solution)/shard_map/ppermute | solution.py:918
  41.5 30.1 %collective-permute-start.15 = (bf16[4,240,384]{2,1,0:T(8,128)(2,1)S(1)}, bf16[4,240,384]{2,1,0:T(8,128)(2,1)S(1)}, u32[]{:S(2)}, u32[]{:S(2)}) collective-permute-start(bf16[4,240,384]{2,1,0:T(8,128)(2,1)S(1)} %pad_maximum_fusion.p0), channel_id=1, source_target_pairs={{0,24},{4,28},{8,16},{12,20},{16,8},{20,12},{24,0},{28,4},{1,25},{... | collective-permute-start | bytes 2211848 | tf_op jit(solution)/shard_map/ppermute | solution.py:922
  43.6 33.1 %collective-permute-start.14 = (bf16[4,240,384]{2,1,0:T(8,128)(2,1)S(1)}, bf16[4,240,384]{2,1,0:T(8,128)(2,1)S(1)}, u32[]{:S(2)}, u32[]{:S(2)}) collective-permute-start(bf16[4,240,384]{2,1,0:T(8,128)(2,1)S(1)} %pad_maximum_fusion.p0), channel_id=1, source_target_pairs={{0,16},{4,20},{8,24},{12,28},{16,0},{20,4},{24,8},{28,12},{1,17},{... | collective-permute-start | bytes 2211848 | tf_op jit(solution)/shard_map/ppermute | solution.py:922
  44.5 32.3 %collective-permute-start.13 = (bf16[4,240,384]{2,1,0:T(8,128)(2,1)S(1)}, bf16[4,240,384]{2,1,0:T(8,128)(2,1)S(1)}, u32[]{:S(2)}, u32[]{:S(2)}) collective-permute-start(bf16[4,240,384]{2,1,0:T(8,128)(2,1)S(1)} %pad_maximum_fusion.p0), channel_id=1, source_target_pairs={{0,8},{4,12},{8,0},{12,4},{16,24},{20,28},{24,16},{28,20},{1,9},{5... | collective-permute-start | bytes 2211848 | tf_op jit(solution)/shard_map/ppermute | solution.py:922
  119.8 8.9 %collective-permute-start.20 = (bf16[4,240,384]{2,1,0:T(8,128)(2,1)}, bf16[4,240,384]{2,1,0:T(8,128)(2,1)S(1)}, u32[]{:S(2)}, u32[]{:S(2)}) collective-permute-start(bf16[4,240,384]{2,1,0:T(8,128)(2,1)} %get-tuple-element.125), channel_id=1, source_target_pairs={{0,4},{4,0},{8,12},{12,8},{16,20},{20,16},{24,28},{28,24},{1,5},{5... | collective-permute-start | bytes 2211848 | tf_op jit(solution)/shard_map/ppermute | solution.py:922
  120.0 8.8 %collective-permute-start.21 = (bf16[4,240,384]{2,1,0:T(8,128)(2,1)}, bf16[4,240,384]{2,1,0:T(8,128)(2,1)S(1)}, u32[]{:S(2)}, u32[]{:S(2)}) collective-permute-start(bf16[4,240,384]{2,1,0:T(8,128)(2,1)} %get-tuple-element.126), channel_id=1, source_target_pairs={{0,4},{4,0},{8,12},{12,8},{16,20},{20,16},{24,28},{28,24},{1,5},{5... | collective-permute-start | bytes 2211848 | tf_op jit(solution)/shard_map/ppermute | solution.py:922
  125.8 38.3 %collective-permute-start.26 = (bf16[4,240,384]{2,1,0:T(8,128)(2,1)}, bf16[4,240,384]{2,1,0:T(8,128)(2,1)S(1)}, u32[]{:S(2)}, u32[]{:S(2)}) collective-permute-start(bf16[4,240,384]{2,1,0:T(8,128)(2,1)} %get-tuple-element.198), channel_id=1, source_target_pairs={{0,8},{4,12},{8,0},{12,4},{16,24},{20,28},{24,16},{28,20},{1,9},{5... | collective-permute-start | bytes 2211848 | tf_op jit(solution)/shard_map/ppermute | solution.py:922
  127.3 36.8 %collective-permute-start.28 = (bf16[4,240,384]{2,1,0:T(8,128)(2,1)}, bf16[4,240,384]{2,1,0:T(8,128)(2,1)S(1)}, u32[]{:S(2)}, u32[]{:S(2)}) collective-permute-start(bf16[4,240,384]{2,1,0:T(8,128)(2,1)} %get-tuple-element.199), channel_id=1, source_target_pairs={{0,24},{4,28},{8,16},{12,20},{16,8},{20,12},{24,0},{28,4},{1,25},{... | collective-permute-start | bytes 2211848 | tf_op jit(solution)/shard_map/ppermute | solution.py:922
  130.1 34.0 %collective-permute-start.27 = (bf16[4,240,384]{2,1,0:T(8,128)(2,1)}, bf16[4,240,384]{2,1,0:T(8,128)(2,1)S(1)}, u32[]{:S(2)}, u32[]{:S(2)}) collective-permute-start(bf16[4,240,384]{2,1,0:T(8,128)(2,1)} %get-tuple-element.196), channel_id=1, source_target_pairs={{0,16},{4,20},{8,24},{12,28},{16,0},{20,4},{24,8},{28,12},{1,17},{... | collective-permute-start | bytes 2211848 | tf_op jit(solution)/shard_map/ppermute | solution.py:922
  164.7 17.9 %collective-permute-start.33 = (bf16[4,192,256]{2,1,0:T(8,128)(2,1)}, bf16[4,192,256]{2,1,0:T(8,128)(2,1)}, u32[]{:S(2)}, u32[]{:S(2)}) collective-permute-start(bf16[4,192,256]{2,1,0:T(8,128)(2,1)} %get-tuple-element.152), channel_id=1, source_target_pairs={{0,8},{4,12},{8,0},{12,4},{16,24},{20,28},{24,16},{28,20},{1,9},{5... | collective-permute-start | bytes 1179656 | tf_op jit(solution)/shard_map/ppermute | solution.py:922
  166.1 18.5 %collective-permute-start.34 = (bf16[4,192,256]{2,1,0:T(8,128)(2,1)S(1)}, bf16[4,192,256]{2,1,0:T(8,128)(2,1)}, u32[]{:S(2)}, u32[]{:S(2)}) collective-permute-start(bf16[4,192,256]{2,1,0:T(8,128)(2,1)S(1)} %get-tuple-element.153), channel_id=1, source_target_pairs={{0,16},{4,20},{8,24},{12,28},{16,0},{20,4},{24,8},{28,12},{1,17},{... | collective-permute-start | bytes 1179656 | tf_op jit(solution)/shard_map/ppermute | solution.py:922
  167.9 17.6 %collective-permute-start.35 = (bf16[4,192,256]{2,1,0:T(8,128)(2,1)}, bf16[4,192,256]{2,1,0:T(8,128)(2,1)}, u32[]{:S(2)}, u32[]{:S(2)}) collective-permute-start(bf16[4,192,256]{2,1,0:T(8,128)(2,1)} %get-tuple-element.203), channel_id=1, source_target_pairs={{0,24},{4,28},{8,16},{12,20},{16,8},{20,12},{24,0},{28,4},{1,25},{... | collective-permute-start | bytes 1179656 | tf_op jit(solution)/shard_map/ppermute | solution.py:922
  170.3 14.4 %collective-permute-start.32 = (bf16[240,384]{1,0:T(8,128)(2,1)}, bf16[240,384]{1,0:T(8,128)(2,1)S(1)}, u32[]{:S(2)}, u32[]{:S(2)}) collective-permute-start(bf16[240,384]{1,0:T(8,128)(2,1)} %get-tuple-element.194), channel_id=1, source_target_pairs={{0,2},{1,3},{2,0},{3,1},{4,6},{5,7},{6,4},{7,5},{8,10},{9,11},{10,... | collective-permute-start | bytes 552968 | tf_op jit(solution)/shard_map/ppermute | solution.py:918
  171.0 13.7 %collective-permute-start.31 = (bf16[240,384]{1,0:T(8,128)(2,1)}, bf16[240,384]{1,0:T(8,128)(2,1)S(1)}, u32[]{:S(2)}, u32[]{:S(2)}) collective-permute-start(bf16[240,384]{1,0:T(8,128)(2,1)} %get-tuple-element.195), channel_id=1, source_target_pairs={{0,1},{1,0},{2,3},{3,2},{4,5},{5,4},{6,7},{7,6},{8,9},{9,8},{10,11... | collective-permute-start | bytes 552968 | tf_op jit(solution)/shard_map/ppermute | solution.py:918
  186.9 9.2 %collective-permute-start.36 = (bf16[192,256]{1,0:T(8,128)(2,1)S(1)}, bf16[192,256]{1,0:T(8,128)(2,1)S(1)}, u32[]{:S(2)}, u32[]{:S(2)}) collective-permute-start(bf16[192,256]{1,0:T(8,128)(2,1)S(1)} %get-tuple-element.200), channel_id=1, source_target_pairs={{0,1},{1,0},{2,3},{3,2},{4,5},{5,4},{6,7},{7,6},{8,9},{9,8},{10,11... | collective-permute-start | bytes 294920 | tf_op jit(solution)/shard_map/ppermute | solution.py:918
  191.4 10.6 %collective-permute-start.45 = (bf16[240,384]{1,0:T(8,128)(2,1)S(1)}, bf16[240,384]{1,0:T(8,128)(2,1)S(1)}, u32[]{:S(2)}, u32[]{:S(2)}) collective-permute-start(bf16[240,384]{1,0:T(8,128)(2,1)S(1)} %add_convert_fusion.p0), channel_id=1, source_target_pairs={{0,24},{4,28},{8,16},{12,20},{16,8},{20,12},{24,0},{28,4},{1,25},{... | collective-permute-start | bytes 552968 | tf_op jit(solution)/shard_map/ppermute | solution.py:922
  192.9 9.7 %collective-permute-start.44 = (bf16[240,384]{1,0:T(8,128)(2,1)S(1)}, bf16[240,384]{1,0:T(8,128)(2,1)S(1)}, u32[]{:S(2)}, u32[]{:S(2)}) collective-permute-start(bf16[240,384]{1,0:T(8,128)(2,1)S(1)} %add_convert_fusion.p0), channel_id=1, source_target_pairs={{0,16},{4,20},{8,24},{12,28},{16,0},{20,4},{24,8},{28,12},{1,17},{... | collective-permute-start | bytes 552968 | tf_op jit(solution)/shard_map/ppermute | solution.py:922
  196.2 8.9 %collective-permute-start.37 = (bf16[192,256]{1,0:T(8,128)(2,1)S(1)}, bf16[192,256]{1,0:T(8,128)(2,1)S(1)}, u32[]{:S(2)}, u32[]{:S(2)}) collective-permute-start(bf16[192,256]{1,0:T(8,128)(2,1)S(1)} %get-tuple-element.202), channel_id=1, source_target_pairs={{0,2},{1,3},{2,0},{3,1},{4,6},{5,7},{6,4},{7,5},{8,10},{9,11},{10,... | collective-permute-start | bytes 294920 | tf_op jit(solution)/shard_map/ppermute | solution.py:918
  (50 other events, 305.1 us)
